TPU v7x, 128 devices: a whole 4x4x4 slice. The times are simulated.
128 devices in a mesh: req: 32 (over y, z, core), grp: 4 (over x).
Axes of the slice: x: 4, y: 4, z: 4, core: 2. Of those that a mesh axis runs over, the one named last changes fastest.
Arguments:
- hidden_in: bfloat16 [16384, 2048], P('req'), may hold values from -6 to 6
- attn_gain: float32 [2048], replicated, may hold values from 0.1 to 1.9
- mlp_gain: float32 [2048], replicated, may hold values from 0.1 to 1.9
- w_query: bfloat16 [2048, 2048], P(None, 'grp'), may hold values from -0.75 to 0.75
- w_key: bfloat16 [2048, 512], P(None, 'grp'), may hold values from -0.125 to 0.125
- w_value: bfloat16 [2048, 512], P(None, 'grp'), may hold values from -0.125 to 0.125
- w_out: bfloat16 [2048, 2048], P('grp'), may hold values from -0.125 to 0.125
- w_gate: bfloat16 [2048, 8192], P(None, 'req'), may hold values from -0.125 to 0.125
- w_up: bfloat16 [2048, 8192], P(None, 'req'), may hold values from -0.125 to 0.125
- w_down: bfloat16 [8192, 2048], P('req'), may hold values from -0.0625 to 0.0625
- cache_k: bfloat16 [16384, 16, 512], P('req', None, 'grp'), may hold values from -4000 to 4000
- cache_v: bfloat16 [16384, 16, 512], P('req', None, 'grp'), may hold values from -6 to 6
- owner_of_row: int32 [16384], P('req'), may hold values from 0 to 31, as said below
- new_len: int32 [32, 32], P('req'), may hold values from 0 to 32, as said below
- prior_len: int32 [32, 32], P('req'), may hold values from 0 to 256, as said below
- page_table: int32 [32, 512], P('req'), may hold values from 0 to 511, each once within a row
Outputs:
- layer_out: bfloat16 [16384, 2048], P(('req', 'grp'))
- new_cache_k: bfloat16 [16384, 16, 512], P('req', None, 'grp')
- new_cache_v: bfloat16 [16384, 16, 512], P('req', None, 'grp')
Inputs may be any that keep to these rules, and one draw needn't show every extreme that they name: `owner_of_row`: rows of one block of 512 that name the same owner are consecutive; each block holds at most one request for each owner, of at most 32 rows; in every draw one owner receives a request of exactly 32 rows from every block. new_len[o, s] is the number of rows of block s of owner_of_row that name o. prior_len[o, s] + new_len[o, s] <= 256.
All inputs are finite; a program needn't handle non-finite values.
Results may differ from a plain program's by a relative error of at most 0.0063.
Values may be sent and summed in bfloat16 or wider, within the bound.
A program may use at most 128 MiB of HBM per device.

v0:
```python
import jax
import jax.numpy as jnp
from jax import lax
from jax.experimental import pallas as pl
from jax.experimental.pallas import tpu as pltpu
from jax.sharding import Mesh, PartitionSpec as P

HD = 64
PAGE = 16
MAXP = 16
CONTEXT = 256


EPSILON = 1e-05
RESIDUAL_MULT = 0.22
SCORE_MULT = 0.015625
ROPE_BASE = 10000000.0


def normalize(values, gain):
    mean_square = jnp.mean(values * values, axis=-1, keepdims=True)
    return values * lax.rsqrt(mean_square + EPSILON) * gain


def rotary(values, positions):
    dim = values.shape[-1]
    half = dim // 2
    freq = jnp.power(ROPE_BASE, -2.0 * jnp.arange(half, dtype=jnp.int32).astype(jnp.float32) / dim)
    angle = positions.astype(jnp.float32)[:, :, None] * freq
    cosine = jnp.cos(angle)[:, :, None, :]
    sine = jnp.sin(angle)[:, :, None, :]
    first = values[..., :half].astype(jnp.float32)
    second = values[..., half:].astype(jnp.float32)
    return jnp.concatenate(
        [first * cosine - second * sine, second * cosine + first * sine], axis=-1
    )


def source_layout(owner_block, peers, pair_rows):
    row_count = owner_block.shape[0]
    owners = jnp.arange(peers, dtype=jnp.int32)
    member = owner_block[None, :] == owners[:, None]
    counts = jnp.sum(member.astype(jnp.int32), axis=1)
    row_ids = jnp.arange(row_count, dtype=jnp.int32)
    starts = jnp.min(jnp.where(member, row_ids[None, :], row_count), axis=1)
    slots = jnp.arange(pair_rows, dtype=jnp.int32)
    gather_rows = jnp.where(
        slots[None, :] < counts[:, None], starts[:, None] + slots[None, :], row_count
    )
    row_start = jnp.sum(jnp.where(member, starts[:, None], 0), axis=0)
    back_rows = owner_block * pair_rows + (row_ids - row_start)
    return (gather_rows.reshape(-1), back_rows)


def attention_kernel(table_ref, prior_ref, len_ref, q_ref, k_ref, v_ref, ck_ref, cv_ref,
                     out_ref, nk_ref, nv_ref, kbuf, vbuf):
    sources, pair_rows, qcols = q_ref.shape
    kcols = k_ref.shape[-1]
    kv_heads = kcols // HD
    group = qcols // kcols

    def per_source(s, carry):
        prior = prior_ref[s]
        length = len_ref[s]
        for i in range(MAXP):
            page = table_ref[s * MAXP + i]
            kbuf[i * PAGE:(i + 1) * PAGE, :] = ck_ref[page]
            vbuf[i * PAGE:(i + 1) * PAGE, :] = cv_ref[page]
        j_col = lax.broadcasted_iota(jnp.int32, (CONTEXT, pair_rows), 0)
        t_row = lax.broadcasted_iota(jnp.int32, (CONTEXT, pair_rows), 1)
        select = jnp.logical_and(j_col == prior + t_row, t_row < length).astype(jnp.bfloat16)
        j_only = lax.broadcasted_iota(jnp.int32, (CONTEXT, kcols), 0)
        fresh = jnp.logical_and(j_only >= prior, j_only < prior + length)
        k_new = jnp.dot(select, k_ref[s], preferred_element_type=jnp.float32).astype(jnp.bfloat16)
        v_new = jnp.dot(select, v_ref[s], preferred_element_type=jnp.float32).astype(jnp.bfloat16)
        keys = jnp.where(fresh, k_new, kbuf[...])
        values = jnp.where(fresh, v_new, vbuf[...])
        for i in range(MAXP):
            page = table_ref[s * MAXP + i]
            nk_ref[page] = keys[i * PAGE:(i + 1) * PAGE, :]
            nv_ref[page] = values[i * PAGE:(i + 1) * PAGE, :]
        q_all = q_ref[s]
        rows = group * pair_rows
        r_idx = lax.broadcasted_iota(jnp.int32, (rows, CONTEXT), 0)
        j_idx = lax.broadcasted_iota(jnp.int32, (rows, CONTEXT), 1)
        allowed = j_idx <= prior + r_idx % pair_rows
        for h in range(kv_heads):
            q_h = jnp.concatenate(
                [q_all[:, (h * group + g) * HD:(h * group + g + 1) * HD] for g in range(group)],
                axis=0,
            )
            k_h = keys[:, h * HD:(h + 1) * HD]
            v_h = values[:, h * HD:(h + 1) * HD]
            scores = lax.dot_general(
                q_h, k_h, (((1,), (1,)), ((), ())), preferred_element_type=jnp.float32
            ) * SCORE_MULT
            scores = jnp.where(allowed, scores, -jnp.inf)
            top = jnp.max(scores, axis=-1, keepdims=True)
            weights = jnp.exp(scores - top)
            probs = (weights / jnp.sum(weights, axis=-1, keepdims=True)).astype(jnp.bfloat16)
            mixed = jnp.dot(probs, v_h, preferred_element_type=jnp.float32).astype(jnp.bfloat16)
            for g in range(group):
                c = h * group + g
                out_ref[s, :, c * HD:(c + 1) * HD] = mixed[g * pair_rows:(g + 1) * pair_rows, :]
        return carry

    lax.fori_loop(0, sources, per_source, 0)


def owner_attention(query_in, key_in, value_in, cache_keys, cache_values, lengths, priors, table):
    sources, pair_rows, qcols = query_in.shape
    kcols = key_in.shape[-1]
    kv_heads = kcols // HD
    slots = jnp.arange(pair_rows, dtype=jnp.int32)
    positions = priors[:, None] + slots[None, :]
    query_rot = rotary(query_in.reshape(sources, pair_rows, qcols // HD, HD), positions).astype(
        jnp.bfloat16
    ).reshape(sources, pair_rows, qcols)
    key_rot = rotary(key_in.reshape(sources, pair_rows, kv_heads, HD), positions).astype(
        jnp.bfloat16
    ).reshape(sources, pair_rows, kcols)
    pool_pages = cache_keys.shape[0]
    smem = pl.BlockSpec(memory_space=pltpu.SMEM)
    vmem = pl.BlockSpec(memory_space=pltpu.VMEM)
    return pl.pallas_call(
        attention_kernel,
        out_shape=(
            jax.ShapeDtypeStruct((sources, pair_rows, qcols), jnp.bfloat16),
            jax.ShapeDtypeStruct(cache_keys.shape, cache_keys.dtype),
            jax.ShapeDtypeStruct(cache_values.shape, cache_values.dtype),
        ),
        in_specs=[smem, smem, smem, vmem, vmem, vmem, vmem, vmem],
        out_specs=(vmem, vmem, vmem),
        scratch_shapes=[
            pltpu.VMEM((CONTEXT, kcols), jnp.bfloat16),
            pltpu.VMEM((CONTEXT, kcols), jnp.bfloat16),
        ],
        compiler_params=pltpu.CompilerParams(vmem_limit_bytes=48 * 1024 * 1024),
    )(table, priors, lengths, query_rot, key_rot, value_in, cache_keys, cache_values)


def body(
    hidden_in,
    attn_gain,
    mlp_gain,
    w_query,
    w_key,
    w_value,
    w_out,
    w_gate,
    w_up,
    w_down,
    cache_k,
    cache_v,
    owner_of_row,
    new_len,
    prior_len,
    page_table,
):
    peers = lax.axis_size(REQ)
    groups = lax.axis_size("grp")
    row_count = hidden_in.shape[0]
    pair_rows = 2 * row_count // peers
    quarter = row_count // groups
    group_index = lax.axis_index("grp")
    gate_w = lax.all_gather(w_gate, "ry", axis=1, tiled=True)
    up_w = lax.all_gather(w_up, "ry", axis=1, tiled=True)
    down_w = lax.all_gather(w_down, "ry", axis=0, tiled=True)
    normed = normalize(hidden_in.astype(jnp.float32), attn_gain).astype(jnp.bfloat16)
    qcols = w_query.shape[1]
    kcols = w_key.shape[1]
    query_rows = jnp.dot(normed, w_query, preferred_element_type=jnp.float32).astype(jnp.bfloat16)
    key_rows = jnp.dot(normed, w_key, preferred_element_type=jnp.float32).astype(jnp.bfloat16)
    value_rows = jnp.dot(normed, w_value, preferred_element_type=jnp.float32).astype(jnp.bfloat16)
    qkv_rows = jnp.concatenate([query_rows, key_rows, value_rows], axis=1)
    gather_rows, back_rows = source_layout(owner_of_row, peers, pair_rows)
    send_qkv = jnp.take(qkv_rows, gather_rows, axis=0, mode="fill", fill_value=0).reshape(
        peers, pair_rows, -1
    )
    recv_qkv = lax.all_to_all(send_qkv, REQ, split_axis=0, concat_axis=0, tiled=True)
    recv_query = recv_qkv[..., :qcols]
    recv_key = recv_qkv[..., qcols : qcols + kcols]
    recv_value = recv_qkv[..., qcols + kcols :]
    mixed, keys_out, values_out = owner_attention(
        recv_query, recv_key, recv_value, cache_k, cache_v, new_len[0], prior_len[0], page_table[0]
    )
    gate_w, up_w, down_w, mixed = lax.optimization_barrier((gate_w, up_w, down_w, mixed))
    returned = lax.all_to_all(mixed, REQ, split_axis=0, concat_axis=0, tiled=True)
    attn_rows = jnp.take(returned.reshape(peers * pair_rows, -1), back_rows, axis=0)
    projected = jnp.dot(attn_rows, w_out, preferred_element_type=jnp.float32)
    attn_part = lax.psum_scatter(
        projected.astype(jnp.bfloat16), "grp", scatter_dimension=0, tiled=True
    ).astype(jnp.float32)
    own_rows = lax.dynamic_slice_in_dim(hidden_in, group_index * quarter, quarter, 0).astype(
        jnp.float32
    )
    residual = own_rows + RESIDUAL_MULT * attn_part
    mlp_in = normalize(residual, mlp_gain).astype(jnp.bfloat16)
    piece = lax.all_gather(mlp_in, "rzc", axis=0, tiled=True)
    gate = jnp.dot(piece, gate_w, preferred_element_type=jnp.float32)
    upper = jnp.dot(piece, up_w, preferred_element_type=jnp.float32)
    hidden = (jax.nn.silu(gate) * upper).astype(jnp.bfloat16)
    down = lax.psum_scatter(
        jnp.dot(hidden, down_w, preferred_element_type=jnp.float32).astype(jnp.bfloat16),
        "rzc",
        scatter_dimension=0,
        tiled=True,
    ).astype(jnp.float32)
    layer_out = (residual + RESIDUAL_MULT * down).astype(jnp.bfloat16)
    return (layer_out, keys_out, values_out)


REQ = ("ry", "rzc")


def solution(mesh):
    req_size = mesh.shape["req"]
    major = 4
    inner = Mesh(
        mesh.devices.reshape(major, req_size // major, mesh.shape["grp"]), ("ry", "rzc", "grp")
    )
    in_specs = (
        P(REQ, None),
        P(),
        P(),
        P(None, "grp"),
        P(None, "grp"),
        P(None, "grp"),
        P("grp", None),
        P(None, REQ),
        P(None, REQ),
        P(REQ, None),
        P(REQ, None, "grp"),
        P(REQ, None, "grp"),
        P(REQ),
        P(REQ, None),
        P(REQ, None),
        P(REQ, None),
    )
    out_specs = (P(REQ + ("grp",), None), P(REQ, None, "grp"), P(REQ, None, "grp"))
    return jax.shard_map(body, mesh=inner, in_specs=in_specs, out_specs=out_specs, check_vma=False)
```

profile of v0, /device:TPU:0, one launch (start us, length us, event | category | flops | bytes accessed | tf_op | source)
XLA Modules:
  0.0 351.6 jit_solution(8313054732930916009)
XLA Ops:
  7.2 0.7 all-gather.5.cloned.1.call-update
  8.0 0.7 all-gather.7.cloned.1.call-update
  8.7 0.7 all-gather.9.cloned.1.call-update
  9.4 0.8 select_reduce_fusion.1
  10.2 0.9 select_reduce_fusion
  11.2 0.1 select_n.66
  11.3 2.2 fusion
  13.5 2.7 convolution_convert_fusion.4
  16.2 0.9 convolution_convert_fusion.3
  17.2 1.4 convolution_convert_fusion.2
  18.6 0.9 pad_maximum_fusion.1
  19.6 1.4 copy.21
  21.0 5.2 %gather_fusion = bf16[1024,768]{1,0:T(8,128)(2,1)} fusion(bf16[512,768]{1,0:T(8,128)(2,1)S(1)} %copy.21, s32[1024]{0:T(1024)S(1)} %broadcast_clamp_fusion), kind=kCustom, calls=%fused_computation | custom fusion | bytes 3149824 | tf_op jit(solution)/shard_map/jit(_take)/gather | solution.py:177
  26.3 2.8 broadcast_select_fusion
  29.1 8.8 %all-to-all-start = ((bf16[32,32,768]{2,1,0:T(8,128)(2,1)}), bf16[32,32,768]{2,1,0:T(8,128)(2,1)}, u32[]{:S(2)}, u32[]{:S(2)}) async-start(bf16[32,32,768]{2,1,0:T(8,128)(2,1)} %broadcast_select_fusion), calls=%async_computation | async-start | bytes 3145728 | tf_op jit(solution)/shard_map/all_to_all | solution.py:180
  38.0 2.9 multiply_cosine_fusion
  40.9 30.3 %all-to-all-done = bf16[32,32,768]{2,1,0:T(8,128)(2,1)} async-done(((bf16[32,32,768]{2,1,0:T(8,128)(2,1)}), bf16[32,32,768]{2,1,0:T(8,128)(2,1)}, u32[]{:S(2)}, u32[]{:S(2)}) %all-to-all-start) | async-done | bytes 1572896 | tf_op jit(solution)/shard_map/all_to_all | solution.py:180
  71.2 1.8 fusion.19
  73.0 0.2 reshape.155
  73.2 1.0 fusion.20
  74.3 1.5 fusion.8
  75.8 0.3 pad_maximum_fusion.2
  76.0 1.3 copy.24
  77.4 1.3 convert_element_type.94.k_ref
  78.7 2.3 slice.32
  81.0 3.9 %reshape.154 = bf16[32,32,8,64]{3,2,1,0:T(8,128)(2,1)} reshape(bf16[32,32,512]{2,1,0:T(8,128)(2,1)} %slice.32) | data formatting | bytes 2097152 | tf_op jit(solution)/shard_map/reshape | solution.py:116
  84.9 4.2 %fusion.4 = (bf16[32,32,8,32]{3,2,1,0:T(8,128)(2,1)S(1)}, bf16[32,32,8,32]{3,2,1,0:T(8,128)(2,1)S(1)}) fusion(f32[32,32,32]{2,1,0:T(8,128)} %get-tuple-element.30, f32[32,32,32]{2,1,0:T(8,128)S(1)} %get-tuple-element.29, bf16[32,32,8,64]{3,2,1,0:T(8,128)(2,1)} %reshape.154), kind=kLoop, calls=%fused_computation.12 | loop fusion | flops 2621440 | bytes 2359296 | tf_op jit(solution)/shard_map/convert.2
  89.1 2.5 pad_maximum_fusion
  91.6 3.3 convert_element_type.91.q_ref
  94.9 1.6 copy-done.2
  96.6 1.0 copy-done.4
  97.5 28.7 %shard_map.175 = (bf16[32,32,512]{2,1,0:T(8,128)(2,1)S(1)}, bf16[512,16,128]{2,1,0:T(8,128)(2,1)}, bf16[512,16,128]{2,1,0:T(8,128)(2,1)}) custom-call(s32[512]{0:T(512)S(1)} %bitcast.17, s32[32]{0:T(128)S(1)} %bitcast.19, s32[32]{0:T(128)S(1)} %bitcast.20, bf16[32,32,512]{2,1,0:T(8,128)(2,1)S(1)} %convert_element_type.91.q_ref, ...), custom_call_target="tpu_custom_call" | custom-call | tf_op jit(solution)/shard_map/pallas_call | solution.py:125
  126.2 1.0 copy-done.3
  127.2 7.7 %all-gather.7.cloned.1.call-done = bf16[2048,1024]{1,0:T(8,128)(2,1)} async-done(((bf16[2048,256]{1,0:T(8,128)(2,1)}), bf16[2048,1024]{1,0:T(8,128)(2,1)}) %all-gather.7.cloned.1.call-update) | async-done | bytes 4194320 | tf_op jit(solution)/shard_map/all_gather | solution.py:167
  135.0 50.8 %all-gather.9.cloned.1.call-done = bf16[1024,2048]{1,0:T(8,128)(2,1)} async-done(((bf16[256,2048]{1,0:T(8,128)(2,1)}), bf16[1024,2048]{1,0:T(8,128)(2,1)}) %all-gather.9.cloned.1.call-update) | async-done | bytes 4194320 | tf_op jit(solution)/shard_map/all_gather | solution.py:168
  185.8 6.3 %all-to-all-start.1 = ((bf16[32,32,512]{2,1,0:T(8,128)(2,1)}), bf16[32,32,512]{2,1,0:T(8,128)(2,1)S(1)}, u32[]{:S(2)}, u32[]{:S(2)}) async-start(bf16[32,32,512]{2,1,0:T(8,128)(2,1)} %copy-done.3), calls=%async_computation.1 | async-start | bytes 2097152 | tf_op jit(solution)/shard_map/all_to_all | solution.py:188
  192.2 16.7 %all-to-all-done.1 = bf16[32,32,512]{2,1,0:T(8,128)(2,1)S(1)} async-done(((bf16[32,32,512]{2,1,0:T(8,128)(2,1)}), bf16[32,32,512]{2,1,0:T(8,128)(2,1)S(1)}, u32[]{:S(2)}, u32[]{:S(2)}) %all-to-all-start.1) | async-done | bytes 1048608 | tf_op jit(solution)/shard_map/all_to_all | solution.py:188
  208.9 2.6 gather_fusion.1
  211.6 3.7 %convolution_convert_fusion.1 = bf16[512,2048]{1,0:T(8,128)(2,1)} fusion(bf16[512,2048]{1,0:T(8,128)(2,1)S(1)} %copy-done, bf16[512,512]{1,0:T(8,128)(2,1)} %gather_fusion.1, pred[512]{0:T(512)(128)(4,1)S(1)} %get-tuple-element.19), kind=kOutput, calls=%fused_computation.17 | convolution fusion | flops 1075052544 | bytes 4719104 | tf_op jit(solution)/shard_map/dot_general | solution.py:190
  215.3 27.8 %reduce-scatter.3.cloned.1.call-done = bf16[128,2048]{1,0:T(8,128)(2,1)} async-done(((bf16[512,2048]{1,0:T(8,128)(2,1)}), bf16[128,2048]{1,0:T(8,128)(2,1)}) %reduce-scatter.3.cloned.1.call-update) | async-done | bytes 524304 | tf_op jit(solution)/shard_map/reduce_scatter | solution.py:191
  243.1 1.5 multiply_reduce_fusion
  244.6 2.2 multiply_convert_fusion.1
  246.9 0.3 reduce-scatter.5.cloned.1.call-start
  247.1 32.0 %all-gather.11.cloned.1.call-done = bf16[1024,2048]{1,0:T(8,128)(2,1)} async-done(((bf16[128,2048]{1,0:T(8,128)(2,1)}), bf16[1024,2048]{1,0:T(8,128)(2,1)}) %all-gather.11.cloned.1.call-update) | async-done | bytes 4194320 | tf_op jit(solution)/shard_map/all_gather | solution.py:199
  279.1 9.9 %fusion.21 = f32[1024,1024]{1,0:T(8,128)} fusion(bf16[1024,2048]{1,0:T(8,128)(2,1)} %all-gather.11.cloned.1.call-done, bf16[2048,1024]{1,0:T(8,128)(2,1)} %all-gather.5.cloned.1.call-done), kind=kOutput, calls=%fused_computation.63 | convolution fusion | flops 4294967296 | bytes 12582912 | tf_op jit(solution)/shard_map/dot_general | solution.py:200
  289.0 15.3 %convolution_convert_fusion = bf16[1024,2048]{1,0:T(8,128)(2,1)} fusion(bf16[1024,2048]{1,0:T(8,128)(2,1)} %all-gather.9.cloned.1.call-done, f32[1024,1024]{1,0:T(8,128)} %fusion.21, bf16[1024,2048]{1,0:T(8,128)(2,1)} %all-gather.11.cloned.1.call-done, bf16[2048,1024]{1,0:T(8,128)(2,1)} %all-gather.7.cloned.1.call-done), kind=kOutput, calls=%fused_computation.16 | convolution fusion | flops 8598323200 | bytes 20971520 | tf_op jit(solution)/shard_map/dot_general | solution.py:204
  304.3 38.1 %reduce-scatter.5.cloned.1.call-done = bf16[128,2048]{1,0:T(8,128)(2,1)} async-done(((bf16[1024,2048]{1,0:T(8,128)(2,1)}), bf16[128,2048]{1,0:T(8,128)(2,1)}) %reduce-scatter.5.cloned.1.call-update) | async-done | bytes 524304 | tf_op jit(solution)/shard_map/reduce_scatter | solution.py:203
  342.5 2.3 add_convert_fusion
  (48 shorter events, 0.6 us)
Async XLA Ops:
  7.2 204.4 %copy-start = (bf16[512,2048]{1,0:T(8,128)(2,1)S(1)}, bf16[512,2048]{1,0:T(8,128)(2,1)}, u32[]{:S(2)}) copy-start(bf16[512,2048]{1,0:T(8,128)(2,1)} %param.22) | copy-start | bytes 6291460
  7.2 6.3 %copy-start.15 = (f32[2048]{0:T(1024)S(1)}, f32[2048]{0:T(1024)}, u32[]{:S(2)}) copy-start(f32[2048]{0:T(1024)} %param.17) | copy-start | bytes 24580
  7.2 6.3 %copy-start.13 = (bf16[2048,128]{1,0:T(8,128)(2,1)S(1)}, bf16[2048,128]{1,0:T(8,128)(2,1)}, u32[]{:S(2)}) copy-start(bf16[2048,128]{1,0:T(8,128)(2,1)} %param.20) | copy-start | bytes 1572868
  7.2 120.0 %all-gather.5.cloned.1.call-start = ((), (), s32[]{:S(2)}) async-start(), calls=%async_computation.4 | async-start | bytes 5242880 | tf_op jit(solution)/shard_map/all_gather | solution.py:166
  7.9 8.3 %copy-start.14 = (bf16[2048,128]{1,0:T(8,128)(2,1)S(1)}, bf16[2048,128]{1,0:T(8,128)(2,1)}, u32[]{:S(2)}) copy-start(bf16[2048,128]{1,0:T(8,128)(2,1)} %param.21) | copy-start | bytes 1572868
  7.9 127.0 %all-gather.7.cloned.1.call-start = ((), (), s32[]{:S(2)}) async-start(), calls=%async_computation.5 | async-start | bytes 5242880 | tf_op jit(solution)/shard_map/all_gather | solution.py:167
  8.7 177.1 %all-gather.9.cloned.1.call-start = ((), (), s32[]{:S(2)}) async-start(), calls=%async_computation.6 | async-start | bytes 5242880 | tf_op jit(solution)/shard_map/all_gather | solution.py:168
  11.3 4.9 %copy-start.8 = (bf16[512,2048]{1,0:T(8,128)(2,1)S(1)}, bf16[512,2048]{1,0:T(8,128)(2,1)}, u32[]{:S(2)}) copy-start(bf16[512,2048]{1,0:T(8,128)(2,1)} %param.16) | copy-start | bytes 6291460
  13.5 3.6 %copy-start.12 = (bf16[2048,512]{1,0:T(8,128)(2,1)S(1)}, bf16[2048,512]{1,0:T(8,128)(2,1)}, u32[]{:S(2)}) copy-start(bf16[2048,512]{1,0:T(8,128)(2,1)} %param.19) | copy-start | bytes 6291460
  26.2 11.7 %copy-start.6 = (s32[1,32]{1,0:T(1,128)S(1)}, s32[1,32]{1,0:T(1,128)}, u32[]{:S(2)}) copy-start(s32[1,32]{1,0:T(1,128)} %param.30) | copy-start | bytes 388
  29.1 42.1 %all-to-all-start = ((bf16[32,32,768]{2,1,0:T(8,128)(2,1)}), bf16[32,32,768]{2,1,0:T(8,128)(2,1)}, u32[]{:S(2)}, u32[]{:S(2)}) async-start(bf16[32,32,768]{2,1,0:T(8,128)(2,1)} %broadcast_select_fusion), calls=%async_computation | async-start | bytes 3145728 | tf_op jit(solution)/shard_map/all_to_all | solution.py:180
  89.1 5.8 %copy-start.5 = (s32[1,512]{1,0:T(1,128)S(1)}, s32[1,512]{1,0:T(1,128)}, u32[]{:S(2)}) copy-start(s32[1,512]{1,0:T(1,128)} %param.31) | copy-start | bytes 6148
  89.1 5.8 %copy-start.7 = (s32[1,32]{1,0:T(1,128)S(1)}, s32[1,32]{1,0:T(1,128)}, u32[]{:S(2)}) copy-start(s32[1,32]{1,0:T(1,128)} %param.29) | copy-start | bytes 388
  94.9 97.3 %copy-start.10 = (s32[512]{0:T(512)S(1)}, s32[512]{0:T(512)}, u32[]{:S(2)}) copy-start(s32[512]{0:T(512)} %param.28) | copy-start | bytes 6148
  94.9 1.6 copy-start.2
  96.6 1.0 copy-start.4
  126.2 1.0 copy-start.3
  185.8 23.1 %all-to-all-start.1 = ((bf16[32,32,512]{2,1,0:T(8,128)(2,1)}), bf16[32,32,512]{2,1,0:T(8,128)(2,1)S(1)}, u32[]{:S(2)}, u32[]{:S(2)}) async-start(bf16[32,32,512]{2,1,0:T(8,128)(2,1)} %copy-done.3), calls=%async_computation.1 | async-start | bytes 2097152 | tf_op jit(solution)/shard_map/all_to_all | solution.py:188
  192.1 51.0 %reduce-scatter.3.cloned.1.call-start = ((), (), s32[]{:S(2)}) async-start(), calls=%async_computation.7 | async-start | bytes 2621440 | tf_op jit(solution)/shard_map/reduce_scatter | solution.py:191
  211.6 33.1 %copy-start.11 = (f32[2048]{0:T(1024)S(1)}, f32[2048]{0:T(1024)}, u32[]{:S(2)}) copy-start(f32[2048]{0:T(1024)} %param.18) | copy-start | bytes 24580
  215.3 63.8 %all-gather.11.cloned.1.call-start = ((), (), s32[]{:S(2)}) async-start(), calls=%async_computation.8 | async-start | bytes 4718592 | tf_op jit(solution)/shard_map/all_gather | solution.py:199
  246.9 95.6 %reduce-scatter.5.cloned.1.call-start = ((), (), s32[]{:S(2)}) async-start(), calls=%async_computation.9 | async-start | bytes 4718592 | tf_op jit(solution)/shard_map/reduce_scatter | solution.py:203
  289.0 55.7 %copy-start.1 = (bf16[512,2048]{1,0:T(8,128)(2,1)S(1)}, bf16[512,2048]{1,0:T(8,128)(2,1)}, u32[]{:S(2)}) copy-start(bf16[512,2048]{1,0:T(8,128)(2,1)} %param.22) | copy-start | bytes 6291460
  304.3 38.2 %copy-start.9 = (bf16[128,2048]{1,0:T(8,128)(2,1)S(1)}, bf16[128,2048]{1,0:T(8,128)(2,1)}, u32[]{:S(2)}) copy-start(bf16[128,2048]{1,0:T(8,128)(2,1)} %reduce-scatter.3.cloned.1.call-done) | copy-start | bytes 1572868
Sparse Core Ops, SparseCore 0:
  9.7 69.3 all-gather.4
  80.8 54.1 all-gather.6
  136.6 49.1 all-gather.8
  215.4 27.6 reduce-scatter.2
  247.0 32.0 all-gather.10
  304.4 37.9 reduce-scatter.4
where the time goes:
time: 352 us
  waiting for transfers between devices  206 us (59%)
  matrix products  33.9 us (10%)
  Pallas kernels  28.7 us (8%)
  local copies, waits for them, and re-layouts  28.2 us (8%)
  other arithmetic  25.3 us (7%)
  starting transfers between devices  15.5 us (4%)
  between operations  14.4 us (4%)
    all_gather x1, waiting for transfers between devices, body(): down_w = lax.all_gather(w_down, 'ry', axis=0, tiled=True)  50.8 us
    reduce_scatter x1, waiting for transfers between devices, body(): lax.psum_scatter(jnp.dot(hidden, down_w, preferred_element_type=jnp.float...  38.1 us
    all_gather x1, waiting for transfers between devices, body(): piece = lax.all_gather(mlp_in, 'rzc', axis=0, tiled=True)  32 us
    all_to_all x1, waiting for transfers between devices, body(): lax.all_to_all(send_qkv, REQ, split_axis=0, concat_axis=0, tiled=True)  30.3 us
    pallas_call x1, Pallas kernels, owner_attention(): pl.pallas_call(attention_kernel, out_shape=(jax.ShapeDtypeStruct((sources...  28.7 us
    reduce_scatter x1, waiting for transfers between devices, body(): lax.psum_scatter(projected.astype(jnp.bfloat16), 'grp', scatter_dimension...  27.8 us
    all_to_all x1, waiting for transfers between devices, body(): lax.all_to_all(mixed, REQ, split_axis=0, concat_axis=0, tiled=True)  16.7 us
    dot_general x1, matrix products, body(): jnp.dot(hidden, down_w, preferred_element_type=jnp.float32)  15.3 us
  transfers between devices with their start and end apart: 8, of which 7 were waited for; matrix products, arithmetic and copies ran while one was open for 13% of the time, Pallas kernels for 8%

commit v1 on v0

--- a/solution.py
+++ b/solution.py
@@ -163,9 +163,9 @@
     pair_rows = 2 * row_count // peers
     quarter = row_count // groups
     group_index = lax.axis_index("grp")
-    gate_w = lax.all_gather(w_gate, "ry", axis=1, tiled=True)
-    up_w = lax.all_gather(w_up, "ry", axis=1, tiled=True)
-    down_w = lax.all_gather(w_down, "ry", axis=0, tiled=True)
+    gate_w = lax.all_gather(w_gate, "rc", axis=1, tiled=True)
+    up_w = lax.all_gather(w_up, "rc", axis=1, tiled=True)
+    down_w = lax.all_gather(w_down, "rc", axis=0, tiled=True)
     normed = normalize(hidden_in.astype(jnp.float32), attn_gain).astype(jnp.bfloat16)
     qcols = w_query.shape[1]
     kcols = w_key.shape[1]
@@ -196,13 +196,13 @@
     )
     residual = own_rows + RESIDUAL_MULT * attn_part
     mlp_in = normalize(residual, mlp_gain).astype(jnp.bfloat16)
-    piece = lax.all_gather(mlp_in, "rzc", axis=0, tiled=True)
+    piece = lax.all_gather(mlp_in, "ryz", axis=0, tiled=True)
     gate = jnp.dot(piece, gate_w, preferred_element_type=jnp.float32)
     upper = jnp.dot(piece, up_w, preferred_element_type=jnp.float32)
     hidden = (jax.nn.silu(gate) * upper).astype(jnp.bfloat16)
     down = lax.psum_scatter(
         jnp.dot(hidden, down_w, preferred_element_type=jnp.float32).astype(jnp.bfloat16),
-        "rzc",
+        "ryz",
         scatter_dimension=0,
         tiled=True,
     ).astype(jnp.float32)
@@ -210,14 +210,14 @@
     return (layer_out, keys_out, values_out)
 
 
-REQ = ("ry", "rzc")
+REQ = ("ryz", "rc")
 
 
 def solution(mesh):
     req_size = mesh.shape["req"]
-    major = 4
+    cores = 2
     inner = Mesh(
-        mesh.devices.reshape(major, req_size // major, mesh.shape["grp"]), ("ry", "rzc", "grp")
+        mesh.devices.reshape(req_size // cores, cores, mesh.shape["grp"]), ("ryz", "rc", "grp")
     )
     in_specs = (
         P(REQ, None),

time: 352 us -> 362 us (1.028)
  waiting for transfers between devices: 206 us -> 221 us
    reduce_scatter x1, waiting for transfers between devices: 38.1 us -> 85 us  [body(): lax.psum_scatter(jnp.dot(hidden, down_w, preferred_element_type=jnp.float...]
    all_gather x4, waiting for transfers between devices: 90.5 us -> 70.5 us  [the longest x1 70.5 us: body(): piece = lax.all_gather(mlp_in, 'ryz', axis=0, tiled=True)]
    all_to_all x1, waiting for transfers between devices: 30.3 us -> 19.4 us  [body(): lax.all_to_all(send_qkv, REQ, split_axis=0, concat_axis=0, tiled=True)]
  transfers between devices with their start and end apart: 8 -> 8, of which waited for: 7 -> 5; matrix products, arithmetic and copies ran while one was open for 13% -> 12% of each run, Pallas kernels for 8% -> 8%
where the time goes in v1:
time: 362 us; the launch traced here: 361 us
  waiting for transfers between devices  221 us (61%)
  matrix products  32.1 us (9%)
  local copies, waits for them, and re-layouts  28.8 us (8%)
  Pallas kernels  28.6 us (8%)
  other arithmetic  22.6 us (6%)
  between operations  14.4 us (4%)
  starting transfers between devices  13 us (4%)
    reduce_scatter x1, waiting for transfers between devices, body(): lax.psum_scatter(jnp.dot(hidden, down_w, preferred_element_type=jnp.float...  85 us
    all_gather x1, waiting for transfers between devices, body(): piece = lax.all_gather(mlp_in, 'ryz', axis=0, tiled=True)  70.5 us
    pallas_call x1, Pallas kernels, owner_attention(): pl.pallas_call(attention_kernel, out_shape=(jax.ShapeDtypeStruct((sources...  28.6 us
    reduce_scatter x1, waiting for transfers between devices, body(): lax.psum_scatter(projected.astype(jnp.bfloat16), 'grp', scatter_dimension...  27.8 us
    all_to_all x1, waiting for transfers between devices, body(): lax.all_to_all(send_qkv, REQ, split_axis=0, concat_axis=0, tiled=True)  19.4 us
    all_to_all x1, waiting for transfers between devices, body(): lax.all_to_all(mixed, REQ, split_axis=0, concat_axis=0, tiled=True)  16.7 us
    dot_general x1, matrix products, body(): jnp.dot(hidden, down_w, preferred_element_type=jnp.float32)  14.6 us
    dot_general x1, matrix products, body(): gate = jnp.dot(piece, gate_w, preferred_element_type=jnp.float32)  10.4 us
  transfers between devices with their start and end apart: 8, of which 5 were waited for; matrix products, arithmetic and copies ran while one was open for 12% of the time, Pallas kernels for 8%

profile of v1, /device:TPU:0, one launch (start us, length us, event | category | flops | bytes accessed | tf_op | source)
XLA Modules:
  0.0 360.8 jit_solution(15306041296538855602)
XLA Ops:
  7.3 0.7 all-gather.5.cloned.1.call-update
  8.0 0.7 all-gather.7.cloned.1.call-update
  8.7 0.1 select_reduce_fusion.1
  8.8 2.2 fusion
  11.0 0.1 select_reduce_fusion
  11.2 0.9 convolution_convert_fusion.4
  12.1 0.1 copy-done.17
  12.2 0.9 convolution_convert_fusion.3
  13.2 0.6 copy-done.14
  13.8 1.4 convolution_convert_fusion.2
  15.4 0.9 pad_maximum_fusion.1
  16.4 1.4 copy.21
  17.8 5.2 %gather_fusion = bf16[1024,768]{1,0:T(8,128)(2,1)} fusion(bf16[512,768]{1,0:T(8,128)(2,1)S(1)} %copy.21, s32[1024]{0:T(1024)S(1)} %broadcast_clamp_fusion), kind=kCustom, calls=%fused_computation | custom fusion | bytes 3149824 | tf_op jit(solution)/shard_map/jit(_take)/gather | solution.py:177
  23.1 3.0 broadcast_select_fusion
  26.1 8.4 %all-to-all-start = ((bf16[32,32,768]{2,1,0:T(8,128)(2,1)}), bf16[32,32,768]{2,1,0:T(8,128)(2,1)}, u32[]{:S(2)}, u32[]{:S(2)}) async-start(bf16[32,32,768]{2,1,0:T(8,128)(2,1)} %broadcast_select_fusion), calls=%async_computation | async-start | bytes 3145728 | tf_op jit(solution)/shard_map/all_to_all | solution.py:180
  34.5 0.2 all-gather.9.cloned.1.call-start
  34.8 0.5 all-gather.9.cloned.1.call-update
  35.4 2.9 multiply_cosine_fusion
  38.3 19.4 %all-to-all-done = bf16[32,32,768]{2,1,0:T(8,128)(2,1)} async-done(((bf16[32,32,768]{2,1,0:T(8,128)(2,1)}), bf16[32,32,768]{2,1,0:T(8,128)(2,1)}, u32[]{:S(2)}, u32[]{:S(2)}) %all-to-all-start) | async-done | bytes 1572896 | tf_op jit(solution)/shard_map/all_to_all | solution.py:180
  57.7 1.8 fusion.19
  59.5 0.2 reshape.155
  59.7 1.0 fusion.20
  60.8 0.4 fusion.8
  61.2 0.3 pad_maximum_fusion.2
  61.5 1.3 copy.24
  62.8 1.3 convert_element_type.94.k_ref
  64.2 2.3 slice.32
  66.5 3.9 %reshape.154 = bf16[32,32,8,64]{3,2,1,0:T(8,128)(2,1)} reshape(bf16[32,32,512]{2,1,0:T(8,128)(2,1)} %slice.32) | data formatting | bytes 2097152 | tf_op jit(solution)/shard_map/reshape | solution.py:116
  70.4 4.2 %fusion.4 = (bf16[32,32,8,32]{3,2,1,0:T(8,128)(2,1)S(1)}, bf16[32,32,8,32]{3,2,1,0:T(8,128)(2,1)S(1)}) fusion(f32[32,32,32]{2,1,0:T(8,128)} %get-tuple-element.30, f32[32,32,32]{2,1,0:T(8,128)S(1)} %get-tuple-element.29, bf16[32,32,8,64]{3,2,1,0:T(8,128)(2,1)} %reshape.154), kind=kLoop, calls=%fused_computation.13 | loop fusion | flops 2621440 | bytes 2359296 | tf_op jit(solution)/shard_map/convert.2
  74.5 2.5 pad_maximum_fusion
  77.0 3.2 convert_element_type.91.q_ref
  80.3 1.6 copy-done.2
  81.8 0.9 copy-done.4
  82.8 28.6 %shard_map.175 = (bf16[32,32,512]{2,1,0:T(8,128)(2,1)S(1)}, bf16[512,16,128]{2,1,0:T(8,128)(2,1)}, bf16[512,16,128]{2,1,0:T(8,128)(2,1)}) custom-call(s32[512]{0:T(512)S(1)} %bitcast.17, s32[32]{0:T(128)S(1)} %bitcast.19, s32[32]{0:T(128)S(1)} %bitcast.20, bf16[32,32,512]{2,1,0:T(8,128)(2,1)S(1)} %convert_element_type.91.q_ref, ...), custom_call_target="tpu_custom_call" | custom-call | tf_op jit(solution)/shard_map/pallas_call | solution.py:125
  111.4 1.0 copy-done.3
  112.4 3.9 %all-to-all-start.1 = ((bf16[32,32,512]{2,1,0:T(8,128)(2,1)}), bf16[32,32,512]{2,1,0:T(8,128)(2,1)S(1)}, u32[]{:S(2)}, u32[]{:S(2)}) async-start(bf16[32,32,512]{2,1,0:T(8,128)(2,1)} %copy-done.3), calls=%async_computation.1 | async-start | bytes 2097152 | tf_op jit(solution)/shard_map/all_to_all | solution.py:188
  116.5 16.7 %all-to-all-done.1 = bf16[32,32,512]{2,1,0:T(8,128)(2,1)S(1)} async-done(((bf16[32,32,512]{2,1,0:T(8,128)(2,1)}), bf16[32,32,512]{2,1,0:T(8,128)(2,1)S(1)}, u32[]{:S(2)}, u32[]{:S(2)}) %all-to-all-start.1) | async-done | bytes 1048608 | tf_op jit(solution)/shard_map/all_to_all | solution.py:188
  133.2 2.6 gather_fusion.1
  135.8 3.7 %convolution_convert_fusion.1 = bf16[512,2048]{1,0:T(8,128)(2,1)} fusion(bf16[512,2048]{1,0:T(8,128)(2,1)S(1)} %copy-done, bf16[512,512]{1,0:T(8,128)(2,1)} %gather_fusion.1, pred[512]{0:T(512)(128)(4,1)S(1)} %get-tuple-element.19), kind=kOutput, calls=%fused_computation.17 | convolution fusion | flops 1075052544 | bytes 4719104 | tf_op jit(solution)/shard_map/dot_general | solution.py:190
  139.6 27.8 %reduce-scatter.3.cloned.1.call-done = bf16[128,2048]{1,0:T(8,128)(2,1)} async-done(((bf16[512,2048]{1,0:T(8,128)(2,1)}), bf16[128,2048]{1,0:T(8,128)(2,1)}) %reduce-scatter.3.cloned.1.call-update) | async-done | bytes 524304 | tf_op jit(solution)/shard_map/reduce_scatter | solution.py:191
  167.4 1.3 multiply_reduce_fusion
  168.7 2.1 multiply_convert_fusion.1
  170.9 0.3 reduce-scatter.5.cloned.1.call-start
  171.1 70.5 %all-gather.11.cloned.1.call-done = bf16[2048,2048]{1,0:T(8,128)(2,1)} async-done(((bf16[128,2048]{1,0:T(8,128)(2,1)}), bf16[2048,2048]{1,0:T(8,128)(2,1)}) %all-gather.11.cloned.1.call-update) | async-done | bytes 8388624 | tf_op jit(solution)/shard_map/all_gather | solution.py:199
  241.6 10.4 %fusion.21 = f32[2048,512]{1,0:T(8,128)} fusion(bf16[2048,2048]{1,0:T(8,128)(2,1)} %all-gather.11.cloned.1.call-done, bf16[2048,512]{1,0:T(8,128)(2,1)} %all-gather.5.cloned.1.call-done), kind=kOutput, calls=%fused_computation.63 | convolution fusion | flops 4294967296 | bytes 14680064 | tf_op jit(solution)/shard_map/dot_general | solution.py:200
  252.0 14.6 %convolution_convert_fusion = bf16[2048,2048]{1,0:T(8,128)(2,1)} fusion(bf16[512,2048]{1,0:T(8,128)(2,1)} %all-gather.9.cloned.1.call-done, f32[2048,512]{1,0:T(8,128)} %fusion.21, bf16[2048,2048]{1,0:T(8,128)(2,1)} %all-gather.11.cloned.1.call-done, bf16[2048,512]{1,0:T(8,128)(2,1)S(1)} %copy-done.15), kind=kOutput, calls=%fused_computation.2 | convolution fusion | flops 8600420352 | bytes 25165824 | tf_op jit(solution)/shard_map/dot_general | solution.py:204
  266.7 85.0 %reduce-scatter.5.cloned.1.call-done = bf16[128,2048]{1,0:T(8,128)(2,1)} async-done(((bf16[2048,2048]{1,0:T(8,128)(2,1)}), bf16[128,2048]{1,0:T(8,128)(2,1)}) %reduce-scatter.5.cloned.1.call-update) | async-done | bytes 524304 | tf_op jit(solution)/shard_map/reduce_scatter | solution.py:203
  351.7 2.3 add_convert_fusion
  (54 shorter events, 0.7 us)
Async XLA Ops:
  7.2 128.6 %copy-start = (bf16[512,2048]{1,0:T(8,128)(2,1)S(1)}, bf16[512,2048]{1,0:T(8,128)(2,1)}, u32[]{:S(2)}) copy-start(bf16[512,2048]{1,0:T(8,128)(2,1)} %param.22) | copy-start | bytes 6291460
  7.2 1.5 copy-start.12
  7.2 4.0 %copy-start.16 = (bf16[2048,128]{1,0:T(8,128)(2,1)S(1)}, bf16[2048,128]{1,0:T(8,128)(2,1)}, u32[]{:S(2)}) copy-start(bf16[2048,128]{1,0:T(8,128)(2,1)} %param.20) | copy-start | bytes 1572868
  7.2 4.0 %copy-start.18 = (f32[2048]{0:T(1024)S(1)}, f32[2048]{0:T(1024)}, u32[]{:S(2)}) copy-start(f32[2048]{0:T(1024)} %param.17) | copy-start | bytes 24580
  7.2 105.2 %all-gather.5.cloned.1.call-start = ((), (), s32[]{:S(2)}) async-start(), calls=%async_computation.4 | async-start | bytes 3145728 | tf_op jit(solution)/shard_map/all_gather | solution.py:166
  7.9 104.5 %all-gather.7.cloned.1.call-start = ((), (), s32[]{:S(2)}) async-start(), calls=%async_computation.5 | async-start | bytes 3145728 | tf_op jit(solution)/shard_map/all_gather | solution.py:167
  8.7 2.5 copy-start.8
  11.2 1.0 copy-start.17
  12.2 1.6 copy-start.14
  26.1 9.2 %copy-start.6 = (s32[1,32]{1,0:T(1,128)S(1)}, s32[1,32]{1,0:T(1,128)}, u32[]{:S(2)}) copy-start(s32[1,32]{1,0:T(1,128)} %param.30) | copy-start | bytes 388
  26.1 31.5 %all-to-all-start = ((bf16[32,32,768]{2,1,0:T(8,128)(2,1)}), bf16[32,32,768]{2,1,0:T(8,128)(2,1)}, u32[]{:S(2)}, u32[]{:S(2)}) async-start(bf16[32,32,768]{2,1,0:T(8,128)(2,1)} %broadcast_select_fusion), calls=%async_computation | async-start | bytes 3145728 | tf_op jit(solution)/shard_map/all_to_all | solution.py:180
  34.5 77.9 %all-gather.9.cloned.1.call-start = ((), (), s32[]{:S(2)}) async-start(), calls=%async_computation.6 | async-start | bytes 3145728 | tf_op jit(solution)/shard_map/all_gather | solution.py:168
  59.7 1.1 copy-start.11
  77.0 3.2 copy-start.5
  77.0 3.2 copy-start.7
  80.3 1.6 copy-start.2
  81.8 0.9 copy-start.4
  111.4 1.0 copy-start.3
  112.4 20.7 %all-to-all-start.1 = ((bf16[32,32,512]{2,1,0:T(8,128)(2,1)}), bf16[32,32,512]{2,1,0:T(8,128)(2,1)S(1)}, u32[]{:S(2)}, u32[]{:S(2)}) async-start(bf16[32,32,512]{2,1,0:T(8,128)(2,1)} %copy-done.3), calls=%async_computation.1 | async-start | bytes 2097152 | tf_op jit(solution)/shard_map/all_to_all | solution.py:188
  116.4 51.0 %reduce-scatter.3.cloned.1.call-start = ((), (), s32[]{:S(2)}) async-start(), calls=%async_computation.7 | async-start | bytes 2621440 | tf_op jit(solution)/shard_map/reduce_scatter | solution.py:191
  139.5 27.9 %copy-start.9 = (bf16[512,2048]{1,0:T(8,128)(2,1)S(1)}, bf16[512,2048]{1,0:T(8,128)(2,1)}, u32[]{:S(2)}) copy-start(bf16[512,2048]{1,0:T(8,128)(2,1)} %param.16) | copy-start | bytes 6291460
  139.5 29.2 %copy-start.13 = (f32[2048]{0:T(1024)S(1)}, f32[2048]{0:T(1024)}, u32[]{:S(2)}) copy-start(f32[2048]{0:T(1024)} %param.18) | copy-start | bytes 24580
  139.5 102.1 %all-gather.11.cloned.1.call-start = ((), (), s32[]{:S(2)}) async-start(), calls=%async_computation.8 | async-start | bytes 8912896 | tf_op jit(solution)/shard_map/all_gather | solution.py:199
  170.8 81.2 %copy-start.15 = (bf16[2048,512]{1,0:T(8,128)(2,1)S(1)}, bf16[2048,512]{1,0:T(8,128)(2,1)}, u32[]{:S(2)}) copy-start(bf16[2048,512]{1,0:T(8,128)(2,1)} %all-gather.7.cloned.1.call-done) | copy-start | bytes 6291460
  170.9 180.8 %reduce-scatter.5.cloned.1.call-start = ((), (), s32[]{:S(2)}) async-start(), calls=%async_computation.9 | async-start | bytes 8912896 | tf_op jit(solution)/shard_map/reduce_scatter | solution.py:203
  266.7 85.0 %copy-start.10 = (bf16[128,2048]{1,0:T(8,128)(2,1)S(1)}, bf16[128,2048]{1,0:T(8,128)(2,1)}, u32[]{:S(2)}) copy-start(bf16[128,2048]{1,0:T(8,128)(2,1)} %reduce-scatter.3.cloned.1.call-done) | copy-start | bytes 1572868
  266.7 87.2 %copy-start.1 = (bf16[512,2048]{1,0:T(8,128)(2,1)S(1)}, bf16[512,2048]{1,0:T(8,128)(2,1)}, u32[]{:S(2)}) copy-start(bf16[512,2048]{1,0:T(8,128)(2,1)} %param.22) | copy-start | bytes 6291460
Sparse Core Ops, SparseCore 0:
  9.7 15.4 all-gather.4
  26.9 14.4 all-gather.6
  43.0 14.6 all-gather.8
  139.6 27.7 reduce-scatter.2
  171.0 70.5 all-gather.10
  266.8 84.8 reduce-scatter.4

commit v2 on v0

--- a/solution.py
+++ b/solution.py
@@ -163,9 +163,18 @@
     pair_rows = 2 * row_count // peers
     quarter = row_count // groups
     group_index = lax.axis_index("grp")
-    gate_w = lax.all_gather(w_gate, "ry", axis=1, tiled=True)
-    up_w = lax.all_gather(w_up, "ry", axis=1, tiled=True)
-    down_w = lax.all_gather(w_down, "ry", axis=0, tiled=True)
+    ring = lax.axis_size("ry")
+    gate_up = jnp.concatenate([w_gate, w_up], axis=1)
+    gate_up_parts = [gate_up]
+    down_parts = [w_down]
+    for shift in range(1, ring):
+        perm = [(i, (i + shift) % ring) for i in range(ring)]
+        gate_up_parts.append(lax.ppermute(gate_up, "ry", perm))
+        down_parts.append(lax.ppermute(w_down, "ry", perm))
+    units = w_gate.shape[1]
+    gate_w = jnp.concatenate([part[:, :units] for part in gate_up_parts], axis=1)
+    up_w = jnp.concatenate([part[:, units:] for part in gate_up_parts], axis=1)
+    down_w = jnp.concatenate(down_parts, axis=0)
     normed = normalize(hidden_in.astype(jnp.float32), attn_gain).astype(jnp.bfloat16)
     qcols = w_query.shape[1]
     kcols = w_key.shape[1]
@@ -184,8 +193,8 @@
     mixed, keys_out, values_out = owner_attention(
         recv_query, recv_key, recv_value, cache_k, cache_v, new_len[0], prior_len[0], page_table[0]
     )
-    gate_w, up_w, down_w, mixed = lax.optimization_barrier((gate_w, up_w, down_w, mixed))
     returned = lax.all_to_all(mixed, REQ, split_axis=0, concat_axis=0, tiled=True)
+    gate_w, up_w, down_w, returned = lax.optimization_barrier((gate_w, up_w, down_w, returned))
     attn_rows = jnp.take(returned.reshape(peers * pair_rows, -1), back_rows, axis=0)
     projected = jnp.dot(attn_rows, w_out, preferred_element_type=jnp.float32)
     attn_part = lax.psum_scatter(

time: 352 us -> 369 us (1.048)
  starting transfers between devices: 15.5 us -> 65.3 us
  waiting for transfers between devices: 206 us -> 157 us
  local copies, waits for them, and re-layouts: 28.2 us -> 36.6 us
  other arithmetic: 25.3 us -> 32.4 us
    all_gather x3 -> x0, waiting for transfers between devices: 58.6 us -> none  [the longest x1 50.8 us: body(): down_w = lax.all_gather(w_down, 'ry', axis=0, tiled=True)]
    ppermute x0 -> x6, waiting for transfers between devices: none -> 51.7 us  [the longest x3 51.7 us: body(): down_parts.append(lax.ppermute(w_down, 'ry', perm))]
    all_to_all x1, starting transfers between devices: 6.32 us -> 47.6 us  [body(): lax.all_to_all(mixed, REQ, split_axis=0, concat_axis=0, tiled=True)]
    all_to_all x1, waiting for transfers between devices: 30.3 us -> 0.01 us  [body(): lax.all_to_all(send_qkv, REQ, split_axis=0, concat_axis=0, tiled=True)]
    all_to_all x1, waiting for transfers between devices: 16.7 us -> 7.4 us  [body(): lax.all_to_all(mixed, REQ, split_axis=0, concat_axis=0, tiled=True)]
    ppermute x0 -> x6, starting transfers between devices: none -> 8.61 us  [the longest x3 6.55 us: body(): down_parts.append(lax.ppermute(w_down, 'ry', perm))]
    concatenate x0 -> x2, other arithmetic: none -> 6.36 us  [the longest x1 4.1 us: body(): jnp.concatenate([part[:, :units] for part in gate_up_parts], axis=1)]
    slice x0 -> x3, local copies, waits for them, and re-layouts: none -> 5.18 us  [body(): up_w = jnp.concatenate([part[:, units:] for part in gate_up_parts], axis=1)]
  transfers between devices with their start and end apart: 8 -> 11, of which waited for: 7 -> 6; matrix products, arithmetic and copies ran while one was open for 13% -> 11% of each run, Pallas kernels for 8% -> 8%
where the time goes in v2:
time: 369 us; the launch traced here: 368 us
  waiting for transfers between devices  157 us (43%)
  starting transfers between devices  65.3 us (18%)
  local copies, waits for them, and re-layouts  36.6 us (10%)
  matrix products  34 us (9%)
  other arithmetic  32.4 us (9%)
  Pallas kernels  28.6 us (8%)
  between operations  14.1 us (4%)
    ppermute x3, waiting for transfers between devices, body(): down_parts.append(lax.ppermute(w_down, 'ry', perm))  51.7 us
    all_to_all x1, starting transfers between devices, body(): lax.all_to_all(mixed, REQ, split_axis=0, concat_axis=0, tiled=True)  47.6 us
    reduce_scatter x1, waiting for transfers between devices, body(): lax.psum_scatter(jnp.dot(hidden, down_w, preferred_element_type=jnp.float...  38.2 us
    all_gather x1, waiting for transfers between devices, body(): piece = lax.all_gather(mlp_in, 'rzc', axis=0, tiled=True)  32 us
    pallas_call x1, Pallas kernels, owner_attention(): pl.pallas_call(attention_kernel, out_shape=(jax.ShapeDtypeStruct((sources...  28.6 us
    reduce_scatter x1, waiting for transfers between devices, body(): lax.psum_scatter(projected.astype(jnp.bfloat16), 'grp', scatter_dimension...  27.8 us
    dot_general x1, matrix products, body(): jnp.dot(hidden, down_w, preferred_element_type=jnp.float32)  15.3 us
    dot_general x1, matrix products, body(): gate = jnp.dot(piece, gate_w, preferred_element_type=jnp.float32)  9.91 us
  transfers between devices with their start and end apart: 11, of which 6 were waited for; matrix products, arithmetic and copies ran while one was open for 11% of the time, Pallas kernels for 8%

profile of v2, /device:TPU:0, one launch (start us, length us, event | category | flops | bytes accessed | tf_op | source)
XLA Modules:
  0.0 368.1 jit_solution(10774283960126102627)
XLA Ops:
  7.2 1.0 select_reduce_fusion.1
  9.2 2.1 fusion
  12.1 2.7 convolution_convert_fusion.4
  14.9 0.9 convolution_convert_fusion.3
  15.8 1.4 convolution_convert_fusion.2
  18.2 1.4 copy.21
  19.6 5.2 %gather_fusion = bf16[1024,768]{1,0:T(8,128)(2,1)} fusion(bf16[512,768]{1,0:T(8,128)(2,1)S(1)} %copy.21, s32[1024]{0:T(1024)S(1)} %get-tuple-element.40), kind=kCustom, calls=%fused_computation | custom fusion | bytes 3149824 | tf_op jit(solution)/shard_map/jit(_take)/gather | solution.py:186
  24.8 2.8 broadcast_select_fusion
  27.7 8.7 %all-to-all-start = ((bf16[32,32,768]{2,1,0:T(8,128)(2,1)}), bf16[32,32,768]{2,1,0:T(8,128)(2,1)}, u32[]{:S(2)}, u32[]{:S(2)}) async-start(bf16[32,32,768]{2,1,0:T(8,128)(2,1)} %broadcast_select_fusion), calls=%async_computation | async-start | bytes 3145728 | tf_op jit(solution)/shard_map/all_to_all | solution.py:189
  36.4 3.3 collective-permute-start.4
  40.3 2.6 collective-permute-start.5
  42.9 1.1 constant_dynamic-update-slice_fusion.1
  44.0 2.3 constant_dynamic-update-slice_fusion
  46.4 1.5 collective-permute-start.1
  47.9 2.9 multiply_cosine_fusion
  50.8 29.7 %collective-permute-done.4 = bf16[256,2048]{1,0:T(8,128)(2,1)S(1)} collective-permute-done((bf16[256,2048]{1,0:T(8,128)(2,1)}, bf16[256,2048]{1,0:T(8,128)(2,1)S(1)}, u32[]{:S(2)}, u32[]{:S(2)}) %collective-permute-start.4) | collective-permute-done | bytes 1048608 | tf_op jit(solution)/shard_map/ppermute | solution.py:173
  81.2 22.0 %collective-permute-done.3 = bf16[256,2048]{1,0:T(8,128)(2,1)S(1)} collective-permute-done((bf16[256,2048]{1,0:T(8,128)(2,1)}, bf16[256,2048]{1,0:T(8,128)(2,1)S(1)}, u32[]{:S(2)}, u32[]{:S(2)}) %collective-permute-start.3) | collective-permute-done | bytes 1048608 | tf_op jit(solution)/shard_map/ppermute | solution.py:173
  103.1 2.3 pad_maximum_fusion.2
  105.4 1.8 fusion.22
  107.4 1.0 fusion.23
  108.5 1.5 fusion.8
  110.3 1.3 copy.24
  111.6 1.3 convert_element_type.94.k_ref
  112.9 2.3 slice.62
  115.2 3.9 %reshape.154 = bf16[32,32,8,64]{3,2,1,0:T(8,128)(2,1)} reshape(bf16[32,32,512]{2,1,0:T(8,128)(2,1)} %slice.62) | data formatting | bytes 2097152 | tf_op jit(solution)/shard_map/reshape | solution.py:116
  119.1 4.2 %fusion.4 = (bf16[32,32,8,32]{3,2,1,0:T(8,128)(2,1)S(1)}, bf16[32,32,8,32]{3,2,1,0:T(8,128)(2,1)S(1)}) fusion(f32[32,32,32]{2,1,0:T(8,128)} %get-tuple-element.36, f32[32,32,32]{2,1,0:T(8,128)S(1)} %get-tuple-element.35, bf16[32,32,8,64]{3,2,1,0:T(8,128)(2,1)} %reshape.154), kind=kLoop, calls=%fused_computation.12 | loop fusion | flops 2621440 | bytes 2359296 | tf_op jit(solution)/shard_map/convert.2
  123.3 2.5 pad_maximum_fusion.3
  125.8 3.2 convert_element_type.91.q_ref
  129.0 1.6 copy-done.2
  130.6 0.9 copy-done.4
  131.6 28.6 %shard_map.175 = (bf16[32,32,512]{2,1,0:T(8,128)(2,1)S(1)}, bf16[512,16,128]{2,1,0:T(8,128)(2,1)}, bf16[512,16,128]{2,1,0:T(8,128)(2,1)}) custom-call(s32[512]{0:T(512)S(1)} %bitcast.17, s32[32]{0:T(128)S(1)} %bitcast.19, s32[32]{0:T(128)S(1)} %bitcast.20, bf16[32,32,512]{2,1,0:T(8,128)(2,1)S(1)} %convert_element_type.91.q_ref, ...), custom_call_target="tpu_custom_call" | custom-call | tf_op jit(solution)/shard_map/pallas_call | solution.py:125
  160.2 1.0 copy-done.3
  161.2 47.6 %all-to-all-start.1 = ((bf16[32,32,512]{2,1,0:T(8,128)(2,1)}), bf16[32,32,512]{2,1,0:T(8,128)(2,1)S(1)}, u32[]{:S(2)}, u32[]{:S(2)}) async-start(bf16[32,32,512]{2,1,0:T(8,128)(2,1)} %copy-done.3), calls=%async_computation.1 | async-start | bytes 2097152 | tf_op jit(solution)/shard_map/all_to_all | solution.py:196
  208.9 1.7 fusion.21
  210.6 1.8 fusion.20
  212.5 1.7 fusion.19
  214.2 4.1 %pad_maximum_fusion = (bf16[2048,1024]{1,0:T(8,128)(2,1)}, bf16[2048,1024]{1,0:T(8,128)(2,1)}) fusion(bf16[2048,256]{1,0:T(8,128)(2,1)S(1)} %get-tuple-element.30, bf16[2048,256]{1,0:T(8,128)(2,1)S(1)} %get-tuple-element.28, bf16[2048,256]{1,0:T(8,128)(2,1)S(1)} %get-tuple-element.26, bf16[2048,256]{1,0:T(8,128)(2,1)S(1)} %copy-done.11, ...), kind=kLoop, calls=%fused_computation.15 | loop fusion | flops 33554432 | bytes 16777216 | tf_op jit(solution)/shard_map/concatenate | solution.py:175
  218.3 7.4 %all-to-all-done.1 = bf16[32,32,512]{2,1,0:T(8,128)(2,1)S(1)} async-done(((bf16[32,32,512]{2,1,0:T(8,128)(2,1)}), bf16[32,32,512]{2,1,0:T(8,128)(2,1)S(1)}, u32[]{:S(2)}, u32[]{:S(2)}) %all-to-all-start.1) | async-done | bytes 1048608 | tf_op jit(solution)/shard_map/all_to_all | solution.py:196
  225.7 2.6 gather_fusion.1
  228.3 3.7 convolution_convert_fusion.1
  232.0 27.8 %reduce-scatter.3.cloned.1.call-done = bf16[128,2048]{1,0:T(8,128)(2,1)} async-done(((bf16[512,2048]{1,0:T(8,128)(2,1)}), bf16[128,2048]{1,0:T(8,128)(2,1)}) %reduce-scatter.3.cloned.1.call-update) | async-done | bytes 524304 | tf_op jit(solution)/shard_map/reduce_scatter | solution.py:200
  259.8 1.5 multiply_reduce_fusion
  261.3 2.2 multiply_convert_fusion.1
  263.9 32.0 %all-gather.2.cloned.1.call-done = bf16[1024,2048]{1,0:T(8,128)(2,1)} async-done(((bf16[128,2048]{1,0:T(8,128)(2,1)}), bf16[1024,2048]{1,0:T(8,128)(2,1)}) %all-gather.2.cloned.1.call-update) | async-done | bytes 4194320 | tf_op jit(solution)/shard_map/all_gather | solution.py:208
  295.9 9.9 %fusion.24 = f32[1024,1024]{1,0:T(8,128)} fusion(bf16[1024,2048]{1,0:T(8,128)(2,1)} %all-gather.2.cloned.1.call-done, bf16[2048,1024]{1,0:T(8,128)(2,1)} %get-tuple-element.12), kind=kOutput, calls=%fused_computation.71 | convolution fusion | flops 4294967296 | bytes 12582912 | tf_op jit(solution)/shard_map/dot_general | solution.py:209
  305.8 15.3 %convolution_convert_fusion = bf16[1024,2048]{1,0:T(8,128)(2,1)} fusion(bf16[1024,2048]{1,0:T(8,128)(2,1)} %pad_maximum_fusion.2, f32[1024,1024]{1,0:T(8,128)} %fusion.24, bf16[1024,2048]{1,0:T(8,128)(2,1)} %all-gather.2.cloned.1.call-done, bf16[2048,1024]{1,0:T(8,128)(2,1)} %get-tuple-element.13), kind=kOutput, calls=%fused_computation.19 | convolution fusion | flops 8598323200 | bytes 20971520 | tf_op jit(solution)/shard_map/dot_general | solution.py:213
  321.1 38.2 %reduce-scatter.5.cloned.1.call-done = bf16[128,2048]{1,0:T(8,128)(2,1)} async-done(((bf16[1024,2048]{1,0:T(8,128)(2,1)}), bf16[128,2048]{1,0:T(8,128)(2,1)}) %reduce-scatter.5.cloned.1.call-update) | async-done | bytes 524304 | tf_op jit(solution)/shard_map/reduce_scatter | solution.py:212
  359.3 2.3 add_convert_fusion
  (61 shorter events, 5.1 us)
Async XLA Ops:
  7.2 221.1 %copy-start = (bf16[512,2048]{1,0:T(8,128)(2,1)S(1)}, bf16[512,2048]{1,0:T(8,128)(2,1)}, u32[]{:S(2)}) copy-start(bf16[512,2048]{1,0:T(8,128)(2,1)} %param.22) | copy-start | bytes 6291460
  7.2 7.7 %copy-start.17 = (f32[2048]{0:T(1024)S(1)}, f32[2048]{0:T(1024)}, u32[]{:S(2)}) copy-start(f32[2048]{0:T(1024)} %param.17) | copy-start | bytes 24580
  7.2 7.7 %copy-start.16 = (bf16[2048,128]{1,0:T(8,128)(2,1)S(1)}, bf16[2048,128]{1,0:T(8,128)(2,1)}, u32[]{:S(2)}) copy-start(bf16[2048,128]{1,0:T(8,128)(2,1)} %param.21) | copy-start | bytes 1572868
  12.1 2.8 copy-start.8
  12.1 3.7 %copy-start.15 = (bf16[2048,512]{1,0:T(8,128)(2,1)S(1)}, bf16[2048,512]{1,0:T(8,128)(2,1)}, u32[]{:S(2)}) copy-start(bf16[2048,512]{1,0:T(8,128)(2,1)} %param.19) | copy-start | bytes 6291460
  24.8 18.1 %copy-start.10 = (bf16[2048,256]{1,0:T(8,128)(2,1)S(1)}, bf16[2048,256]{1,0:T(8,128)(2,1)}, u32[]{:S(2)}) copy-start(bf16[2048,256]{1,0:T(8,128)(2,1)} %param.23) | copy-start | bytes 3145732
  27.7 20.1 %copy-start.6 = (s32[1,32]{1,0:T(1,128)S(1)}, s32[1,32]{1,0:T(1,128)}, u32[]{:S(2)}) copy-start(s32[1,32]{1,0:T(1,128)} %param.30) | copy-start | bytes 388
  27.7 77.7 %all-to-all-start = ((bf16[32,32,768]{2,1,0:T(8,128)(2,1)}), bf16[32,32,768]{2,1,0:T(8,128)(2,1)}, u32[]{:S(2)}, u32[]{:S(2)}) async-start(bf16[32,32,768]{2,1,0:T(8,128)(2,1)} %broadcast_select_fusion), calls=%async_computation | async-start | bytes 3145728 | tf_op jit(solution)/shard_map/all_to_all | solution.py:189
  36.4 66.8 %copy-start.13 = (bf16[256,2048]{1,0:T(8,128)(2,1)S(1)}, bf16[256,2048]{1,0:T(8,128)(2,1)}, u32[]{:S(2)}) copy-start(bf16[256,2048]{1,0:T(8,128)(2,1)} %param.25) | copy-start | bytes 3145732
  36.4 44.2 %collective-permute-start.4 = (bf16[256,2048]{1,0:T(8,128)(2,1)}, bf16[256,2048]{1,0:T(8,128)(2,1)S(1)}, u32[]{:S(2)}, u32[]{:S(2)}) collective-permute-start(bf16[256,2048]{1,0:T(8,128)(2,1)} %param.25), channel_id=1, source_target_pairs={{0,64},{32,96},{64,0},{96,32},{1,65},{33,97},{65,1},{97,33},{2,66}... | collective-permute-start | bytes 3145736 | tf_op jit(solution)/shard_map/ppermute | solution.py:173
  39.7 63.4 %collective-permute-start.3 = (bf16[256,2048]{1,0:T(8,128)(2,1)}, bf16[256,2048]{1,0:T(8,128)(2,1)S(1)}, u32[]{:S(2)}, u32[]{:S(2)}) collective-permute-start(bf16[256,2048]{1,0:T(8,128)(2,1)} %param.25), channel_id=1, source_target_pairs={{0,32},{32,64},{64,96},{96,0},{1,33},{33,65},{65,97},{97,1},{2,34}... | collective-permute-start | bytes 3145736 | tf_op jit(solution)/shard_map/ppermute | solution.py:173
  40.3 62.8 %collective-permute-start.5 = (bf16[256,2048]{1,0:T(8,128)(2,1)}, bf16[256,2048]{1,0:T(8,128)(2,1)S(1)}, u32[]{:S(2)}, u32[]{:S(2)}) collective-permute-start(bf16[256,2048]{1,0:T(8,128)(2,1)} %param.25), channel_id=1, source_target_pairs={{0,96},{32,0},{64,32},{96,64},{1,97},{33,1},{65,33},{97,65},{2,98}... | collective-permute-start | bytes 3145736 | tf_op jit(solution)/shard_map/ppermute | solution.py:173
  46.4 162.5 %collective-permute-start.2 = (bf16[2048,512]{1,0:T(8,128)(2,1)}, bf16[2048,512]{1,0:T(8,128)(2,1)}, u32[]{:S(2)}, u32[]{:S(2)}) collective-permute-start(bf16[2048,512]{1,0:T(8,128)(2,1)} %constant_dynamic-update-slice_fusion), channel_id=1, source_target_pairs={{0,96},{32,0},{64,32},{96,64},{1,97},{33,1},{65,33},{97,65},{2,98}... | collective-permute-start | bytes 6291464 | tf_op jit(solution)/shard_map/ppermute | solution.py:172
  46.4 164.3 %collective-permute-start.1 = (bf16[2048,512]{1,0:T(8,128)(2,1)}, bf16[2048,512]{1,0:T(8,128)(2,1)}, u32[]{:S(2)}, u32[]{:S(2)}) collective-permute-start(bf16[2048,512]{1,0:T(8,128)(2,1)} %constant_dynamic-update-slice_fusion), channel_id=1, source_target_pairs={{0,64},{32,96},{64,0},{96,32},{1,65},{33,97},{65,1},{97,33},{2,66}... | collective-permute-start | bytes 6291464 | tf_op jit(solution)/shard_map/ppermute | solution.py:172
  80.6 131.9 %collective-permute-start = (bf16[2048,512]{1,0:T(8,128)(2,1)}, bf16[2048,512]{1,0:T(8,128)(2,1)}, u32[]{:S(2)}, u32[]{:S(2)}) collective-permute-start(bf16[2048,512]{1,0:T(8,128)(2,1)} %constant_dynamic-update-slice_fusion), channel_id=1, source_target_pairs={{0,32},{32,64},{64,96},{96,0},{1,33},{33,65},{65,97},{97,1},{2,34}... | collective-permute-start | bytes 6291464 | tf_op jit(solution)/shard_map/ppermute | solution.py:172
  123.3 5.7 %copy-start.5 = (s32[1,512]{1,0:T(1,128)S(1)}, s32[1,512]{1,0:T(1,128)}, u32[]{:S(2)}) copy-start(s32[1,512]{1,0:T(1,128)} %param.31) | copy-start | bytes 6148
  123.3 5.7 %copy-start.7 = (s32[1,32]{1,0:T(1,128)S(1)}, s32[1,32]{1,0:T(1,128)}, u32[]{:S(2)}) copy-start(s32[1,32]{1,0:T(1,128)} %param.29) | copy-start | bytes 388
  129.0 1.6 copy-start.2
  130.6 0.9 copy-start.4
  160.2 1.0 copy-start.3
  161.2 64.4 %all-to-all-start.1 = ((bf16[32,32,512]{2,1,0:T(8,128)(2,1)}), bf16[32,32,512]{2,1,0:T(8,128)(2,1)S(1)}, u32[]{:S(2)}, u32[]{:S(2)}) async-start(bf16[32,32,512]{2,1,0:T(8,128)(2,1)} %copy-done.3), calls=%async_computation.1 | async-start | bytes 2097152 | tf_op jit(solution)/shard_map/all_to_all | solution.py:196
  208.8 51.0 %reduce-scatter.3.cloned.1.call-start = ((), (), s32[]{:S(2)}) async-start(), calls=%async_computation.4 | async-start | bytes 2621440 | tf_op jit(solution)/shard_map/reduce_scatter | solution.py:200
  210.6 3.6 copy-start.11
  210.6 3.6 copy-start.12
  228.3 33.1 %copy-start.14 = (f32[2048]{0:T(1024)S(1)}, f32[2048]{0:T(1024)}, u32[]{:S(2)}) copy-start(f32[2048]{0:T(1024)} %param.18) | copy-start | bytes 24580
  232.0 63.9 %all-gather.2.cloned.1.call-start = ((), (), s32[]{:S(2)}) async-start(), calls=%async_computation.5 | async-start | bytes 4718592 | tf_op jit(solution)/shard_map/all_gather | solution.py:208
  263.6 95.7 %reduce-scatter.5.cloned.1.call-start = ((), (), s32[]{:S(2)}) async-start(), calls=%async_computation.6 | async-start | bytes 4718592 | tf_op jit(solution)/shard_map/reduce_scatter | solution.py:212
  305.8 55.8 %copy-start.1 = (bf16[512,2048]{1,0:T(8,128)(2,1)S(1)}, bf16[512,2048]{1,0:T(8,128)(2,1)}, u32[]{:S(2)}) copy-start(bf16[512,2048]{1,0:T(8,128)(2,1)} %param.22) | copy-start | bytes 6291460
  321.1 38.2 %copy-start.9 = (bf16[128,2048]{1,0:T(8,128)(2,1)S(1)}, bf16[128,2048]{1,0:T(8,128)(2,1)}, u32[]{:S(2)}) copy-start(bf16[128,2048]{1,0:T(8,128)(2,1)} %reduce-scatter.3.cloned.1.call-done) | copy-start | bytes 1572868
Sparse Core Ops, SparseCore 0:
  232.1 27.7 reduce-scatter.2
  263.7 32.0 all-gather.1
  321.2 38.0 reduce-scatter.4

commit v3 on v0

--- a/solution.py
+++ b/solution.py
@@ -165,7 +165,13 @@
     group_index = lax.axis_index("grp")
     gate_w = lax.all_gather(w_gate, "ry", axis=1, tiled=True)
     up_w = lax.all_gather(w_up, "ry", axis=1, tiled=True)
-    down_w = lax.all_gather(w_down, "ry", axis=0, tiled=True)
+    ring = lax.axis_size("ry")
+    down_parts = [w_down] + [
+        lax.ppermute(w_down, "ry", [(i, (i + shift) % ring) for i in range(ring)])
+        for shift in range(1, ring)
+    ]
+    part_at = (lax.axis_index("ry") - jnp.arange(ring, dtype=jnp.int32)) % ring
+    down_w = jnp.take(jnp.stack(down_parts), part_at, axis=0).reshape(-1, w_down.shape[1])
     normed = normalize(hidden_in.astype(jnp.float32), attn_gain).astype(jnp.bfloat16)
     qcols = w_query.shape[1]
     kcols = w_key.shape[1]
@@ -184,7 +190,7 @@
     mixed, keys_out, values_out = owner_attention(
         recv_query, recv_key, recv_value, cache_k, cache_v, new_len[0], prior_len[0], page_table[0]
     )
-    gate_w, up_w, down_w, mixed = lax.optimization_barrier((gate_w, up_w, down_w, mixed))
+    gate_w, up_w, mixed = lax.optimization_barrier((gate_w, up_w, mixed))
     returned = lax.all_to_all(mixed, REQ, split_axis=0, concat_axis=0, tiled=True)
     attn_rows = jnp.take(returned.reshape(peers * pair_rows, -1), back_rows, axis=0)
     projected = jnp.dot(attn_rows, w_out, preferred_element_type=jnp.float32)
@@ -197,6 +203,7 @@
     residual = own_rows + RESIDUAL_MULT * attn_part
     mlp_in = normalize(residual, mlp_gain).astype(jnp.bfloat16)
     piece = lax.all_gather(mlp_in, "rzc", axis=0, tiled=True)
+    down_w, piece = lax.optimization_barrier((down_w, piece))
     gate = jnp.dot(piece, gate_w, preferred_element_type=jnp.float32)
     upper = jnp.dot(piece, up_w, preferred_element_type=jnp.float32)
     hidden = (jax.nn.silu(gate) * upper).astype(jnp.bfloat16)

time: 352 us -> 331 us (0.940)
  waiting for transfers between devices: 206 us -> 166 us
  other arithmetic: 25.3 us -> 33.1 us
  starting transfers between devices: 15.5 us -> 21 us
  local copies, waits for them, and re-layouts: 28.2 us -> 33.3 us
    all_gather x1 -> x0, waiting for transfers between devices: 50.8 us -> none  [body(): down_w = lax.all_gather(w_down, 'ry', axis=0, tiled=True)]
    ppermute x0 -> x3, waiting for transfers between devices: none -> 44.5 us  [body(): lax.ppermute(w_down, 'ry', [(i, (i + shift) % ring) for i in range(ring)])]
    all_gather x1, waiting for transfers between devices: 32 us -> 0.01 us  [body(): piece = lax.all_gather(mlp_in, 'rzc', axis=0, tiled=True)]
    ppermute x0 -> x3, starting transfers between devices: none -> 5.12 us  [body(): lax.ppermute(w_down, 'ry', [(i, (i + shift) % ring) for i in range(ring)])]
    gather x0 -> x1, local copies, waits for them, and re-layouts: none -> 4.94 us  [body(): jnp.take(jnp.stack(down_parts), part_at, axis=0)]
    select_n x0 -> x2, other arithmetic: none -> 4.58 us  [body(): jnp.take(jnp.stack(down_parts), part_at, axis=0)]
    another operation x2 -> x3, other arithmetic: 5.68 us -> 8.94 us
  transfers between devices with their start and end apart: 8 -> 10, of which waited for: 7 -> 8; matrix products, arithmetic and copies ran while one was open for 13% -> 18% of each run, Pallas kernels for 8% -> 9%
where the time goes in v3:
time: 331 us; the launch traced here: 330 us
  waiting for transfers between devices  166 us (50%)
  matrix products  34 us (10%)
  local copies, waits for them, and re-layouts  33.3 us (10%)
  other arithmetic  33.1 us (10%)
  Pallas kernels  28.7 us (9%)
  starting transfers between devices  21 us (6%)
  between operations  14.1 us (4%)
    ppermute x3, waiting for transfers between devices, body(): lax.ppermute(w_down, 'ry', [(i, (i + shift) % ring) for i in range(ring)])  44.5 us
    reduce_scatter x1, waiting for transfers between devices, body(): lax.psum_scatter(jnp.dot(hidden, down_w, preferred_element_type=jnp.float...  37.1 us
    all_to_all x1, waiting for transfers between devices, body(): lax.all_to_all(send_qkv, REQ, split_axis=0, concat_axis=0, tiled=True)  29.9 us
    pallas_call x1, Pallas kernels, owner_attention(): pl.pallas_call(attention_kernel, out_shape=(jax.ShapeDtypeStruct((sources...  28.7 us
    reduce_scatter x1, waiting for transfers between devices, body(): lax.psum_scatter(projected.astype(jnp.bfloat16), 'grp', scatter_dimension...  27.9 us
    all_to_all x1, waiting for transfers between devices, body(): lax.all_to_all(mixed, REQ, split_axis=0, concat_axis=0, tiled=True)  16.7 us
    dot_general x1, matrix products, body(): jnp.dot(hidden, down_w, preferred_element_type=jnp.float32)  15.3 us
    dot_general x1, matrix products, body(): gate = jnp.dot(piece, gate_w, preferred_element_type=jnp.float32)  9.89 us
  transfers between devices with their start and end apart: 10, of which 8 were waited for; matrix products, arithmetic and copies ran while one was open for 18% of the time, Pallas kernels for 9%

profile of v3, /device:TPU:0, one launch (start us, length us, event | category | flops | bytes accessed | tf_op | source)
XLA Modules:
  0.0 330.2 jit_solution(6539872858766553796)
XLA Ops:
  8.7 0.8 select_reduce_fusion.1
  9.5 0.9 select_reduce_fusion
  10.5 2.2 fusion
  12.8 2.6 convolution_convert_fusion.4
  15.5 1.0 convolution_convert_fusion.3
  16.4 1.4 convolution_convert_fusion.2
  17.9 0.9 pad_maximum_fusion.2
  18.8 1.4 copy.21
  20.3 5.2 %gather_fusion = bf16[1024,768]{1,0:T(8,128)(2,1)} fusion(bf16[512,768]{1,0:T(8,128)(2,1)S(1)} %copy.21, s32[1024]{0:T(1024)S(1)} %broadcast_clamp_fusion), kind=kCustom, calls=%fused_computation | custom fusion | bytes 3149824 | tf_op jit(solution)/shard_map/jit(_take)/gather | solution.py:183
  25.6 2.8 broadcast_select_fusion
  28.4 8.8 %all-to-all-start = ((bf16[32,32,768]{2,1,0:T(8,128)(2,1)}), bf16[32,32,768]{2,1,0:T(8,128)(2,1)}, u32[]{:S(2)}, u32[]{:S(2)}) async-start(bf16[32,32,768]{2,1,0:T(8,128)(2,1)} %broadcast_select_fusion), calls=%async_computation | async-start | bytes 3145728 | tf_op jit(solution)/shard_map/all_to_all | solution.py:186
  37.2 2.9 multiply_cosine_fusion
  40.2 29.9 %all-to-all-done = bf16[32,32,768]{2,1,0:T(8,128)(2,1)} async-done(((bf16[32,32,768]{2,1,0:T(8,128)(2,1)}), bf16[32,32,768]{2,1,0:T(8,128)(2,1)}, u32[]{:S(2)}, u32[]{:S(2)}) %all-to-all-start) | async-done | bytes 1572896 | tf_op jit(solution)/shard_map/all_to_all | solution.py:186
  70.1 1.8 fusion.22
  72.1 1.0 fusion.23
  73.2 1.5 fusion.8
  75.0 1.3 copy.24
  76.3 1.3 convert_element_type.94.k_ref
  77.6 2.3 slice.34
  79.9 3.9 %reshape.211 = bf16[32,32,8,64]{3,2,1,0:T(8,128)(2,1)} reshape(bf16[32,32,512]{2,1,0:T(8,128)(2,1)} %slice.34) | data formatting | bytes 2097152 | tf_op jit(solution)/shard_map/reshape | solution.py:116
  83.8 4.2 %fusion.4 = (bf16[32,32,8,32]{3,2,1,0:T(8,128)(2,1)S(1)}, bf16[32,32,8,32]{3,2,1,0:T(8,128)(2,1)S(1)}) fusion(f32[32,32,32]{2,1,0:T(8,128)} %get-tuple-element.32, f32[32,32,32]{2,1,0:T(8,128)S(1)} %get-tuple-element.31, bf16[32,32,8,64]{3,2,1,0:T(8,128)(2,1)} %reshape.211), kind=kLoop, calls=%fused_computation.13 | loop fusion | flops 2621440 | bytes 2359296 | tf_op jit(solution)/shard_map/convert.2
  88.0 2.5 pad_maximum_fusion.1
  90.5 3.3 %convert_element_type.91.q_ref = bf16[32,32,512]{2,1,0:T(8,128)(2,1)S(1)} reshape(bf16[32,32,8,64]{3,2,1,0:T(8,128)(2,1)} %pad_maximum_fusion.1) | data formatting | bytes 2097152 | tf_op jit(solution)/shard_map/convert_element_type | solution.py:116
  93.9 1.6 copy-done.2
  95.5 1.0 copy-done.4
  96.5 28.7 %shard_map.175 = (bf16[32,32,512]{2,1,0:T(8,128)(2,1)S(1)}, bf16[512,16,128]{2,1,0:T(8,128)(2,1)}, bf16[512,16,128]{2,1,0:T(8,128)(2,1)}) custom-call(s32[512]{0:T(512)S(1)} %bitcast.25, s32[32]{0:T(128)S(1)} %bitcast.27, s32[32]{0:T(128)S(1)} %bitcast.28, bf16[32,32,512]{2,1,0:T(8,128)(2,1)S(1)} %convert_element_type.91.q_ref, ...), custom_call_target="tpu_custom_call" | custom-call | tf_op jit(solution)/shard_map/pallas_call | solution.py:125
  125.2 1.1 copy-done.3
  126.2 8.4 %all-gather.6.cloned.1.call-done = bf16[2048,1024]{1,0:T(8,128)(2,1)} async-done(((bf16[2048,256]{1,0:T(8,128)(2,1)}), bf16[2048,1024]{1,0:T(8,128)(2,1)}) %all-gather.6.cloned.1.call-update) | async-done | bytes 4194320 | tf_op jit(solution)/shard_map/all_gather | solution.py:167
  134.6 6.9 %all-to-all-start.1 = ((bf16[32,32,512]{2,1,0:T(8,128)(2,1)}), bf16[32,32,512]{2,1,0:T(8,128)(2,1)S(1)}, u32[]{:S(2)}, u32[]{:S(2)}) async-start(bf16[32,32,512]{2,1,0:T(8,128)(2,1)} %copy-done.3), calls=%async_computation.1 | async-start | bytes 2097152 | tf_op jit(solution)/shard_map/all_to_all | solution.py:194
  141.6 16.7 %all-to-all-done.1 = bf16[32,32,512]{2,1,0:T(8,128)(2,1)S(1)} async-done(((bf16[32,32,512]{2,1,0:T(8,128)(2,1)}), bf16[32,32,512]{2,1,0:T(8,128)(2,1)S(1)}, u32[]{:S(2)}, u32[]{:S(2)}) %all-to-all-start.1) | async-done | bytes 1048608 | tf_op jit(solution)/shard_map/all_to_all | solution.py:194
  158.3 2.6 gather_fusion.1
  160.9 3.8 %convolution_convert_fusion.1 = bf16[512,2048]{1,0:T(8,128)(2,1)} fusion(bf16[512,2048]{1,0:T(8,128)(2,1)S(1)} %copy-done, bf16[512,512]{1,0:T(8,128)(2,1)} %gather_fusion.1, pred[512]{0:T(512)(128)(4,1)S(1)} %get-tuple-element.21), kind=kOutput, calls=%fused_computation.20 | convolution fusion | flops 1075052544 | bytes 4719104 | tf_op jit(solution)/shard_map/dot_general | solution.py:196
  164.8 27.9 %reduce-scatter.3.cloned.1.call-done = bf16[128,2048]{1,0:T(8,128)(2,1)} async-done(((bf16[512,2048]{1,0:T(8,128)(2,1)}), bf16[128,2048]{1,0:T(8,128)(2,1)}) %reduce-scatter.3.cloned.1.call-update) | async-done | bytes 524304 | tf_op jit(solution)/shard_map/reduce_scatter | solution.py:197
  192.7 1.5 multiply_reduce_fusion
  194.2 2.2 multiply_convert_fusion.1
  196.5 1.6 collective-permute-start
  198.1 1.7 collective-permute-start.2
  199.8 1.8 collective-permute-start.1
  201.8 21.1 %collective-permute-done = bf16[256,2048]{1,0:T(8,128)(2,1)S(1)} collective-permute-done((bf16[256,2048]{1,0:T(8,128)(2,1)S(1)}, bf16[256,2048]{1,0:T(8,128)(2,1)S(1)}, u32[]{:S(2)}, u32[]{:S(2)}) %collective-permute-start) | collective-permute-done | bytes 1048608 | tf_op jit(solution)/shard_map/ppermute | solution.py:170
  222.9 21.6 %collective-permute-done.2 = bf16[256,2048]{1,0:T(8,128)(2,1)S(1)} collective-permute-done((bf16[256,2048]{1,0:T(8,128)(2,1)S(1)}, bf16[256,2048]{1,0:T(8,128)(2,1)S(1)}, u32[]{:S(2)}, u32[]{:S(2)}) %collective-permute-start.2) | collective-permute-done | bytes 1048608 | tf_op jit(solution)/shard_map/ppermute | solution.py:170
  244.5 1.8 collective-permute-done.1
  246.3 3.3 pad_maximum_fusion
  249.5 4.9 %gather_fusion.2 = bf16[4,256,2048]{2,1,0:T(8,128)(2,1)} fusion(bf16[4,256,2048]{2,1,0:T(8,128)(2,1)} %pad_maximum_fusion, s32[1024]{0:T(1024)S(1)} %pad_clamp_fusion), kind=kCustom, calls=%fused_computation.2 | custom fusion | bytes 8388624 | tf_op jit(solution)/shard_map/jit(_take)/gather | solution.py:174
  254.5 4.6 %bitcast_select_fusion = bf16[1024,2048]{1,0:T(8,128)(2,1)} fusion(bf16[4,256,2048]{2,1,0:T(8,128)(2,1)} %gather_fusion.2, pred[1024]{0:T(1024)(128)(4,1)S(1)} %broadcast_in_dim.99), kind=kLoop, calls=%fused_computation.17 | loop fusion | flops 2097152 | bytes 8389632 | tf_op jit(solution)/shard_map/jit(_take)/select_n | solution.py:174
  259.1 9.9 %fusion.24 = f32[1024,1024]{1,0:T(8,128)} fusion(bf16[1024,2048]{1,0:T(8,128)(2,1)} %all-gather.8.cloned.1.call-done, bf16[2048,1024]{1,0:T(8,128)(2,1)} %all-gather.4.cloned.1.call-done), kind=kOutput, calls=%fused_computation.79 | convolution fusion | flops 4294967296 | bytes 12582912 | tf_op jit(solution)/shard_map/dot_general | solution.py:207
  268.9 15.3 %convolution_convert_fusion = bf16[1024,2048]{1,0:T(8,128)(2,1)} fusion(bf16[1024,2048]{1,0:T(8,128)(2,1)} %bitcast_select_fusion, f32[1024,1024]{1,0:T(8,128)} %fusion.24, bf16[1024,2048]{1,0:T(8,128)(2,1)} %all-gather.8.cloned.1.call-done, bf16[2048,1024]{1,0:T(8,128)(2,1)} %all-gather.6.cloned.1.call-done), kind=kOutput, calls=%fused_computation.19 | convolution fusion | flops 8598323200 | bytes 20971520 | tf_op jit(solution)/shard_map/dot_general | solution.py:211
  284.3 37.1 %reduce-scatter.5.cloned.1.call-done = bf16[128,2048]{1,0:T(8,128)(2,1)} async-done(((bf16[1024,2048]{1,0:T(8,128)(2,1)}), bf16[128,2048]{1,0:T(8,128)(2,1)}) %reduce-scatter.5.cloned.1.call-update) | async-done | bytes 524304 | tf_op jit(solution)/shard_map/reduce_scatter | solution.py:210
  321.4 2.3 add_convert_fusion
  (61 shorter events, 2.7 us)
Async XLA Ops:
  7.2 153.8 %copy-start = (bf16[512,2048]{1,0:T(8,128)(2,1)S(1)}, bf16[512,2048]{1,0:T(8,128)(2,1)}, u32[]{:S(2)}) copy-start(bf16[512,2048]{1,0:T(8,128)(2,1)} %param.22) | copy-start | bytes 6291460
  7.2 5.6 %copy-start.16 = (f32[2048]{0:T(1024)S(1)}, f32[2048]{0:T(1024)}, u32[]{:S(2)}) copy-start(f32[2048]{0:T(1024)} %param.17) | copy-start | bytes 24580
  7.2 5.6 %copy-start.14 = (bf16[2048,128]{1,0:T(8,128)(2,1)S(1)}, bf16[2048,128]{1,0:T(8,128)(2,1)}, u32[]{:S(2)}) copy-start(bf16[2048,128]{1,0:T(8,128)(2,1)} %param.20) | copy-start | bytes 1572868
  7.2 8.3 %copy-start.15 = (bf16[2048,128]{1,0:T(8,128)(2,1)S(1)}, bf16[2048,128]{1,0:T(8,128)(2,1)}, u32[]{:S(2)}) copy-start(bf16[2048,128]{1,0:T(8,128)(2,1)} %param.21) | copy-start | bytes 1572868
  7.2 119.0 %all-gather.4.cloned.1.call-start = ((), (), s32[]{:S(2)}) async-start(), calls=%async_computation.4 | async-start | bytes 5242880 | tf_op jit(solution)/shard_map/all_gather | solution.py:166
  7.9 126.6 %all-gather.6.cloned.1.call-start = ((), (), s32[]{:S(2)}) async-start(), calls=%async_computation.5 | async-start | bytes 5242880 | tf_op jit(solution)/shard_map/all_gather | solution.py:167
  10.5 4.9 %copy-start.8 = (bf16[512,2048]{1,0:T(8,128)(2,1)S(1)}, bf16[512,2048]{1,0:T(8,128)(2,1)}, u32[]{:S(2)}) copy-start(bf16[512,2048]{1,0:T(8,128)(2,1)} %param.16) | copy-start | bytes 6291460
  12.8 3.6 %copy-start.13 = (bf16[2048,512]{1,0:T(8,128)(2,1)S(1)}, bf16[2048,512]{1,0:T(8,128)(2,1)}, u32[]{:S(2)}) copy-start(bf16[2048,512]{1,0:T(8,128)(2,1)} %param.19) | copy-start | bytes 6291460
  25.5 11.7 %copy-start.6 = (s32[1,32]{1,0:T(1,128)S(1)}, s32[1,32]{1,0:T(1,128)}, u32[]{:S(2)}) copy-start(s32[1,32]{1,0:T(1,128)} %param.30) | copy-start | bytes 388
  28.4 41.7 %all-to-all-start = ((bf16[32,32,768]{2,1,0:T(8,128)(2,1)}), bf16[32,32,768]{2,1,0:T(8,128)(2,1)}, u32[]{:S(2)}, u32[]{:S(2)}) async-start(bf16[32,32,768]{2,1,0:T(8,128)(2,1)} %broadcast_select_fusion), calls=%async_computation | async-start | bytes 3145728 | tf_op jit(solution)/shard_map/all_to_all | solution.py:186
  88.0 5.9 %copy-start.5 = (s32[1,512]{1,0:T(1,128)S(1)}, s32[1,512]{1,0:T(1,128)}, u32[]{:S(2)}) copy-start(s32[1,512]{1,0:T(1,128)} %param.31) | copy-start | bytes 6148
  88.0 5.9 %copy-start.7 = (s32[1,32]{1,0:T(1,128)S(1)}, s32[1,32]{1,0:T(1,128)}, u32[]{:S(2)}) copy-start(s32[1,32]{1,0:T(1,128)} %param.29) | copy-start | bytes 388
  93.9 47.7 %copy-start.11 = (s32[512]{0:T(512)S(1)}, s32[512]{0:T(512)}, u32[]{:S(2)}) copy-start(s32[512]{0:T(512)} %param.28) | copy-start | bytes 6148
  93.9 1.6 copy-start.2
  95.5 1.0 copy-start.4
  125.1 1.1 copy-start.3
  134.6 23.7 %all-to-all-start.1 = ((bf16[32,32,512]{2,1,0:T(8,128)(2,1)}), bf16[32,32,512]{2,1,0:T(8,128)(2,1)S(1)}, u32[]{:S(2)}, u32[]{:S(2)}) async-start(bf16[32,32,512]{2,1,0:T(8,128)(2,1)} %copy-done.3), calls=%async_computation.1 | async-start | bytes 2097152 | tf_op jit(solution)/shard_map/all_to_all | solution.py:194
  141.5 51.2 %reduce-scatter.3.cloned.1.call-start = ((), (), s32[]{:S(2)}) async-start(), calls=%async_computation.6 | async-start | bytes 2621440 | tf_op jit(solution)/shard_map/reduce_scatter | solution.py:197
  160.9 33.3 %copy-start.12 = (f32[2048]{0:T(1024)S(1)}, f32[2048]{0:T(1024)}, u32[]{:S(2)}) copy-start(f32[2048]{0:T(1024)} %param.18) | copy-start | bytes 24580
  164.7 31.8 %copy-start.10 = (bf16[256,2048]{1,0:T(8,128)(2,1)S(1)}, bf16[256,2048]{1,0:T(8,128)(2,1)}, u32[]{:S(2)}) copy-start(bf16[256,2048]{1,0:T(8,128)(2,1)} %param.25) | copy-start | bytes 3145732
  164.7 94.3 %all-gather.8.cloned.1.call-start = ((), (), s32[]{:S(2)}) async-start(), calls=%async_computation.7 | async-start | bytes 4718592 | tf_op jit(solution)/shard_map/all_gather | solution.py:205
  196.4 125.0 %reduce-scatter.5.cloned.1.call-start = ((), (), s32[]{:S(2)}) async-start(), calls=%async_computation.8 | async-start | bytes 4718592 | tf_op jit(solution)/shard_map/reduce_scatter | solution.py:210
  196.5 26.4 %collective-permute-start = (bf16[256,2048]{1,0:T(8,128)(2,1)S(1)}, bf16[256,2048]{1,0:T(8,128)(2,1)S(1)}, u32[]{:S(2)}, u32[]{:S(2)}) collective-permute-start(bf16[256,2048]{1,0:T(8,128)(2,1)S(1)} %copy-done.10), channel_id=1, source_target_pairs={{0,32},{32,64},{64,96},{96,0},{1,33},{33,65},{65,97},{97,1},{2,34}... | collective-permute-start | bytes 3145736 | tf_op jit(solution)/shard_map/ppermute | solution.py:170
  198.1 46.4 %collective-permute-start.2 = (bf16[256,2048]{1,0:T(8,128)(2,1)S(1)}, bf16[256,2048]{1,0:T(8,128)(2,1)S(1)}, u32[]{:S(2)}, u32[]{:S(2)}) collective-permute-start(bf16[256,2048]{1,0:T(8,128)(2,1)S(1)} %copy-done.10), channel_id=1, source_target_pairs={{0,96},{32,0},{64,32},{96,64},{1,97},{33,1},{65,33},{97,65},{2,98}... | collective-permute-start | bytes 3145736 | tf_op jit(solution)/shard_map/ppermute | solution.py:170
  199.8 46.5 %collective-permute-start.1 = (bf16[256,2048]{1,0:T(8,128)(2,1)S(1)}, bf16[256,2048]{1,0:T(8,128)(2,1)}, u32[]{:S(2)}, u32[]{:S(2)}) collective-permute-start(bf16[256,2048]{1,0:T(8,128)(2,1)S(1)} %copy-done.10), channel_id=1, source_target_pairs={{0,64},{32,96},{64,0},{96,32},{1,65},{33,97},{65,1},{97,33},{2,66}... | collective-permute-start | bytes 3145736 | tf_op jit(solution)/shard_map/ppermute | solution.py:170
  268.9 54.7 %copy-start.1 = (bf16[512,2048]{1,0:T(8,128)(2,1)S(1)}, bf16[512,2048]{1,0:T(8,128)(2,1)}, u32[]{:S(2)}) copy-start(bf16[512,2048]{1,0:T(8,128)(2,1)} %param.22) | copy-start | bytes 6291460
  284.3 37.1 %copy-start.9 = (bf16[128,2048]{1,0:T(8,128)(2,1)S(1)}, bf16[128,2048]{1,0:T(8,128)(2,1)}, u32[]{:S(2)}) copy-start(bf16[128,2048]{1,0:T(8,128)(2,1)} %reduce-scatter.3.cloned.1.call-done) | copy-start | bytes 1572868
Sparse Core Ops, SparseCore 0:
  9.7 69.6 all-gather.3
  81.1 53.4 all-gather.5
  164.8 27.7 reduce-scatter.2
  196.6 32.0 all-gather.7
  284.4 36.9 reduce-scatter.4

commit v4 on v3

--- a/solution.py
+++ b/solution.py
@@ -170,8 +170,6 @@
         lax.ppermute(w_down, "ry", [(i, (i + shift) % ring) for i in range(ring)])
         for shift in range(1, ring)
     ]
-    part_at = (lax.axis_index("ry") - jnp.arange(ring, dtype=jnp.int32)) % ring
-    down_w = jnp.take(jnp.stack(down_parts), part_at, axis=0).reshape(-1, w_down.shape[1])
     normed = normalize(hidden_in.astype(jnp.float32), attn_gain).astype(jnp.bfloat16)
     qcols = w_query.shape[1]
     kcols = w_key.shape[1]
@@ -203,12 +201,22 @@
     residual = own_rows + RESIDUAL_MULT * attn_part
     mlp_in = normalize(residual, mlp_gain).astype(jnp.bfloat16)
     piece = lax.all_gather(mlp_in, "rzc", axis=0, tiled=True)
-    down_w, piece = lax.optimization_barrier((down_w, piece))
     gate = jnp.dot(piece, gate_w, preferred_element_type=jnp.float32)
     upper = jnp.dot(piece, up_w, preferred_element_type=jnp.float32)
     hidden = (jax.nn.silu(gate) * upper).astype(jnp.bfloat16)
+    down_parts, hidden = lax.optimization_barrier((down_parts, hidden))
+    units = w_down.shape[0]
+    partial = None
+    for shift, part in enumerate(down_parts):
+        block = (lax.axis_index("ry") - shift) % ring
+        term = jnp.dot(
+            lax.dynamic_slice_in_dim(hidden, block * units, units, axis=1),
+            part,
+            preferred_element_type=jnp.float32,
+        )
+        partial = term if partial is None else partial + term
     down = lax.psum_scatter(
-        jnp.dot(hidden, down_w, preferred_element_type=jnp.float32).astype(jnp.bfloat16),
+        partial.astype(jnp.bfloat16),
         "rzc",
         scatter_dimension=0,
         tiled=True,

time: 331 us -> 314 us (0.949)
  waiting for transfers between devices: 166 us -> 151 us
  matrix products: 34 us -> 43 us
  other arithmetic: 33.1 us -> 25.3 us
  local copies, waits for them, and re-layouts: 33.3 us -> 28.3 us
    ppermute x3, waiting for transfers between devices: 44.5 us -> 4.05 us  [body(): lax.ppermute(w_down, 'ry', [(i, (i + shift) % ring) for i in range(ring)])]
    all_gather x1, waiting for transfers between devices: 0.01 us -> 25.9 us  [body(): piece = lax.all_gather(mlp_in, 'rzc', axis=0, tiled=True)]
    dot_general x1 -> x5, matrix products: 15.3 us -> 26.6 us  [the longest x4 21.4 us: body(): jnp.dot(lax.dynamic_slice_in_dim(hidden, block * units, units, axis=1), p...]
    gather x1 -> x0, local copies, waits for them, and re-layouts: 4.94 us -> none  [body(): jnp.take(jnp.stack(down_parts), part_at, axis=0)]
    select_n x2 -> x0, other arithmetic: 4.58 us -> none  [body(): jnp.take(jnp.stack(down_parts), part_at, axis=0)]
    another operation x3 -> x2, other arithmetic: 8.94 us -> 5.74 us
  transfers between devices with their start and end apart: 10 -> 10, of which waited for: 8 -> 7; matrix products, arithmetic and copies ran while one was open for 18% -> 19% of each run, Pallas kernels for 9% -> 9%
where the time goes in v4:
time: 314 us; the launch traced here: 313 us
  waiting for transfers between devices  151 us (48%)
  matrix products  43 us (14%)
  Pallas kernels  28.7 us (9%)
  local copies, waits for them, and re-layouts  28.3 us (9%)
  other arithmetic  25.3 us (8%)
  starting transfers between devices  22.4 us (7%)
  between operations  14.1 us (4%)
    reduce_scatter x1, waiting for transfers between devices, body(): lax.psum_scatter(partial.astype(jnp.bfloat16), 'rzc', scatter_dimension=0...  37.6 us
    all_to_all x1, waiting for transfers between devices, body(): lax.all_to_all(send_qkv, REQ, split_axis=0, concat_axis=0, tiled=True)  29.9 us
    pallas_call x1, Pallas kernels, owner_attention(): pl.pallas_call(attention_kernel, out_shape=(jax.ShapeDtypeStruct((sources...  28.7 us
    reduce_scatter x1, waiting for transfers between devices, body(): lax.psum_scatter(projected.astype(jnp.bfloat16), 'grp', scatter_dimension...  27.6 us
    all_gather x1, waiting for transfers between devices, body(): piece = lax.all_gather(mlp_in, 'rzc', axis=0, tiled=True)  25.9 us
    dot_general x4, matrix products, body(): jnp.dot(lax.dynamic_slice_in_dim(hidden, block * units, units, axis=1), p...  21.4 us
    all_to_all x1, waiting for transfers between devices, body(): lax.all_to_all(mixed, REQ, split_axis=0, concat_axis=0, tiled=True)  16.7 us
    all_to_all x1, starting transfers between devices, body(): lax.all_to_all(send_qkv, REQ, split_axis=0, concat_axis=0, tiled=True)  8.77 us
  transfers between devices with their start and end apart: 10, of which 7 were waited for; matrix products, arithmetic and copies ran while one was open for 19% of the time, Pallas kernels for 9%

profile of v4, /device:TPU:0, one launch (start us, length us, event | category | flops | bytes accessed | tf_op | source)
XLA Modules:
  0.0 313.3 jit_solution(8577246740692611599)
XLA Ops:
  8.0 0.7 all-gather.6.cloned.1.call-update
  8.7 0.8 select_reduce_fusion.1
  9.5 0.9 select_reduce_fusion
  10.5 2.2 fusion
  12.8 2.6 convolution_convert_fusion.3
  15.5 1.0 convolution_convert_fusion.2
  16.4 1.4 convolution_convert_fusion.1
  17.9 0.9 pad_maximum_fusion.1
  18.8 1.4 copy.21
  20.3 5.2 %gather_fusion = bf16[1024,768]{1,0:T(8,128)(2,1)} fusion(bf16[512,768]{1,0:T(8,128)(2,1)S(1)} %copy.21, s32[1024]{0:T(1024)S(1)} %broadcast_clamp_fusion), kind=kCustom, calls=%fused_computation | custom fusion | bytes 3149824 | tf_op jit(solution)/shard_map/jit(_take)/gather | solution.py:181
  25.6 2.8 broadcast_select_fusion
  28.4 8.8 %all-to-all-start = ((bf16[32,32,768]{2,1,0:T(8,128)(2,1)}), bf16[32,32,768]{2,1,0:T(8,128)(2,1)}, u32[]{:S(2)}, u32[]{:S(2)}) async-start(bf16[32,32,768]{2,1,0:T(8,128)(2,1)} %broadcast_select_fusion), calls=%async_computation | async-start | bytes 3145728 | tf_op jit(solution)/shard_map/all_to_all | solution.py:184
  37.2 2.9 multiply_cosine_fusion
  40.2 29.9 %all-to-all-done = bf16[32,32,768]{2,1,0:T(8,128)(2,1)} async-done(((bf16[32,32,768]{2,1,0:T(8,128)(2,1)}), bf16[32,32,768]{2,1,0:T(8,128)(2,1)}, u32[]{:S(2)}, u32[]{:S(2)}) %all-to-all-start) | async-done | bytes 1572896 | tf_op jit(solution)/shard_map/all_to_all | solution.py:184
  70.1 1.8 fusion.32
  72.1 1.0 fusion.33
  73.2 1.5 fusion.8
  75.0 1.3 copy.24
  76.3 1.3 convert_element_type.94.k_ref
  77.6 2.3 slice.32
  79.9 3.9 %reshape.154 = bf16[32,32,8,64]{3,2,1,0:T(8,128)(2,1)} reshape(bf16[32,32,512]{2,1,0:T(8,128)(2,1)} %slice.32) | data formatting | bytes 2097152 | tf_op jit(solution)/shard_map/reshape | solution.py:116
  83.8 4.3 %fusion.4 = (bf16[32,32,8,32]{3,2,1,0:T(8,128)(2,1)S(1)}, bf16[32,32,8,32]{3,2,1,0:T(8,128)(2,1)S(1)}) fusion(f32[32,32,32]{2,1,0:T(8,128)} %get-tuple-element.38, f32[32,32,32]{2,1,0:T(8,128)S(1)} %get-tuple-element.37, bf16[32,32,8,64]{3,2,1,0:T(8,128)(2,1)} %reshape.154), kind=kLoop, calls=%fused_computation.13 | loop fusion | flops 2621440 | bytes 2359296 | tf_op jit(solution)/shard_map/convert.2
  88.1 2.5 pad_maximum_fusion
  90.6 3.3 %convert_element_type.91.q_ref = bf16[32,32,512]{2,1,0:T(8,128)(2,1)S(1)} reshape(bf16[32,32,8,64]{3,2,1,0:T(8,128)(2,1)} %pad_maximum_fusion) | data formatting | bytes 2097152 | tf_op jit(solution)/shard_map/convert_element_type | solution.py:116
  94.0 1.6 copy-done.2
  95.6 1.0 copy-done.4
  96.5 28.7 %shard_map.175 = (bf16[32,32,512]{2,1,0:T(8,128)(2,1)S(1)}, bf16[512,16,128]{2,1,0:T(8,128)(2,1)}, bf16[512,16,128]{2,1,0:T(8,128)(2,1)}) custom-call(s32[512]{0:T(512)S(1)} %bitcast.20, s32[32]{0:T(128)S(1)} %bitcast.22, s32[32]{0:T(128)S(1)} %bitcast.23, bf16[32,32,512]{2,1,0:T(8,128)(2,1)S(1)} %convert_element_type.91.q_ref, ...), custom_call_target="tpu_custom_call" | custom-call | tf_op jit(solution)/shard_map/pallas_call | solution.py:125
  125.2 1.1 copy-done.3
  126.3 8.3 %all-gather.6.cloned.1.call-done = bf16[2048,1024]{1,0:T(8,128)(2,1)} async-done(((bf16[2048,256]{1,0:T(8,128)(2,1)}), bf16[2048,1024]{1,0:T(8,128)(2,1)}) %all-gather.6.cloned.1.call-update) | async-done | bytes 4194320 | tf_op jit(solution)/shard_map/all_gather | solution.py:167
  134.6 7.1 %all-to-all-start.1 = ((bf16[32,32,512]{2,1,0:T(8,128)(2,1)}), bf16[32,32,512]{2,1,0:T(8,128)(2,1)S(1)}, u32[]{:S(2)}, u32[]{:S(2)}) async-start(bf16[32,32,512]{2,1,0:T(8,128)(2,1)} %copy-done.3), calls=%async_computation.1 | async-start | bytes 2097152 | tf_op jit(solution)/shard_map/all_to_all | solution.py:192
  141.7 16.7 %all-to-all-done.1 = bf16[32,32,512]{2,1,0:T(8,128)(2,1)S(1)} async-done(((bf16[32,32,512]{2,1,0:T(8,128)(2,1)}), bf16[32,32,512]{2,1,0:T(8,128)(2,1)S(1)}, u32[]{:S(2)}, u32[]{:S(2)}) %all-to-all-start.1) | async-done | bytes 1048608 | tf_op jit(solution)/shard_map/all_to_all | solution.py:192
  158.5 2.6 gather_fusion.1
  161.1 3.8 %convolution_convert_fusion = bf16[512,2048]{1,0:T(8,128)(2,1)} fusion(bf16[512,2048]{1,0:T(8,128)(2,1)S(1)} %copy-done, bf16[512,512]{1,0:T(8,128)(2,1)} %gather_fusion.1, pred[512]{0:T(512)(128)(4,1)S(1)} %get-tuple-element.27), kind=kOutput, calls=%fused_computation.17 | convolution fusion | flops 1075052544 | bytes 4719104 | tf_op jit(solution)/shard_map/dot_general | solution.py:194
  164.9 27.6 %reduce-scatter.3.cloned.1.call-done = bf16[128,2048]{1,0:T(8,128)(2,1)} async-done(((bf16[512,2048]{1,0:T(8,128)(2,1)}), bf16[128,2048]{1,0:T(8,128)(2,1)}) %reduce-scatter.3.cloned.1.call-update) | async-done | bytes 524304 | tf_op jit(solution)/shard_map/reduce_scatter | solution.py:195
  192.5 1.5 multiply_reduce_fusion
  194.0 2.2 multiply_convert_fusion.1
  196.3 3.1 collective-permute-start.1
  200.0 2.6 collective-permute-start.2
  202.7 25.9 %all-gather.8.cloned.1.call-done = bf16[1024,2048]{1,0:T(8,128)(2,1)} async-done(((bf16[128,2048]{1,0:T(8,128)(2,1)}), bf16[1024,2048]{1,0:T(8,128)(2,1)}) %all-gather.8.cloned.1.call-update) | async-done | bytes 4194320 | tf_op jit(solution)/shard_map/all_gather | solution.py:203
  228.5 7.7 %fusion.34 = f32[1024,1024]{1,0:T(8,128)S(1)} fusion(bf16[1024,2048]{1,0:T(8,128)(2,1)} %all-gather.8.cloned.1.call-done, bf16[2048,1024]{1,0:T(8,128)(2,1)} %all-gather.4.cloned.1.call-done), kind=kOutput, calls=%fused_computation.74 | convolution fusion | flops 4294967296 | bytes 12582912 | tf_op jit(solution)/shard_map/dot_general | solution.py:204
  236.2 5.2 %multiply_convert_fusion = bf16[1024,1024]{1,0:T(8,128)(2,1)S(1)} fusion(f32[1024,1024]{1,0:T(8,128)S(1)} %fusion.34, bf16[1024,2048]{1,0:T(8,128)(2,1)S(1)} %copy-done.14, bf16[2048,1024]{1,0:T(8,128)(2,1)S(1)} %copy-done.13), kind=kOutput, calls=%fused_computation.16 | convolution fusion | flops 4301258752 | bytes 14680064 | tf_op jit(solution)/shard_map/dot_general | solution.py:205
  241.4 4.0 %collective-permute-done = bf16[256,2048]{1,0:T(8,128)(2,1)} collective-permute-done((bf16[256,2048]{1,0:T(8,128)(2,1)S(1)}, bf16[256,2048]{1,0:T(8,128)(2,1)}, u32[]{:S(2)}, u32[]{:S(2)}) %collective-permute-start) | collective-permute-done | bytes 1048608 | tf_op jit(solution)/shard_map/ppermute | solution.py:170
  245.5 1.3 fusion.19
  246.7 5.8 %fusion.17 = f32[1024,2048]{1,0:T(8,128)} fusion(bf16[256,2048]{1,0:T(8,128)(2,1)} %collective-permute-done, bf16[1024,1024]{1,0:T(8,128)(2,1)S(1)} %multiply_convert_fusion, s32[]{:T(128)S(6)} %select_n.104), kind=kOutput, calls=%fused_computation.43 | convolution fusion | flops 1073741824 | bytes 9961476 | tf_op jit(solution)/shard_map/dot_general | solution.py:212
  252.5 4.5 %fusion.15 = f32[1024,2048]{1,0:T(8,128)} fusion(bf16[256,2048]{1,0:T(8,128)(2,1)S(1)} %collective-permute-done.1, bf16[1024,1024]{1,0:T(8,128)(2,1)S(1)} %multiply_convert_fusion, s32[]{:T(128)S(6)} %select_n.106), kind=kOutput, calls=%fused_computation.41 | convolution fusion | flops 1073741824 | bytes 9961476 | tf_op jit(solution)/shard_map/dot_general | solution.py:212
  257.0 9.8 %add_convert_fusion = bf16[1024,2048]{1,0:T(8,128)(2,1)} fusion(f32[1024,2048]{1,0:T(8,128)} %fusion.15, f32[1024,2048]{1,0:T(8,128)S(1)} %fusion.19, f32[1024,2048]{1,0:T(8,128)} %fusion.17, bf16[256,2048]{1,0:T(8,128)(2,1)S(1)} %collective-permute-done.2, bf16[1024,1024]{1,0:T(8,128)(2,1)S(1)} %multiply_convert_fusion, s32[]{:T(128)S(6)} %select_n.108), kind=kOutput, calls=%fused_computation.2 | convolution fusion | flops 1082130432 | bytes 30932996 | tf_op jit(solution)/shard_map/dot_general | solution.py:212
  266.9 37.6 %reduce-scatter.5.cloned.1.call-done = bf16[128,2048]{1,0:T(8,128)(2,1)} async-done(((bf16[1024,2048]{1,0:T(8,128)(2,1)}), bf16[128,2048]{1,0:T(8,128)(2,1)}) %reduce-scatter.5.cloned.1.call-update) | async-done | bytes 524304 | tf_op jit(solution)/shard_map/reduce_scatter | solution.py:218
  304.5 2.3 add_convert_fusion.1
  (61 shorter events, 2.5 us)
Async XLA Ops:
  7.2 153.9 %copy-start = (bf16[512,2048]{1,0:T(8,128)(2,1)S(1)}, bf16[512,2048]{1,0:T(8,128)(2,1)}, u32[]{:S(2)}) copy-start(bf16[512,2048]{1,0:T(8,128)(2,1)} %param.22) | copy-start | bytes 6291460
  7.2 5.6 %copy-start.18 = (f32[2048]{0:T(1024)S(1)}, f32[2048]{0:T(1024)}, u32[]{:S(2)}) copy-start(f32[2048]{0:T(1024)} %param.17) | copy-start | bytes 24580
  7.2 5.6 %copy-start.16 = (bf16[2048,128]{1,0:T(8,128)(2,1)S(1)}, bf16[2048,128]{1,0:T(8,128)(2,1)}, u32[]{:S(2)}) copy-start(bf16[2048,128]{1,0:T(8,128)(2,1)} %param.20) | copy-start | bytes 1572868
  7.2 8.3 %copy-start.17 = (bf16[2048,128]{1,0:T(8,128)(2,1)S(1)}, bf16[2048,128]{1,0:T(8,128)(2,1)}, u32[]{:S(2)}) copy-start(bf16[2048,128]{1,0:T(8,128)(2,1)} %param.21) | copy-start | bytes 1572868
  7.2 119.1 %all-gather.4.cloned.1.call-start = ((), (), s32[]{:S(2)}) async-start(), calls=%async_computation.4 | async-start | bytes 5242880 | tf_op jit(solution)/shard_map/all_gather | solution.py:166
  7.9 126.6 %all-gather.6.cloned.1.call-start = ((), (), s32[]{:S(2)}) async-start(), calls=%async_computation.5 | async-start | bytes 5242880 | tf_op jit(solution)/shard_map/all_gather | solution.py:167
  10.5 4.9 %copy-start.8 = (bf16[512,2048]{1,0:T(8,128)(2,1)S(1)}, bf16[512,2048]{1,0:T(8,128)(2,1)}, u32[]{:S(2)}) copy-start(bf16[512,2048]{1,0:T(8,128)(2,1)} %param.16) | copy-start | bytes 6291460
  12.8 3.6 %copy-start.15 = (bf16[2048,512]{1,0:T(8,128)(2,1)S(1)}, bf16[2048,512]{1,0:T(8,128)(2,1)}, u32[]{:S(2)}) copy-start(bf16[2048,512]{1,0:T(8,128)(2,1)} %param.19) | copy-start | bytes 6291460
  25.5 11.7 %copy-start.6 = (s32[1,32]{1,0:T(1,128)S(1)}, s32[1,32]{1,0:T(1,128)}, u32[]{:S(2)}) copy-start(s32[1,32]{1,0:T(1,128)} %param.30) | copy-start | bytes 388
  28.4 41.7 %all-to-all-start = ((bf16[32,32,768]{2,1,0:T(8,128)(2,1)}), bf16[32,32,768]{2,1,0:T(8,128)(2,1)}, u32[]{:S(2)}, u32[]{:S(2)}) async-start(bf16[32,32,768]{2,1,0:T(8,128)(2,1)} %broadcast_select_fusion), calls=%async_computation | async-start | bytes 3145728 | tf_op jit(solution)/shard_map/all_to_all | solution.py:184
  88.1 5.9 %copy-start.5 = (s32[1,512]{1,0:T(1,128)S(1)}, s32[1,512]{1,0:T(1,128)}, u32[]{:S(2)}) copy-start(s32[1,512]{1,0:T(1,128)} %param.31) | copy-start | bytes 6148
  88.1 5.9 %copy-start.7 = (s32[1,32]{1,0:T(1,128)S(1)}, s32[1,32]{1,0:T(1,128)}, u32[]{:S(2)}) copy-start(s32[1,32]{1,0:T(1,128)} %param.29) | copy-start | bytes 388
  93.9 47.8 %copy-start.11 = (s32[512]{0:T(512)S(1)}, s32[512]{0:T(512)}, u32[]{:S(2)}) copy-start(s32[512]{0:T(512)} %param.28) | copy-start | bytes 6148
  93.9 1.6 copy-start.2
  95.6 1.0 copy-start.4
  125.2 1.1 copy-start.3
  134.6 23.9 %all-to-all-start.1 = ((bf16[32,32,512]{2,1,0:T(8,128)(2,1)}), bf16[32,32,512]{2,1,0:T(8,128)(2,1)S(1)}, u32[]{:S(2)}, u32[]{:S(2)}) async-start(bf16[32,32,512]{2,1,0:T(8,128)(2,1)} %copy-done.3), calls=%async_computation.1 | async-start | bytes 2097152 | tf_op jit(solution)/shard_map/all_to_all | solution.py:192
  141.6 50.9 %reduce-scatter.3.cloned.1.call-start = ((), (), s32[]{:S(2)}) async-start(), calls=%async_computation.6 | async-start | bytes 2621440 | tf_op jit(solution)/shard_map/reduce_scatter | solution.py:195
  161.1 32.9 %copy-start.12 = (f32[2048]{0:T(1024)S(1)}, f32[2048]{0:T(1024)}, u32[]{:S(2)}) copy-start(f32[2048]{0:T(1024)} %param.18) | copy-start | bytes 24580
  164.8 31.5 %copy-start.10 = (bf16[256,2048]{1,0:T(8,128)(2,1)S(1)}, bf16[256,2048]{1,0:T(8,128)(2,1)}, u32[]{:S(2)}) copy-start(bf16[256,2048]{1,0:T(8,128)(2,1)} %param.25) | copy-start | bytes 3145732
  164.9 63.7 %all-gather.8.cloned.1.call-start = ((), (), s32[]{:S(2)}) async-start(), calls=%async_computation.7 | async-start | bytes 4718592 | tf_op jit(solution)/shard_map/all_gather | solution.py:203
  196.3 108.2 %reduce-scatter.5.cloned.1.call-start = ((), (), s32[]{:S(2)}) async-start(), calls=%async_computation.8 | async-start | bytes 4718592 | tf_op jit(solution)/shard_map/reduce_scatter | solution.py:218
  196.3 45.1 %collective-permute-start.1 = (bf16[256,2048]{1,0:T(8,128)(2,1)S(1)}, bf16[256,2048]{1,0:T(8,128)(2,1)S(1)}, u32[]{:S(2)}, u32[]{:S(2)}) collective-permute-start(bf16[256,2048]{1,0:T(8,128)(2,1)S(1)} %copy-done.10), channel_id=1, source_target_pairs={{0,64},{32,96},{64,0},{96,32},{1,65},{33,97},{65,1},{97,33},{2,66}... | collective-permute-start | bytes 3145736 | tf_op jit(solution)/shard_map/ppermute | solution.py:170
  199.4 46.0 %collective-permute-start = (bf16[256,2048]{1,0:T(8,128)(2,1)S(1)}, bf16[256,2048]{1,0:T(8,128)(2,1)}, u32[]{:S(2)}, u32[]{:S(2)}) collective-permute-start(bf16[256,2048]{1,0:T(8,128)(2,1)S(1)} %copy-done.10), channel_id=1, source_target_pairs={{0,32},{32,64},{64,96},{96,0},{1,33},{33,65},{65,97},{97,1},{2,34}... | collective-permute-start | bytes 3145736 | tf_op jit(solution)/shard_map/ppermute | solution.py:170
  200.0 45.4 %collective-permute-start.2 = (bf16[256,2048]{1,0:T(8,128)(2,1)S(1)}, bf16[256,2048]{1,0:T(8,128)(2,1)S(1)}, u32[]{:S(2)}, u32[]{:S(2)}) collective-permute-start(bf16[256,2048]{1,0:T(8,128)(2,1)S(1)} %copy-done.10), channel_id=1, source_target_pairs={{0,96},{32,0},{64,32},{96,64},{1,97},{33,1},{65,33},{97,65},{2,98}... | collective-permute-start | bytes 3145736 | tf_op jit(solution)/shard_map/ppermute | solution.py:170
  228.5 7.7 %copy-start.13 = (bf16[2048,1024]{1,0:T(8,128)(2,1)S(1)}, bf16[2048,1024]{1,0:T(8,128)(2,1)}, u32[]{:S(2)}) copy-start(bf16[2048,1024]{1,0:T(8,128)(2,1)} %all-gather.6.cloned.1.call-done) | copy-start | bytes 12582916
  228.5 7.7 %copy-start.14 = (bf16[1024,2048]{1,0:T(8,128)(2,1)S(1)}, bf16[1024,2048]{1,0:T(8,128)(2,1)}, u32[]{:S(2)}) copy-start(bf16[1024,2048]{1,0:T(8,128)(2,1)} %all-gather.8.cloned.1.call-done) | copy-start | bytes 12582916
  257.0 49.7 %copy-start.1 = (bf16[512,2048]{1,0:T(8,128)(2,1)S(1)}, bf16[512,2048]{1,0:T(8,128)(2,1)}, u32[]{:S(2)}) copy-start(bf16[512,2048]{1,0:T(8,128)(2,1)} %param.22) | copy-start | bytes 6291460
  266.8 37.6 %copy-start.9 = (bf16[128,2048]{1,0:T(8,128)(2,1)S(1)}, bf16[128,2048]{1,0:T(8,128)(2,1)}, u32[]{:S(2)}) copy-start(bf16[128,2048]{1,0:T(8,128)(2,1)} %reduce-scatter.3.cloned.1.call-done) | copy-start | bytes 1572868
Sparse Core Ops, SparseCore 0:
  9.7 69.6 all-gather.3
  81.1 53.4 all-gather.5
  165.0 27.4 reduce-scatter.2
  196.4 32.0 all-gather.7
  267.0 37.4 reduce-scatter.4

commit v5 on v4

--- a/solution.py
+++ b/solution.py
@@ -1,3 +1,5 @@
+import functools
+
 import jax
 import jax.numpy as jnp
 from jax import lax
@@ -139,6 +141,70 @@
     )(table, priors, lengths, query_rot, key_rot, value_in, cache_keys, cache_values)
 
 
+def exchange_kernel(shape, x_ref, o_ref, local_sem, send_sems, recv_sems):
+    rows_axis, cols_axis = shape
+    peers = rows_axis * cols_axis
+    me = lax.axis_index("ry") * cols_axis + lax.axis_index("rzc")
+    grp = lax.axis_index("grp")
+
+    def device(peer):
+        return (peer // cols_axis, peer % cols_axis, grp)
+
+    barrier = pltpu.get_barrier_semaphore()
+
+    def greet(k, carry):
+        pl.semaphore_signal(
+            barrier, inc=1, device_id=device((me + k) % peers), device_id_type=pl.DeviceIdType.MESH
+        )
+        return carry
+
+    lax.fori_loop(1, peers, greet, 0)
+    pl.semaphore_wait(barrier, peers - 1)
+    local = pltpu.make_async_copy(x_ref.at[me], o_ref.at[me], local_sem)
+    local.start()
+
+    def remote(k):
+        peer = (me + k) % peers
+        return pltpu.make_async_remote_copy(
+            src_ref=x_ref.at[peer],
+            dst_ref=o_ref.at[me],
+            send_sem=send_sems.at[k],
+            recv_sem=recv_sems.at[k],
+            device_id=device(peer),
+            device_id_type=pl.DeviceIdType.MESH,
+        )
+
+    def send(k, carry):
+        remote(k).start()
+        return carry
+
+    def finish(k, carry):
+        remote(k).wait()
+        return carry
+
+    lax.fori_loop(1, peers, send, 0)
+    local.wait()
+    lax.fori_loop(1, peers, finish, 0)
+
+
+def exchange(x, collective_id):
+    shape = (lax.axis_size("ry"), lax.axis_size("rzc"))
+    peers = shape[0] * shape[1]
+    any_space = pl.BlockSpec(memory_space=pl.ANY)
+    return pl.pallas_call(
+        functools.partial(exchange_kernel, shape),
+        out_shape=jax.ShapeDtypeStruct(x.shape, x.dtype),
+        in_specs=[any_space],
+        out_specs=any_space,
+        scratch_shapes=[
+            pltpu.SemaphoreType.DMA,
+            pltpu.SemaphoreType.DMA((peers,)),
+            pltpu.SemaphoreType.DMA((peers,)),
+        ],
+        compiler_params=pltpu.CompilerParams(collective_id=collective_id, has_side_effects=True),
+    )(x)
+
+
 def body(
     hidden_in,
     attn_gain,
@@ -181,7 +247,7 @@
     send_qkv = jnp.take(qkv_rows, gather_rows, axis=0, mode="fill", fill_value=0).reshape(
         peers, pair_rows, -1
     )
-    recv_qkv = lax.all_to_all(send_qkv, REQ, split_axis=0, concat_axis=0, tiled=True)
+    recv_qkv = exchange(send_qkv, 0)
     recv_query = recv_qkv[..., :qcols]
     recv_key = recv_qkv[..., qcols : qcols + kcols]
     recv_value = recv_qkv[..., qcols + kcols :]
@@ -189,7 +255,7 @@
         recv_query, recv_key, recv_value, cache_k, cache_v, new_len[0], prior_len[0], page_table[0]
     )
     gate_w, up_w, mixed = lax.optimization_barrier((gate_w, up_w, mixed))
-    returned = lax.all_to_all(mixed, REQ, split_axis=0, concat_axis=0, tiled=True)
+    returned = exchange(mixed, 1)
     attn_rows = jnp.take(returned.reshape(peers * pair_rows, -1), back_rows, axis=0)
     projected = jnp.dot(attn_rows, w_out, preferred_element_type=jnp.float32)
     attn_part = lax.psum_scatter(

time: 314 us -> 317 us (level)
  Pallas kernels: 28.7 us -> 88.3 us
  waiting for transfers between devices: 151 us -> 115 us
  starting transfers between devices: 22.4 us -> 6.75 us
    pallas_call x0 -> x2, Pallas kernels: none -> 59.5 us  [exchange(): pl.pallas_call(functools.partial(exchange_kernel, shape), out_shape=jax.S...]
    all_to_all x2 -> x0, waiting for transfers between devices: 46.6 us -> none  [the longest x1 29.9 us: body(): lax.all_to_all(send_qkv, REQ, split_axis=0, concat_axis=0, tiled=True)]
    all_to_all x2 -> x0, starting transfers between devices: 15.8 us -> none  [the longest x1 8.77 us: body(): lax.all_to_all(send_qkv, REQ, split_axis=0, concat_axis=0, tiled=True)]
    all_gather x1, waiting for transfers between devices: 8.28 us -> 13.6 us  [body(): up_w = lax.all_gather(w_up, 'ry', axis=1, tiled=True)]
    reduce_scatter x1, waiting for transfers between devices: 27.6 us -> 32 us  [body(): lax.psum_scatter(projected.astype(jnp.bfloat16), 'grp', scatter_dimension...]
  transfers between devices with their start and end apart: 10 -> 8, of which waited for: 7 -> 5; matrix products, arithmetic and copies ran while one was open for 19% -> 18% of each run, Pallas kernels for 9% -> 21%
where the time goes in v5:
time: 317 us; the launch traced here: 316 us
  waiting for transfers between devices  115 us (36%)
  Pallas kernels  88.3 us (28%)
  matrix products  41.9 us (13%)
  local copies, waits for them, and re-layouts  27.3 us (9%)
  other arithmetic  23.4 us (7%)
  between operations  14.2 us (4%)
  starting transfers between devices  6.75 us (2%)
    pallas_call x2, Pallas kernels, exchange(): pl.pallas_call(functools.partial(exchange_kernel, shape), out_shape=jax.S...  59.5 us
    reduce_scatter x1, waiting for transfers between devices, body(): lax.psum_scatter(partial.astype(jnp.bfloat16), 'rzc', scatter_dimension=0...  37.6 us
    reduce_scatter x1, waiting for transfers between devices, body(): lax.psum_scatter(projected.astype(jnp.bfloat16), 'grp', scatter_dimension...  32 us
    pallas_call x1, Pallas kernels, owner_attention(): pl.pallas_call(attention_kernel, out_shape=(jax.ShapeDtypeStruct((sources...  28.8 us
    all_gather x1, waiting for transfers between devices, body(): piece = lax.all_gather(mlp_in, 'rzc', axis=0, tiled=True)  25.9 us
    dot_general x4, matrix products, body(): jnp.dot(lax.dynamic_slice_in_dim(hidden, block * units, units, axis=1), p...  21.4 us
    all_gather x1, waiting for transfers between devices, body(): up_w = lax.all_gather(w_up, 'ry', axis=1, tiled=True)  13.6 us
    dot_general x1, matrix products, body(): gate = jnp.dot(piece, gate_w, preferred_element_type=jnp.float32)  7.64 us
  transfers between devices with their start and end apart: 8, of which 5 were waited for; matrix products, arithmetic and copies ran while one was open for 18% of the time, Pallas kernels for 21%

profile of v5, /device:TPU:0, one launch (start us, length us, event | category | flops | bytes accessed | tf_op | source)
XLA Modules:
  0.0 316.4 jit_solution(8361087546238643318)
XLA Ops:
  7.3 0.7 all-gather.4.cloned.1.call-update
  8.0 0.7 all-gather.6.cloned.1.call-update
  8.7 0.8 select_reduce_fusion.1
  9.5 0.9 select_reduce_fusion
  10.6 2.2 fusion
  12.9 2.6 convolution_convert_fusion.3
  15.5 0.9 convolution_convert_fusion.2
  16.5 1.4 convolution_convert_fusion.1
  17.9 0.9 pad_maximum_fusion.1
  18.9 1.4 copy.21
  20.3 5.4 %gather_fusion = bf16[1024,768]{1,0:T(8,128)(2,1)} fusion(bf16[512,768]{1,0:T(8,128)(2,1)S(1)} %copy.21, s32[1024]{0:T(1024)S(1)} %broadcast_clamp_fusion), kind=kCustom, calls=%fused_computation | custom fusion | bytes 3149824 | tf_op jit(solution)/shard_map/jit(_take)/gather | solution.py:247
  25.8 2.8 broadcast_select_fusion.x_ref
  28.6 39.1 %shard_map.175 = bf16[32,32,768]{2,1,0:T(8,128)(2,1)} custom-call(bf16[32,32,768]{2,1,0:T(8,128)(2,1)} %broadcast_select_fusion.x_ref), custom_call_target="tpu_custom_call" | custom-call | tf_op jit(solution)/shard_map/pallas_call | solution.py:194
  67.7 1.8 fusion.32
  69.5 1.0 reshape.155
  70.6 1.9 multiply_cosine_fusion
  72.6 2.6 fusion.33
  75.2 0.4 fusion.8
  76.0 1.3 copy.24
  77.3 1.3 convert_element_type.94.k_ref
  78.6 2.1 reshape.154
  80.7 4.4 %fusion.4 = (bf16[32,32,8,32]{3,2,1,0:T(8,128)(2,1)S(1)}, bf16[32,32,8,32]{3,2,1,0:T(8,128)(2,1)S(1)}) fusion(f32[32,32,32]{2,1,0:T(8,128)} %copy-done.11, f32[32,32,32]{2,1,0:T(8,128)} %copy-done.10, bf16[32,32,8,64]{3,2,1,0:T(8,128)(2,1)} %reshape.154), kind=kLoop, calls=%fused_computation.13 | loop fusion | flops 2621440 | bytes 2359296 | tf_op jit(solution)/shard_map/convert.2
  85.1 2.5 pad_maximum_fusion
  87.6 3.2 %convert_element_type.91.q_ref = bf16[32,32,512]{2,1,0:T(8,128)(2,1)S(1)} reshape(bf16[32,32,8,64]{3,2,1,0:T(8,128)(2,1)} %pad_maximum_fusion) | data formatting | bytes 2097152 | tf_op jit(solution)/shard_map/convert_element_type | solution.py:118
  90.8 1.6 copy-done.2
  92.4 1.0 copy-done.4
  93.4 28.8 %shard_map.176 = (bf16[32,32,512]{2,1,0:T(8,128)(2,1)S(1)}, bf16[512,16,128]{2,1,0:T(8,128)(2,1)}, bf16[512,16,128]{2,1,0:T(8,128)(2,1)}) custom-call(s32[512]{0:T(512)S(1)} %bitcast.20, s32[32]{0:T(128)S(1)} %bitcast.22, s32[32]{0:T(128)S(1)} %bitcast.23, bf16[32,32,512]{2,1,0:T(8,128)(2,1)S(1)} %convert_element_type.91.q_ref, ...), custom_call_target="tpu_custom_call" | custom-call | tf_op jit(solution)/shard_map/pallas_call | solution.py:127
  122.2 1.1 copy-done.3
  123.3 13.6 %all-gather.6.cloned.1.call-done = bf16[2048,1024]{1,0:T(8,128)(2,1)} async-done(((bf16[2048,256]{1,0:T(8,128)(2,1)}), bf16[2048,1024]{1,0:T(8,128)(2,1)}) %all-gather.6.cloned.1.call-update) | async-done | bytes 4194320 | tf_op jit(solution)/shard_map/all_gather | solution.py:233
  137.0 20.3 %shard_map.177 = bf16[32,32,512]{2,1,0:T(8,128)(2,1)} custom-call(bf16[32,32,512]{2,1,0:T(8,128)(2,1)} %copy-done.3), custom_call_target="tpu_custom_call" | custom-call | tf_op jit(solution)/shard_map/pallas_call | solution.py:194
  157.3 3.3 %gather_fusion.1 = bf16[512,512]{1,0:T(8,128)(2,1)S(1)} fusion(bf16[1024,512]{1,0:T(8,128)(2,1)} %bitcast.24, s32[1024]{0:T(1024)S(1)} %pad_clamp_fusion), kind=kCustom, calls=%fused_computation.1 | custom fusion | bytes 1050624 | tf_op jit(solution)/shard_map/jit(_take)/gather | solution.py:259
  160.7 2.7 convolution_convert_fusion
  163.7 32.0 %reduce-scatter.3.cloned.1.call-done = bf16[128,2048]{1,0:T(8,128)(2,1)} async-done(((bf16[512,2048]{1,0:T(8,128)(2,1)}), bf16[128,2048]{1,0:T(8,128)(2,1)}) %reduce-scatter.3.cloned.1.call-update) | async-done | bytes 524304 | tf_op jit(solution)/shard_map/reduce_scatter | solution.py:261
  195.6 1.5 multiply_reduce_fusion
  197.1 2.2 multiply_convert_fusion.1
  199.5 3.1 collective-permute-start.1
  202.5 0.6 collective-permute-start
  203.2 2.6 collective-permute-start.2
  205.8 25.9 %all-gather.8.cloned.1.call-done = bf16[1024,2048]{1,0:T(8,128)(2,1)} async-done(((bf16[128,2048]{1,0:T(8,128)(2,1)}), bf16[1024,2048]{1,0:T(8,128)(2,1)}) %all-gather.8.cloned.1.call-update) | async-done | bytes 4194320 | tf_op jit(solution)/shard_map/all_gather | solution.py:269
  231.7 7.6 %fusion.34 = f32[1024,1024]{1,0:T(8,128)S(1)} fusion(bf16[1024,2048]{1,0:T(8,128)(2,1)} %all-gather.8.cloned.1.call-done, bf16[2048,1024]{1,0:T(8,128)(2,1)} %all-gather.4.cloned.1.call-done), kind=kOutput, calls=%fused_computation.74 | convolution fusion | flops 4294967296 | bytes 12582912 | tf_op jit(solution)/shard_map/dot_general | solution.py:270
  239.3 5.2 %multiply_convert_fusion = bf16[1024,1024]{1,0:T(8,128)(2,1)S(1)} fusion(f32[1024,1024]{1,0:T(8,128)S(1)} %fusion.34, bf16[1024,2048]{1,0:T(8,128)(2,1)S(1)} %copy-done.16, bf16[2048,1024]{1,0:T(8,128)(2,1)S(1)} %copy-done.15), kind=kOutput, calls=%fused_computation.16 | convolution fusion | flops 4301258752 | bytes 14680064 | tf_op jit(solution)/shard_map/dot_general | solution.py:271
  244.5 4.1 %collective-permute-done = bf16[256,2048]{1,0:T(8,128)(2,1)} collective-permute-done((bf16[256,2048]{1,0:T(8,128)(2,1)S(1)}, bf16[256,2048]{1,0:T(8,128)(2,1)}, u32[]{:S(2)}, u32[]{:S(2)}) %collective-permute-start) | collective-permute-done | bytes 1048608 | tf_op jit(solution)/shard_map/ppermute | solution.py:236
  248.6 1.3 fusion.19
  249.8 5.8 %fusion.17 = f32[1024,2048]{1,0:T(8,128)} fusion(bf16[256,2048]{1,0:T(8,128)(2,1)} %collective-permute-done, bf16[1024,1024]{1,0:T(8,128)(2,1)S(1)} %multiply_convert_fusion, s32[]{:T(128)S(6)} %select_n.104), kind=kOutput, calls=%fused_computation.43 | convolution fusion | flops 1073741824 | bytes 9961476 | tf_op jit(solution)/shard_map/dot_general | solution.py:278
  255.6 4.5 %fusion.15 = f32[1024,2048]{1,0:T(8,128)} fusion(bf16[256,2048]{1,0:T(8,128)(2,1)S(1)} %collective-permute-done.1, bf16[1024,1024]{1,0:T(8,128)(2,1)S(1)} %multiply_convert_fusion, s32[]{:T(128)S(6)} %select_n.106), kind=kOutput, calls=%fused_computation.41 | convolution fusion | flops 1073741824 | bytes 9961476 | tf_op jit(solution)/shard_map/dot_general | solution.py:278
  260.1 9.8 %add_convert_fusion = bf16[1024,2048]{1,0:T(8,128)(2,1)} fusion(f32[1024,2048]{1,0:T(8,128)} %fusion.15, f32[1024,2048]{1,0:T(8,128)S(1)} %fusion.19, f32[1024,2048]{1,0:T(8,128)} %fusion.17, bf16[256,2048]{1,0:T(8,128)(2,1)S(1)} %collective-permute-done.2, bf16[1024,1024]{1,0:T(8,128)(2,1)S(1)} %multiply_convert_fusion, s32[]{:T(128)S(6)} %select_n.108), kind=kOutput, calls=%fused_computation.2 | convolution fusion | flops 1082130432 | bytes 30932996 | tf_op jit(solution)/shard_map/dot_general | solution.py:278
  270.0 37.6 %reduce-scatter.5.cloned.1.call-done = bf16[128,2048]{1,0:T(8,128)(2,1)} async-done(((bf16[1024,2048]{1,0:T(8,128)(2,1)}), bf16[128,2048]{1,0:T(8,128)(2,1)}) %reduce-scatter.5.cloned.1.call-update) | async-done | bytes 524304 | tf_op jit(solution)/shard_map/reduce_scatter | solution.py:284
  307.6 2.3 add_convert_fusion.1
  (64 shorter events, 1.2 us)
Async XLA Ops:
  7.2 153.5 %copy-start = (bf16[512,2048]{1,0:T(8,128)(2,1)S(1)}, bf16[512,2048]{1,0:T(8,128)(2,1)}, u32[]{:S(2)}) copy-start(bf16[512,2048]{1,0:T(8,128)(2,1)} %param.22) | copy-start | bytes 6291460
  7.2 5.6 %copy-start.20 = (f32[2048]{0:T(1024)S(1)}, f32[2048]{0:T(1024)}, u32[]{:S(2)}) copy-start(f32[2048]{0:T(1024)} %param.17) | copy-start | bytes 24580
  7.2 5.6 %copy-start.18 = (bf16[2048,128]{1,0:T(8,128)(2,1)S(1)}, bf16[2048,128]{1,0:T(8,128)(2,1)}, u32[]{:S(2)}) copy-start(bf16[2048,128]{1,0:T(8,128)(2,1)} %param.20) | copy-start | bytes 1572868
  7.2 8.3 %copy-start.19 = (bf16[2048,128]{1,0:T(8,128)(2,1)S(1)}, bf16[2048,128]{1,0:T(8,128)(2,1)}, u32[]{:S(2)}) copy-start(bf16[2048,128]{1,0:T(8,128)(2,1)} %param.21) | copy-start | bytes 1572868
  7.2 116.1 %all-gather.4.cloned.1.call-start = ((), (), s32[]{:S(2)}) async-start(), calls=%async_computation.2 | async-start | bytes 5242880 | tf_op jit(solution)/shard_map/all_gather | solution.py:232
  7.9 129.0 %all-gather.6.cloned.1.call-start = ((), (), s32[]{:S(2)}) async-start(), calls=%async_computation.3 | async-start | bytes 5242880 | tf_op jit(solution)/shard_map/all_gather | solution.py:233
  8.7 186.9 %reduce-scatter.3.cloned.1.call-start = ((), (), s32[]{:S(2)}) async-start(), calls=%async_computation.4 | async-start | bytes 2621440 | tf_op jit(solution)/shard_map/reduce_scatter | solution.py:261
  10.6 4.9 %copy-start.8 = (bf16[512,2048]{1,0:T(8,128)(2,1)S(1)}, bf16[512,2048]{1,0:T(8,128)(2,1)}, u32[]{:S(2)}) copy-start(bf16[512,2048]{1,0:T(8,128)(2,1)} %param.16) | copy-start | bytes 6291460
  12.8 3.6 %copy-start.17 = (bf16[2048,512]{1,0:T(8,128)(2,1)S(1)}, bf16[2048,512]{1,0:T(8,128)(2,1)}, u32[]{:S(2)}) copy-start(bf16[2048,512]{1,0:T(8,128)(2,1)} %param.19) | copy-start | bytes 6291460
  28.6 42.0 %copy-start.6 = (s32[1,32]{1,0:T(1,128)S(1)}, s32[1,32]{1,0:T(1,128)}, u32[]{:S(2)}) copy-start(s32[1,32]{1,0:T(1,128)} %param.30) | copy-start | bytes 388
  72.5 3.4 %copy-start.10 = (f32[32,32,32]{2,1,0:T(8,128)}, f32[32,32,32]{2,1,0:T(8,128)S(1)}, u32[]{:S(2)}) copy-start(f32[32,32,32]{2,1,0:T(8,128)S(1)} %get-tuple-element.37) | copy-start | bytes 393220
  72.6 3.4 %copy-start.11 = (f32[32,32,32]{2,1,0:T(8,128)}, f32[32,32,32]{2,1,0:T(8,128)S(1)}, u32[]{:S(2)}) copy-start(f32[32,32,32]{2,1,0:T(8,128)S(1)} %get-tuple-element.38) | copy-start | bytes 393220
  72.6 6.0 %slice-start = ((bf16[32,32,768]{2,1,0:T(8,128)(2,1)}), bf16[32,32,512]{2,1,0:T(8,128)(2,1)S(1)}, s32[]{:S(2)}) async-start(bf16[32,32,768]{2,1,0:T(8,128)(2,1)} %shard_map.175), calls=%async_computation.7 | async-start | bytes 2097152 | tf_op jit(solution)/shard_map/slice | solution.py:251
  85.1 5.7 %copy-start.5 = (s32[1,512]{1,0:T(1,128)S(1)}, s32[1,512]{1,0:T(1,128)}, u32[]{:S(2)}) copy-start(s32[1,512]{1,0:T(1,128)} %param.31) | copy-start | bytes 6148
  85.1 5.7 %copy-start.7 = (s32[1,32]{1,0:T(1,128)S(1)}, s32[1,32]{1,0:T(1,128)}, u32[]{:S(2)}) copy-start(s32[1,32]{1,0:T(1,128)} %param.29) | copy-start | bytes 388
  87.6 35.7 %copy-start.13 = (s32[512]{0:T(512)S(1)}, s32[512]{0:T(512)}, u32[]{:S(2)}) copy-start(s32[512]{0:T(512)} %param.28) | copy-start | bytes 6148
  90.8 1.6 copy-start.2
  92.4 1.0 copy-start.4
  122.2 1.1 copy-start.3
  160.7 36.5 %copy-start.14 = (f32[2048]{0:T(1024)S(1)}, f32[2048]{0:T(1024)}, u32[]{:S(2)}) copy-start(f32[2048]{0:T(1024)} %param.18) | copy-start | bytes 24580
  163.4 36.1 %copy-start.12 = (bf16[256,2048]{1,0:T(8,128)(2,1)S(1)}, bf16[256,2048]{1,0:T(8,128)(2,1)}, u32[]{:S(2)}) copy-start(bf16[256,2048]{1,0:T(8,128)(2,1)} %param.25) | copy-start | bytes 3145732
  163.4 68.3 %all-gather.8.cloned.1.call-start = ((), (), s32[]{:S(2)}) async-start(), calls=%async_computation.5 | async-start | bytes 4718592 | tf_op jit(solution)/shard_map/all_gather | solution.py:269
  199.4 108.2 %reduce-scatter.5.cloned.1.call-start = ((), (), s32[]{:S(2)}) async-start(), calls=%async_computation.6 | async-start | bytes 4718592 | tf_op jit(solution)/shard_map/reduce_scatter | solution.py:284
  199.5 45.1 %collective-permute-start.1 = (bf16[256,2048]{1,0:T(8,128)(2,1)S(1)}, bf16[256,2048]{1,0:T(8,128)(2,1)S(1)}, u32[]{:S(2)}, u32[]{:S(2)}) collective-permute-start(bf16[256,2048]{1,0:T(8,128)(2,1)S(1)} %copy-done.12), channel_id=1, source_target_pairs={{0,64},{32,96},{64,0},{96,32},{1,65},{33,97},{65,1},{97,33},{2,66}... | collective-permute-start | bytes 3145736 | tf_op jit(solution)/shard_map/ppermute | solution.py:236
  202.5 46.0 %collective-permute-start = (bf16[256,2048]{1,0:T(8,128)(2,1)S(1)}, bf16[256,2048]{1,0:T(8,128)(2,1)}, u32[]{:S(2)}, u32[]{:S(2)}) collective-permute-start(bf16[256,2048]{1,0:T(8,128)(2,1)S(1)} %copy-done.12), channel_id=1, source_target_pairs={{0,32},{32,64},{64,96},{96,0},{1,33},{33,65},{65,97},{97,1},{2,34}... | collective-permute-start | bytes 3145736 | tf_op jit(solution)/shard_map/ppermute | solution.py:236
  203.2 45.4 %collective-permute-start.2 = (bf16[256,2048]{1,0:T(8,128)(2,1)S(1)}, bf16[256,2048]{1,0:T(8,128)(2,1)S(1)}, u32[]{:S(2)}, u32[]{:S(2)}) collective-permute-start(bf16[256,2048]{1,0:T(8,128)(2,1)S(1)} %copy-done.12), channel_id=1, source_target_pairs={{0,96},{32,0},{64,32},{96,64},{1,97},{33,1},{65,33},{97,65},{2,98}... | collective-permute-start | bytes 3145736 | tf_op jit(solution)/shard_map/ppermute | solution.py:236
  231.6 7.7 %copy-start.15 = (bf16[2048,1024]{1,0:T(8,128)(2,1)S(1)}, bf16[2048,1024]{1,0:T(8,128)(2,1)}, u32[]{:S(2)}) copy-start(bf16[2048,1024]{1,0:T(8,128)(2,1)} %all-gather.6.cloned.1.call-done) | copy-start | bytes 12582916
  231.7 7.7 %copy-start.16 = (bf16[1024,2048]{1,0:T(8,128)(2,1)S(1)}, bf16[1024,2048]{1,0:T(8,128)(2,1)}, u32[]{:S(2)}) copy-start(bf16[1024,2048]{1,0:T(8,128)(2,1)} %all-gather.8.cloned.1.call-done) | copy-start | bytes 12582916
  260.1 49.8 %copy-start.1 = (bf16[512,2048]{1,0:T(8,128)(2,1)S(1)}, bf16[512,2048]{1,0:T(8,128)(2,1)}, u32[]{:S(2)}) copy-start(bf16[512,2048]{1,0:T(8,128)(2,1)} %param.22) | copy-start | bytes 6291460
  270.0 37.6 %copy-start.9 = (bf16[128,2048]{1,0:T(8,128)(2,1)S(1)}, bf16[128,2048]{1,0:T(8,128)(2,1)}, u32[]{:S(2)}) copy-start(bf16[128,2048]{1,0:T(8,128)(2,1)} %reduce-scatter.3.cloned.1.call-done) | copy-start | bytes 1572868
Sparse Core Ops, SparseCore 0:
  9.7 69.4 all-gather.3
  80.9 56.0 all-gather.5
  163.5 32.0 reduce-scatter.2
  199.5 32.0 all-gather.7
  270.1 37.4 reduce-scatter.4

commit v6 on v3

--- a/solution.py
+++ b/solution.py
@@ -170,8 +170,6 @@
         lax.ppermute(w_down, "ry", [(i, (i + shift) % ring) for i in range(ring)])
         for shift in range(1, ring)
     ]
-    part_at = (lax.axis_index("ry") - jnp.arange(ring, dtype=jnp.int32)) % ring
-    down_w = jnp.take(jnp.stack(down_parts), part_at, axis=0).reshape(-1, w_down.shape[1])
     normed = normalize(hidden_in.astype(jnp.float32), attn_gain).astype(jnp.bfloat16)
     qcols = w_query.shape[1]
     kcols = w_key.shape[1]
@@ -202,17 +200,31 @@
     )
     residual = own_rows + RESIDUAL_MULT * attn_part
     mlp_in = normalize(residual, mlp_gain).astype(jnp.bfloat16)
-    piece = lax.all_gather(mlp_in, "rzc", axis=0, tiled=True)
-    down_w, piece = lax.optimization_barrier((down_w, piece))
-    gate = jnp.dot(piece, gate_w, preferred_element_type=jnp.float32)
-    upper = jnp.dot(piece, up_w, preferred_element_type=jnp.float32)
-    hidden = (jax.nn.silu(gate) * upper).astype(jnp.bfloat16)
-    down = lax.psum_scatter(
-        jnp.dot(hidden, down_w, preferred_element_type=jnp.float32).astype(jnp.bfloat16),
-        "rzc",
-        scatter_dimension=0,
-        tiled=True,
-    ).astype(jnp.float32)
+    halves = []
+    half_rows = mlp_in.shape[0] // 2
+    for half in range(2):
+        piece = lax.all_gather(
+            mlp_in[half * half_rows:(half + 1) * half_rows], "rzc", axis=0, tiled=True
+        )
+        gate = jnp.dot(piece, gate_w, preferred_element_type=jnp.float32)
+        upper = jnp.dot(piece, up_w, preferred_element_type=jnp.float32)
+        hidden = (jax.nn.silu(gate) * upper).astype(jnp.bfloat16)
+        if half == 0:
+            down_parts, hidden = lax.optimization_barrier((down_parts, hidden))
+        units = w_down.shape[0]
+        partial = None
+        for shift, part in enumerate(down_parts):
+            block = (lax.axis_index("ry") - shift) % ring
+            term = jnp.dot(
+                lax.dynamic_slice_in_dim(hidden, block * units, units, axis=1),
+                part,
+                preferred_element_type=jnp.float32,
+            )
+            partial = term if partial is None else partial + term
+        halves.append(
+            lax.psum_scatter(partial.astype(jnp.bfloat16), "rzc", scatter_dimension=0, tiled=True)
+        )
+    down = jnp.concatenate(halves, axis=0).astype(jnp.float32)
     layer_out = (residual + RESIDUAL_MULT * down).astype(jnp.bfloat16)
     return (layer_out, keys_out, values_out)
 

time: 331 us -> 341 us (1.030)
  waiting for transfers between devices: 166 us -> 187 us
  other arithmetic: 33.1 us -> 20.6 us
    ppermute x3, waiting for transfers between devices: 44.5 us -> 16.3 us  [body(): lax.ppermute(w_down, 'ry', [(i, (i + shift) % ring) for i in range(ring)])]
    reduce_scatter x1 -> x2, waiting for transfers between devices: 37.1 us -> 63.3 us  [body(): lax.psum_scatter(partial.astype(jnp.bfloat16), 'rzc', scatter_dimension=0...]
    all_gather x1 -> x2, waiting for transfers between devices: 0.01 us -> 21.8 us  [body(): lax.all_gather(mlp_in[half * half_rows:(half + 1) * half_rows], 'rzc', ax...]
    gather x1 -> x0, local copies, waits for them, and re-layouts: 4.94 us -> none  [body(): jnp.take(jnp.stack(down_parts), part_at, axis=0)]
    select_n x2 -> x0, other arithmetic: 4.58 us -> none  [body(): jnp.take(jnp.stack(down_parts), part_at, axis=0)]
    another operation x3 -> x2, other arithmetic: 8.94 us -> 4.64 us
    dot_general x1 -> x10, matrix products: 15.3 us -> 17.4 us  [the longest x8 11.4 us: body(): jnp.dot(lax.dynamic_slice_in_dim(hidden, block * units, units, axis=1), p...]
    dot_general x1 -> x2, matrix products: 9.89 us -> 10.6 us  [body(): gate = jnp.dot(piece, gate_w, preferred_element_type=jnp.float32)]
  transfers between devices with their start and end apart: 10 -> 12, of which waited for: 8 -> 9; matrix products, arithmetic and copies ran while one was open for 18% -> 17% of each run, Pallas kernels for 9% -> 8%
where the time goes in v6:
time: 341 us; the launch traced here: 340 us
  waiting for transfers between devices  187 us (55%)
  matrix products  35.1 us (10%)
  local copies, waits for them, and re-layouts  31.8 us (9%)
  Pallas kernels  28.7 us (8%)
  starting transfers between devices  22.2 us (7%)
  other arithmetic  20.6 us (6%)
  between operations  14.5 us (4%)
    reduce_scatter x2, waiting for transfers between devices, body(): lax.psum_scatter(partial.astype(jnp.bfloat16), 'rzc', scatter_dimension=0...  63.3 us
    all_to_all x1, waiting for transfers between devices, body(): lax.all_to_all(send_qkv, REQ, split_axis=0, concat_axis=0, tiled=True)  30.4 us
    pallas_call x1, Pallas kernels, owner_attention(): pl.pallas_call(attention_kernel, out_shape=(jax.ShapeDtypeStruct((sources...  28.7 us
    reduce_scatter x1, waiting for transfers between devices, body(): lax.psum_scatter(projected.astype(jnp.bfloat16), 'grp', scatter_dimension...  27.5 us
    all_gather x2, waiting for transfers between devices, body(): lax.all_gather(mlp_in[half * half_rows:(half + 1) * half_rows], 'rzc', ax...  21.8 us
    all_to_all x1, waiting for transfers between devices, body(): lax.all_to_all(mixed, REQ, split_axis=0, concat_axis=0, tiled=True)  16.7 us
    ppermute x3, waiting for transfers between devices, body(): lax.ppermute(w_down, 'ry', [(i, (i + shift) % ring) for i in range(ring)])  16.3 us
    dot_general x8, matrix products, body(): jnp.dot(lax.dynamic_slice_in_dim(hidden, block * units, units, axis=1), p...  11.4 us
  transfers between devices with their start and end apart: 12, of which 9 were waited for; matrix products, arithmetic and copies ran while one was open for 17% of the time, Pallas kernels for 8%

profile of v6, /device:TPU:0, one launch (start us, length us, event | category | flops | bytes accessed | tf_op | source)
XLA Modules:
  0.0 340.4 jit_solution(4797048625966002532)
XLA Ops:
  8.7 2.2 fusion
  12.0 0.9 convolution_convert_fusion.3
  13.6 1.4 convolution_convert_fusion.1
  16.0 1.4 copy.21
  17.8 5.2 %gather_fusion = bf16[1024,768]{1,0:T(8,128)(2,1)} fusion(bf16[512,768]{1,0:T(8,128)(2,1)S(1)} %copy.21, s32[1024]{0:T(1024)S(1)} %broadcast_clamp_fusion), kind=kCustom, calls=%fused_computation | custom fusion | bytes 3149824 | tf_op jit(solution)/shard_map/jit(_take)/gather | solution.py:181
  23.1 2.8 broadcast_select_fusion
  25.9 8.8 %all-to-all-start = ((bf16[32,32,768]{2,1,0:T(8,128)(2,1)}), bf16[32,32,768]{2,1,0:T(8,128)(2,1)}, u32[]{:S(2)}, u32[]{:S(2)}) async-start(bf16[32,32,768]{2,1,0:T(8,128)(2,1)} %broadcast_select_fusion), calls=%async_computation | async-start | bytes 3145728 | tf_op jit(solution)/shard_map/all_to_all | solution.py:184
  34.9 1.9 multiply_cosine_fusion
  36.8 30.4 %all-to-all-done = bf16[32,32,768]{2,1,0:T(8,128)(2,1)} async-done(((bf16[32,32,768]{2,1,0:T(8,128)(2,1)}), bf16[32,32,768]{2,1,0:T(8,128)(2,1)}, u32[]{:S(2)}, u32[]{:S(2)}) %all-to-all-start) | async-done | bytes 1572896 | tf_op jit(solution)/shard_map/all_to_all | solution.py:184
  67.2 2.3 slice.40
  69.5 3.9 %reshape.154 = bf16[32,32,8,64]{3,2,1,0:T(8,128)(2,1)} reshape(bf16[32,32,512]{2,1,0:T(8,128)(2,1)} %slice.40) | data formatting | bytes 2097152 | tf_op jit(solution)/shard_map/reshape | solution.py:116
  73.4 4.2 %fusion.4 = (bf16[32,32,8,32]{3,2,1,0:T(8,128)(2,1)S(1)}, bf16[32,32,8,32]{3,2,1,0:T(8,128)(2,1)S(1)}) fusion(f32[32,32,32]{2,1,0:T(8,128)S(1)} %get-tuple-element.40, f32[32,32,32]{2,1,0:T(8,128)S(1)} %get-tuple-element.39, bf16[32,32,8,64]{3,2,1,0:T(8,128)(2,1)} %reshape.154), kind=kLoop, calls=%fused_computation.12 | loop fusion | flops 2621440 | bytes 2359296 | tf_op jit(solution)/shard_map/convert.2
  77.6 2.5 pad_maximum_fusion
  80.1 3.2 convert_element_type.97.q_ref
  83.3 1.8 fusion.46
  85.1 1.0 reshape.155
  86.1 2.3 fusion.48
  89.2 1.3 copy.24
  90.5 1.4 convert_element_type.100.k_ref
  91.9 1.6 copy-done.2
  93.6 1.0 copy-done.4
  94.5 28.7 %shard_map.175 = (bf16[32,32,512]{2,1,0:T(8,128)(2,1)S(1)}, bf16[512,16,128]{2,1,0:T(8,128)(2,1)}, bf16[512,16,128]{2,1,0:T(8,128)(2,1)}) custom-call(s32[512]{0:T(512)S(1)} %bitcast.28, s32[32]{0:T(128)S(1)} %bitcast.30, s32[32]{0:T(128)S(1)} %bitcast.31, bf16[32,32,512]{2,1,0:T(8,128)(2,1)S(1)} %convert_element_type.97.q_ref, ...), custom_call_target="tpu_custom_call" | custom-call | tf_op jit(solution)/shard_map/pallas_call | solution.py:125
  123.2 1.0 copy-done.3
  124.2 9.3 %all-gather.7.cloned.1.call-done = bf16[2048,1024]{1,0:T(8,128)(2,1)} async-done(((bf16[2048,256]{1,0:T(8,128)(2,1)}), bf16[2048,1024]{1,0:T(8,128)(2,1)}) %all-gather.7.cloned.1.call-update) | async-done | bytes 4194320 | tf_op jit(solution)/shard_map/all_gather | solution.py:167
  133.6 6.9 %all-to-all-start.1 = ((bf16[32,32,512]{2,1,0:T(8,128)(2,1)}), bf16[32,32,512]{2,1,0:T(8,128)(2,1)S(1)}, u32[]{:S(2)}, u32[]{:S(2)}) async-start(bf16[32,32,512]{2,1,0:T(8,128)(2,1)} %copy-done.3), calls=%async_computation.1 | async-start | bytes 2097152 | tf_op jit(solution)/shard_map/all_to_all | solution.py:192
  140.5 16.7 %all-to-all-done.1 = bf16[32,32,512]{2,1,0:T(8,128)(2,1)S(1)} async-done(((bf16[32,32,512]{2,1,0:T(8,128)(2,1)}), bf16[32,32,512]{2,1,0:T(8,128)(2,1)S(1)}, u32[]{:S(2)}, u32[]{:S(2)}) %all-to-all-start.1) | async-done | bytes 1048608 | tf_op jit(solution)/shard_map/all_to_all | solution.py:192
  157.3 2.6 gather_fusion.1
  159.9 3.7 %convolution_convert_fusion = bf16[512,2048]{1,0:T(8,128)(2,1)} fusion(bf16[512,2048]{1,0:T(8,128)(2,1)S(1)} %copy-done, bf16[512,512]{1,0:T(8,128)(2,1)} %gather_fusion.1, pred[512]{0:T(512)(128)(4,1)S(1)} %get-tuple-element.27), kind=kOutput, calls=%fused_computation.17 | convolution fusion | flops 1075052544 | bytes 4719104 | tf_op jit(solution)/shard_map/dot_general | solution.py:194
  163.9 27.5 %reduce-scatter.4.cloned.1.call-done = bf16[128,2048]{1,0:T(8,128)(2,1)} async-done(((bf16[512,2048]{1,0:T(8,128)(2,1)}), bf16[128,2048]{1,0:T(8,128)(2,1)}) %reduce-scatter.4.cloned.1.call-update) | async-done | bytes 524304 | tf_op jit(solution)/shard_map/reduce_scatter | solution.py:195
  191.5 1.3 multiply_reduce_fusion
  192.8 1.3 multiply_convert_fusion.2
  195.6 1.5 collective-permute-start
  197.2 2.7 collective-permute-start.1
  199.9 1.4 collective-permute-start.2
  201.3 18.9 %all-gather.9.cloned.1.call-done = bf16[512,2048]{1,0:T(8,128)(2,1)} async-done(((bf16[64,2048]{1,0:T(8,128)(2,1)}), bf16[512,2048]{1,0:T(8,128)(2,1)}) %all-gather.9.cloned.1.call-update) | async-done | bytes 2097168 | tf_op jit(solution)/shard_map/all_gather | solution.py:206
  220.2 5.3 %fusion.49 = f32[512,1024]{1,0:T(8,128)S(1)} fusion(bf16[512,2048]{1,0:T(8,128)(2,1)} %all-gather.9.cloned.1.call-done, bf16[2048,1024]{1,0:T(8,128)(2,1)} %all-gather.5.cloned.1.call-done), kind=kOutput, calls=%fused_computation.89 | convolution fusion | flops 2147483648 | bytes 8388608 | tf_op jit(solution)/shard_map/dot_general | solution.py:209
  225.6 3.5 %multiply_convert_fusion.1 = bf16[512,1024]{1,0:T(8,128)(2,1)} fusion(f32[512,1024]{1,0:T(8,128)S(1)} %fusion.49, bf16[512,2048]{1,0:T(8,128)(2,1)S(1)} %copy-done.23, bf16[2048,1024]{1,0:T(8,128)(2,1)S(1)} %copy-done.19), kind=kOutput, calls=%fused_computation.20 | convolution fusion | flops 2150629376 | bytes 9437184 | tf_op jit(solution)/shard_map/dot_general | solution.py:210
  229.1 16.3 %collective-permute-done.1 = bf16[256,2048]{1,0:T(8,128)(2,1)} collective-permute-done((bf16[256,2048]{1,0:T(8,128)(2,1)S(1)}, bf16[256,2048]{1,0:T(8,128)(2,1)}, u32[]{:S(2)}, u32[]{:S(2)}) %collective-permute-start.1) | collective-permute-done | bytes 1048608 | tf_op jit(solution)/shard_map/ppermute | solution.py:170
  245.4 2.9 all-gather.11.cloned.1.call-done
  248.3 5.3 %fusion.50 = f32[512,1024]{1,0:T(8,128)S(1)} fusion(bf16[512,2048]{1,0:T(8,128)(2,1)} %all-gather.11.cloned.1.call-done, bf16[2048,1024]{1,0:T(8,128)(2,1)} %all-gather.5.cloned.1.call-done), kind=kOutput, calls=%fused_computation.90 | convolution fusion | flops 2147483648 | bytes 8388608 | tf_op jit(solution)/shard_map/dot_general | solution.py:209
  253.6 2.5 multiply_convert_fusion
  256.1 1.9 fusion.17
  259.5 2.2 add_convert_fusion
  262.1 2.1 fusion.27
  265.7 2.2 add_convert_fusion.1
  268.0 28.2 %reduce-scatter.8.cloned.1.call-done = bf16[64,2048]{1,0:T(8,128)(2,1)} async-done(((bf16[512,2048]{1,0:T(8,128)(2,1)}), bf16[64,2048]{1,0:T(8,128)(2,1)}) %reduce-scatter.8.cloned.1.call-update) | async-done | bytes 262160 | tf_op jit(solution)/shard_map/reduce_scatter | solution.py:225
  296.2 35.1 %reduce-scatter.6.cloned.1.call-done = bf16[64,2048]{1,0:T(8,128)(2,1)} async-done(((bf16[512,2048]{1,0:T(8,128)(2,1)}), bf16[64,2048]{1,0:T(8,128)(2,1)}) %reduce-scatter.6.cloned.1.call-update) | async-done | bytes 262160 | tf_op jit(solution)/shard_map/reduce_scatter | solution.py:225
  331.3 2.3 add_convert_fusion.2
  (90 shorter events, 10.6 us)
Async XLA Ops:
  7.2 152.7 %copy-start = (bf16[512,2048]{1,0:T(8,128)(2,1)S(1)}, bf16[512,2048]{1,0:T(8,128)(2,1)}, u32[]{:S(2)}) copy-start(bf16[512,2048]{1,0:T(8,128)(2,1)} %param.22) | copy-start | bytes 6291460
  7.2 3.8 %copy-start.24 = (bf16[2048,128]{1,0:T(8,128)(2,1)S(1)}, bf16[2048,128]{1,0:T(8,128)(2,1)}, u32[]{:S(2)}) copy-start(bf16[2048,128]{1,0:T(8,128)(2,1)} %param.21) | copy-start | bytes 1572868
  7.2 3.8 %copy-start.26 = (f32[2048]{0:T(1024)S(1)}, f32[2048]{0:T(1024)}, u32[]{:S(2)}) copy-start(f32[2048]{0:T(1024)} %param.17) | copy-start | bytes 24580
  7.2 117.0 %all-gather.5.cloned.1.call-start = ((), (), s32[]{:S(2)}) async-start(), calls=%async_computation.5 | async-start | bytes 5242880 | tf_op jit(solution)/shard_map/all_gather | solution.py:166
  7.9 125.6 %all-gather.7.cloned.1.call-start = ((), (), s32[]{:S(2)}) async-start(), calls=%async_computation.6 | async-start | bytes 5242880 | tf_op jit(solution)/shard_map/all_gather | solution.py:167
  8.7 2.3 copy-start.8
  11.0 1.0 copy-start.25
  12.0 1.6 copy-start.21
  15.0 2.4 copy-start.17
  25.9 8.9 %copy-start.6 = (s32[1,32]{1,0:T(1,128)S(1)}, s32[1,32]{1,0:T(1,128)}, u32[]{:S(2)}) copy-start(s32[1,32]{1,0:T(1,128)} %param.30) | copy-start | bytes 388
  25.9 41.3 %all-to-all-start = ((bf16[32,32,768]{2,1,0:T(8,128)(2,1)}), bf16[32,32,768]{2,1,0:T(8,128)(2,1)}, u32[]{:S(2)}, u32[]{:S(2)}) async-start(bf16[32,32,768]{2,1,0:T(8,128)(2,1)} %broadcast_select_fusion), calls=%async_computation | async-start | bytes 3145728 | tf_op jit(solution)/shard_map/all_to_all | solution.py:184
  36.8 36.6 %copy-start.11 = (f32[32,32,32]{2,1,0:T(8,128)}, f32[32,32,32]{2,1,0:T(8,128)S(1)}, u32[]{:S(2)}) copy-start(f32[32,32,32]{2,1,0:T(8,128)S(1)} %get-tuple-element.39) | copy-start | bytes 393220
  36.8 36.6 %copy-start.13 = (f32[32,32,32]{2,1,0:T(8,128)}, f32[32,32,32]{2,1,0:T(8,128)S(1)}, u32[]{:S(2)}) copy-start(f32[32,32,32]{2,1,0:T(8,128)S(1)} %get-tuple-element.40) | copy-start | bytes 393220
  86.1 2.3 copy-start.12
  86.1 2.3 copy-start.14
  88.9 3.0 copy-start.5
  88.9 3.0 copy-start.7
  91.9 1.7 copy-start.2
  93.6 1.0 copy-start.4
  123.2 1.0 copy-start.3
  133.6 23.7 %all-to-all-start.1 = ((bf16[32,32,512]{2,1,0:T(8,128)(2,1)}), bf16[32,32,512]{2,1,0:T(8,128)(2,1)S(1)}, u32[]{:S(2)}, u32[]{:S(2)}) async-start(bf16[32,32,512]{2,1,0:T(8,128)(2,1)} %copy-done.3), calls=%async_computation.1 | async-start | bytes 2097152 | tf_op jit(solution)/shard_map/all_to_all | solution.py:192
  140.5 51.0 %reduce-scatter.4.cloned.1.call-start = ((), (), s32[]{:S(2)}) async-start(), calls=%async_computation.7 | async-start | bytes 2621440 | tf_op jit(solution)/shard_map/reduce_scatter | solution.py:195
  163.6 27.9 %copy-start.9 = (bf16[512,2048]{1,0:T(8,128)(2,1)S(1)}, bf16[512,2048]{1,0:T(8,128)(2,1)}, u32[]{:S(2)}) copy-start(bf16[512,2048]{1,0:T(8,128)(2,1)} %param.16) | copy-start | bytes 6291460
  163.6 29.2 %copy-start.18 = (f32[2048]{0:T(1024)S(1)}, f32[2048]{0:T(1024)}, u32[]{:S(2)}) copy-start(f32[2048]{0:T(1024)} %param.18) | copy-start | bytes 24580
  163.6 56.6 %all-gather.9.cloned.1.call-start = ((), (), s32[]{:S(2)}) async-start(), calls=%async_computation.8 | async-start | bytes 2359296 | tf_op jit(solution)/shard_map/all_gather | solution.py:206
  163.9 31.7 %copy-start.15 = (bf16[256,2048]{1,0:T(8,128)(2,1)S(1)}, bf16[256,2048]{1,0:T(8,128)(2,1)}, u32[]{:S(2)}) copy-start(bf16[256,2048]{1,0:T(8,128)(2,1)} %param.25) | copy-start | bytes 3145732
  195.0 53.3 %all-gather.11.cloned.1.call-start = ((), (), s32[]{:S(2)}) async-start(), calls=%async_computation.10 | async-start | bytes 2359296 | tf_op jit(solution)/shard_map/all_gather | solution.py:206
  195.6 100.6 %reduce-scatter.8.cloned.1.call-start = ((), (), s32[]{:S(2)}) async-start(), calls=%async_computation.11 | async-start | bytes 2359296 | tf_op jit(solution)/shard_map/reduce_scatter | solution.py:225
  195.6 33.4 %collective-permute-start = (bf16[256,2048]{1,0:T(8,128)(2,1)S(1)}, bf16[256,2048]{1,0:T(8,128)(2,1)S(1)}, u32[]{:S(2)}, u32[]{:S(2)}) collective-permute-start(bf16[256,2048]{1,0:T(8,128)(2,1)S(1)} %copy-done.15), channel_id=1, source_target_pairs={{0,32},{32,64},{64,96},{96,0},{1,33},{33,65},{65,97},{97,1},{2,34}... | collective-permute-start | bytes 3145736 | tf_op jit(solution)/shard_map/ppermute | solution.py:170
  197.2 48.2 %collective-permute-start.1 = (bf16[256,2048]{1,0:T(8,128)(2,1)S(1)}, bf16[256,2048]{1,0:T(8,128)(2,1)}, u32[]{:S(2)}, u32[]{:S(2)}) collective-permute-start(bf16[256,2048]{1,0:T(8,128)(2,1)S(1)} %copy-done.15), channel_id=1, source_target_pairs={{0,64},{32,96},{64,0},{96,32},{1,65},{33,97},{65,1},{97,33},{2,66}... | collective-permute-start | bytes 3145736 | tf_op jit(solution)/shard_map/ppermute | solution.py:170
  199.9 45.5 %collective-permute-start.2 = (bf16[256,2048]{1,0:T(8,128)(2,1)S(1)}, bf16[256,2048]{1,0:T(8,128)(2,1)S(1)}, u32[]{:S(2)}, u32[]{:S(2)}) collective-permute-start(bf16[256,2048]{1,0:T(8,128)(2,1)S(1)} %copy-done.15), channel_id=1, source_target_pairs={{0,96},{32,0},{64,32},{96,64},{1,97},{33,1},{65,33},{97,65},{2,98}... | collective-permute-start | bytes 3145736 | tf_op jit(solution)/shard_map/ppermute | solution.py:170
  220.2 5.3 %copy-start.19 = (bf16[2048,1024]{1,0:T(8,128)(2,1)S(1)}, bf16[2048,1024]{1,0:T(8,128)(2,1)}, u32[]{:S(2)}) copy-start(bf16[2048,1024]{1,0:T(8,128)(2,1)} %all-gather.7.cloned.1.call-done) | copy-start | bytes 12582916
  220.2 5.3 %copy-start.23 = (bf16[512,2048]{1,0:T(8,128)(2,1)S(1)}, bf16[512,2048]{1,0:T(8,128)(2,1)}, u32[]{:S(2)}) copy-start(bf16[512,2048]{1,0:T(8,128)(2,1)} %all-gather.9.cloned.1.call-done) | copy-start | bytes 6291460
  248.3 5.3 %copy-start.20 = (bf16[2048,1024]{1,0:T(8,128)(2,1)S(1)}, bf16[2048,1024]{1,0:T(8,128)(2,1)}, u32[]{:S(2)}) copy-start(bf16[2048,1024]{1,0:T(8,128)(2,1)} %all-gather.7.cloned.1.call-done) | copy-start | bytes 12582916
  248.3 5.3 %copy-start.22 = (bf16[512,2048]{1,0:T(8,128)(2,1)S(1)}, bf16[512,2048]{1,0:T(8,128)(2,1)}, u32[]{:S(2)}) copy-start(bf16[512,2048]{1,0:T(8,128)(2,1)} %all-gather.11.cloned.1.call-done) | copy-start | bytes 6291460
  261.8 69.5 %reduce-scatter.6.cloned.1.call-start = ((), (), s32[]{:S(2)}) async-start(), calls=%async_computation.9 | async-start | bytes 2359296 | tf_op jit(solution)/shard_map/reduce_scatter | solution.py:225
  262.1 2.1 copy-start.16
  267.9 63.4 %copy-start.10 = (bf16[128,2048]{1,0:T(8,128)(2,1)S(1)}, bf16[128,2048]{1,0:T(8,128)(2,1)}, u32[]{:S(2)}) copy-start(bf16[128,2048]{1,0:T(8,128)(2,1)} %reduce-scatter.4.cloned.1.call-done) | copy-start | bytes 1572868
  268.0 65.6 %copy-start.1 = (bf16[512,2048]{1,0:T(8,128)(2,1)S(1)}, bf16[512,2048]{1,0:T(8,128)(2,1)}, u32[]{:S(2)}) copy-start(bf16[512,2048]{1,0:T(8,128)(2,1)} %param.22) | copy-start | bytes 6291460
Sparse Core Ops, SparseCore 0:
  9.7 68.4 all-gather.4
  79.9 53.6 all-gather.6
  163.8 27.6 reduce-scatter.3
  195.1 25.1 all-gather.8
  222.5 25.7 all-gather.10
  261.9 34.1 reduce-scatter.7
  298.7 32.5 reduce-scatter.5

commit v7 on v4

--- a/solution.py
+++ b/solution.py
@@ -170,6 +170,10 @@
         lax.ppermute(w_down, "ry", [(i, (i + shift) % ring) for i in range(ring)])
         for shift in range(1, ring)
     ]
+    out_parts = [w_out] + [
+        lax.ppermute(w_out, "grp", [(i, (i + shift) % groups) for i in range(groups)])
+        for shift in range(1, groups)
+    ]
     normed = normalize(hidden_in.astype(jnp.float32), attn_gain).astype(jnp.bfloat16)
     qcols = w_query.shape[1]
     kcols = w_key.shape[1]
@@ -188,13 +192,18 @@
     mixed, keys_out, values_out = owner_attention(
         recv_query, recv_key, recv_value, cache_k, cache_v, new_len[0], prior_len[0], page_table[0]
     )
-    gate_w, up_w, mixed = lax.optimization_barrier((gate_w, up_w, mixed))
+    gate_w, up_w, out_parts, mixed = lax.optimization_barrier((gate_w, up_w, out_parts, mixed))
     returned = lax.all_to_all(mixed, REQ, split_axis=0, concat_axis=0, tiled=True)
     attn_rows = jnp.take(returned.reshape(peers * pair_rows, -1), back_rows, axis=0)
-    projected = jnp.dot(attn_rows, w_out, preferred_element_type=jnp.float32)
-    attn_part = lax.psum_scatter(
-        projected.astype(jnp.bfloat16), "grp", scatter_dimension=0, tiled=True
-    ).astype(jnp.float32)
+    quarters = lax.all_to_all(
+        attn_rows.reshape(groups, quarter, -1), "grp", split_axis=0, concat_axis=0, tiled=True
+    )
+    attn_part = None
+    for shift, part in enumerate(out_parts):
+        block = (group_index - shift) % groups
+        term = jnp.dot(quarters[block], part, preferred_element_type=jnp.float32)
+        term = term.astype(jnp.bfloat16).astype(jnp.float32)
+        attn_part = term if attn_part is None else attn_part + term
     own_rows = lax.dynamic_slice_in_dim(hidden_in, group_index * quarter, quarter, 0).astype(
         jnp.float32
     )

time: 314 us -> 298 us (0.949)
  other arithmetic: 25.3 us -> 15 us
  waiting for transfers between devices: 151 us -> 142 us
  starting transfers between devices: 22.4 us -> 31 us
  local copies, waits for them, and re-layouts: 28.3 us -> 20.7 us
    reduce_scatter x1 -> x0, waiting for transfers between devices: 27.6 us -> none  [body(): lax.psum_scatter(projected.astype(jnp.bfloat16), 'grp', scatter_dimension...]
    ppermute x0 -> x3, waiting for transfers between devices: none -> 13.8 us  [body(): lax.ppermute(w_out, 'grp', [(i, (i + shift) % groups) for i in range(grou...]
    all_to_all x0 -> x1, waiting for transfers between devices: none -> 10 us  [body(): lax.all_to_all(attn_rows.reshape(groups, quarter, -1), 'grp', split_axis=...]
    ppermute x0 -> x3, starting transfers between devices: none -> 6.34 us  [body(): lax.ppermute(w_out, 'grp', [(i, (i + shift) % groups) for i in range(grou...]
    all_to_all x1, waiting for transfers between devices: 29.9 us -> 25 us  [body(): lax.all_to_all(send_qkv, REQ, split_axis=0, concat_axis=0, tiled=True)]
    dot_general x1 -> x4, matrix products: 3.76 us -> 8.44 us  [body(): term = jnp.dot(quarters[block], part, preferred_element_type=jnp.float32)]
    all_to_all x0 -> x1, starting transfers between devices: none -> 4.11 us  [body(): lax.all_to_all(attn_rows.reshape(groups, quarter, -1), 'grp', split_axis=...]
    ppermute x3, waiting for transfers between devices: 4.05 us -> 7.48 us  [body(): lax.ppermute(w_down, 'ry', [(i, (i + shift) % ring) for i in range(ring)])]
  transfers between devices with their start and end apart: 10 -> 13, of which waited for: 7 -> 9; matrix products, arithmetic and copies ran while one was open for 19% -> 15% of each run, Pallas kernels for 9% -> 10%
where the time goes in v7:
time: 298 us; the launch traced here: 297 us
  waiting for transfers between devices  142 us (48%)
  matrix products  46.1 us (15%)
  starting transfers between devices  31 us (10%)
  Pallas kernels  28.6 us (10%)
  local copies, waits for them, and re-layouts  20.7 us (7%)
  other arithmetic  15 us (5%)
  between operations  14.1 us (5%)
    reduce_scatter x1, waiting for transfers between devices, body(): lax.psum_scatter(partial.astype(jnp.bfloat16), 'rzc', scatter_dimension=0...  34.4 us
    pallas_call x1, Pallas kernels, owner_attention(): pl.pallas_call(attention_kernel, out_shape=(jax.ShapeDtypeStruct((sources...  28.6 us
    all_to_all x1, waiting for transfers between devices, body(): lax.all_to_all(send_qkv, REQ, split_axis=0, concat_axis=0, tiled=True)  25 us
    all_gather x1, waiting for transfers between devices, body(): piece = lax.all_gather(mlp_in, 'rzc', axis=0, tiled=True)  23.2 us
    dot_general x4, matrix products, body(): jnp.dot(lax.dynamic_slice_in_dim(hidden, block * units, units, axis=1), p...  21.5 us
    all_to_all x1, waiting for transfers between devices, body(): lax.all_to_all(mixed, REQ, split_axis=0, concat_axis=0, tiled=True)  16.8 us
    ppermute x3, waiting for transfers between devices, body(): lax.ppermute(w_out, 'grp', [(i, (i + shift) % groups) for i in range(grou...  13.8 us
    all_to_all x1, waiting for transfers between devices, body(): lax.all_to_all(attn_rows.reshape(groups, quarter, -1), 'grp', split_axis=...  10 us
  transfers between devices with their start and end apart: 13, of which 9 were waited for; matrix products, arithmetic and copies ran while one was open for 15% of the time, Pallas kernels for 10%

profile of v7, /device:TPU:0, one launch (start us, length us, event | category | flops | bytes accessed | tf_op | source)
XLA Modules:
  0.0 297.1 jit_solution(14225392525473703571)
XLA Ops:
  9.1 2.2 fusion
  11.4 0.9 convolution_convert_fusion.6
  12.4 0.9 convolution_convert_fusion.5
  13.4 1.4 convolution_convert_fusion.4
  15.2 4.0 %gather_fusion = bf16[1024,768]{1,0:T(8,128)(2,1)S(1)} fusion(bf16[512,768]{1,0:T(8,128)(2,1)S(1)} %copy.21, s32[1024]{0:T(1024)S(1)} %broadcast_clamp_fusion), kind=kCustom, calls=%fused_computation | custom fusion | bytes 3149824 | tf_op jit(solution)/shard_map/jit(_take)/gather | solution.py:185
  19.3 1.4 broadcast_select_fusion
  20.6 8.5 %all-to-all-start = ((bf16[32,32,768]{2,1,0:T(8,128)(2,1)}), bf16[32,32,768]{2,1,0:T(8,128)(2,1)S(1)}, u32[]{:S(2)}, u32[]{:S(2)}) async-start(bf16[32,32,768]{2,1,0:T(8,128)(2,1)} %broadcast_select_fusion), calls=%async_computation | async-start | bytes 3145728 | tf_op jit(solution)/shard_map/all_to_all | solution.py:188
  29.2 3.1 %collective-permute-start.1 = (bf16[512,2048]{1,0:T(8,128)(2,1)}, bf16[512,2048]{1,0:T(8,128)(2,1)}, u32[]{:S(2)}, u32[]{:S(2)}) collective-permute-start(bf16[512,2048]{1,0:T(8,128)(2,1)} %param.22), channel_id=1, source_target_pairs={{0,2},{1,3},{2,0},{3,1},{4,6},{5,7},{6,4},{7,5},{8,10},{9,11},{10,... | collective-permute-start | bytes 6291464 | tf_op jit(solution)/shard_map/ppermute | solution.py:174
  32.9 2.6 collective-permute-start.2
  35.6 1.9 multiply_cosine_fusion
  37.5 25.0 %all-to-all-done = bf16[32,32,768]{2,1,0:T(8,128)(2,1)S(1)} async-done(((bf16[32,32,768]{2,1,0:T(8,128)(2,1)}), bf16[32,32,768]{2,1,0:T(8,128)(2,1)S(1)}, u32[]{:S(2)}, u32[]{:S(2)}) %all-to-all-start) | async-done | bytes 1572896 | tf_op jit(solution)/shard_map/all_to_all | solution.py:188
  62.5 0.8 fusion.49
  63.5 1.0 fusion.50
  65.3 1.3 copy.24
  66.6 1.3 convert_element_type.112.k_ref
  68.0 1.1 slice.32
  69.0 2.8 reshape.161
  71.8 1.9 fusion.4
  73.7 2.5 pad_maximum_fusion
  76.2 3.3 %convert_element_type.109.q_ref = bf16[32,32,512]{2,1,0:T(8,128)(2,1)S(1)} reshape(bf16[32,32,8,64]{3,2,1,0:T(8,128)(2,1)} %pad_maximum_fusion) | data formatting | bytes 2097152 | tf_op jit(solution)/shard_map/convert_element_type | solution.py:116
  79.6 0.9 copy-done.4
  80.6 28.6 %shard_map.175 = (bf16[32,32,512]{2,1,0:T(8,128)(2,1)S(1)}, bf16[512,16,128]{2,1,0:T(8,128)(2,1)}, bf16[512,16,128]{2,1,0:T(8,128)(2,1)}) custom-call(s32[512]{0:T(512)S(1)} %bitcast.40, s32[32]{0:T(128)S(1)} %bitcast.42, s32[32]{0:T(128)S(1)} %bitcast.43, bf16[32,32,512]{2,1,0:T(8,128)(2,1)S(1)} %convert_element_type.109.q_ref, ...), custom_call_target="tpu_custom_call" | custom-call | tf_op jit(solution)/shard_map/pallas_call | solution.py:125
  109.2 1.0 copy-done.3
  110.2 13.7 %collective-permute-done = bf16[512,2048]{1,0:T(8,128)(2,1)} collective-permute-done((bf16[512,2048]{1,0:T(8,128)(2,1)}, bf16[512,2048]{1,0:T(8,128)(2,1)}, u32[]{:S(2)}, u32[]{:S(2)}) %collective-permute-start) | collective-permute-done | bytes 2097184 | tf_op jit(solution)/shard_map/ppermute | solution.py:174
  124.0 9.5 %all-gather.6.cloned.1.call-done = bf16[2048,1024]{1,0:T(8,128)(2,1)} async-done(((bf16[2048,256]{1,0:T(8,128)(2,1)}), bf16[2048,1024]{1,0:T(8,128)(2,1)}) %all-gather.6.cloned.1.call-update) | async-done | bytes 4194320 | tf_op jit(solution)/shard_map/all_gather | solution.py:167
  133.5 7.1 %all-to-all-start.1 = ((bf16[32,32,512]{2,1,0:T(8,128)(2,1)}), bf16[32,32,512]{2,1,0:T(8,128)(2,1)S(1)}, u32[]{:S(2)}, u32[]{:S(2)}) async-start(bf16[32,32,512]{2,1,0:T(8,128)(2,1)} %copy-done.3), calls=%async_computation.1 | async-start | bytes 2097152 | tf_op jit(solution)/shard_map/all_to_all | solution.py:196
  140.6 16.8 %all-to-all-done.1 = bf16[32,32,512]{2,1,0:T(8,128)(2,1)S(1)} async-done(((bf16[32,32,512]{2,1,0:T(8,128)(2,1)}), bf16[32,32,512]{2,1,0:T(8,128)(2,1)S(1)}, u32[]{:S(2)}, u32[]{:S(2)}) %all-to-all-start.1) | async-done | bytes 1048608 | tf_op jit(solution)/shard_map/all_to_all | solution.py:196
  157.3 2.0 gather_fusion.1
  159.3 0.9 broadcast_select_fusion.1
  160.3 4.1 %all-to-all-start.2 = ((bf16[4,128,512]{2,1,0:T(8,128)(2,1)}), bf16[4,128,512]{2,1,0:T(8,128)(2,1)S(1)}, u32[]{:S(2)}, u32[]{:S(2)}) async-start(bf16[4,128,512]{2,1,0:T(8,128)(2,1)} %broadcast_select_fusion.1), calls=%async_computation.2 | async-start | bytes 1048576 | tf_op jit(solution)/shard_map/all_to_all | solution.py:198
  164.4 10.0 %all-to-all-done.2 = bf16[4,128,512]{2,1,0:T(8,128)(2,1)S(1)} async-done(((bf16[4,128,512]{2,1,0:T(8,128)(2,1)}), bf16[4,128,512]{2,1,0:T(8,128)(2,1)S(1)}, u32[]{:S(2)}, u32[]{:S(2)}) %all-to-all-start.2) | async-done | bytes 524320 | tf_op jit(solution)/shard_map/all_to_all | solution.py:198
  174.4 2.0 fusion.15
  176.4 2.0 fusion.14
  178.5 2.0 fusion.12
  180.5 2.3 multiply_reduce_fusion
  182.9 0.9 multiply_convert_fusion.1
  184.3 1.5 collective-permute-start.4
  186.1 2.9 collective-permute-start.5
  189.1 23.2 %all-gather.8.cloned.1.call-done = bf16[1024,2048]{1,0:T(8,128)(2,1)} async-done(((bf16[128,2048]{1,0:T(8,128)(2,1)}), bf16[1024,2048]{1,0:T(8,128)(2,1)}) %all-gather.8.cloned.1.call-update) | async-done | bytes 4194320 | tf_op jit(solution)/shard_map/all_gather | solution.py:212
  212.3 7.6 %fusion.51 = f32[1024,1024]{1,0:T(8,128)S(1)} fusion(bf16[1024,2048]{1,0:T(8,128)(2,1)} %all-gather.8.cloned.1.call-done, bf16[2048,1024]{1,0:T(8,128)(2,1)} %all-gather.4.cloned.1.call-done), kind=kOutput, calls=%fused_computation.94 | convolution fusion | flops 4294967296 | bytes 12582912 | tf_op jit(solution)/shard_map/dot_general | solution.py:213
  220.0 5.2 %multiply_convert_fusion = bf16[1024,1024]{1,0:T(8,128)(2,1)S(1)} fusion(f32[1024,1024]{1,0:T(8,128)S(1)} %fusion.51, bf16[1024,2048]{1,0:T(8,128)(2,1)S(1)} %copy-done.13, bf16[2048,1024]{1,0:T(8,128)(2,1)S(1)} %copy-done.12), kind=kOutput, calls=%fused_computation.16 | convolution fusion | flops 4301258752 | bytes 14680064 | tf_op jit(solution)/shard_map/dot_general | solution.py:214
  225.2 7.5 %collective-permute-done.3 = bf16[256,2048]{1,0:T(8,128)(2,1)} collective-permute-done((bf16[256,2048]{1,0:T(8,128)(2,1)S(1)}, bf16[256,2048]{1,0:T(8,128)(2,1)}, u32[]{:S(2)}, u32[]{:S(2)}) %collective-permute-start.3) | collective-permute-done | bytes 1048608 | tf_op jit(solution)/shard_map/ppermute | solution.py:170
  232.7 1.3 fusion.28
  233.9 5.8 %fusion.26 = f32[1024,2048]{1,0:T(8,128)} fusion(bf16[256,2048]{1,0:T(8,128)(2,1)} %collective-permute-done.3, bf16[1024,1024]{1,0:T(8,128)(2,1)S(1)} %multiply_convert_fusion, s32[]{:T(128)S(6)} %select_n.141), kind=kOutput, calls=%fused_computation.54 | convolution fusion | flops 1073741824 | bytes 9961476 | tf_op jit(solution)/shard_map/dot_general | solution.py:221
  239.7 4.5 %fusion.24 = f32[1024,2048]{1,0:T(8,128)} fusion(bf16[256,2048]{1,0:T(8,128)(2,1)S(1)} %collective-permute-done.4, bf16[1024,1024]{1,0:T(8,128)(2,1)S(1)} %multiply_convert_fusion, s32[]{:T(128)S(6)} %select_n.143), kind=kOutput, calls=%fused_computation.52 | convolution fusion | flops 1073741824 | bytes 9961476 | tf_op jit(solution)/shard_map/dot_general | solution.py:221
  244.2 10.0 %add_convert_fusion = bf16[1024,2048]{1,0:T(8,128)(2,1)} fusion(f32[1024,2048]{1,0:T(8,128)} %fusion.24, f32[1024,2048]{1,0:T(8,128)S(1)} %fusion.28, f32[1024,2048]{1,0:T(8,128)} %fusion.26, bf16[256,2048]{1,0:T(8,128)(2,1)} %collective-permute-done.5, bf16[1024,1024]{1,0:T(8,128)(2,1)S(1)} %multiply_convert_fusion, s32[]{:T(128)S(6)} %select_n.145), kind=kOutput, calls=%fused_computation.2 | convolution fusion | flops 1082130432 | bytes 30932996 | tf_op jit(solution)/shard_map/dot_general | solution.py:221
  254.2 34.4 %reduce-scatter.2.cloned.1.call-done = bf16[128,2048]{1,0:T(8,128)(2,1)} async-done(((bf16[1024,2048]{1,0:T(8,128)(2,1)}), bf16[128,2048]{1,0:T(8,128)(2,1)}) %reduce-scatter.2.cloned.1.call-update) | async-done | bytes 524304 | tf_op jit(solution)/shard_map/reduce_scatter | solution.py:227
  288.6 2.0 add_convert_fusion.1
  (65 shorter events, 5.0 us)
Async XLA Ops:
  7.2 6.2 %copy-start = (bf16[2048,512]{1,0:T(8,128)(2,1)S(1)}, bf16[2048,512]{1,0:T(8,128)(2,1)}, u32[]{:S(2)}) copy-start(bf16[2048,512]{1,0:T(8,128)(2,1)} %param.19) | copy-start | bytes 6291460
  7.2 1.5 copy-start.10
  7.2 4.2 %copy-start.16 = (f32[2048]{0:T(1024)S(1)}, f32[2048]{0:T(1024)}, u32[]{:S(2)}) copy-start(f32[2048]{0:T(1024)} %param.17) | copy-start | bytes 24580
  7.2 4.2 %copy-start.14 = (bf16[2048,128]{1,0:T(8,128)(2,1)S(1)}, bf16[2048,128]{1,0:T(8,128)(2,1)}, u32[]{:S(2)}) copy-start(bf16[2048,128]{1,0:T(8,128)(2,1)} %param.20) | copy-start | bytes 1572868
  7.2 116.8 %all-gather.4.cloned.1.call-start = ((), (), s32[]{:S(2)}) async-start(), calls=%async_computation.4 | async-start | bytes 5242880 | tf_op jit(solution)/shard_map/all_gather | solution.py:166
  7.9 125.5 %all-gather.6.cloned.1.call-start = ((), (), s32[]{:S(2)}) async-start(), calls=%async_computation.5 | async-start | bytes 5242880 | tf_op jit(solution)/shard_map/all_gather | solution.py:167
  9.1 2.3 copy-start.8
  11.4 1.0 copy-start.15
  20.6 14.9 %copy-start.6 = (s32[1,32]{1,0:T(1,128)S(1)}, s32[1,32]{1,0:T(1,128)}, u32[]{:S(2)}) copy-start(s32[1,32]{1,0:T(1,128)} %param.30) | copy-start | bytes 388
  20.6 41.9 %all-to-all-start = ((bf16[32,32,768]{2,1,0:T(8,128)(2,1)}), bf16[32,32,768]{2,1,0:T(8,128)(2,1)S(1)}, u32[]{:S(2)}, u32[]{:S(2)}) async-start(bf16[32,32,768]{2,1,0:T(8,128)(2,1)} %broadcast_select_fusion), calls=%async_computation | async-start | bytes 3145728 | tf_op jit(solution)/shard_map/all_to_all | solution.py:188
  29.2 81.0 %collective-permute-start.1 = (bf16[512,2048]{1,0:T(8,128)(2,1)}, bf16[512,2048]{1,0:T(8,128)(2,1)}, u32[]{:S(2)}, u32[]{:S(2)}) collective-permute-start(bf16[512,2048]{1,0:T(8,128)(2,1)} %param.22), channel_id=1, source_target_pairs={{0,2},{1,3},{2,0},{3,1},{4,6},{5,7},{6,4},{7,5},{8,10},{9,11},{10,... | collective-permute-start | bytes 6291464 | tf_op jit(solution)/shard_map/ppermute | solution.py:174
  32.3 91.5 %collective-permute-start = (bf16[512,2048]{1,0:T(8,128)(2,1)}, bf16[512,2048]{1,0:T(8,128)(2,1)}, u32[]{:S(2)}, u32[]{:S(2)}) collective-permute-start(bf16[512,2048]{1,0:T(8,128)(2,1)} %param.22), channel_id=1, source_target_pairs={{0,1},{1,2},{2,3},{3,0},{4,5},{5,6},{6,7},{7,4},{8,9},{9,10},{10,1... | collective-permute-start | bytes 6291464 | tf_op jit(solution)/shard_map/ppermute | solution.py:174
  32.9 91.1 %collective-permute-start.2 = (bf16[512,2048]{1,0:T(8,128)(2,1)}, bf16[512,2048]{1,0:T(8,128)(2,1)}, u32[]{:S(2)}, u32[]{:S(2)}) collective-permute-start(bf16[512,2048]{1,0:T(8,128)(2,1)} %param.22), channel_id=1, source_target_pairs={{0,3},{1,0},{2,1},{3,2},{4,7},{5,4},{6,5},{7,6},{8,11},{9,8},{10,9... | collective-permute-start | bytes 6291464 | tf_op jit(solution)/shard_map/ppermute | solution.py:174
  76.2 3.4 %copy-start.2 = (bf16[512,16,128]{2,1,0:T(8,128)(2,1)S(1)}, bf16[512,16,128]{2,1,0:T(8,128)(2,1)}, u32[]{:S(2)}) copy-start(bf16[512,16,128]{2,1,0:T(8,128)(2,1)} %ck_ref.1) | copy-start | bytes 6291460
  76.2 3.4 %copy-start.5 = (s32[1,512]{1,0:T(1,128)S(1)}, s32[1,512]{1,0:T(1,128)}, u32[]{:S(2)}) copy-start(s32[1,512]{1,0:T(1,128)} %param.31) | copy-start | bytes 6148
  76.2 3.4 %copy-start.7 = (s32[1,32]{1,0:T(1,128)S(1)}, s32[1,32]{1,0:T(1,128)}, u32[]{:S(2)}) copy-start(s32[1,32]{1,0:T(1,128)} %param.29) | copy-start | bytes 388
  79.6 1.0 copy-start.4
  109.2 1.0 copy-start.3
  133.5 23.9 %all-to-all-start.1 = ((bf16[32,32,512]{2,1,0:T(8,128)(2,1)}), bf16[32,32,512]{2,1,0:T(8,128)(2,1)S(1)}, u32[]{:S(2)}, u32[]{:S(2)}) async-start(bf16[32,32,512]{2,1,0:T(8,128)(2,1)} %copy-done.3), calls=%async_computation.1 | async-start | bytes 2097152 | tf_op jit(solution)/shard_map/all_to_all | solution.py:196
  160.3 14.1 %all-to-all-start.2 = ((bf16[4,128,512]{2,1,0:T(8,128)(2,1)}), bf16[4,128,512]{2,1,0:T(8,128)(2,1)S(1)}, u32[]{:S(2)}, u32[]{:S(2)}) async-start(bf16[4,128,512]{2,1,0:T(8,128)(2,1)} %broadcast_select_fusion.1), calls=%async_computation.2 | async-start | bytes 1048576 | tf_op jit(solution)/shard_map/all_to_all | solution.py:198
  164.4 47.9 %all-gather.8.cloned.1.call-start = ((), (), s32[]{:S(2)}) async-start(), calls=%async_computation.6 | async-start | bytes 4718592 | tf_op jit(solution)/shard_map/all_gather | solution.py:212
  180.5 2.4 copy-start.11
  182.9 1.4 copy-start.9
  183.9 104.8 %reduce-scatter.2.cloned.1.call-start = ((), (), s32[]{:S(2)}) async-start(), calls=%async_computation.7 | async-start | bytes 4718592 | tf_op jit(solution)/shard_map/reduce_scatter | solution.py:227
  184.3 40.9 %collective-permute-start.4 = (bf16[256,2048]{1,0:T(8,128)(2,1)S(1)}, bf16[256,2048]{1,0:T(8,128)(2,1)S(1)}, u32[]{:S(2)}, u32[]{:S(2)}) collective-permute-start(bf16[256,2048]{1,0:T(8,128)(2,1)S(1)} %copy-done.9), channel_id=1, source_target_pairs={{0,64},{32,96},{64,0},{96,32},{1,65},{33,97},{65,1},{97,33},{2,66}... | collective-permute-start | bytes 3145736 | tf_op jit(solution)/shard_map/ppermute | solution.py:170
  185.8 46.8 %collective-permute-start.3 = (bf16[256,2048]{1,0:T(8,128)(2,1)S(1)}, bf16[256,2048]{1,0:T(8,128)(2,1)}, u32[]{:S(2)}, u32[]{:S(2)}) collective-permute-start(bf16[256,2048]{1,0:T(8,128)(2,1)S(1)} %copy-done.9), channel_id=1, source_target_pairs={{0,32},{32,64},{64,96},{96,0},{1,33},{33,65},{65,97},{97,1},{2,34}... | collective-permute-start | bytes 3145736 | tf_op jit(solution)/shard_map/ppermute | solution.py:170
  186.1 46.5 %collective-permute-start.5 = (bf16[256,2048]{1,0:T(8,128)(2,1)S(1)}, bf16[256,2048]{1,0:T(8,128)(2,1)}, u32[]{:S(2)}, u32[]{:S(2)}) collective-permute-start(bf16[256,2048]{1,0:T(8,128)(2,1)S(1)} %copy-done.9), channel_id=1, source_target_pairs={{0,96},{32,0},{64,32},{96,64},{1,97},{33,1},{65,33},{97,65},{2,98}... | collective-permute-start | bytes 3145736 | tf_op jit(solution)/shard_map/ppermute | solution.py:170
  212.3 7.7 %copy-start.12 = (bf16[2048,1024]{1,0:T(8,128)(2,1)S(1)}, bf16[2048,1024]{1,0:T(8,128)(2,1)}, u32[]{:S(2)}) copy-start(bf16[2048,1024]{1,0:T(8,128)(2,1)} %all-gather.6.cloned.1.call-done) | copy-start | bytes 12582916
  212.3 7.7 %copy-start.13 = (bf16[1024,2048]{1,0:T(8,128)(2,1)S(1)}, bf16[1024,2048]{1,0:T(8,128)(2,1)}, u32[]{:S(2)}) copy-start(bf16[1024,2048]{1,0:T(8,128)(2,1)} %all-gather.8.cloned.1.call-done) | copy-start | bytes 12582916
  254.2 36.4 %copy-start.1 = (bf16[2048,512]{1,0:T(8,128)(2,1)S(1)}, bf16[2048,512]{1,0:T(8,128)(2,1)}, u32[]{:S(2)}) copy-start(bf16[2048,512]{1,0:T(8,128)(2,1)} %param.19) | copy-start | bytes 6291460
Sparse Core Ops, SparseCore 0:
  9.7 69.0 all-gather.3
  80.5 52.9 all-gather.5
  184.0 28.2 all-gather.7
  254.3 34.2 reduce-scatter.1

commit v8 on v7

--- a/solution.py
+++ b/solution.py
@@ -192,8 +192,9 @@
     mixed, keys_out, values_out = owner_attention(
         recv_query, recv_key, recv_value, cache_k, cache_v, new_len[0], prior_len[0], page_table[0]
     )
-    gate_w, up_w, out_parts, mixed = lax.optimization_barrier((gate_w, up_w, out_parts, mixed))
+    mixed = lax.optimization_barrier(mixed)
     returned = lax.all_to_all(mixed, REQ, split_axis=0, concat_axis=0, tiled=True)
+    gate_w, up_w, out_parts, returned = lax.optimization_barrier((gate_w, up_w, out_parts, returned))
     attn_rows = jnp.take(returned.reshape(peers * pair_rows, -1), back_rows, axis=0)
     quarters = lax.all_to_all(
         attn_rows.reshape(groups, quarter, -1), "grp", split_axis=0, concat_axis=0, tiled=True

time: 298 us -> 285 us (0.956)
  waiting for transfers between devices: 142 us -> 131 us
  starting transfers between devices: 31 us -> 27.7 us
    all_gather x1, waiting for transfers between devices: 9.48 us -> 0.84 us  [body(): up_w = lax.all_gather(w_up, 'ry', axis=1, tiled=True)]
    ppermute x3, waiting for transfers between devices: 13.8 us -> 7.75 us  [body(): lax.ppermute(w_out, 'grp', [(i, (i + shift) % groups) for i in range(grou...]
    all_to_all x1, starting transfers between devices: 7.07 us -> 4.08 us  [body(): lax.all_to_all(mixed, REQ, split_axis=0, concat_axis=0, tiled=True)]
  transfers between devices with their start and end apart: 13 -> 13, of which waited for: 9 -> 9; matrix products, arithmetic and copies ran while one was open for 15% -> 16% of each run, Pallas kernels for 10% -> 10%
where the time goes in v8:
time: 285 us
  waiting for transfers between devices  131 us (46%)
  matrix products  47.9 us (17%)
  Pallas kernels  28.6 us (10%)
  starting transfers between devices  27.7 us (10%)
  local copies, waits for them, and re-layouts  20.6 us (7%)
  other arithmetic  14.8 us (5%)
  between operations  14.2 us (5%)
    reduce_scatter x1, waiting for transfers between devices, body(): lax.psum_scatter(partial.astype(jnp.bfloat16), 'rzc', scatter_dimension=0...  35.1 us
    pallas_call x1, Pallas kernels, owner_attention(): pl.pallas_call(attention_kernel, out_shape=(jax.ShapeDtypeStruct((sources...  28.6 us
    all_to_all x1, waiting for transfers between devices, body(): lax.all_to_all(send_qkv, REQ, split_axis=0, concat_axis=0, tiled=True)  26.9 us
    all_gather x1, waiting for transfers between devices, body(): piece = lax.all_gather(mlp_in, 'rzc', axis=0, tiled=True)  25.2 us
    dot_general x4, matrix products, body(): jnp.dot(lax.dynamic_slice_in_dim(hidden, block * units, units, axis=1), p...  21.5 us
    all_to_all x1, waiting for transfers between devices, body(): lax.all_to_all(mixed, REQ, split_axis=0, concat_axis=0, tiled=True)  17.6 us
    all_to_all x1, waiting for transfers between devices, body(): lax.all_to_all(attn_rows.reshape(groups, quarter, -1), 'grp', split_axis=...  10.2 us
    all_to_all x1, starting transfers between devices, body(): lax.all_to_all(send_qkv, REQ, split_axis=0, concat_axis=0, tiled=True)  8.55 us
  transfers between devices with their start and end apart: 13, of which 9 were waited for; matrix products, arithmetic and copies ran while one was open for 16% of the time, Pallas kernels for 10%

profile of v8, /device:TPU:0, one launch (start us, length us, event | category | flops | bytes accessed | tf_op | source)
XLA Modules:
  0.0 284.5 jit_solution(851181216424397113)
XLA Ops:
  8.8 2.1 fusion
  11.2 2.7 convolution_convert_fusion.6
  13.9 1.0 convolution_convert_fusion.5
  14.9 1.4 convolution_convert_fusion.4
  16.7 4.0 %gather_fusion = bf16[1024,768]{1,0:T(8,128)(2,1)S(1)} fusion(bf16[512,768]{1,0:T(8,128)(2,1)S(1)} %copy.21, s32[1024]{0:T(1024)S(1)} %broadcast_clamp_fusion), kind=kCustom, calls=%fused_computation | custom fusion | bytes 3149824 | tf_op jit(solution)/shard_map/jit(_take)/gather | solution.py:185
  20.8 1.4 broadcast_select_fusion
  22.1 8.5 %all-to-all-start = ((bf16[32,32,768]{2,1,0:T(8,128)(2,1)}), bf16[32,32,768]{2,1,0:T(8,128)(2,1)S(1)}, u32[]{:S(2)}, u32[]{:S(2)}) async-start(bf16[32,32,768]{2,1,0:T(8,128)(2,1)} %broadcast_select_fusion), calls=%async_computation | async-start | bytes 3145728 | tf_op jit(solution)/shard_map/all_to_all | solution.py:188
  30.7 3.1 %collective-permute-start.1 = (bf16[512,2048]{1,0:T(8,128)(2,1)}, bf16[512,2048]{1,0:T(8,128)(2,1)}, u32[]{:S(2)}, u32[]{:S(2)}) collective-permute-start(bf16[512,2048]{1,0:T(8,128)(2,1)} %param.22), channel_id=1, source_target_pairs={{0,2},{1,3},{2,0},{3,1},{4,6},{5,7},{6,4},{7,5},{8,10},{9,11},{10,... | collective-permute-start | bytes 6291464 | tf_op jit(solution)/shard_map/ppermute | solution.py:174
  34.4 2.6 collective-permute-start.2
  37.1 1.9 multiply_cosine_fusion
  39.0 26.9 %all-to-all-done = bf16[32,32,768]{2,1,0:T(8,128)(2,1)S(1)} async-done(((bf16[32,32,768]{2,1,0:T(8,128)(2,1)}), bf16[32,32,768]{2,1,0:T(8,128)(2,1)S(1)}, u32[]{:S(2)}, u32[]{:S(2)}) %all-to-all-start) | async-done | bytes 1572896 | tf_op jit(solution)/shard_map/all_to_all | solution.py:188
  67.0 1.0 fusion.50
  68.7 1.3 copy.24
  70.1 1.3 convert_element_type.112.k_ref
  71.4 1.1 slice.32
  72.5 2.8 reshape.161
  75.2 1.9 fusion.4
  77.2 2.5 pad_maximum_fusion
  79.6 3.3 %convert_element_type.109.q_ref = bf16[32,32,512]{2,1,0:T(8,128)(2,1)S(1)} reshape(bf16[32,32,8,64]{3,2,1,0:T(8,128)(2,1)} %pad_maximum_fusion) | data formatting | bytes 2097152 | tf_op jit(solution)/shard_map/convert_element_type | solution.py:116
  83.0 0.9 copy-done.4
  84.0 28.6 %shard_map.175 = (bf16[32,32,512]{2,1,0:T(8,128)(2,1)S(1)}, bf16[512,16,128]{2,1,0:T(8,128)(2,1)}, bf16[512,16,128]{2,1,0:T(8,128)(2,1)}) custom-call(s32[512]{0:T(512)S(1)} %bitcast.40, s32[32]{0:T(128)S(1)} %bitcast.42, s32[32]{0:T(128)S(1)} %bitcast.43, bf16[32,32,512]{2,1,0:T(8,128)(2,1)S(1)} %convert_element_type.109.q_ref, ...), custom_call_target="tpu_custom_call" | custom-call | tf_op jit(solution)/shard_map/pallas_call | solution.py:125
  112.6 1.0 copy-done.3
  113.6 4.1 %all-to-all-start.1 = ((bf16[32,32,512]{2,1,0:T(8,128)(2,1)}), bf16[32,32,512]{2,1,0:T(8,128)(2,1)S(1)}, u32[]{:S(2)}, u32[]{:S(2)}) async-start(bf16[32,32,512]{2,1,0:T(8,128)(2,1)} %copy-done.3), calls=%async_computation.1 | async-start | bytes 2097152 | tf_op jit(solution)/shard_map/all_to_all | solution.py:196
  117.7 7.6 %collective-permute-done = bf16[512,2048]{1,0:T(8,128)(2,1)} collective-permute-done((bf16[512,2048]{1,0:T(8,128)(2,1)}, bf16[512,2048]{1,0:T(8,128)(2,1)}, u32[]{:S(2)}, u32[]{:S(2)}) %collective-permute-start) | collective-permute-done | bytes 2097184 | tf_op jit(solution)/shard_map/ppermute | solution.py:174
  125.5 17.6 %all-to-all-done.1 = bf16[32,32,512]{2,1,0:T(8,128)(2,1)S(1)} async-done(((bf16[32,32,512]{2,1,0:T(8,128)(2,1)}), bf16[32,32,512]{2,1,0:T(8,128)(2,1)S(1)}, u32[]{:S(2)}, u32[]{:S(2)}) %all-to-all-start.1) | async-done | bytes 1048608 | tf_op jit(solution)/shard_map/all_to_all | solution.py:196
  143.1 0.8 all-gather.6.cloned.1.call-done
  144.0 2.0 gather_fusion.1
  145.9 0.9 broadcast_select_fusion.1
  146.9 4.1 %all-to-all-start.2 = ((bf16[4,128,512]{2,1,0:T(8,128)(2,1)}), bf16[4,128,512]{2,1,0:T(8,128)(2,1)S(1)}, u32[]{:S(2)}, u32[]{:S(2)}) async-start(bf16[4,128,512]{2,1,0:T(8,128)(2,1)} %broadcast_select_fusion.1), calls=%async_computation.2 | async-start | bytes 1048576 | tf_op jit(solution)/shard_map/all_to_all | solution.py:199
  151.0 10.2 %all-to-all-done.2 = bf16[4,128,512]{2,1,0:T(8,128)(2,1)S(1)} async-done(((bf16[4,128,512]{2,1,0:T(8,128)(2,1)}), bf16[4,128,512]{2,1,0:T(8,128)(2,1)S(1)}, u32[]{:S(2)}, u32[]{:S(2)}) %all-to-all-start.2) | async-done | bytes 524320 | tf_op jit(solution)/shard_map/all_to_all | solution.py:199
  161.2 2.0 fusion.15
  163.2 2.0 fusion.14
  165.3 2.0 fusion.12
  167.3 2.3 multiply_reduce_fusion
  169.7 0.9 multiply_convert_fusion.1
  171.1 1.2 collective-permute-start.4
  172.3 1.1 collective-permute-start.3
  173.4 2.2 collective-permute-start.5
  175.6 25.2 %all-gather.8.cloned.1.call-done = bf16[1024,2048]{1,0:T(8,128)(2,1)} async-done(((bf16[128,2048]{1,0:T(8,128)(2,1)}), bf16[1024,2048]{1,0:T(8,128)(2,1)}) %all-gather.8.cloned.1.call-update) | async-done | bytes 4194320 | tf_op jit(solution)/shard_map/all_gather | solution.py:213
  200.7 7.7 %fusion.51 = f32[1024,1024]{1,0:T(8,128)S(1)} fusion(bf16[1024,2048]{1,0:T(8,128)(2,1)} %all-gather.8.cloned.1.call-done, bf16[2048,1024]{1,0:T(8,128)(2,1)} %all-gather.4.cloned.1.call-done), kind=kOutput, calls=%fused_computation.94 | convolution fusion | flops 4294967296 | bytes 12582912 | tf_op jit(solution)/shard_map/dot_general | solution.py:214
  208.4 5.2 %multiply_convert_fusion = bf16[1024,1024]{1,0:T(8,128)(2,1)S(1)} fusion(f32[1024,1024]{1,0:T(8,128)S(1)} %fusion.51, bf16[1024,2048]{1,0:T(8,128)(2,1)S(1)} %copy-done.13, bf16[2048,1024]{1,0:T(8,128)(2,1)S(1)} %copy-done.12), kind=kOutput, calls=%fused_computation.16 | convolution fusion | flops 4301258752 | bytes 14680064 | tf_op jit(solution)/shard_map/dot_general | solution.py:215
  213.6 5.7 %collective-permute-done.3 = bf16[256,2048]{1,0:T(8,128)(2,1)} collective-permute-done((bf16[256,2048]{1,0:T(8,128)(2,1)S(1)}, bf16[256,2048]{1,0:T(8,128)(2,1)}, u32[]{:S(2)}, u32[]{:S(2)}) %collective-permute-start.3) | collective-permute-done | bytes 1048608 | tf_op jit(solution)/shard_map/ppermute | solution.py:170
  219.4 1.3 fusion.28
  220.7 5.8 %fusion.26 = f32[1024,2048]{1,0:T(8,128)} fusion(bf16[256,2048]{1,0:T(8,128)(2,1)} %collective-permute-done.3, bf16[1024,1024]{1,0:T(8,128)(2,1)S(1)} %multiply_convert_fusion, s32[]{:T(128)S(6)} %select_n.141), kind=kOutput, calls=%fused_computation.54 | convolution fusion | flops 1073741824 | bytes 9961476 | tf_op jit(solution)/shard_map/dot_general | solution.py:222
  226.4 4.5 %fusion.24 = f32[1024,2048]{1,0:T(8,128)} fusion(bf16[256,2048]{1,0:T(8,128)(2,1)S(1)} %collective-permute-done.4, bf16[1024,1024]{1,0:T(8,128)(2,1)S(1)} %multiply_convert_fusion, s32[]{:T(128)S(6)} %select_n.143), kind=kOutput, calls=%fused_computation.52 | convolution fusion | flops 1073741824 | bytes 9961476 | tf_op jit(solution)/shard_map/dot_general | solution.py:222
  230.9 10.0 %add_convert_fusion = bf16[1024,2048]{1,0:T(8,128)(2,1)} fusion(f32[1024,2048]{1,0:T(8,128)} %fusion.24, f32[1024,2048]{1,0:T(8,128)S(1)} %fusion.28, f32[1024,2048]{1,0:T(8,128)} %fusion.26, bf16[256,2048]{1,0:T(8,128)(2,1)} %collective-permute-done.5, bf16[1024,1024]{1,0:T(8,128)(2,1)S(1)} %multiply_convert_fusion, s32[]{:T(128)S(6)} %select_n.145), kind=kOutput, calls=%fused_computation.2 | convolution fusion | flops 1082130432 | bytes 30932996 | tf_op jit(solution)/shard_map/dot_general | solution.py:222
  241.0 35.1 %reduce-scatter.2.cloned.1.call-done = bf16[128,2048]{1,0:T(8,128)(2,1)} async-done(((bf16[1024,2048]{1,0:T(8,128)(2,1)}), bf16[128,2048]{1,0:T(8,128)(2,1)}) %reduce-scatter.2.cloned.1.call-update) | async-done | bytes 524304 | tf_op jit(solution)/shard_map/reduce_scatter | solution.py:228
  276.0 2.0 add_convert_fusion.1
  (65 shorter events, 5.4 us)
Async XLA Ops:
  7.2 7.7 %copy-start = (bf16[2048,512]{1,0:T(8,128)(2,1)S(1)}, bf16[2048,512]{1,0:T(8,128)(2,1)}, u32[]{:S(2)}) copy-start(bf16[2048,512]{1,0:T(8,128)(2,1)} %param.19) | copy-start | bytes 6291460
  7.2 1.5 copy-start.10
  7.2 4.0 %copy-start.16 = (f32[2048]{0:T(1024)S(1)}, f32[2048]{0:T(1024)}, u32[]{:S(2)}) copy-start(f32[2048]{0:T(1024)} %param.17) | copy-start | bytes 24580
  7.2 4.0 %copy-start.14 = (bf16[2048,128]{1,0:T(8,128)(2,1)S(1)}, bf16[2048,128]{1,0:T(8,128)(2,1)}, u32[]{:S(2)}) copy-start(bf16[2048,128]{1,0:T(8,128)(2,1)} %param.20) | copy-start | bytes 1572868
  7.2 135.9 %all-gather.4.cloned.1.call-start = ((), (), s32[]{:S(2)}) async-start(), calls=%async_computation.4 | async-start | bytes 5242880 | tf_op jit(solution)/shard_map/all_gather | solution.py:166
  7.9 136.0 %all-gather.6.cloned.1.call-start = ((), (), s32[]{:S(2)}) async-start(), calls=%async_computation.5 | async-start | bytes 5242880 | tf_op jit(solution)/shard_map/all_gather | solution.py:167
  11.2 2.7 copy-start.8
  11.2 2.7 copy-start.15
  22.1 14.9 %copy-start.6 = (s32[1,32]{1,0:T(1,128)S(1)}, s32[1,32]{1,0:T(1,128)}, u32[]{:S(2)}) copy-start(s32[1,32]{1,0:T(1,128)} %param.30) | copy-start | bytes 388
  22.1 43.8 %all-to-all-start = ((bf16[32,32,768]{2,1,0:T(8,128)(2,1)}), bf16[32,32,768]{2,1,0:T(8,128)(2,1)S(1)}, u32[]{:S(2)}, u32[]{:S(2)}) async-start(bf16[32,32,768]{2,1,0:T(8,128)(2,1)} %broadcast_select_fusion), calls=%async_computation | async-start | bytes 3145728 | tf_op jit(solution)/shard_map/all_to_all | solution.py:188
  30.7 87.0 %collective-permute-start.1 = (bf16[512,2048]{1,0:T(8,128)(2,1)}, bf16[512,2048]{1,0:T(8,128)(2,1)}, u32[]{:S(2)}, u32[]{:S(2)}) collective-permute-start(bf16[512,2048]{1,0:T(8,128)(2,1)} %param.22), channel_id=1, source_target_pairs={{0,2},{1,3},{2,0},{3,1},{4,6},{5,7},{6,4},{7,5},{8,10},{9,11},{10,... | collective-permute-start | bytes 6291464 | tf_op jit(solution)/shard_map/ppermute | solution.py:174
  33.8 91.5 %collective-permute-start = (bf16[512,2048]{1,0:T(8,128)(2,1)}, bf16[512,2048]{1,0:T(8,128)(2,1)}, u32[]{:S(2)}, u32[]{:S(2)}) collective-permute-start(bf16[512,2048]{1,0:T(8,128)(2,1)} %param.22), channel_id=1, source_target_pairs={{0,1},{1,2},{2,3},{3,0},{4,5},{5,6},{6,7},{7,4},{8,9},{9,10},{10,1... | collective-permute-start | bytes 6291464 | tf_op jit(solution)/shard_map/ppermute | solution.py:174
  34.4 91.1 %collective-permute-start.2 = (bf16[512,2048]{1,0:T(8,128)(2,1)}, bf16[512,2048]{1,0:T(8,128)(2,1)}, u32[]{:S(2)}, u32[]{:S(2)}) collective-permute-start(bf16[512,2048]{1,0:T(8,128)(2,1)} %param.22), channel_id=1, source_target_pairs={{0,3},{1,0},{2,1},{3,2},{4,7},{5,4},{6,5},{7,6},{8,11},{9,8},{10,9... | collective-permute-start | bytes 6291464 | tf_op jit(solution)/shard_map/ppermute | solution.py:174
  79.6 3.4 %copy-start.2 = (bf16[512,16,128]{2,1,0:T(8,128)(2,1)S(1)}, bf16[512,16,128]{2,1,0:T(8,128)(2,1)}, u32[]{:S(2)}) copy-start(bf16[512,16,128]{2,1,0:T(8,128)(2,1)} %ck_ref.1) | copy-start | bytes 6291460
  79.6 3.4 %copy-start.5 = (s32[1,512]{1,0:T(1,128)S(1)}, s32[1,512]{1,0:T(1,128)}, u32[]{:S(2)}) copy-start(s32[1,512]{1,0:T(1,128)} %param.31) | copy-start | bytes 6148
  79.6 3.4 %copy-start.7 = (s32[1,32]{1,0:T(1,128)S(1)}, s32[1,32]{1,0:T(1,128)}, u32[]{:S(2)}) copy-start(s32[1,32]{1,0:T(1,128)} %param.29) | copy-start | bytes 388
  83.0 1.0 copy-start.4
  112.6 1.0 copy-start.3
  113.6 29.5 %all-to-all-start.1 = ((bf16[32,32,512]{2,1,0:T(8,128)(2,1)}), bf16[32,32,512]{2,1,0:T(8,128)(2,1)S(1)}, u32[]{:S(2)}, u32[]{:S(2)}) async-start(bf16[32,32,512]{2,1,0:T(8,128)(2,1)} %copy-done.3), calls=%async_computation.1 | async-start | bytes 2097152 | tf_op jit(solution)/shard_map/all_to_all | solution.py:196
  146.9 14.3 %all-to-all-start.2 = ((bf16[4,128,512]{2,1,0:T(8,128)(2,1)}), bf16[4,128,512]{2,1,0:T(8,128)(2,1)S(1)}, u32[]{:S(2)}, u32[]{:S(2)}) async-start(bf16[4,128,512]{2,1,0:T(8,128)(2,1)} %broadcast_select_fusion.1), calls=%async_computation.2 | async-start | bytes 1048576 | tf_op jit(solution)/shard_map/all_to_all | solution.py:199
  151.0 49.8 %all-gather.8.cloned.1.call-start = ((), (), s32[]{:S(2)}) async-start(), calls=%async_computation.6 | async-start | bytes 4718592 | tf_op jit(solution)/shard_map/all_gather | solution.py:213
  167.3 2.4 copy-start.11
  169.7 1.4 copy-start.9
  170.7 105.3 %reduce-scatter.2.cloned.1.call-start = ((), (), s32[]{:S(2)}) async-start(), calls=%async_computation.7 | async-start | bytes 4718592 | tf_op jit(solution)/shard_map/reduce_scatter | solution.py:228
  171.1 42.5 %collective-permute-start.4 = (bf16[256,2048]{1,0:T(8,128)(2,1)S(1)}, bf16[256,2048]{1,0:T(8,128)(2,1)S(1)}, u32[]{:S(2)}, u32[]{:S(2)}) collective-permute-start(bf16[256,2048]{1,0:T(8,128)(2,1)S(1)} %copy-done.9), channel_id=1, source_target_pairs={{0,64},{32,96},{64,0},{96,32},{1,65},{33,97},{65,1},{97,33},{2,66}... | collective-permute-start | bytes 3145736 | tf_op jit(solution)/shard_map/ppermute | solution.py:170
  172.3 47.1 %collective-permute-start.3 = (bf16[256,2048]{1,0:T(8,128)(2,1)S(1)}, bf16[256,2048]{1,0:T(8,128)(2,1)}, u32[]{:S(2)}, u32[]{:S(2)}) collective-permute-start(bf16[256,2048]{1,0:T(8,128)(2,1)S(1)} %copy-done.9), channel_id=1, source_target_pairs={{0,32},{32,64},{64,96},{96,0},{1,33},{33,65},{65,97},{97,1},{2,34}... | collective-permute-start | bytes 3145736 | tf_op jit(solution)/shard_map/ppermute | solution.py:170
  173.4 46.0 %collective-permute-start.5 = (bf16[256,2048]{1,0:T(8,128)(2,1)S(1)}, bf16[256,2048]{1,0:T(8,128)(2,1)}, u32[]{:S(2)}, u32[]{:S(2)}) collective-permute-start(bf16[256,2048]{1,0:T(8,128)(2,1)S(1)} %copy-done.9), channel_id=1, source_target_pairs={{0,96},{32,0},{64,32},{96,64},{1,97},{33,1},{65,33},{97,65},{2,98}... | collective-permute-start | bytes 3145736 | tf_op jit(solution)/shard_map/ppermute | solution.py:170
  200.7 7.7 %copy-start.12 = (bf16[2048,1024]{1,0:T(8,128)(2,1)S(1)}, bf16[2048,1024]{1,0:T(8,128)(2,1)}, u32[]{:S(2)}) copy-start(bf16[2048,1024]{1,0:T(8,128)(2,1)} %all-gather.6.cloned.1.call-done) | copy-start | bytes 12582916
  200.7 7.7 %copy-start.13 = (bf16[1024,2048]{1,0:T(8,128)(2,1)S(1)}, bf16[1024,2048]{1,0:T(8,128)(2,1)}, u32[]{:S(2)}) copy-start(bf16[1024,2048]{1,0:T(8,128)(2,1)} %all-gather.8.cloned.1.call-done) | copy-start | bytes 12582916
  240.9 37.0 %copy-start.1 = (bf16[2048,512]{1,0:T(8,128)(2,1)S(1)}, bf16[2048,512]{1,0:T(8,128)(2,1)}, u32[]{:S(2)}) copy-start(bf16[2048,512]{1,0:T(8,128)(2,1)} %param.19) | copy-start | bytes 6291460
Sparse Core Ops, SparseCore 0:
  9.7 69.0 all-gather.3
  80.4 63.4 all-gather.5
  170.8 29.9 all-gather.7
  241.1 34.9 reduce-scatter.1

commit v9 on v8

--- a/solution.py
+++ b/solution.py
@@ -52,12 +52,13 @@
     return (gather_rows.reshape(-1), back_rows)
 
 
-def attention_kernel(table_ref, prior_ref, len_ref, q_ref, k_ref, v_ref, ck_ref, cv_ref,
-                     out_ref, nk_ref, nv_ref, kbuf, vbuf):
-    sources, pair_rows, qcols = q_ref.shape
-    kcols = k_ref.shape[-1]
+def attention_kernel(table_ref, prior_ref, len_ref, qkv_ref, k_ref, cos_ref, sin_ref, ck_ref,
+                     cv_ref, out_ref, nk_ref, nv_ref, kbuf, vbuf):
+    sources, pair_rows, kcols = k_ref.shape
+    qcols = qkv_ref.shape[-1] - 2 * kcols
     kv_heads = kcols // HD
     group = qcols // kcols
+    half = HD // 2
 
     def per_source(s, carry):
         prior = prior_ref[s]
@@ -71,30 +72,40 @@
         select = jnp.logical_and(j_col == prior + t_row, t_row < length).astype(jnp.bfloat16)
         j_only = lax.broadcasted_iota(jnp.int32, (CONTEXT, kcols), 0)
         fresh = jnp.logical_and(j_only >= prior, j_only < prior + length)
+        v_in = qkv_ref[s, :, qcols + kcols:qcols + 2 * kcols]
         k_new = jnp.dot(select, k_ref[s], preferred_element_type=jnp.float32).astype(jnp.bfloat16)
-        v_new = jnp.dot(select, v_ref[s], preferred_element_type=jnp.float32).astype(jnp.bfloat16)
+        v_new = jnp.dot(select, v_in, preferred_element_type=jnp.float32).astype(jnp.bfloat16)
         keys = jnp.where(fresh, k_new, kbuf[...])
         values = jnp.where(fresh, v_new, vbuf[...])
         for i in range(MAXP):
             page = table_ref[s * MAXP + i]
             nk_ref[page] = keys[i * PAGE:(i + 1) * PAGE, :]
             nv_ref[page] = values[i * PAGE:(i + 1) * PAGE, :]
-        q_all = q_ref[s]
+        cosine = cos_ref[s]
+        sine = sin_ref[s]
         rows = group * pair_rows
         r_idx = lax.broadcasted_iota(jnp.int32, (rows, CONTEXT), 0)
         j_idx = lax.broadcasted_iota(jnp.int32, (rows, CONTEXT), 1)
         allowed = j_idx <= prior + r_idx % pair_rows
         for h in range(kv_heads):
-            q_h = jnp.concatenate(
-                [q_all[:, (h * group + g) * HD:(h * group + g + 1) * HD] for g in range(group)],
-                axis=0,
+            firsts, seconds = [], []
+            for g in range(group):
+                c = h * group + g
+                u = qkv_ref[s, :, c * HD:c * HD + half].astype(jnp.float32)
+                w = qkv_ref[s, :, c * HD + half:(c + 1) * HD].astype(jnp.float32)
+                firsts.append((u * cosine - w * sine).astype(jnp.bfloat16))
+                seconds.append((w * cosine + u * sine).astype(jnp.bfloat16))
+            q_first = jnp.concatenate(firsts, axis=0)
+            q_second = jnp.concatenate(seconds, axis=0)
+            k_first = keys[:, h * HD:h * HD + half]
+            k_second = keys[:, h * HD + half:(h + 1) * HD]
+            v_h = values[:, h * HD:(h + 1) * HD]
+            dims = (((1,), (1,)), ((), ()))
+            scores = lax.dot_general(q_first, k_first, dims, preferred_element_type=jnp.float32)
+            scores = scores + lax.dot_general(
+                q_second, k_second, dims, preferred_element_type=jnp.float32
             )
-            k_h = keys[:, h * HD:(h + 1) * HD]
-            v_h = values[:, h * HD:(h + 1) * HD]
-            scores = lax.dot_general(
-                q_h, k_h, (((1,), (1,)), ((), ())), preferred_element_type=jnp.float32
-            ) * SCORE_MULT
-            scores = jnp.where(allowed, scores, -jnp.inf)
+            scores = jnp.where(allowed, scores * SCORE_MULT, -jnp.inf)
             top = jnp.max(scores, axis=-1, keepdims=True)
             weights = jnp.exp(scores - top)
             probs = (weights / jnp.sum(weights, axis=-1, keepdims=True)).astype(jnp.bfloat16)
@@ -107,19 +118,20 @@
     lax.fori_loop(0, sources, per_source, 0)
 
 
-def owner_attention(query_in, key_in, value_in, cache_keys, cache_values, lengths, priors, table):
-    sources, pair_rows, qcols = query_in.shape
-    kcols = key_in.shape[-1]
+def owner_attention(qkv_in, qcols, cache_keys, cache_values, lengths, priors, table):
+    sources, pair_rows, width = qkv_in.shape
+    kcols = (width - qcols) // 2
     kv_heads = kcols // HD
     slots = jnp.arange(pair_rows, dtype=jnp.int32)
     positions = priors[:, None] + slots[None, :]
-    query_rot = rotary(query_in.reshape(sources, pair_rows, qcols // HD, HD), positions).astype(
-        jnp.bfloat16
-    ).reshape(sources, pair_rows, qcols)
+    key_in = qkv_in[..., qcols:qcols + kcols]
     key_rot = rotary(key_in.reshape(sources, pair_rows, kv_heads, HD), positions).astype(
         jnp.bfloat16
     ).reshape(sources, pair_rows, kcols)
-    pool_pages = cache_keys.shape[0]
+    freq = jnp.power(ROPE_BASE, -2.0 * jnp.arange(HD // 2, dtype=jnp.int32).astype(jnp.float32) / HD)
+    angle = positions.astype(jnp.float32)[:, :, None] * freq
+    cosine = jnp.cos(angle)
+    sine = jnp.sin(angle)
     smem = pl.BlockSpec(memory_space=pltpu.SMEM)
     vmem = pl.BlockSpec(memory_space=pltpu.VMEM)
     return pl.pallas_call(
@@ -129,14 +141,14 @@
             jax.ShapeDtypeStruct(cache_keys.shape, cache_keys.dtype),
             jax.ShapeDtypeStruct(cache_values.shape, cache_values.dtype),
         ),
-        in_specs=[smem, smem, smem, vmem, vmem, vmem, vmem, vmem],
+        in_specs=[smem, smem, smem] + [vmem] * 6,
         out_specs=(vmem, vmem, vmem),
         scratch_shapes=[
             pltpu.VMEM((CONTEXT, kcols), jnp.bfloat16),
             pltpu.VMEM((CONTEXT, kcols), jnp.bfloat16),
         ],
         compiler_params=pltpu.CompilerParams(vmem_limit_bytes=48 * 1024 * 1024),
-    )(table, priors, lengths, query_rot, key_rot, value_in, cache_keys, cache_values)
+    )(table, priors, lengths, qkv_in, key_rot, cosine, sine, cache_keys, cache_values)
 
 
 def body(
@@ -186,11 +198,8 @@
         peers, pair_rows, -1
     )
     recv_qkv = lax.all_to_all(send_qkv, REQ, split_axis=0, concat_axis=0, tiled=True)
-    recv_query = recv_qkv[..., :qcols]
-    recv_key = recv_qkv[..., qcols : qcols + kcols]
-    recv_value = recv_qkv[..., qcols + kcols :]
     mixed, keys_out, values_out = owner_attention(
-        recv_query, recv_key, recv_value, cache_k, cache_v, new_len[0], prior_len[0], page_table[0]
+        recv_qkv, qcols, cache_k, cache_v, new_len[0], prior_len[0], page_table[0]
     )
     mixed = lax.optimization_barrier(mixed)
     returned = lax.all_to_all(mixed, REQ, split_axis=0, concat_axis=0, tiled=True)

time: 285 us -> 290 us (1.018)
  Pallas kernels: 28.6 us -> 44.4 us
  waiting for transfers between devices: 131 us -> 122 us
  local copies, waits for them, and re-layouts: 20.6 us -> 16.3 us
  starting transfers between devices: 27.7 us -> 30.7 us
    pallas_call x1, Pallas kernels: 28.6 us -> 44.4 us  [owner_attention(): pl.pallas_call(attention_kernel, out_shape=(jax.ShapeDtypeStruct((sources...]
    ppermute x3, waiting for transfers between devices: 7.75 us -> 1.32 us  [body(): lax.ppermute(w_out, 'grp', [(i, (i + shift) % groups) for i in range(grou...]
    convert_element_type x1 -> x0, local copies, waits for them, and re-layouts: 3.34 us -> none  [owner_attention(): rotary(query_in.reshape(sources, pair_rows, qcols // HD, HD), positions)]
  transfers between devices with their start and end apart: 13 -> 13, of which waited for: 9 -> 8; matrix products, arithmetic and copies ran while one was open for 16% -> 12% of each run, Pallas kernels for 10% -> 15%
where the time goes in v9:
time: 290 us; the launch traced here: 289 us
  waiting for transfers between devices  122 us (42%)
  matrix products  48.8 us (17%)
  Pallas kernels  44.4 us (15%)
  starting transfers between devices  30.7 us (11%)
  local copies, waits for them, and re-layouts  16.3 us (6%)
  between operations  14.1 us (5%)
  other arithmetic  12.2 us (4%)
    pallas_call x1, Pallas kernels, owner_attention(): pl.pallas_call(attention_kernel, out_shape=(jax.ShapeDtypeStruct((sources...  44.4 us
    reduce_scatter x1, waiting for transfers between devices, body(): lax.psum_scatter(partial.astype(jnp.bfloat16), 'rzc', scatter_dimension=0...  34.6 us
    all_to_all x1, waiting for transfers between devices, body(): lax.all_to_all(send_qkv, REQ, split_axis=0, concat_axis=0, tiled=True)  25.7 us
    dot_general x4, matrix products, body(): jnp.dot(lax.dynamic_slice_in_dim(hidden, block * units, units, axis=1), p...  23.9 us
    all_gather x1, waiting for transfers between devices, body(): piece = lax.all_gather(mlp_in, 'rzc', axis=0, tiled=True)  23.6 us
    all_to_all x1, waiting for transfers between devices, body(): lax.all_to_all(mixed, REQ, split_axis=0, concat_axis=0, tiled=True)  18.7 us
    all_to_all x1, waiting for transfers between devices, body(): lax.all_to_all(attn_rows.reshape(groups, quarter, -1), 'grp', split_axis=...  10.3 us
    dot_general x4, matrix products, body(): term = jnp.dot(quarters[block], part, preferred_element_type=jnp.float32)  8.66 us
  transfers between devices with their start and end apart: 13, of which 8 were waited for; matrix products, arithmetic and copies ran while one was open for 12% of the time, Pallas kernels for 15%

profile of v9, /device:TPU:0, one launch (start us, length us, event | category | flops | bytes accessed | tf_op | source)
XLA Modules:
  0.0 288.8 jit_solution(4776987629334090435)
XLA Ops:
  7.3 0.7 all-gather.4.cloned.1.call-update
  8.0 0.7 all-gather.6.cloned.1.call-update
  9.1 2.2 fusion
  11.4 0.9 convolution_convert_fusion.6
  12.4 0.9 convolution_convert_fusion.5
  13.4 1.4 convolution_convert_fusion.4
  14.9 0.3 copy.21
  15.2 5.2 %gather_fusion = bf16[1024,768]{1,0:T(8,128)(2,1)} fusion(bf16[512,768]{1,0:T(8,128)(2,1)S(1)} %copy.21, s32[1024]{0:T(1024)S(1)} %broadcast_clamp_fusion), kind=kCustom, calls=%fused_computation | custom fusion | bytes 3149824 | tf_op jit(solution)/shard_map/jit(_take)/gather | solution.py:197
  20.5 2.9 %broadcast_select_fusion = bf16[32,32,768]{2,1,0:T(8,128)(2,1)} fusion(bf16[32,32,768]{2,1,0:T(8,128)(2,1)} %bitcast.43, pred[32,32]{1,0:T(8,128)(4,1)S(1)} %compare_and_fusion), kind=kLoop, calls=%fused_computation.22 | loop fusion | flops 786432 | bytes 3146752 | tf_op jit(solution)/shard_map/jit(_take)/select_n | solution.py:197
  23.4 8.6 %all-to-all-start = ((bf16[32,32,768]{2,1,0:T(8,128)(2,1)}), bf16[32,32,768]{2,1,0:T(8,128)(2,1)S(1)}, u32[]{:S(2)}, u32[]{:S(2)}) async-start(bf16[32,32,768]{2,1,0:T(8,128)(2,1)} %broadcast_select_fusion), calls=%async_computation | async-start | bytes 3145728 | tf_op jit(solution)/shard_map/all_to_all | solution.py:200
  32.0 3.1 %collective-permute-start.1 = (bf16[512,2048]{1,0:T(8,128)(2,1)}, bf16[512,2048]{1,0:T(8,128)(2,1)}, u32[]{:S(2)}, u32[]{:S(2)}) collective-permute-start(bf16[512,2048]{1,0:T(8,128)(2,1)} %param.22), channel_id=1, source_target_pairs={{0,2},{1,3},{2,0},{3,1},{4,6},{5,7},{6,4},{7,5},{8,10},{9,11},{10,... | collective-permute-start | bytes 6291464 | tf_op jit(solution)/shard_map/ppermute | solution.py:186
  35.1 0.6 collective-permute-start
  35.7 2.6 collective-permute-start.2
  38.4 1.9 multiply_cosine_fusion
  40.3 25.7 %all-to-all-done.qkv_ref = bf16[32,32,768]{2,1,0:T(8,128)(2,1)S(1)} async-done(((bf16[32,32,768]{2,1,0:T(8,128)(2,1)}), bf16[32,32,768]{2,1,0:T(8,128)(2,1)S(1)}, u32[]{:S(2)}, u32[]{:S(2)}) %all-to-all-start) | async-done | bytes 1572896 | tf_op jit(solution)/shard_map/all_to_all | solution.py:200
  66.0 1.1 reshape.155
  67.1 2.2 fusion.45
  69.4 0.4 fusion.13
  69.8 0.3 pad_maximum_fusion.1
  70.1 1.3 copy.24
  71.4 1.3 convert_element_type.98.k_ref
  72.8 1.6 copy-done.2
  74.4 44.4 %shard_map.175 = (bf16[32,32,512]{2,1,0:T(8,128)(2,1)S(1)}, bf16[512,16,128]{2,1,0:T(8,128)(2,1)}, bf16[512,16,128]{2,1,0:T(8,128)(2,1)}) custom-call(s32[512]{0:T(512)S(1)} %bitcast.38, s32[32]{0:T(128)S(1)} %bitcast.40, s32[32]{0:T(128)S(1)} %bitcast.41, bf16[32,32,768]{2,1,0:T(8,128)(2,1)S(1)} %all-to-all-done.qkv_ref, ...), custom_call_target="tpu_custom_call" | custom-call | tf_op jit(solution)/shard_map/pallas_call | solution.py:137
  118.8 1.0 copy-done.3
  119.8 5.6 %all-to-all-start.1 = ((bf16[32,32,512]{2,1,0:T(8,128)(2,1)}), bf16[32,32,512]{2,1,0:T(8,128)(2,1)S(1)}, u32[]{:S(2)}, u32[]{:S(2)}) async-start(bf16[32,32,512]{2,1,0:T(8,128)(2,1)} %copy-done.3), calls=%async_computation.1 | async-start | bytes 2097152 | tf_op jit(solution)/shard_map/all_to_all | solution.py:205
  125.4 1.2 collective-permute-done
  126.7 18.7 %all-to-all-done.1 = bf16[32,32,512]{2,1,0:T(8,128)(2,1)S(1)} async-done(((bf16[32,32,512]{2,1,0:T(8,128)(2,1)}), bf16[32,32,512]{2,1,0:T(8,128)(2,1)S(1)}, u32[]{:S(2)}, u32[]{:S(2)}) %all-to-all-start.1) | async-done | bytes 1048608 | tf_op jit(solution)/shard_map/all_to_all | solution.py:205
  145.5 2.0 gather_fusion.1
  147.4 0.9 broadcast_select_fusion.1
  148.4 4.1 %all-to-all-start.2 = ((bf16[4,128,512]{2,1,0:T(8,128)(2,1)}), bf16[4,128,512]{2,1,0:T(8,128)(2,1)S(1)}, u32[]{:S(2)}, u32[]{:S(2)}) async-start(bf16[4,128,512]{2,1,0:T(8,128)(2,1)} %broadcast_select_fusion.1), calls=%async_computation.2 | async-start | bytes 1048576 | tf_op jit(solution)/shard_map/all_to_all | solution.py:208
  152.5 10.3 %all-to-all-done.2 = bf16[4,128,512]{2,1,0:T(8,128)(2,1)S(1)} async-done(((bf16[4,128,512]{2,1,0:T(8,128)(2,1)}), bf16[4,128,512]{2,1,0:T(8,128)(2,1)S(1)}, u32[]{:S(2)}, u32[]{:S(2)}) %all-to-all-start.2) | async-done | bytes 524320 | tf_op jit(solution)/shard_map/all_to_all | solution.py:208
  162.9 2.2 fusion.11
  165.1 2.0 fusion.10
  167.1 2.0 fusion.8
  169.2 2.4 multiply_reduce_fusion
  171.6 0.9 multiply_convert_fusion.1
  172.6 2.7 collective-permute-start.4
  175.3 3.2 %collective-permute-start.5 = (bf16[256,2048]{1,0:T(8,128)(2,1)}, bf16[256,2048]{1,0:T(8,128)(2,1)}, u32[]{:S(2)}, u32[]{:S(2)}) collective-permute-start(bf16[256,2048]{1,0:T(8,128)(2,1)} %param.25), channel_id=1, source_target_pairs={{0,96},{32,0},{64,32},{96,64},{1,97},{33,1},{65,33},{97,65},{2,98}... | collective-permute-start | bytes 3145736 | tf_op jit(solution)/shard_map/ppermute | solution.py:182
  178.5 23.6 %all-gather.8.cloned.1.call-done = bf16[1024,2048]{1,0:T(8,128)(2,1)} async-done(((bf16[128,2048]{1,0:T(8,128)(2,1)}), bf16[1024,2048]{1,0:T(8,128)(2,1)}) %all-gather.8.cloned.1.call-update) | async-done | bytes 4194320 | tf_op jit(solution)/shard_map/all_gather | solution.py:222
  202.2 7.6 %fusion.46 = f32[1024,1024]{1,0:T(8,128)S(1)} fusion(bf16[1024,2048]{1,0:T(8,128)(2,1)} %all-gather.8.cloned.1.call-done, bf16[2048,1024]{1,0:T(8,128)(2,1)} %all-gather.4.cloned.1.call-done), kind=kOutput, calls=%fused_computation.84 | convolution fusion | flops 4294967296 | bytes 12582912 | tf_op jit(solution)/shard_map/dot_general | solution.py:223
  209.9 5.2 %multiply_convert_fusion = bf16[1024,1024]{1,0:T(8,128)(2,1)S(1)} fusion(f32[1024,1024]{1,0:T(8,128)S(1)} %fusion.46, bf16[1024,2048]{1,0:T(8,128)(2,1)S(1)} %copy-done.12, bf16[2048,1024]{1,0:T(8,128)(2,1)S(1)} %copy-done.11), kind=kOutput, calls=%fused_computation.8 | convolution fusion | flops 4301258752 | bytes 14680064 | tf_op jit(solution)/shard_map/dot_general | solution.py:224
  215.1 6.6 %collective-permute-done.3 = bf16[256,2048]{1,0:T(8,128)(2,1)} collective-permute-done((bf16[256,2048]{1,0:T(8,128)(2,1)}, bf16[256,2048]{1,0:T(8,128)(2,1)}, u32[]{:S(2)}, u32[]{:S(2)}) %collective-permute-start.3) | collective-permute-done | bytes 1048608 | tf_op jit(solution)/shard_map/ppermute | solution.py:182
  221.7 2.5 fusion.24
  224.2 5.8 %fusion.22 = f32[1024,2048]{1,0:T(8,128)} fusion(bf16[256,2048]{1,0:T(8,128)(2,1)} %collective-permute-done.3, bf16[1024,1024]{1,0:T(8,128)(2,1)S(1)} %multiply_convert_fusion, s32[]{:T(128)S(6)} %select_n.141), kind=kOutput, calls=%fused_computation.45 | convolution fusion | flops 1073741824 | bytes 9961476 | tf_op jit(solution)/shard_map/dot_general | solution.py:231
  229.9 5.7 %fusion.20 = f32[1024,2048]{1,0:T(8,128)} fusion(bf16[256,2048]{1,0:T(8,128)(2,1)} %collective-permute-done.4, bf16[1024,1024]{1,0:T(8,128)(2,1)S(1)} %multiply_convert_fusion, s32[]{:T(128)S(6)} %select_n.143), kind=kOutput, calls=%fused_computation.43 | convolution fusion | flops 1073741824 | bytes 9961476 | tf_op jit(solution)/shard_map/dot_general | solution.py:231
  235.7 10.0 %add_convert_fusion = bf16[1024,2048]{1,0:T(8,128)(2,1)} fusion(f32[1024,2048]{1,0:T(8,128)} %fusion.20, f32[1024,2048]{1,0:T(8,128)S(1)} %fusion.24, f32[1024,2048]{1,0:T(8,128)} %fusion.22, bf16[256,2048]{1,0:T(8,128)(2,1)} %collective-permute-done.5, bf16[1024,1024]{1,0:T(8,128)(2,1)S(1)} %multiply_convert_fusion, s32[]{:T(128)S(6)} %select_n.145), kind=kOutput, calls=%fused_computation.2 | convolution fusion | flops 1082130432 | bytes 30932996 | tf_op jit(solution)/shard_map/dot_general | solution.py:231
  245.7 34.6 %reduce-scatter.2.cloned.1.call-done = bf16[128,2048]{1,0:T(8,128)(2,1)} async-done(((bf16[1024,2048]{1,0:T(8,128)(2,1)}), bf16[128,2048]{1,0:T(8,128)(2,1)}) %reduce-scatter.2.cloned.1.call-update) | async-done | bytes 524304 | tf_op jit(solution)/shard_map/reduce_scatter | solution.py:237
  280.3 2.0 add_convert_fusion.1
  (58 shorter events, 1.1 us)
Async XLA Ops:
  7.2 6.2 %copy-start = (bf16[2048,512]{1,0:T(8,128)(2,1)S(1)}, bf16[2048,512]{1,0:T(8,128)(2,1)}, u32[]{:S(2)}) copy-start(bf16[2048,512]{1,0:T(8,128)(2,1)} %param.19) | copy-start | bytes 6291460
  7.2 1.5 copy-start.9
  7.2 4.2 %copy-start.15 = (f32[2048]{0:T(1024)S(1)}, f32[2048]{0:T(1024)}, u32[]{:S(2)}) copy-start(f32[2048]{0:T(1024)} %param.17) | copy-start | bytes 24580
  7.2 4.2 %copy-start.13 = (bf16[2048,128]{1,0:T(8,128)(2,1)S(1)}, bf16[2048,128]{1,0:T(8,128)(2,1)}, u32[]{:S(2)}) copy-start(bf16[2048,128]{1,0:T(8,128)(2,1)} %param.20) | copy-start | bytes 1572868
  7.2 138.3 %all-gather.4.cloned.1.call-start = ((), (), s32[]{:S(2)}) async-start(), calls=%async_computation.4 | async-start | bytes 5242880 | tf_op jit(solution)/shard_map/all_gather | solution.py:178
  7.9 137.5 %all-gather.6.cloned.1.call-start = ((), (), s32[]{:S(2)}) async-start(), calls=%async_computation.5 | async-start | bytes 5242880 | tf_op jit(solution)/shard_map/all_gather | solution.py:179
  9.1 2.3 copy-start.7
  11.4 1.0 copy-start.14
  23.4 14.9 %copy-start.5 = (s32[1,32]{1,0:T(1,128)S(1)}, s32[1,32]{1,0:T(1,128)}, u32[]{:S(2)}) copy-start(s32[1,32]{1,0:T(1,128)} %param.30) | copy-start | bytes 388
  23.4 42.6 %all-to-all-start = ((bf16[32,32,768]{2,1,0:T(8,128)(2,1)}), bf16[32,32,768]{2,1,0:T(8,128)(2,1)S(1)}, u32[]{:S(2)}, u32[]{:S(2)}) async-start(bf16[32,32,768]{2,1,0:T(8,128)(2,1)} %broadcast_select_fusion), calls=%async_computation | async-start | bytes 3145728 | tf_op jit(solution)/shard_map/all_to_all | solution.py:200
  32.0 93.4 %collective-permute-start.1 = (bf16[512,2048]{1,0:T(8,128)(2,1)}, bf16[512,2048]{1,0:T(8,128)(2,1)}, u32[]{:S(2)}, u32[]{:S(2)}) collective-permute-start(bf16[512,2048]{1,0:T(8,128)(2,1)} %param.22), channel_id=1, source_target_pairs={{0,2},{1,3},{2,0},{3,1},{4,6},{5,7},{6,4},{7,5},{8,10},{9,11},{10,... | collective-permute-start | bytes 6291464 | tf_op jit(solution)/shard_map/ppermute | solution.py:186
  35.1 91.6 %collective-permute-start = (bf16[512,2048]{1,0:T(8,128)(2,1)}, bf16[512,2048]{1,0:T(8,128)(2,1)}, u32[]{:S(2)}, u32[]{:S(2)}) collective-permute-start(bf16[512,2048]{1,0:T(8,128)(2,1)} %param.22), channel_id=1, source_target_pairs={{0,1},{1,2},{2,3},{3,0},{4,5},{5,6},{6,7},{7,4},{8,9},{9,10},{10,1... | collective-permute-start | bytes 6291464 | tf_op jit(solution)/shard_map/ppermute | solution.py:186
  35.7 91.1 %collective-permute-start.2 = (bf16[512,2048]{1,0:T(8,128)(2,1)}, bf16[512,2048]{1,0:T(8,128)(2,1)}, u32[]{:S(2)}, u32[]{:S(2)}) collective-permute-start(bf16[512,2048]{1,0:T(8,128)(2,1)} %param.22), channel_id=1, source_target_pairs={{0,3},{1,0},{2,1},{3,2},{4,7},{5,4},{6,5},{7,6},{8,11},{9,8},{10,9... | collective-permute-start | bytes 6291464 | tf_op jit(solution)/shard_map/ppermute | solution.py:186
  69.8 3.0 %copy-start.4 = (s32[1,512]{1,0:T(1,128)S(1)}, s32[1,512]{1,0:T(1,128)}, u32[]{:S(2)}) copy-start(s32[1,512]{1,0:T(1,128)} %param.31) | copy-start | bytes 6148
  69.8 3.0 %copy-start.6 = (s32[1,32]{1,0:T(1,128)S(1)}, s32[1,32]{1,0:T(1,128)}, u32[]{:S(2)}) copy-start(s32[1,32]{1,0:T(1,128)} %param.29) | copy-start | bytes 388
  72.8 1.6 copy-start.2
  118.8 1.0 copy-start.3
  119.8 25.7 %all-to-all-start.1 = ((bf16[32,32,512]{2,1,0:T(8,128)(2,1)}), bf16[32,32,512]{2,1,0:T(8,128)(2,1)S(1)}, u32[]{:S(2)}, u32[]{:S(2)}) async-start(bf16[32,32,512]{2,1,0:T(8,128)(2,1)} %copy-done.3), calls=%async_computation.1 | async-start | bytes 2097152 | tf_op jit(solution)/shard_map/all_to_all | solution.py:205
  148.4 14.5 %all-to-all-start.2 = ((bf16[4,128,512]{2,1,0:T(8,128)(2,1)}), bf16[4,128,512]{2,1,0:T(8,128)(2,1)S(1)}, u32[]{:S(2)}, u32[]{:S(2)}) async-start(bf16[4,128,512]{2,1,0:T(8,128)(2,1)} %broadcast_select_fusion.1), calls=%async_computation.2 | async-start | bytes 1048576 | tf_op jit(solution)/shard_map/all_to_all | solution.py:208
  152.5 49.7 %all-gather.8.cloned.1.call-start = ((), (), s32[]{:S(2)}) async-start(), calls=%async_computation.6 | async-start | bytes 4718592 | tf_op jit(solution)/shard_map/all_gather | solution.py:222
  162.9 4.3 %copy-start.8 = (bf16[4,128,512]{2,1,0:T(8,128)(2,1)}, bf16[4,128,512]{2,1,0:T(8,128)(2,1)S(1)}, u32[]{:S(2)}) copy-start(bf16[4,128,512]{2,1,0:T(8,128)(2,1)S(1)} %all-to-all-done.2) | copy-start | bytes 1572868
  169.2 2.4 copy-start.10
  172.6 107.8 %reduce-scatter.2.cloned.1.call-start = ((), (), s32[]{:S(2)}) async-start(), calls=%async_computation.7 | async-start | bytes 4718592 | tf_op jit(solution)/shard_map/reduce_scatter | solution.py:237
  172.6 42.5 %collective-permute-start.4 = (bf16[256,2048]{1,0:T(8,128)(2,1)}, bf16[256,2048]{1,0:T(8,128)(2,1)}, u32[]{:S(2)}, u32[]{:S(2)}) collective-permute-start(bf16[256,2048]{1,0:T(8,128)(2,1)} %param.25), channel_id=1, source_target_pairs={{0,64},{32,96},{64,0},{96,32},{1,65},{33,97},{65,1},{97,33},{2,66}... | collective-permute-start | bytes 3145736 | tf_op jit(solution)/shard_map/ppermute | solution.py:182
  175.3 46.4 %collective-permute-start.3 = (bf16[256,2048]{1,0:T(8,128)(2,1)}, bf16[256,2048]{1,0:T(8,128)(2,1)}, u32[]{:S(2)}, u32[]{:S(2)}) collective-permute-start(bf16[256,2048]{1,0:T(8,128)(2,1)} %param.25), channel_id=1, source_target_pairs={{0,32},{32,64},{64,96},{96,0},{1,33},{33,65},{65,97},{97,1},{2,34}... | collective-permute-start | bytes 3145736 | tf_op jit(solution)/shard_map/ppermute | solution.py:182
  175.3 46.4 %collective-permute-start.5 = (bf16[256,2048]{1,0:T(8,128)(2,1)}, bf16[256,2048]{1,0:T(8,128)(2,1)}, u32[]{:S(2)}, u32[]{:S(2)}) collective-permute-start(bf16[256,2048]{1,0:T(8,128)(2,1)} %param.25), channel_id=1, source_target_pairs={{0,96},{32,0},{64,32},{96,64},{1,97},{33,1},{65,33},{97,65},{2,98}... | collective-permute-start | bytes 3145736 | tf_op jit(solution)/shard_map/ppermute | solution.py:182
  202.2 7.7 %copy-start.11 = (bf16[2048,1024]{1,0:T(8,128)(2,1)S(1)}, bf16[2048,1024]{1,0:T(8,128)(2,1)}, u32[]{:S(2)}) copy-start(bf16[2048,1024]{1,0:T(8,128)(2,1)} %all-gather.6.cloned.1.call-done) | copy-start | bytes 12582916
  202.2 7.7 %copy-start.12 = (bf16[1024,2048]{1,0:T(8,128)(2,1)S(1)}, bf16[1024,2048]{1,0:T(8,128)(2,1)}, u32[]{:S(2)}) copy-start(bf16[1024,2048]{1,0:T(8,128)(2,1)} %all-gather.8.cloned.1.call-done) | copy-start | bytes 12582916
  245.7 36.6 %copy-start.1 = (bf16[2048,512]{1,0:T(8,128)(2,1)S(1)}, bf16[2048,512]{1,0:T(8,128)(2,1)}, u32[]{:S(2)}) copy-start(bf16[2048,512]{1,0:T(8,128)(2,1)} %param.19) | copy-start | bytes 6291460
Sparse Core Ops, SparseCore 0:
  9.7 67.7 all-gather.3
  79.1 61.3 all-gather.5
  172.7 29.4 all-gather.7
  245.8 34.4 reduce-scatter.1

commit v10 on v8

--- a/solution.py
+++ b/solution.py
@@ -216,15 +216,18 @@
     hidden = (jax.nn.silu(gate) * upper).astype(jnp.bfloat16)
     down_parts, hidden = lax.optimization_barrier((down_parts, hidden))
     units = w_down.shape[0]
-    partial = None
-    for shift, part in enumerate(down_parts):
-        block = (lax.axis_index("ry") - shift) % ring
-        term = jnp.dot(
-            lax.dynamic_slice_in_dim(hidden, block * units, units, axis=1),
-            part,
-            preferred_element_type=jnp.float32,
-        )
-        partial = term if partial is None else partial + term
+    hidden = jnp.concatenate(
+        [
+            lax.dynamic_slice_in_dim(
+                hidden, ((lax.axis_index("ry") - shift) % ring) * units, units, axis=1
+            )
+            for shift in range(ring)
+        ],
+        axis=1,
+    )
+    partial = jnp.dot(
+        hidden, jnp.concatenate(down_parts, axis=0), preferred_element_type=jnp.float32
+    )
     down = lax.psum_scatter(
         partial.astype(jnp.bfloat16),
         "rzc",

time: 285 us -> 274 us (0.961)
  matrix products: 47.9 us -> 34.8 us
    dot_general x4 -> x1, matrix products: 21.5 us -> 8.48 us  [body(): jnp.dot(hidden, jnp.concatenate(down_parts, axis=0), preferred_element_ty...]
where the time goes in v10:
time: 274 us; the launch traced here: 273 us
  waiting for transfers between devices  133 us (49%)
  matrix products  34.8 us (13%)
  Pallas kernels  28.6 us (10%)
  starting transfers between devices  27.2 us (10%)
  local copies, waits for them, and re-layouts  20.4 us (7%)
  other arithmetic  15 us (5%)
  between operations  14.2 us (5%)
    reduce_scatter x1, waiting for transfers between devices, body(): lax.psum_scatter(partial.astype(jnp.bfloat16), 'rzc', scatter_dimension=0...  37.1 us
    pallas_call x1, Pallas kernels, owner_attention(): pl.pallas_call(attention_kernel, out_shape=(jax.ShapeDtypeStruct((sources...  28.6 us
    all_to_all x1, waiting for transfers between devices, body(): lax.all_to_all(send_qkv, REQ, split_axis=0, concat_axis=0, tiled=True)  26.8 us
    all_gather x1, waiting for transfers between devices, body(): piece = lax.all_gather(mlp_in, 'rzc', axis=0, tiled=True)  26.4 us
    all_to_all x1, waiting for transfers between devices, body(): lax.all_to_all(mixed, REQ, split_axis=0, concat_axis=0, tiled=True)  17.4 us
    all_to_all x1, waiting for transfers between devices, body(): lax.all_to_all(attn_rows.reshape(groups, quarter, -1), 'grp', split_axis=...  9.58 us
    dot_general x4, matrix products, body(): term = jnp.dot(quarters[block], part, preferred_element_type=jnp.float32)  8.54 us
    dot_general x1, matrix products, body(): jnp.dot(hidden, jnp.concatenate(down_parts, axis=0), preferred_element_ty...  8.48 us
  transfers between devices with their start and end apart: 13, of which 9 were waited for; matrix products, arithmetic and copies ran while one was open for 16% of the time, Pallas kernels for 10%

profile of v10, /device:TPU:0, one launch (start us, length us, event | category | flops | bytes accessed | tf_op | source)
XLA Modules:
  0.0 273.2 jit_solution(10863402793439197658)
XLA Ops:
  7.3 0.7 all-gather.4.cloned.1.call-update
  8.0 0.7 all-gather.6.cloned.1.call-update
  8.7 2.2 fusion
  11.0 2.5 convolution_convert_fusion.5
  13.5 0.9 convolution_convert_fusion.6
  14.5 1.4 convolution_convert_fusion.4
  16.7 4.0 %gather_fusion = bf16[1024,768]{1,0:T(8,128)(2,1)S(1)} fusion(bf16[512,768]{1,0:T(8,128)(2,1)S(1)} %copy.21, s32[1024]{0:T(1024)S(1)} %broadcast_clamp_fusion), kind=kCustom, calls=%fused_computation | custom fusion | bytes 3149824 | tf_op jit(solution)/shard_map/jit(_take)/gather | solution.py:185
  20.8 1.4 broadcast_select_fusion
  22.2 8.4 %all-to-all-start = ((bf16[32,32,768]{2,1,0:T(8,128)(2,1)}), bf16[32,32,768]{2,1,0:T(8,128)(2,1)S(1)}, u32[]{:S(2)}, u32[]{:S(2)}) async-start(bf16[32,32,768]{2,1,0:T(8,128)(2,1)} %broadcast_select_fusion), calls=%async_computation | async-start | bytes 3145728 | tf_op jit(solution)/shard_map/all_to_all | solution.py:188
  30.6 1.6 collective-permute-start
  32.1 2.7 collective-permute-start.1
  34.9 1.4 collective-permute-start.2
  36.4 1.9 multiply_cosine_fusion
  38.3 26.8 %all-to-all-done = bf16[32,32,768]{2,1,0:T(8,128)(2,1)S(1)} async-done(((bf16[32,32,768]{2,1,0:T(8,128)(2,1)}), bf16[32,32,768]{2,1,0:T(8,128)(2,1)S(1)}, u32[]{:S(2)}, u32[]{:S(2)}) %all-to-all-start) | async-done | bytes 1572896 | tf_op jit(solution)/shard_map/all_to_all | solution.py:188
  65.1 0.8 fusion.54
  66.2 1.0 fusion.55
  68.0 1.3 copy.24
  69.3 1.3 convert_element_type.112.k_ref
  70.6 1.1 slice.32
  71.7 2.8 %reshape.161 = bf16[32,32,8,64]{3,2,1,0:T(8,128)(2,1)S(1)} reshape(bf16[32,32,512]{2,1,0:T(8,128)(2,1)} %slice.32) | data formatting | bytes 2097152 | tf_op jit(solution)/shard_map/reshape | solution.py:116
  74.5 1.9 fusion.4
  76.4 2.5 pad_maximum_fusion
  78.9 3.2 %convert_element_type.109.q_ref = bf16[32,32,512]{2,1,0:T(8,128)(2,1)S(1)} reshape(bf16[32,32,8,64]{3,2,1,0:T(8,128)(2,1)} %pad_maximum_fusion) | data formatting | bytes 2097152 | tf_op jit(solution)/shard_map/convert_element_type | solution.py:116
  82.1 0.9 copy-done.4
  83.1 28.6 %shard_map.175 = (bf16[32,32,512]{2,1,0:T(8,128)(2,1)S(1)}, bf16[512,16,128]{2,1,0:T(8,128)(2,1)}, bf16[512,16,128]{2,1,0:T(8,128)(2,1)}) custom-call(s32[512]{0:T(512)S(1)} %bitcast.36, s32[32]{0:T(128)S(1)} %bitcast.38, s32[32]{0:T(128)S(1)} %bitcast.39, bf16[32,32,512]{2,1,0:T(8,128)(2,1)S(1)} %convert_element_type.109.q_ref, ...), custom_call_target="tpu_custom_call" | custom-call | tf_op jit(solution)/shard_map/pallas_call | solution.py:125
  111.7 1.0 copy-done.3
  112.7 4.8 %all-to-all-start.1 = ((bf16[32,32,512]{2,1,0:T(8,128)(2,1)}), bf16[32,32,512]{2,1,0:T(8,128)(2,1)S(1)}, u32[]{:S(2)}, u32[]{:S(2)}) async-start(bf16[32,32,512]{2,1,0:T(8,128)(2,1)} %copy-done.3), calls=%async_computation.1 | async-start | bytes 2097152 | tf_op jit(solution)/shard_map/all_to_all | solution.py:196
  117.5 8.4 %collective-permute-done.1 = bf16[512,2048]{1,0:T(8,128)(2,1)} collective-permute-done((bf16[512,2048]{1,0:T(8,128)(2,1)}, bf16[512,2048]{1,0:T(8,128)(2,1)}, u32[]{:S(2)}, u32[]{:S(2)}) %collective-permute-start.1) | collective-permute-done | bytes 2097184 | tf_op jit(solution)/shard_map/ppermute | solution.py:174
  125.9 17.4 %all-to-all-done.1 = bf16[32,32,512]{2,1,0:T(8,128)(2,1)S(1)} async-done(((bf16[32,32,512]{2,1,0:T(8,128)(2,1)}), bf16[32,32,512]{2,1,0:T(8,128)(2,1)S(1)}, u32[]{:S(2)}, u32[]{:S(2)}) %all-to-all-start.1) | async-done | bytes 1048608 | tf_op jit(solution)/shard_map/all_to_all | solution.py:196
  143.3 0.7 all-gather.6.cloned.1.call-done
  144.0 2.0 gather_fusion.1
  145.9 0.9 broadcast_select_fusion.1
  146.9 4.3 %all-to-all-start.2 = ((bf16[4,128,512]{2,1,0:T(8,128)(2,1)}), bf16[4,128,512]{2,1,0:T(8,128)(2,1)S(1)}, u32[]{:S(2)}, u32[]{:S(2)}) async-start(bf16[4,128,512]{2,1,0:T(8,128)(2,1)} %broadcast_select_fusion.1), calls=%async_computation.2 | async-start | bytes 1048576 | tf_op jit(solution)/shard_map/all_to_all | solution.py:199
  151.2 9.6 %all-to-all-done.2 = bf16[4,128,512]{2,1,0:T(8,128)(2,1)S(1)} async-done(((bf16[4,128,512]{2,1,0:T(8,128)(2,1)}), bf16[4,128,512]{2,1,0:T(8,128)(2,1)S(1)}, u32[]{:S(2)}, u32[]{:S(2)}) %all-to-all-start.2) | async-done | bytes 524320 | tf_op jit(solution)/shard_map/all_to_all | solution.py:199
  160.8 2.0 fusion.26
  162.8 2.0 fusion.25
  164.9 2.0 fusion.23
  167.0 2.4 multiply_reduce_fusion
  169.4 0.9 multiply_convert_fusion.1
  170.8 2.8 %collective-permute-start.4 = (bf16[256,2048]{1,0:T(8,128)(2,1)S(1)}, bf16[256,2048]{1,0:T(8,128)(2,1)}, u32[]{:S(2)}, u32[]{:S(2)}) collective-permute-start(bf16[256,2048]{1,0:T(8,128)(2,1)S(1)} %copy-done.13), channel_id=1, source_target_pairs={{0,64},{32,96},{64,0},{96,32},{1,65},{33,97},{65,1},{97,33},{2,66}... | collective-permute-start | bytes 3145736 | tf_op jit(solution)/shard_map/ppermute | solution.py:170
  173.6 0.7 collective-permute-start.5
  174.3 26.4 %all-gather.8.cloned.1.call-done = bf16[1024,2048]{1,0:T(8,128)(2,1)} async-done(((bf16[128,2048]{1,0:T(8,128)(2,1)}), bf16[1024,2048]{1,0:T(8,128)(2,1)}) %all-gather.8.cloned.1.call-update) | async-done | bytes 4194320 | tf_op jit(solution)/shard_map/all_gather | solution.py:213
  200.7 7.6 %fusion.56 = f32[1024,1024]{1,0:T(8,128)S(1)} fusion(bf16[1024,2048]{1,0:T(8,128)(2,1)} %all-gather.8.cloned.1.call-done, bf16[2048,1024]{1,0:T(8,128)(2,1)} %all-gather.4.cloned.1.call-done), kind=kOutput, calls=%fused_computation.102 | convolution fusion | flops 4294967296 | bytes 12582912 | tf_op jit(solution)/shard_map/dot_general | solution.py:214
  208.3 5.2 %multiply_convert_fusion = bf16[1024,1024]{1,0:T(8,128)(2,1)S(1)} fusion(f32[1024,1024]{1,0:T(8,128)S(1)} %fusion.56, bf16[1024,2048]{1,0:T(8,128)(2,1)S(1)} %copy-done.12, bf16[2048,1024]{1,0:T(8,128)(2,1)S(1)} %copy-done.11), kind=kOutput, calls=%fused_computation.23 | convolution fusion | flops 4301258752 | bytes 14680064 | tf_op jit(solution)/shard_map/dot_general | solution.py:215
  213.5 4.7 %collective-permute-done.4 = bf16[256,2048]{1,0:T(8,128)(2,1)} collective-permute-done((bf16[256,2048]{1,0:T(8,128)(2,1)S(1)}, bf16[256,2048]{1,0:T(8,128)(2,1)}, u32[]{:S(2)}, u32[]{:S(2)}) %collective-permute-start.4) | collective-permute-done | bytes 1048608 | tf_op jit(solution)/shard_map/ppermute | solution.py:170
  219.0 8.5 %fusion.15 = bf16[1024,2048]{1,0:T(8,128)(2,1)} fusion(bf16[256,2048]{1,0:T(8,128)(2,1)} %collective-permute-done.5, bf16[256,2048]{1,0:T(8,128)(2,1)} %collective-permute-done.4, bf16[256,2048]{1,0:T(8,128)(2,1)} %collective-permute-done.3, bf16[256,2048]{1,0:T(8,128)(2,1)S(1)} %copy-done.14, bf16[1024,256]{1,0:T(8,128)(2,1)S(1)} %get-tuple-element.40, ...), kind=kOutput, calls=%fused_computation.24 | convolution fusion | flops 4322230272 | bytes 10485760 | tf_op jit(solution)/shard_map/dot_general | solution.py:228
  227.5 37.1 %reduce-scatter.2.cloned.1.call-done = bf16[128,2048]{1,0:T(8,128)(2,1)} async-done(((bf16[1024,2048]{1,0:T(8,128)(2,1)}), bf16[128,2048]{1,0:T(8,128)(2,1)}) %reduce-scatter.2.cloned.1.call-update) | async-done | bytes 524304 | tf_op jit(solution)/shard_map/reduce_scatter | solution.py:231
  264.7 2.0 add_convert_fusion
  (65 shorter events, 3.3 us)
Async XLA Ops:
  7.2 7.3 %copy-start = (bf16[2048,512]{1,0:T(8,128)(2,1)S(1)}, bf16[2048,512]{1,0:T(8,128)(2,1)}, u32[]{:S(2)}) copy-start(bf16[2048,512]{1,0:T(8,128)(2,1)} %param.19) | copy-start | bytes 6291460
  7.2 3.8 %copy-start.17 = (f32[2048]{0:T(1024)S(1)}, f32[2048]{0:T(1024)}, u32[]{:S(2)}) copy-start(f32[2048]{0:T(1024)} %param.17) | copy-start | bytes 24580
  7.2 3.8 %copy-start.15 = (bf16[2048,128]{1,0:T(8,128)(2,1)S(1)}, bf16[2048,128]{1,0:T(8,128)(2,1)}, u32[]{:S(2)}) copy-start(bf16[2048,128]{1,0:T(8,128)(2,1)} %param.21) | copy-start | bytes 1572868
  7.2 6.3 %copy-start.16 = (bf16[2048,128]{1,0:T(8,128)(2,1)S(1)}, bf16[2048,128]{1,0:T(8,128)(2,1)}, u32[]{:S(2)}) copy-start(bf16[2048,128]{1,0:T(8,128)(2,1)} %param.20) | copy-start | bytes 1572868
  7.2 136.1 %all-gather.4.cloned.1.call-start = ((), (), s32[]{:S(2)}) async-start(), calls=%async_computation.4 | async-start | bytes 5242880 | tf_op jit(solution)/shard_map/all_gather | solution.py:166
  7.9 136.0 %all-gather.6.cloned.1.call-start = ((), (), s32[]{:S(2)}) async-start(), calls=%async_computation.5 | async-start | bytes 5242880 | tf_op jit(solution)/shard_map/all_gather | solution.py:167
  8.7 4.8 %copy-start.8 = (bf16[512,2048]{1,0:T(8,128)(2,1)S(1)}, bf16[512,2048]{1,0:T(8,128)(2,1)}, u32[]{:S(2)}) copy-start(bf16[512,2048]{1,0:T(8,128)(2,1)} %param.16) | copy-start | bytes 6291460
  14.5 1.8 copy-start.9
  20.7 15.6 %copy-start.6 = (s32[1,32]{1,0:T(1,128)S(1)}, s32[1,32]{1,0:T(1,128)}, u32[]{:S(2)}) copy-start(s32[1,32]{1,0:T(1,128)} %param.30) | copy-start | bytes 388
  22.2 43.0 %all-to-all-start = ((bf16[32,32,768]{2,1,0:T(8,128)(2,1)}), bf16[32,32,768]{2,1,0:T(8,128)(2,1)S(1)}, u32[]{:S(2)}, u32[]{:S(2)}) async-start(bf16[32,32,768]{2,1,0:T(8,128)(2,1)} %broadcast_select_fusion), calls=%async_computation | async-start | bytes 3145728 | tf_op jit(solution)/shard_map/all_to_all | solution.py:188
  30.6 86.9 %collective-permute-start = (bf16[512,2048]{1,0:T(8,128)(2,1)}, bf16[512,2048]{1,0:T(8,128)(2,1)}, u32[]{:S(2)}, u32[]{:S(2)}) collective-permute-start(bf16[512,2048]{1,0:T(8,128)(2,1)} %param.22), channel_id=1, source_target_pairs={{0,1},{1,2},{2,3},{3,0},{4,5},{5,6},{6,7},{7,4},{8,9},{9,10},{10,1... | collective-permute-start | bytes 6291464 | tf_op jit(solution)/shard_map/ppermute | solution.py:174
  32.1 93.8 %collective-permute-start.1 = (bf16[512,2048]{1,0:T(8,128)(2,1)}, bf16[512,2048]{1,0:T(8,128)(2,1)}, u32[]{:S(2)}, u32[]{:S(2)}) collective-permute-start(bf16[512,2048]{1,0:T(8,128)(2,1)} %param.22), channel_id=1, source_target_pairs={{0,2},{1,3},{2,0},{3,1},{4,6},{5,7},{6,4},{7,5},{8,10},{9,11},{10,... | collective-permute-start | bytes 6291464 | tf_op jit(solution)/shard_map/ppermute | solution.py:174
  34.9 91.0 %collective-permute-start.2 = (bf16[512,2048]{1,0:T(8,128)(2,1)}, bf16[512,2048]{1,0:T(8,128)(2,1)}, u32[]{:S(2)}, u32[]{:S(2)}) collective-permute-start(bf16[512,2048]{1,0:T(8,128)(2,1)} %param.22), channel_id=1, source_target_pairs={{0,3},{1,0},{2,1},{3,2},{4,7},{5,4},{6,5},{7,6},{8,11},{9,8},{10,9... | collective-permute-start | bytes 6291464 | tf_op jit(solution)/shard_map/ppermute | solution.py:174
  76.4 5.7 %copy-start.2 = (bf16[512,16,128]{2,1,0:T(8,128)(2,1)S(1)}, bf16[512,16,128]{2,1,0:T(8,128)(2,1)}, u32[]{:S(2)}) copy-start(bf16[512,16,128]{2,1,0:T(8,128)(2,1)} %ck_ref.1) | copy-start | bytes 6291460
  76.4 5.7 %copy-start.5 = (s32[1,512]{1,0:T(1,128)S(1)}, s32[1,512]{1,0:T(1,128)}, u32[]{:S(2)}) copy-start(s32[1,512]{1,0:T(1,128)} %param.31) | copy-start | bytes 6148
  76.4 5.7 %copy-start.7 = (s32[1,32]{1,0:T(1,128)S(1)}, s32[1,32]{1,0:T(1,128)}, u32[]{:S(2)}) copy-start(s32[1,32]{1,0:T(1,128)} %param.29) | copy-start | bytes 388
  82.1 1.0 copy-start.4
  111.7 1.0 copy-start.3
  112.7 30.6 %all-to-all-start.1 = ((bf16[32,32,512]{2,1,0:T(8,128)(2,1)}), bf16[32,32,512]{2,1,0:T(8,128)(2,1)S(1)}, u32[]{:S(2)}, u32[]{:S(2)}) async-start(bf16[32,32,512]{2,1,0:T(8,128)(2,1)} %copy-done.3), calls=%async_computation.1 | async-start | bytes 2097152 | tf_op jit(solution)/shard_map/all_to_all | solution.py:196
  146.9 13.9 %all-to-all-start.2 = ((bf16[4,128,512]{2,1,0:T(8,128)(2,1)}), bf16[4,128,512]{2,1,0:T(8,128)(2,1)S(1)}, u32[]{:S(2)}, u32[]{:S(2)}) async-start(bf16[4,128,512]{2,1,0:T(8,128)(2,1)} %broadcast_select_fusion.1), calls=%async_computation.2 | async-start | bytes 1048576 | tf_op jit(solution)/shard_map/all_to_all | solution.py:199
  151.2 49.4 %all-gather.8.cloned.1.call-start = ((), (), s32[]{:S(2)}) async-start(), calls=%async_computation.6 | async-start | bytes 4718592 | tf_op jit(solution)/shard_map/all_gather | solution.py:213
  164.9 4.5 %copy-start.10 = (f32[2048]{0:T(1024)S(1)}, f32[2048]{0:T(1024)}, u32[]{:S(2)}) copy-start(f32[2048]{0:T(1024)} %param.18) | copy-start | bytes 24580
  167.0 3.5 %copy-start.13 = (bf16[256,2048]{1,0:T(8,128)(2,1)S(1)}, bf16[256,2048]{1,0:T(8,128)(2,1)}, u32[]{:S(2)}) copy-start(bf16[256,2048]{1,0:T(8,128)(2,1)} %param.25) | copy-start | bytes 3145732
  170.4 94.3 %reduce-scatter.2.cloned.1.call-start = ((), (), s32[]{:S(2)}) async-start(), calls=%async_computation.7 | async-start | bytes 4718592 | tf_op jit(solution)/shard_map/reduce_scatter | solution.py:231
  170.4 43.1 %collective-permute-start.3 = (bf16[256,2048]{1,0:T(8,128)(2,1)S(1)}, bf16[256,2048]{1,0:T(8,128)(2,1)}, u32[]{:S(2)}, u32[]{:S(2)}) collective-permute-start(bf16[256,2048]{1,0:T(8,128)(2,1)S(1)} %copy-done.13), channel_id=1, source_target_pairs={{0,32},{32,64},{64,96},{96,0},{1,33},{33,65},{65,97},{97,1},{2,34}... | collective-permute-start | bytes 3145736 | tf_op jit(solution)/shard_map/ppermute | solution.py:170
  170.8 47.5 %collective-permute-start.4 = (bf16[256,2048]{1,0:T(8,128)(2,1)S(1)}, bf16[256,2048]{1,0:T(8,128)(2,1)}, u32[]{:S(2)}, u32[]{:S(2)}) collective-permute-start(bf16[256,2048]{1,0:T(8,128)(2,1)S(1)} %copy-done.13), channel_id=1, source_target_pairs={{0,64},{32,96},{64,0},{96,32},{1,65},{33,97},{65,1},{97,33},{2,66}... | collective-permute-start | bytes 3145736 | tf_op jit(solution)/shard_map/ppermute | solution.py:170
  173.6 45.2 %collective-permute-start.5 = (bf16[256,2048]{1,0:T(8,128)(2,1)S(1)}, bf16[256,2048]{1,0:T(8,128)(2,1)}, u32[]{:S(2)}, u32[]{:S(2)}) collective-permute-start(bf16[256,2048]{1,0:T(8,128)(2,1)S(1)} %copy-done.13), channel_id=1, source_target_pairs={{0,96},{32,0},{64,32},{96,64},{1,97},{33,1},{65,33},{97,65},{2,98}... | collective-permute-start | bytes 3145736 | tf_op jit(solution)/shard_map/ppermute | solution.py:170
  200.6 7.7 %copy-start.11 = (bf16[2048,1024]{1,0:T(8,128)(2,1)S(1)}, bf16[2048,1024]{1,0:T(8,128)(2,1)}, u32[]{:S(2)}) copy-start(bf16[2048,1024]{1,0:T(8,128)(2,1)} %all-gather.6.cloned.1.call-done) | copy-start | bytes 12582916
  200.7 7.7 %copy-start.12 = (bf16[1024,2048]{1,0:T(8,128)(2,1)S(1)}, bf16[1024,2048]{1,0:T(8,128)(2,1)}, u32[]{:S(2)}) copy-start(bf16[1024,2048]{1,0:T(8,128)(2,1)} %all-gather.8.cloned.1.call-done) | copy-start | bytes 12582916
  213.5 5.5 %copy-start.14 = (bf16[256,2048]{1,0:T(8,128)(2,1)S(1)}, bf16[256,2048]{1,0:T(8,128)(2,1)}, u32[]{:S(2)}) copy-start(bf16[256,2048]{1,0:T(8,128)(2,1)} %param.25) | copy-start | bytes 3145732
  219.0 47.6 %copy-start.1 = (bf16[2048,512]{1,0:T(8,128)(2,1)S(1)}, bf16[2048,512]{1,0:T(8,128)(2,1)}, u32[]{:S(2)}) copy-start(bf16[2048,512]{1,0:T(8,128)(2,1)} %param.19) | copy-start | bytes 6291460
Sparse Core Ops, SparseCore 0:
  9.7 68.4 all-gather.3
  79.8 64.0 all-gather.5
  170.5 30.1 all-gather.7
  227.7 36.9 reduce-scatter.1

commit v11 on v10

--- a/solution.py
+++ b/solution.py
@@ -163,8 +163,7 @@
     pair_rows = 2 * row_count // peers
     quarter = row_count // groups
     group_index = lax.axis_index("grp")
-    gate_w = lax.all_gather(w_gate, "ry", axis=1, tiled=True)
-    up_w = lax.all_gather(w_up, "ry", axis=1, tiled=True)
+    gate_up_w = lax.all_gather(jnp.concatenate([w_gate, w_up], axis=1), "ry", axis=1, tiled=True)
     ring = lax.axis_size("ry")
     down_parts = [w_down] + [
         lax.ppermute(w_down, "ry", [(i, (i + shift) % ring) for i in range(ring)])
@@ -194,7 +193,7 @@
     )
     mixed = lax.optimization_barrier(mixed)
     returned = lax.all_to_all(mixed, REQ, split_axis=0, concat_axis=0, tiled=True)
-    gate_w, up_w, out_parts, returned = lax.optimization_barrier((gate_w, up_w, out_parts, returned))
+    gate_up_w, out_parts, returned = lax.optimization_barrier((gate_up_w, out_parts, returned))
     attn_rows = jnp.take(returned.reshape(peers * pair_rows, -1), back_rows, axis=0)
     quarters = lax.all_to_all(
         attn_rows.reshape(groups, quarter, -1), "grp", split_axis=0, concat_axis=0, tiled=True
@@ -211,9 +210,16 @@
     residual = own_rows + RESIDUAL_MULT * attn_part
     mlp_in = normalize(residual, mlp_gain).astype(jnp.bfloat16)
     piece = lax.all_gather(mlp_in, "rzc", axis=0, tiled=True)
-    gate = jnp.dot(piece, gate_w, preferred_element_type=jnp.float32)
-    upper = jnp.dot(piece, up_w, preferred_element_type=jnp.float32)
-    hidden = (jax.nn.silu(gate) * upper).astype(jnp.bfloat16)
+    both = jnp.dot(piece, gate_up_w, preferred_element_type=jnp.float32)
+    width = w_gate.shape[1]
+    hidden = jnp.concatenate(
+        [
+            jax.nn.silu(both[:, 2 * k * width:(2 * k + 1) * width])
+            * both[:, (2 * k + 1) * width:(2 * k + 2) * width]
+            for k in range(ring)
+        ],
+        axis=1,
+    ).astype(jnp.bfloat16)
     down_parts, hidden = lax.optimization_barrier((down_parts, hidden))
     units = w_down.shape[0]
     hidden = jnp.concatenate(

time: 274 us -> 269 us (0.982)
  waiting for transfers between devices: 133 us -> 123 us
  other arithmetic: 15 us -> 19.8 us
    all_to_all x1, waiting for transfers between devices: 17.4 us -> 12.8 us  [body(): lax.all_to_all(mixed, REQ, split_axis=0, concat_axis=0, tiled=True)]
    ppermute x3, waiting for transfers between devices: 8.44 us -> 3.94 us  [body(): lax.ppermute(w_out, 'grp', [(i, (i + shift) % groups) for i in range(grou...]
    all_to_all x1, waiting for transfers between devices: 26.8 us -> 30.7 us  [body(): lax.all_to_all(send_qkv, REQ, split_axis=0, concat_axis=0, tiled=True)]
    concatenate x0 -> x2, other arithmetic: none -> 3.48 us  [the longest x1 3.2 us: body(): jnp.concatenate([w_gate, w_up], axis=1)]
    dot_general x2 -> x1, matrix products: 12.8 us -> 12.5 us  [body(): both = jnp.dot(piece, gate_up_w, preferred_element_type=jnp.float32)]
  transfers between devices with their start and end apart: 13 -> 12, of which waited for: 9 -> 8; matrix products, arithmetic and copies ran while one was open for 16% -> 17% of each run, Pallas kernels for 10% -> 11%
where the time goes in v11:
time: 269 us; the launch traced here: 268 us
  waiting for transfers between devices  123 us (46%)
  matrix products  32.3 us (12%)
  Pallas kernels  28.6 us (11%)
  starting transfers between devices  28.1 us (10%)
  local copies, waits for them, and re-layouts  21.4 us (8%)
  other arithmetic  19.8 us (7%)
  between operations  14.1 us (5%)
    reduce_scatter x1, waiting for transfers between devices, body(): lax.psum_scatter(partial.astype(jnp.bfloat16), 'rzc', scatter_dimension=0...  35.6 us
    all_to_all x1, waiting for transfers between devices, body(): lax.all_to_all(send_qkv, REQ, split_axis=0, concat_axis=0, tiled=True)  30.7 us
    pallas_call x1, Pallas kernels, owner_attention(): pl.pallas_call(attention_kernel, out_shape=(jax.ShapeDtypeStruct((sources...  28.6 us
    all_gather x1, waiting for transfers between devices, body(): piece = lax.all_gather(mlp_in, 'rzc', axis=0, tiled=True)  23.8 us
    all_to_all x1, waiting for transfers between devices, body(): lax.all_to_all(mixed, REQ, split_axis=0, concat_axis=0, tiled=True)  12.8 us
    dot_general x1, matrix products, body(): both = jnp.dot(piece, gate_up_w, preferred_element_type=jnp.float32)  12.5 us
    all_to_all x1, waiting for transfers between devices, body(): lax.all_to_all(attn_rows.reshape(groups, quarter, -1), 'grp', split_axis=...  10 us
    all_to_all x1, starting transfers between devices, body(): lax.all_to_all(send_qkv, REQ, split_axis=0, concat_axis=0, tiled=True)  8.54 us
  transfers between devices with their start and end apart: 12, of which 8 were waited for; matrix products, arithmetic and copies ran while one was open for 17% of the time, Pallas kernels for 11%

profile of v11, /device:TPU:0, one launch (start us, length us, event | category | flops | bytes accessed | tf_op | source)
XLA Modules:
  0.0 267.8 jit_solution(3764275215222480113)
XLA Ops:
  7.2 3.2 %pad_maximum_fusion = bf16[2048,512]{1,0:T(8,128)(2,1)} fusion(bf16[2048,256]{1,0:T(8,128)(2,1)} %param.24, bf16[2048,256]{1,0:T(8,128)(2,1)} %param.23), kind=kLoop, calls=%fused_computation.37 | loop fusion | flops 4194304 | bytes 4194304 | tf_op jit(solution)/shard_map/concatenate | solution.py:166
  10.5 2.2 fusion
  12.9 0.9 convolution_convert_fusion.5
  13.9 1.0 convolution_convert_fusion.6
  14.9 1.4 convolution_convert_fusion.4
  17.4 4.0 %gather_fusion = bf16[1024,768]{1,0:T(8,128)(2,1)S(1)} fusion(bf16[512,768]{1,0:T(8,128)(2,1)S(1)} %copy.21, s32[1024]{0:T(1024)S(1)} %broadcast_clamp_fusion), kind=kCustom, calls=%fused_computation | custom fusion | bytes 3149824 | tf_op jit(solution)/shard_map/jit(_take)/gather | solution.py:184
  21.5 1.4 broadcast_select_fusion
  22.9 8.5 %all-to-all-start = ((bf16[32,32,768]{2,1,0:T(8,128)(2,1)}), bf16[32,32,768]{2,1,0:T(8,128)(2,1)S(1)}, u32[]{:S(2)}, u32[]{:S(2)}) async-start(bf16[32,32,768]{2,1,0:T(8,128)(2,1)} %broadcast_select_fusion), calls=%async_computation | async-start | bytes 3145728 | tf_op jit(solution)/shard_map/all_to_all | solution.py:187
  31.4 1.6 collective-permute-start
  33.0 2.7 %collective-permute-start.1 = (bf16[512,2048]{1,0:T(8,128)(2,1)}, bf16[512,2048]{1,0:T(8,128)(2,1)}, u32[]{:S(2)}, u32[]{:S(2)}) collective-permute-start(bf16[512,2048]{1,0:T(8,128)(2,1)} %param.22), channel_id=1, source_target_pairs={{0,2},{1,3},{2,0},{3,1},{4,6},{5,7},{6,4},{7,5},{8,10},{9,11},{10,... | collective-permute-start | bytes 6291464 | tf_op jit(solution)/shard_map/ppermute | solution.py:173
  35.7 1.4 collective-permute-start.2
  37.2 1.9 multiply_cosine_fusion
  39.1 30.7 %all-to-all-done = bf16[32,32,768]{2,1,0:T(8,128)(2,1)S(1)} async-done(((bf16[32,32,768]{2,1,0:T(8,128)(2,1)}), bf16[32,32,768]{2,1,0:T(8,128)(2,1)S(1)}, u32[]{:S(2)}, u32[]{:S(2)}) %all-to-all-start) | async-done | bytes 1572896 | tf_op jit(solution)/shard_map/all_to_all | solution.py:187
  69.8 0.8 fusion.58
  70.9 1.0 fusion.59
  71.9 0.4 fusion.35
  72.7 1.3 copy.24
  74.0 1.3 convert_element_type.110.k_ref
  75.3 1.1 slice.64
  76.4 2.8 %reshape.161 = bf16[32,32,8,64]{3,2,1,0:T(8,128)(2,1)S(1)} reshape(bf16[32,32,512]{2,1,0:T(8,128)(2,1)} %slice.64) | data formatting | bytes 2097152 | tf_op jit(solution)/shard_map/reshape | solution.py:116
  79.2 1.9 fusion.4
  81.1 2.5 pad_maximum_fusion.1
  83.6 3.3 %convert_element_type.107.q_ref = bf16[32,32,512]{2,1,0:T(8,128)(2,1)S(1)} reshape(bf16[32,32,8,64]{3,2,1,0:T(8,128)(2,1)} %pad_maximum_fusion.1) | data formatting | bytes 2097152 | tf_op jit(solution)/shard_map/convert_element_type | solution.py:116
  87.0 0.9 copy-done.4
  87.9 28.6 %shard_map.175 = (bf16[32,32,512]{2,1,0:T(8,128)(2,1)S(1)}, bf16[512,16,128]{2,1,0:T(8,128)(2,1)}, bf16[512,16,128]{2,1,0:T(8,128)(2,1)}) custom-call(s32[512]{0:T(512)S(1)} %bitcast.34, s32[32]{0:T(128)S(1)} %bitcast.36, s32[32]{0:T(128)S(1)} %bitcast.37, bf16[32,32,512]{2,1,0:T(8,128)(2,1)S(1)} %convert_element_type.107.q_ref, ...), custom_call_target="tpu_custom_call" | custom-call | tf_op jit(solution)/shard_map/pallas_call | solution.py:125
  116.5 1.0 copy-done.3
  117.5 5.2 %all-to-all-start.1 = ((bf16[32,32,512]{2,1,0:T(8,128)(2,1)}), bf16[32,32,512]{2,1,0:T(8,128)(2,1)S(1)}, u32[]{:S(2)}, u32[]{:S(2)}) async-start(bf16[32,32,512]{2,1,0:T(8,128)(2,1)} %copy-done.3), calls=%async_computation.1 | async-start | bytes 2097152 | tf_op jit(solution)/shard_map/all_to_all | solution.py:195
  122.8 3.9 %collective-permute-done.1 = bf16[512,2048]{1,0:T(8,128)(2,1)} collective-permute-done((bf16[512,2048]{1,0:T(8,128)(2,1)}, bf16[512,2048]{1,0:T(8,128)(2,1)}, u32[]{:S(2)}, u32[]{:S(2)}) %collective-permute-start.1) | collective-permute-done | bytes 2097184 | tf_op jit(solution)/shard_map/ppermute | solution.py:173
  126.7 12.8 %all-to-all-done.1 = bf16[32,32,512]{2,1,0:T(8,128)(2,1)S(1)} async-done(((bf16[32,32,512]{2,1,0:T(8,128)(2,1)}), bf16[32,32,512]{2,1,0:T(8,128)(2,1)S(1)}, u32[]{:S(2)}, u32[]{:S(2)}) %all-to-all-start.1) | async-done | bytes 1048608 | tf_op jit(solution)/shard_map/all_to_all | solution.py:195
  139.6 2.0 gather_fusion.1
  141.6 0.9 broadcast_select_fusion.1
  142.5 4.3 %all-to-all-start.2 = ((bf16[4,128,512]{2,1,0:T(8,128)(2,1)}), bf16[4,128,512]{2,1,0:T(8,128)(2,1)S(1)}, u32[]{:S(2)}, u32[]{:S(2)}) async-start(bf16[4,128,512]{2,1,0:T(8,128)(2,1)} %broadcast_select_fusion.1), calls=%async_computation.2 | async-start | bytes 1048576 | tf_op jit(solution)/shard_map/all_to_all | solution.py:198
  146.8 10.0 %all-to-all-done.2 = bf16[4,128,512]{2,1,0:T(8,128)(2,1)S(1)} async-done(((bf16[4,128,512]{2,1,0:T(8,128)(2,1)}), bf16[4,128,512]{2,1,0:T(8,128)(2,1)S(1)}, u32[]{:S(2)}, u32[]{:S(2)}) %all-to-all-start.2) | async-done | bytes 524320 | tf_op jit(solution)/shard_map/all_to_all | solution.py:198
  156.8 2.0 fusion.26
  158.8 2.0 fusion.25
  160.9 2.0 fusion.23
  162.9 2.3 multiply_reduce_fusion
  165.3 0.9 multiply_convert_fusion
  166.7 2.5 collective-permute-start.4
  169.2 1.7 collective-permute-start.5
  170.9 23.8 %all-gather.5.cloned.1.call-done = bf16[1024,2048]{1,0:T(8,128)(2,1)} async-done(((bf16[128,2048]{1,0:T(8,128)(2,1)}), bf16[1024,2048]{1,0:T(8,128)(2,1)}) %all-gather.5.cloned.1.call-update) | async-done | bytes 4194320 | tf_op jit(solution)/shard_map/all_gather | solution.py:212
  194.7 12.5 %fusion.60 = f32[1024,2048]{1,0:T(8,128)S(1)} fusion(bf16[1024,2048]{1,0:T(8,128)(2,1)} %all-gather.5.cloned.1.call-done, bf16[2048,2048]{1,0:T(8,128)(2,1)} %all-gather.3.cloned.1.call-done), kind=kOutput, calls=%fused_computation.111 | convolution fusion | flops 8589934592 | bytes 20971520 | tf_op jit(solution)/shard_map/dot_general | solution.py:213
  207.2 1.4 fusion.41
  208.9 5.8 %collective-permute-done.3 = bf16[256,2048]{1,0:T(8,128)(2,1)S(1)} collective-permute-done((bf16[256,2048]{1,0:T(8,128)(2,1)S(1)}, bf16[256,2048]{1,0:T(8,128)(2,1)S(1)}, u32[]{:S(2)}, u32[]{:S(2)}) %collective-permute-start.3) | collective-permute-done | bytes 1048608 | tf_op jit(solution)/shard_map/ppermute | solution.py:169
  214.7 0.7 collective-permute-done.5
  215.7 8.0 %fusion.15 = bf16[1024,2048]{1,0:T(8,128)(2,1)} fusion(bf16[256,2048]{1,0:T(8,128)(2,1)} %collective-permute-done.5, bf16[256,2048]{1,0:T(8,128)(2,1)} %collective-permute-done.4, bf16[256,2048]{1,0:T(8,128)(2,1)S(1)} %collective-permute-done.3, bf16[256,2048]{1,0:T(8,128)(2,1)S(1)} %copy-done.11, bf16[1024,256]{1,0:T(8,128)(2,1)S(1)} %get-tuple-element.42, ...), kind=kOutput, calls=%fused_computation.23 | convolution fusion | flops 4322230272 | bytes 10485760 | tf_op jit(solution)/shard_map/dot_general | solution.py:234
  223.7 35.6 %reduce-scatter.2.cloned.1.call-done = bf16[128,2048]{1,0:T(8,128)(2,1)} async-done(((bf16[1024,2048]{1,0:T(8,128)(2,1)}), bf16[128,2048]{1,0:T(8,128)(2,1)}) %reduce-scatter.2.cloned.1.call-update) | async-done | bytes 524304 | tf_op jit(solution)/shard_map/reduce_scatter | solution.py:237
  259.3 2.0 add_convert_fusion
  (58 shorter events, 3.2 us)
Async XLA Ops:
  7.2 7.7 %copy-start = (bf16[2048,512]{1,0:T(8,128)(2,1)S(1)}, bf16[2048,512]{1,0:T(8,128)(2,1)}, u32[]{:S(2)}) copy-start(bf16[2048,512]{1,0:T(8,128)(2,1)} %param.19) | copy-start | bytes 6291460
  7.2 132.4 %all-gather.3.cloned.1.call-start = ((), (), s32[]{:S(2)}) async-start(), calls=%async_computation.4 | async-start | bytes 10485760 | tf_op jit(solution)/shard_map/all_gather | solution.py:166
  10.4 2.3 copy-start.12
  10.4 2.3 copy-start.14
  10.5 2.4 copy-start.8
  12.9 1.0 copy-start.13
  16.3 0.7 copy-start.9
  22.9 14.3 %copy-start.6 = (s32[1,32]{1,0:T(1,128)S(1)}, s32[1,32]{1,0:T(1,128)}, u32[]{:S(2)}) copy-start(s32[1,32]{1,0:T(1,128)} %param.30) | copy-start | bytes 388
  22.9 47.0 %all-to-all-start = ((bf16[32,32,768]{2,1,0:T(8,128)(2,1)}), bf16[32,32,768]{2,1,0:T(8,128)(2,1)S(1)}, u32[]{:S(2)}, u32[]{:S(2)}) async-start(bf16[32,32,768]{2,1,0:T(8,128)(2,1)} %broadcast_select_fusion), calls=%async_computation | async-start | bytes 3145728 | tf_op jit(solution)/shard_map/all_to_all | solution.py:187
  31.4 91.4 %collective-permute-start = (bf16[512,2048]{1,0:T(8,128)(2,1)}, bf16[512,2048]{1,0:T(8,128)(2,1)}, u32[]{:S(2)}, u32[]{:S(2)}) collective-permute-start(bf16[512,2048]{1,0:T(8,128)(2,1)} %param.22), channel_id=1, source_target_pairs={{0,1},{1,2},{2,3},{3,0},{4,5},{5,6},{6,7},{7,4},{8,9},{9,10},{10,1... | collective-permute-start | bytes 6291464 | tf_op jit(solution)/shard_map/ppermute | solution.py:173
  33.0 93.8 %collective-permute-start.1 = (bf16[512,2048]{1,0:T(8,128)(2,1)}, bf16[512,2048]{1,0:T(8,128)(2,1)}, u32[]{:S(2)}, u32[]{:S(2)}) collective-permute-start(bf16[512,2048]{1,0:T(8,128)(2,1)} %param.22), channel_id=1, source_target_pairs={{0,2},{1,3},{2,0},{3,1},{4,6},{5,7},{6,4},{7,5},{8,10},{9,11},{10,... | collective-permute-start | bytes 6291464 | tf_op jit(solution)/shard_map/ppermute | solution.py:173
  35.7 91.0 %collective-permute-start.2 = (bf16[512,2048]{1,0:T(8,128)(2,1)}, bf16[512,2048]{1,0:T(8,128)(2,1)}, u32[]{:S(2)}, u32[]{:S(2)}) collective-permute-start(bf16[512,2048]{1,0:T(8,128)(2,1)} %param.22), channel_id=1, source_target_pairs={{0,3},{1,0},{2,1},{3,2},{4,7},{5,4},{6,5},{7,6},{8,11},{9,8},{10,9... | collective-permute-start | bytes 6291464 | tf_op jit(solution)/shard_map/ppermute | solution.py:173
  83.5 3.4 %copy-start.2 = (bf16[512,16,128]{2,1,0:T(8,128)(2,1)S(1)}, bf16[512,16,128]{2,1,0:T(8,128)(2,1)}, u32[]{:S(2)}) copy-start(bf16[512,16,128]{2,1,0:T(8,128)(2,1)} %ck_ref.1) | copy-start | bytes 6291460
  83.5 3.4 %copy-start.5 = (s32[1,512]{1,0:T(1,128)S(1)}, s32[1,512]{1,0:T(1,128)}, u32[]{:S(2)}) copy-start(s32[1,512]{1,0:T(1,128)} %param.31) | copy-start | bytes 6148
  83.6 3.4 %copy-start.7 = (s32[1,32]{1,0:T(1,128)S(1)}, s32[1,32]{1,0:T(1,128)}, u32[]{:S(2)}) copy-start(s32[1,32]{1,0:T(1,128)} %param.29) | copy-start | bytes 388
  86.9 1.0 copy-start.4
  116.5 1.0 copy-start.3
  117.5 22.1 %all-to-all-start.1 = ((bf16[32,32,512]{2,1,0:T(8,128)(2,1)}), bf16[32,32,512]{2,1,0:T(8,128)(2,1)S(1)}, u32[]{:S(2)}, u32[]{:S(2)}) async-start(bf16[32,32,512]{2,1,0:T(8,128)(2,1)} %copy-done.3), calls=%async_computation.1 | async-start | bytes 2097152 | tf_op jit(solution)/shard_map/all_to_all | solution.py:195
  142.5 14.3 %all-to-all-start.2 = ((bf16[4,128,512]{2,1,0:T(8,128)(2,1)}), bf16[4,128,512]{2,1,0:T(8,128)(2,1)S(1)}, u32[]{:S(2)}, u32[]{:S(2)}) async-start(bf16[4,128,512]{2,1,0:T(8,128)(2,1)} %broadcast_select_fusion.1), calls=%async_computation.2 | async-start | bytes 1048576 | tf_op jit(solution)/shard_map/all_to_all | solution.py:198
  146.8 47.9 %all-gather.5.cloned.1.call-start = ((), (), s32[]{:S(2)}) async-start(), calls=%async_computation.5 | async-start | bytes 4718592 | tf_op jit(solution)/shard_map/all_gather | solution.py:212
  162.9 2.4 copy-start.10
  165.3 1.4 copy-start.11
  166.3 93.0 %reduce-scatter.2.cloned.1.call-start = ((), (), s32[]{:S(2)}) async-start(), calls=%async_computation.6 | async-start | bytes 4718592 | tf_op jit(solution)/shard_map/reduce_scatter | solution.py:237
  166.7 48.0 %collective-permute-start.3 = (bf16[256,2048]{1,0:T(8,128)(2,1)S(1)}, bf16[256,2048]{1,0:T(8,128)(2,1)S(1)}, u32[]{:S(2)}, u32[]{:S(2)}) collective-permute-start(bf16[256,2048]{1,0:T(8,128)(2,1)S(1)} %copy-done.11), channel_id=1, source_target_pairs={{0,32},{32,64},{64,96},{96,0},{1,33},{33,65},{65,97},{97,1},{2,34}... | collective-permute-start | bytes 3145736 | tf_op jit(solution)/shard_map/ppermute | solution.py:169
  166.7 48.0 %collective-permute-start.4 = (bf16[256,2048]{1,0:T(8,128)(2,1)S(1)}, bf16[256,2048]{1,0:T(8,128)(2,1)}, u32[]{:S(2)}, u32[]{:S(2)}) collective-permute-start(bf16[256,2048]{1,0:T(8,128)(2,1)S(1)} %copy-done.11), channel_id=1, source_target_pairs={{0,64},{32,96},{64,0},{96,32},{1,65},{33,97},{65,1},{97,33},{2,66}... | collective-permute-start | bytes 3145736 | tf_op jit(solution)/shard_map/ppermute | solution.py:169
  169.2 46.2 %collective-permute-start.5 = (bf16[256,2048]{1,0:T(8,128)(2,1)S(1)}, bf16[256,2048]{1,0:T(8,128)(2,1)}, u32[]{:S(2)}, u32[]{:S(2)}) collective-permute-start(bf16[256,2048]{1,0:T(8,128)(2,1)S(1)} %copy-done.11), channel_id=1, source_target_pairs={{0,96},{32,0},{64,32},{96,64},{1,97},{33,1},{65,33},{97,65},{2,98}... | collective-permute-start | bytes 3145736 | tf_op jit(solution)/shard_map/ppermute | solution.py:169
  223.7 37.6 %copy-start.1 = (bf16[2048,512]{1,0:T(8,128)(2,1)S(1)}, bf16[2048,512]{1,0:T(8,128)(2,1)}, u32[]{:S(2)}) copy-start(bf16[2048,512]{1,0:T(8,128)(2,1)} %param.19) | copy-start | bytes 6291460
Sparse Core Ops, SparseCore 0:
  10.6 102.4 all-gather.2
  166.4 28.2 all-gather.4
  223.8 35.4 reduce-scatter.1

commit v12 on v11

--- a/solution.py
+++ b/solution.py
@@ -193,7 +193,9 @@
     )
     mixed = lax.optimization_barrier(mixed)
     returned = lax.all_to_all(mixed, REQ, split_axis=0, concat_axis=0, tiled=True)
-    gate_up_w, out_parts, returned = lax.optimization_barrier((gate_up_w, out_parts, returned))
+    gate_up_w, out_parts, down_parts, returned = lax.optimization_barrier(
+        (gate_up_w, out_parts, down_parts, returned)
+    )
     attn_rows = jnp.take(returned.reshape(peers * pair_rows, -1), back_rows, axis=0)
     quarters = lax.all_to_all(
         attn_rows.reshape(groups, quarter, -1), "grp", split_axis=0, concat_axis=0, tiled=True
@@ -220,7 +222,6 @@
         ],
         axis=1,
     ).astype(jnp.bfloat16)
-    down_parts, hidden = lax.optimization_barrier((down_parts, hidden))
     units = w_down.shape[0]
     hidden = jnp.concatenate(
         [

time: 269 us -> 305 us (1.13)
  waiting for transfers between devices: 123 us -> 145 us
  other arithmetic: 19.8 us -> 24.3 us
  starting transfers between devices: 28.1 us -> 32.5 us
  local copies, waits for them, and re-layouts: 21.4 us -> 25.6 us
    ppermute x3, waiting for transfers between devices: 6.54 us -> 27.1 us  [body(): lax.ppermute(w_down, 'ry', [(i, (i + shift) % ring) for i in range(ring)])]
    all_to_all x1, waiting for transfers between devices: 30.7 us -> 25.4 us  [body(): lax.all_to_all(send_qkv, REQ, split_axis=0, concat_axis=0, tiled=True)]
    ppermute x3, starting transfers between devices: 4.18 us -> 8.88 us  [body(): lax.ppermute(w_down, 'ry', [(i, (i + shift) % ring) for i in range(ring)])]
    all_gather x1, waiting for transfers between devices: 23.8 us -> 28.1 us  [body(): piece = lax.all_gather(mlp_in, 'rzc', axis=0, tiled=True)]
    ppermute x3, waiting for transfers between devices: 3.94 us -> 0.01 us  [body(): lax.ppermute(w_out, 'grp', [(i, (i + shift) % groups) for i in range(grou...]
    all_to_all x1, waiting for transfers between devices: 12.8 us -> 16.7 us  [body(): lax.all_to_all(mixed, REQ, split_axis=0, concat_axis=0, tiled=True)]
  transfers between devices with their start and end apart: 12 -> 12, of which waited for: 8 -> 6; matrix products, arithmetic and copies ran while one was open for 17% -> 13% of each run, Pallas kernels for 11% -> 9%
where the time goes in v12:
time: 305 us; the launch traced here: 304 us
  waiting for transfers between devices  145 us (48%)
  matrix products  33.1 us (11%)
  starting transfers between devices  32.5 us (11%)
  Pallas kernels  28.6 us (9%)
  local copies, waits for them, and re-layouts  25.6 us (8%)
  other arithmetic  24.3 us (8%)
  between operations  14.2 us (5%)
    reduce_scatter x1, waiting for transfers between devices, body(): lax.psum_scatter(partial.astype(jnp.bfloat16), 'rzc', scatter_dimension=0...  38.1 us
    pallas_call x1, Pallas kernels, owner_attention(): pl.pallas_call(attention_kernel, out_shape=(jax.ShapeDtypeStruct((sources...  28.6 us
    all_gather x1, waiting for transfers between devices, body(): piece = lax.all_gather(mlp_in, 'rzc', axis=0, tiled=True)  28.1 us
    ppermute x3, waiting for transfers between devices, body(): lax.ppermute(w_down, 'ry', [(i, (i + shift) % ring) for i in range(ring)])  27.1 us
    all_to_all x1, waiting for transfers between devices, body(): lax.all_to_all(send_qkv, REQ, split_axis=0, concat_axis=0, tiled=True)  25.4 us
    all_to_all x1, waiting for transfers between devices, body(): lax.all_to_all(mixed, REQ, split_axis=0, concat_axis=0, tiled=True)  16.7 us
    dot_general x1, matrix products, body(): both = jnp.dot(piece, gate_up_w, preferred_element_type=jnp.float32)  12.5 us
    all_to_all x1, waiting for transfers between devices, body(): lax.all_to_all(attn_rows.reshape(groups, quarter, -1), 'grp', split_axis=...  10 us
  transfers between devices with their start and end apart: 12, of which 6 were waited for; matrix products, arithmetic and copies ran while one was open for 13% of the time, Pallas kernels for 9%

profile of v12, /device:TPU:0, one launch (start us, length us, event | category | flops | bytes accessed | tf_op | source)
XLA Modules:
  0.0 303.7 jit_solution(72605560635116255)
XLA Ops:
  7.2 3.2 %pad_maximum_fusion = bf16[2048,512]{1,0:T(8,128)(2,1)} fusion(bf16[2048,256]{1,0:T(8,128)(2,1)} %param.24, bf16[2048,256]{1,0:T(8,128)(2,1)} %param.23), kind=kLoop, calls=%fused_computation.37 | loop fusion | flops 4194304 | bytes 4194304 | tf_op jit(solution)/shard_map/concatenate | solution.py:166
  10.5 2.2 fusion
  12.9 0.9 convolution_convert_fusion.5
  13.9 0.9 convolution_convert_fusion.6
  14.9 1.4 convolution_convert_fusion.4
  17.4 5.2 %gather_fusion = bf16[1024,768]{1,0:T(8,128)(2,1)} fusion(bf16[512,768]{1,0:T(8,128)(2,1)S(1)} %copy.21, s32[1024]{0:T(1024)S(1)} %broadcast_clamp_fusion), kind=kCustom, calls=%fused_computation | custom fusion | bytes 3149824 | tf_op jit(solution)/shard_map/jit(_take)/gather | solution.py:184
  22.7 3.0 broadcast_select_fusion
  25.7 8.7 %all-to-all-start = ((bf16[32,32,768]{2,1,0:T(8,128)(2,1)}), bf16[32,32,768]{2,1,0:T(8,128)(2,1)}, u32[]{:S(2)}, u32[]{:S(2)}) async-start(bf16[32,32,768]{2,1,0:T(8,128)(2,1)} %broadcast_select_fusion), calls=%async_computation | async-start | bytes 3145728 | tf_op jit(solution)/shard_map/all_to_all | solution.py:187
  34.4 1.6 collective-permute-start
  35.9 2.7 collective-permute-start.1
  38.6 1.4 collective-permute-start.2
  40.1 1.7 collective-permute-start.3
  41.8 2.7 collective-permute-start.4
  44.6 2.9 multiply_cosine_fusion
  47.5 25.4 %all-to-all-done = bf16[32,32,768]{2,1,0:T(8,128)(2,1)} async-done(((bf16[32,32,768]{2,1,0:T(8,128)(2,1)}), bf16[32,32,768]{2,1,0:T(8,128)(2,1)}, u32[]{:S(2)}, u32[]{:S(2)}) %all-to-all-start) | async-done | bytes 1572896 | tf_op jit(solution)/shard_map/all_to_all | solution.py:187
  73.0 2.3 slice.64
  75.3 2.8 reshape.161
  78.1 1.8 fusion.58
  80.1 2.9 fusion.4
  83.0 2.5 pad_maximum_fusion.1
  85.4 1.0 fusion.59
  86.5 0.4 fusion.35
  86.9 27.1 %collective-permute-done.3 = bf16[256,2048]{1,0:T(8,128)(2,1)} collective-permute-done((bf16[256,2048]{1,0:T(8,128)(2,1)}, bf16[256,2048]{1,0:T(8,128)(2,1)}, u32[]{:S(2)}, u32[]{:S(2)}) %collective-permute-start.3) | collective-permute-done | bytes 1048608 | tf_op jit(solution)/shard_map/ppermute | solution.py:169
  114.0 4.4 %collective-permute-start.5 = (bf16[256,2048]{1,0:T(8,128)(2,1)}, bf16[256,2048]{1,0:T(8,128)(2,1)}, u32[]{:S(2)}, u32[]{:S(2)}) collective-permute-start(bf16[256,2048]{1,0:T(8,128)(2,1)} %param.25), channel_id=1, source_target_pairs={{0,96},{32,0},{64,32},{96,64},{1,97},{33,1},{65,33},{97,65},{2,98}... | collective-permute-start | bytes 3145736 | tf_op jit(solution)/shard_map/ppermute | solution.py:169
  118.5 1.1 pad_maximum_fusion.4
  119.5 3.3 %convert_element_type.107.q_ref = bf16[32,32,512]{2,1,0:T(8,128)(2,1)S(1)} reshape(bf16[32,32,8,64]{3,2,1,0:T(8,128)(2,1)} %pad_maximum_fusion.1) | data formatting | bytes 2097152 | tf_op jit(solution)/shard_map/convert_element_type | solution.py:116
  122.9 2.4 copy.24
  125.2 1.3 convert_element_type.110.k_ref
  126.6 0.9 copy-done.4
  127.6 28.6 %shard_map.175 = (bf16[32,32,512]{2,1,0:T(8,128)(2,1)S(1)}, bf16[512,16,128]{2,1,0:T(8,128)(2,1)}, bf16[512,16,128]{2,1,0:T(8,128)(2,1)}) custom-call(s32[512]{0:T(512)S(1)} %bitcast.34, s32[32]{0:T(128)S(1)} %bitcast.36, s32[32]{0:T(128)S(1)} %bitcast.37, bf16[32,32,512]{2,1,0:T(8,128)(2,1)S(1)} %convert_element_type.107.q_ref, ...), custom_call_target="tpu_custom_call" | custom-call | tf_op jit(solution)/shard_map/pallas_call | solution.py:125
  156.2 1.0 copy-done.3
  157.2 4.6 %all-to-all-start.1 = ((bf16[32,32,512]{2,1,0:T(8,128)(2,1)}), bf16[32,32,512]{2,1,0:T(8,128)(2,1)S(1)}, u32[]{:S(2)}, u32[]{:S(2)}) async-start(bf16[32,32,512]{2,1,0:T(8,128)(2,1)} %copy-done.3), calls=%async_computation.1 | async-start | bytes 2097152 | tf_op jit(solution)/shard_map/all_to_all | solution.py:195
  161.9 16.7 %all-to-all-done.1 = bf16[32,32,512]{2,1,0:T(8,128)(2,1)S(1)} async-done(((bf16[32,32,512]{2,1,0:T(8,128)(2,1)}), bf16[32,32,512]{2,1,0:T(8,128)(2,1)S(1)}, u32[]{:S(2)}, u32[]{:S(2)}) %all-to-all-start.1) | async-done | bytes 1048608 | tf_op jit(solution)/shard_map/all_to_all | solution.py:195
  178.6 2.0 gather_fusion.1
  180.6 0.9 broadcast_select_fusion.1
  181.5 4.3 %all-to-all-start.2 = ((bf16[4,128,512]{2,1,0:T(8,128)(2,1)}), bf16[4,128,512]{2,1,0:T(8,128)(2,1)S(1)}, u32[]{:S(2)}, u32[]{:S(2)}) async-start(bf16[4,128,512]{2,1,0:T(8,128)(2,1)} %broadcast_select_fusion.1), calls=%async_computation.2 | async-start | bytes 1048576 | tf_op jit(solution)/shard_map/all_to_all | solution.py:200
  185.8 10.0 %all-to-all-done.2 = bf16[4,128,512]{2,1,0:T(8,128)(2,1)S(1)} async-done(((bf16[4,128,512]{2,1,0:T(8,128)(2,1)}), bf16[4,128,512]{2,1,0:T(8,128)(2,1)S(1)}, u32[]{:S(2)}, u32[]{:S(2)}) %all-to-all-start.2) | async-done | bytes 524320 | tf_op jit(solution)/shard_map/all_to_all | solution.py:200
  195.8 2.2 fusion.26
  198.1 2.0 fusion.25
  200.1 2.0 fusion.23
  202.2 2.4 multiply_reduce_fusion
  204.6 0.9 multiply_convert_fusion
  205.9 28.1 %all-gather.5.cloned.1.call-done = bf16[1024,2048]{1,0:T(8,128)(2,1)} async-done(((bf16[128,2048]{1,0:T(8,128)(2,1)}), bf16[1024,2048]{1,0:T(8,128)(2,1)}) %all-gather.5.cloned.1.call-update) | async-done | bytes 4194320 | tf_op jit(solution)/shard_map/all_gather | solution.py:214
  234.0 12.5 %fusion.60 = f32[1024,2048]{1,0:T(8,128)S(1)} fusion(bf16[1024,2048]{1,0:T(8,128)(2,1)} %all-gather.5.cloned.1.call-done, bf16[2048,2048]{1,0:T(8,128)(2,1)} %all-gather.3.cloned.1.call-done), kind=kOutput, calls=%fused_computation.111 | convolution fusion | flops 8589934592 | bytes 20971520 | tf_op jit(solution)/shard_map/dot_general | solution.py:215
  246.4 1.4 fusion.41
  248.4 8.7 %fusion.15 = bf16[1024,2048]{1,0:T(8,128)(2,1)} fusion(bf16[256,2048]{1,0:T(8,128)(2,1)} %collective-permute-done.5, bf16[256,2048]{1,0:T(8,128)(2,1)} %collective-permute-done.4, bf16[256,2048]{1,0:T(8,128)(2,1)} %collective-permute-done.3, bf16[256,2048]{1,0:T(8,128)(2,1)} %param.25, bf16[1024,256]{1,0:T(8,128)(2,1)S(1)} %get-tuple-element.40, ...), kind=kOutput, calls=%fused_computation.23 | convolution fusion | flops 4322230272 | bytes 10485760 | tf_op jit(solution)/shard_map/dot_general | solution.py:235
  257.1 38.1 %reduce-scatter.2.cloned.1.call-done = bf16[128,2048]{1,0:T(8,128)(2,1)} async-done(((bf16[1024,2048]{1,0:T(8,128)(2,1)}), bf16[128,2048]{1,0:T(8,128)(2,1)}) %reduce-scatter.2.cloned.1.call-update) | async-done | bytes 524304 | tf_op jit(solution)/shard_map/reduce_scatter | solution.py:238
  295.2 2.0 add_convert_fusion
  (60 shorter events, 2.7 us)
Async XLA Ops:
  7.2 7.7 %copy-start = (bf16[2048,512]{1,0:T(8,128)(2,1)S(1)}, bf16[2048,512]{1,0:T(8,128)(2,1)}, u32[]{:S(2)}) copy-start(bf16[2048,512]{1,0:T(8,128)(2,1)} %param.19) | copy-start | bytes 6291460
  7.2 171.4 %all-gather.3.cloned.1.call-start = ((), (), s32[]{:S(2)}) async-start(), calls=%async_computation.4 | async-start | bytes 10485760 | tf_op jit(solution)/shard_map/all_gather | solution.py:166
  10.4 2.3 copy-start.13
  10.4 2.3 copy-start.15
  10.5 2.4 copy-start.9
  12.9 1.0 copy-start.14
  16.3 0.7 copy-start.11
  25.7 18.8 %copy-start.6 = (s32[1,32]{1,0:T(1,128)S(1)}, s32[1,32]{1,0:T(1,128)}, u32[]{:S(2)}) copy-start(s32[1,32]{1,0:T(1,128)} %param.30) | copy-start | bytes 388
  25.7 47.3 %all-to-all-start = ((bf16[32,32,768]{2,1,0:T(8,128)(2,1)}), bf16[32,32,768]{2,1,0:T(8,128)(2,1)}, u32[]{:S(2)}, u32[]{:S(2)}) async-start(bf16[32,32,768]{2,1,0:T(8,128)(2,1)} %broadcast_select_fusion), calls=%async_computation | async-start | bytes 3145728 | tf_op jit(solution)/shard_map/all_to_all | solution.py:187
  34.4 127.5 %collective-permute-start = (bf16[512,2048]{1,0:T(8,128)(2,1)}, bf16[512,2048]{1,0:T(8,128)(2,1)}, u32[]{:S(2)}, u32[]{:S(2)}) collective-permute-start(bf16[512,2048]{1,0:T(8,128)(2,1)} %param.22), channel_id=1, source_target_pairs={{0,1},{1,2},{2,3},{3,0},{4,5},{5,6},{6,7},{7,4},{8,9},{9,10},{10,1... | collective-permute-start | bytes 6291464 | tf_op jit(solution)/shard_map/ppermute | solution.py:173
  35.9 126.0 %collective-permute-start.1 = (bf16[512,2048]{1,0:T(8,128)(2,1)}, bf16[512,2048]{1,0:T(8,128)(2,1)}, u32[]{:S(2)}, u32[]{:S(2)}) collective-permute-start(bf16[512,2048]{1,0:T(8,128)(2,1)} %param.22), channel_id=1, source_target_pairs={{0,2},{1,3},{2,0},{3,1},{4,6},{5,7},{6,4},{7,5},{8,10},{9,11},{10,... | collective-permute-start | bytes 6291464 | tf_op jit(solution)/shard_map/ppermute | solution.py:173
  38.6 123.3 %collective-permute-start.2 = (bf16[512,2048]{1,0:T(8,128)(2,1)}, bf16[512,2048]{1,0:T(8,128)(2,1)}, u32[]{:S(2)}, u32[]{:S(2)}) collective-permute-start(bf16[512,2048]{1,0:T(8,128)(2,1)} %param.22), channel_id=1, source_target_pairs={{0,3},{1,0},{2,1},{3,2},{4,7},{5,4},{6,5},{7,6},{8,11},{9,8},{10,9... | collective-permute-start | bytes 6291464 | tf_op jit(solution)/shard_map/ppermute | solution.py:173
  40.1 73.9 %collective-permute-start.3 = (bf16[256,2048]{1,0:T(8,128)(2,1)}, bf16[256,2048]{1,0:T(8,128)(2,1)}, u32[]{:S(2)}, u32[]{:S(2)}) collective-permute-start(bf16[256,2048]{1,0:T(8,128)(2,1)} %param.25), channel_id=1, source_target_pairs={{0,32},{32,64},{64,96},{96,0},{1,33},{33,65},{65,97},{97,1},{2,34}... | collective-permute-start | bytes 3145736 | tf_op jit(solution)/shard_map/ppermute | solution.py:169
  41.8 120.0 %collective-permute-start.4 = (bf16[256,2048]{1,0:T(8,128)(2,1)}, bf16[256,2048]{1,0:T(8,128)(2,1)}, u32[]{:S(2)}, u32[]{:S(2)}) collective-permute-start(bf16[256,2048]{1,0:T(8,128)(2,1)} %param.25), channel_id=1, source_target_pairs={{0,64},{32,96},{64,0},{96,32},{1,65},{33,97},{65,1},{97,33},{2,66}... | collective-permute-start | bytes 3145736 | tf_op jit(solution)/shard_map/ppermute | solution.py:169
  85.4 1.1 copy-start.8
  114.0 47.8 %collective-permute-start.5 = (bf16[256,2048]{1,0:T(8,128)(2,1)}, bf16[256,2048]{1,0:T(8,128)(2,1)}, u32[]{:S(2)}, u32[]{:S(2)}) collective-permute-start(bf16[256,2048]{1,0:T(8,128)(2,1)} %param.25), channel_id=1, source_target_pairs={{0,96},{32,0},{64,32},{96,64},{1,97},{33,1},{65,33},{97,65},{2,98}... | collective-permute-start | bytes 3145736 | tf_op jit(solution)/shard_map/ppermute | solution.py:169
  119.5 7.0 %copy-start.2 = (bf16[512,16,128]{2,1,0:T(8,128)(2,1)S(1)}, bf16[512,16,128]{2,1,0:T(8,128)(2,1)}, u32[]{:S(2)}) copy-start(bf16[512,16,128]{2,1,0:T(8,128)(2,1)} %ck_ref.1) | copy-start | bytes 6291460
  119.5 7.0 %copy-start.5 = (s32[1,512]{1,0:T(1,128)S(1)}, s32[1,512]{1,0:T(1,128)}, u32[]{:S(2)}) copy-start(s32[1,512]{1,0:T(1,128)} %param.31) | copy-start | bytes 6148
  119.5 7.0 %copy-start.7 = (s32[1,32]{1,0:T(1,128)S(1)}, s32[1,32]{1,0:T(1,128)}, u32[]{:S(2)}) copy-start(s32[1,32]{1,0:T(1,128)} %param.29) | copy-start | bytes 388
  126.6 1.0 copy-start.4
  156.2 1.0 copy-start.3
  157.2 21.5 %all-to-all-start.1 = ((bf16[32,32,512]{2,1,0:T(8,128)(2,1)}), bf16[32,32,512]{2,1,0:T(8,128)(2,1)S(1)}, u32[]{:S(2)}, u32[]{:S(2)}) async-start(bf16[32,32,512]{2,1,0:T(8,128)(2,1)} %copy-done.3), calls=%async_computation.1 | async-start | bytes 2097152 | tf_op jit(solution)/shard_map/all_to_all | solution.py:195
  181.5 14.3 %all-to-all-start.2 = ((bf16[4,128,512]{2,1,0:T(8,128)(2,1)}), bf16[4,128,512]{2,1,0:T(8,128)(2,1)S(1)}, u32[]{:S(2)}, u32[]{:S(2)}) async-start(bf16[4,128,512]{2,1,0:T(8,128)(2,1)} %broadcast_select_fusion.1), calls=%async_computation.2 | async-start | bytes 1048576 | tf_op jit(solution)/shard_map/all_to_all | solution.py:200
  185.8 48.2 %all-gather.5.cloned.1.call-start = ((), (), s32[]{:S(2)}) async-start(), calls=%async_computation.5 | async-start | bytes 4718592 | tf_op jit(solution)/shard_map/all_gather | solution.py:214
  195.8 4.3 %copy-start.10 = (bf16[4,128,512]{2,1,0:T(8,128)(2,1)}, bf16[4,128,512]{2,1,0:T(8,128)(2,1)S(1)}, u32[]{:S(2)}) copy-start(bf16[4,128,512]{2,1,0:T(8,128)(2,1)S(1)} %all-to-all-done.2) | copy-start | bytes 1572868
  202.2 2.4 copy-start.12
  205.5 89.6 %reduce-scatter.2.cloned.1.call-start = ((), (), s32[]{:S(2)}) async-start(), calls=%async_computation.6 | async-start | bytes 4718592 | tf_op jit(solution)/shard_map/reduce_scatter | solution.py:238
  257.1 40.1 %copy-start.1 = (bf16[2048,512]{1,0:T(8,128)(2,1)S(1)}, bf16[2048,512]{1,0:T(8,128)(2,1)}, u32[]{:S(2)}) copy-start(bf16[2048,512]{1,0:T(8,128)(2,1)} %param.19) | copy-start | bytes 6291460
Sparse Core Ops, SparseCore 0:
  10.6 142.6 all-gather.2
  205.7 28.2 all-gather.4
  257.2 37.9 reduce-scatter.1

commit v13 on v11

--- a/solution.py
+++ b/solution.py
@@ -193,17 +193,16 @@
     )
     mixed = lax.optimization_barrier(mixed)
     returned = lax.all_to_all(mixed, REQ, split_axis=0, concat_axis=0, tiled=True)
-    gate_up_w, out_parts, returned = lax.optimization_barrier((gate_up_w, out_parts, returned))
+    out_w = jnp.concatenate(out_parts, axis=0)
+    gate_up_w, out_w, returned = lax.optimization_barrier((gate_up_w, out_w, returned))
     attn_rows = jnp.take(returned.reshape(peers * pair_rows, -1), back_rows, axis=0)
     quarters = lax.all_to_all(
         attn_rows.reshape(groups, quarter, -1), "grp", split_axis=0, concat_axis=0, tiled=True
     )
-    attn_part = None
-    for shift, part in enumerate(out_parts):
-        block = (group_index - shift) % groups
-        term = jnp.dot(quarters[block], part, preferred_element_type=jnp.float32)
-        term = term.astype(jnp.bfloat16).astype(jnp.float32)
-        attn_part = term if attn_part is None else attn_part + term
+    ordered = jnp.concatenate(
+        [quarters[(group_index - shift) % groups] for shift in range(groups)], axis=1
+    )
+    attn_part = jnp.dot(ordered, out_w, preferred_element_type=jnp.float32)
     own_rows = lax.dynamic_slice_in_dim(hidden_in, group_index * quarter, quarter, 0).astype(
         jnp.float32
     )

time: 269 us -> 266 us (0.989)
  other arithmetic: 19.8 us -> 26.9 us
  waiting for transfers between devices: 123 us -> 116 us
    all_to_all x1, waiting for transfers between devices: 12.8 us -> 5.71 us  [body(): lax.all_to_all(mixed, REQ, split_axis=0, concat_axis=0, tiled=True)]
    concatenate x0 -> x1, other arithmetic: none -> 7.03 us  [body(): out_w = jnp.concatenate(out_parts, axis=0)]
    dot_general x4 -> x1, matrix products: 8.44 us -> 4.9 us  [body(): attn_part = jnp.dot(ordered, out_w, preferred_element_type=jnp.float32)]
  transfers between devices with their start and end apart: 12 -> 12, of which waited for: 8 -> 8; matrix products, arithmetic and copies ran while one was open for 17% -> 20% of each run, Pallas kernels for 11% -> 11%
where the time goes in v13:
time: 266 us
  waiting for transfers between devices  116 us (44%)
  matrix products  30.8 us (12%)
  Pallas kernels  28.6 us (11%)
  starting transfers between devices  28 us (11%)
  other arithmetic  26.9 us (10%)
  local copies, waits for them, and re-layouts  20.8 us (8%)
  between operations  14.1 us (5%)
    reduce_scatter x1, waiting for transfers between devices, body(): lax.psum_scatter(partial.astype(jnp.bfloat16), 'rzc', scatter_dimension=0...  35.3 us
    all_to_all x1, waiting for transfers between devices, body(): lax.all_to_all(send_qkv, REQ, split_axis=0, concat_axis=0, tiled=True)  30.7 us
    pallas_call x1, Pallas kernels, owner_attention(): pl.pallas_call(attention_kernel, out_shape=(jax.ShapeDtypeStruct((sources...  28.6 us
    all_gather x1, waiting for transfers between devices, body(): piece = lax.all_gather(mlp_in, 'rzc', axis=0, tiled=True)  24.1 us
    dot_general x1, matrix products, body(): both = jnp.dot(piece, gate_up_w, preferred_element_type=jnp.float32)  12.5 us
    all_to_all x1, waiting for transfers between devices, body(): lax.all_to_all(attn_rows.reshape(groups, quarter, -1), 'grp', split_axis=...  10 us
    dot_general x1, matrix products, body(): jnp.dot(hidden, jnp.concatenate(down_parts, axis=0), preferred_element_ty...  8.49 us
    all_to_all x1, starting transfers between devices, body(): lax.all_to_all(send_qkv, REQ, split_axis=0, concat_axis=0, tiled=True)  8.41 us
  transfers between devices with their start and end apart: 12, of which 8 were waited for; matrix products, arithmetic and copies ran while one was open for 20% of the time, Pallas kernels for 11%

profile of v13, /device:TPU:0, one launch (start us, length us, event | category | flops | bytes accessed | tf_op | source)
XLA Modules:
  0.0 265.6 jit_solution(16523814516043102437)
XLA Ops:
  7.2 3.2 %pad_maximum_fusion.1 = bf16[2048,512]{1,0:T(8,128)(2,1)} fusion(bf16[2048,256]{1,0:T(8,128)(2,1)} %param.24, bf16[2048,256]{1,0:T(8,128)(2,1)} %param.23), kind=kLoop, calls=%fused_computation.27 | loop fusion | flops 4194304 | bytes 4194304 | tf_op jit(solution)/shard_map/concatenate | solution.py:166
  10.5 2.2 fusion
  12.7 2.5 convolution_convert_fusion.1
  15.3 0.9 convolution_convert_fusion.2
  16.3 1.4 convolution_convert_fusion
  18.5 4.0 %gather_fusion = bf16[1024,768]{1,0:T(8,128)(2,1)S(1)} fusion(bf16[512,768]{1,0:T(8,128)(2,1)S(1)} %copy.21, s32[1024]{0:T(1024)S(1)} %broadcast_clamp_fusion), kind=kCustom, calls=%fused_computation | custom fusion | bytes 3149824 | tf_op jit(solution)/shard_map/jit(_take)/gather | solution.py:184
  22.6 1.4 broadcast_select_fusion
  23.9 8.4 %all-to-all-start = ((bf16[32,32,768]{2,1,0:T(8,128)(2,1)}), bf16[32,32,768]{2,1,0:T(8,128)(2,1)S(1)}, u32[]{:S(2)}, u32[]{:S(2)}) async-start(bf16[32,32,768]{2,1,0:T(8,128)(2,1)} %broadcast_select_fusion), calls=%async_computation | async-start | bytes 3145728 | tf_op jit(solution)/shard_map/all_to_all | solution.py:187
  32.4 1.6 collective-permute-start
  33.9 2.7 %collective-permute-start.1 = (bf16[512,2048]{1,0:T(8,128)(2,1)}, bf16[512,2048]{1,0:T(8,128)(2,1)}, u32[]{:S(2)}, u32[]{:S(2)}) collective-permute-start(bf16[512,2048]{1,0:T(8,128)(2,1)} %param.22), channel_id=1, source_target_pairs={{0,2},{1,3},{2,0},{3,1},{4,6},{5,7},{6,4},{7,5},{8,10},{9,11},{10,... | collective-permute-start | bytes 6291464 | tf_op jit(solution)/shard_map/ppermute | solution.py:173
  36.7 1.4 collective-permute-start.2
  38.2 1.9 multiply_cosine_fusion
  40.1 30.7 %all-to-all-done = bf16[32,32,768]{2,1,0:T(8,128)(2,1)S(1)} async-done(((bf16[32,32,768]{2,1,0:T(8,128)(2,1)}), bf16[32,32,768]{2,1,0:T(8,128)(2,1)S(1)}, u32[]{:S(2)}, u32[]{:S(2)}) %all-to-all-start) | async-done | bytes 1572896 | tf_op jit(solution)/shard_map/all_to_all | solution.py:187
  70.8 0.8 fusion.46
  71.8 1.0 fusion.47
  72.9 0.4 fusion.27
  73.3 0.3 pad_maximum_fusion.5
  73.6 1.3 copy.24
  74.9 1.3 convert_element_type.86.k_ref
  76.3 1.1 slice.64
  77.3 2.8 %reshape.161 = bf16[32,32,8,64]{3,2,1,0:T(8,128)(2,1)S(1)} reshape(bf16[32,32,512]{2,1,0:T(8,128)(2,1)} %slice.64) | data formatting | bytes 2097152 | tf_op jit(solution)/shard_map/reshape | solution.py:116
  80.1 1.9 fusion.4
  82.1 2.5 pad_maximum_fusion.2
  84.5 3.2 %convert_element_type.83.q_ref = bf16[32,32,512]{2,1,0:T(8,128)(2,1)S(1)} reshape(bf16[32,32,8,64]{3,2,1,0:T(8,128)(2,1)} %pad_maximum_fusion.2) | data formatting | bytes 2097152 | tf_op jit(solution)/shard_map/convert_element_type | solution.py:116
  87.8 0.9 copy-done.4
  88.7 28.6 %shard_map.175 = (bf16[32,32,512]{2,1,0:T(8,128)(2,1)S(1)}, bf16[512,16,128]{2,1,0:T(8,128)(2,1)}, bf16[512,16,128]{2,1,0:T(8,128)(2,1)}) custom-call(s32[512]{0:T(512)S(1)} %bitcast.25, s32[32]{0:T(128)S(1)} %bitcast.27, s32[32]{0:T(128)S(1)} %bitcast.28, bf16[32,32,512]{2,1,0:T(8,128)(2,1)S(1)} %convert_element_type.83.q_ref, ...), custom_call_target="tpu_custom_call" | custom-call | tf_op jit(solution)/shard_map/pallas_call | solution.py:125
  117.4 1.0 copy-done.3
  118.4 5.2 %all-to-all-start.1 = ((bf16[32,32,512]{2,1,0:T(8,128)(2,1)}), bf16[32,32,512]{2,1,0:T(8,128)(2,1)S(1)}, u32[]{:S(2)}, u32[]{:S(2)}) async-start(bf16[32,32,512]{2,1,0:T(8,128)(2,1)} %copy-done.3), calls=%async_computation.1 | async-start | bytes 2097152 | tf_op jit(solution)/shard_map/all_to_all | solution.py:195
  123.7 4.0 %collective-permute-done.1 = bf16[512,2048]{1,0:T(8,128)(2,1)} collective-permute-done((bf16[512,2048]{1,0:T(8,128)(2,1)}, bf16[512,2048]{1,0:T(8,128)(2,1)}, u32[]{:S(2)}, u32[]{:S(2)}) %collective-permute-start.1) | collective-permute-done | bytes 2097184 | tf_op jit(solution)/shard_map/ppermute | solution.py:173
  127.7 7.0 %pad_maximum_fusion = bf16[2048,2048]{1,0:T(8,128)(2,1)} fusion(bf16[512,2048]{1,0:T(8,128)(2,1)} %collective-permute-done.2, bf16[512,2048]{1,0:T(8,128)(2,1)} %collective-permute-done.1, bf16[512,2048]{1,0:T(8,128)(2,1)} %collective-permute-done, bf16[512,2048]{1,0:T(8,128)(2,1)} %param.22), kind=kLoop, calls=%fused_computation.2 | loop fusion | flops 33554432 | bytes 16777216 | tf_op jit(solution)/shard_map/concatenate | solution.py:196
  134.7 5.7 %all-to-all-done.1 = bf16[32,32,512]{2,1,0:T(8,128)(2,1)S(1)} async-done(((bf16[32,32,512]{2,1,0:T(8,128)(2,1)}), bf16[32,32,512]{2,1,0:T(8,128)(2,1)S(1)}, u32[]{:S(2)}, u32[]{:S(2)}) %all-to-all-start.1) | async-done | bytes 1048608 | tf_op jit(solution)/shard_map/all_to_all | solution.py:195
  140.5 2.0 gather_fusion.1
  142.4 0.9 broadcast_select_fusion.1
  143.4 4.3 %all-to-all-start.2 = ((bf16[4,128,512]{2,1,0:T(8,128)(2,1)}), bf16[4,128,512]{2,1,0:T(8,128)(2,1)S(1)}, u32[]{:S(2)}, u32[]{:S(2)}) async-start(bf16[4,128,512]{2,1,0:T(8,128)(2,1)} %broadcast_select_fusion.1), calls=%async_computation.2 | async-start | bytes 1048576 | tf_op jit(solution)/shard_map/all_to_all | solution.py:199
  147.7 10.0 %all-to-all-done.2 = bf16[4,128,512]{2,1,0:T(8,128)(2,1)S(1)} async-done(((bf16[4,128,512]{2,1,0:T(8,128)(2,1)}), bf16[4,128,512]{2,1,0:T(8,128)(2,1)S(1)}, u32[]{:S(2)}, u32[]{:S(2)}) %all-to-all-start.2) | async-done | bytes 524320 | tf_op jit(solution)/shard_map/all_to_all | solution.py:199
  157.7 4.9 %multiply_reduce_fusion = (f32[128]{0:T(128)S(1)}, f32[128,2048]{1,0:T(8,128)S(1)}) fusion(bf16[2048,2048]{1,0:T(8,128)(2,1)} %pad_maximum_fusion, bf16[128,512]{1,0:T(8,128)(2,1)S(1)} %get-tuple-element.44, bf16[128,512]{1,0:T(8,128)(2,1)S(1)} %get-tuple-element.45, bf16[128,512]{1,0:T(8,128)(2,1)S(1)} %get-tuple-element.46, ...), kind=kOutput, calls=%fused_computation.59 | convolution fusion | flops 1077149568 | bytes 10486276 | tf_op jit(solution)/shard_map/dot_general | solution.py:205
  162.6 0.9 multiply_convert_fusion
  163.8 2.5 collective-permute-start.4
  166.2 1.7 collective-permute-start.5
  167.9 24.1 %all-gather.5.cloned.1.call-done = bf16[1024,2048]{1,0:T(8,128)(2,1)} async-done(((bf16[128,2048]{1,0:T(8,128)(2,1)}), bf16[1024,2048]{1,0:T(8,128)(2,1)}) %all-gather.5.cloned.1.call-update) | async-done | bytes 4194320 | tf_op jit(solution)/shard_map/all_gather | solution.py:211
  192.1 12.5 %fusion.48 = f32[1024,2048]{1,0:T(8,128)S(1)} fusion(bf16[1024,2048]{1,0:T(8,128)(2,1)} %all-gather.5.cloned.1.call-done, bf16[2048,2048]{1,0:T(8,128)(2,1)} %all-gather.3.cloned.1.call-done), kind=kOutput, calls=%fused_computation.101 | convolution fusion | flops 8589934592 | bytes 20971520 | tf_op jit(solution)/shard_map/dot_general | solution.py:212
  204.5 1.4 fusion.33
  206.2 5.7 %collective-permute-done.3 = bf16[256,2048]{1,0:T(8,128)(2,1)S(1)} collective-permute-done((bf16[256,2048]{1,0:T(8,128)(2,1)}, bf16[256,2048]{1,0:T(8,128)(2,1)S(1)}, u32[]{:S(2)}, u32[]{:S(2)}) %collective-permute-start.3) | collective-permute-done | bytes 1048608 | tf_op jit(solution)/shard_map/ppermute | solution.py:169
  211.9 0.7 collective-permute-done.5
  212.9 0.3 copy-done.13
  213.3 8.5 %fusion.15 = bf16[1024,2048]{1,0:T(8,128)(2,1)} fusion(bf16[256,2048]{1,0:T(8,128)(2,1)} %collective-permute-done.5, bf16[256,2048]{1,0:T(8,128)(2,1)} %copy-done.13, bf16[256,2048]{1,0:T(8,128)(2,1)} %copy-done.12, bf16[256,2048]{1,0:T(8,128)(2,1)S(1)} %copy-done.11, bf16[1024,256]{1,0:T(8,128)(2,1)S(1)} %get-tuple-element.36, ...), kind=kOutput, calls=%fused_computation.24 | convolution fusion | flops 4322230272 | bytes 10485760 | tf_op jit(solution)/shard_map/dot_general | solution.py:233
  221.8 35.3 %reduce-scatter.2.cloned.1.call-done = bf16[128,2048]{1,0:T(8,128)(2,1)} async-done(((bf16[1024,2048]{1,0:T(8,128)(2,1)}), bf16[128,2048]{1,0:T(8,128)(2,1)}) %reduce-scatter.2.cloned.1.call-update) | async-done | bytes 524304 | tf_op jit(solution)/shard_map/reduce_scatter | solution.py:236
  257.1 2.0 add_convert_fusion
  (61 shorter events, 2.1 us)
Async XLA Ops:
  7.2 9.1 %copy-start = (bf16[2048,512]{1,0:T(8,128)(2,1)S(1)}, bf16[2048,512]{1,0:T(8,128)(2,1)}, u32[]{:S(2)}) copy-start(bf16[2048,512]{1,0:T(8,128)(2,1)} %param.19) | copy-start | bytes 6291460
  7.2 5.5 %copy-start.16 = (f32[2048]{0:T(1024)S(1)}, f32[2048]{0:T(1024)}, u32[]{:S(2)}) copy-start(f32[2048]{0:T(1024)} %param.17) | copy-start | bytes 24580
  7.2 5.5 %copy-start.14 = (bf16[2048,128]{1,0:T(8,128)(2,1)S(1)}, bf16[2048,128]{1,0:T(8,128)(2,1)}, u32[]{:S(2)}) copy-start(bf16[2048,128]{1,0:T(8,128)(2,1)} %param.21) | copy-start | bytes 1572868
  7.2 133.3 %all-gather.3.cloned.1.call-start = ((), (), s32[]{:S(2)}) async-start(), calls=%async_computation.4 | async-start | bytes 10485760 | tf_op jit(solution)/shard_map/all_gather | solution.py:166
  10.4 4.8 %copy-start.15 = (bf16[2048,128]{1,0:T(8,128)(2,1)S(1)}, bf16[2048,128]{1,0:T(8,128)(2,1)}, u32[]{:S(2)}) copy-start(bf16[2048,128]{1,0:T(8,128)(2,1)} %param.20) | copy-start | bytes 1572868
  10.5 4.8 %copy-start.8 = (bf16[512,2048]{1,0:T(8,128)(2,1)S(1)}, bf16[512,2048]{1,0:T(8,128)(2,1)}, u32[]{:S(2)}) copy-start(bf16[512,2048]{1,0:T(8,128)(2,1)} %param.16) | copy-start | bytes 6291460
  16.2 1.8 copy-start.9
  22.5 15.6 %copy-start.6 = (s32[1,32]{1,0:T(1,128)S(1)}, s32[1,32]{1,0:T(1,128)}, u32[]{:S(2)}) copy-start(s32[1,32]{1,0:T(1,128)} %param.30) | copy-start | bytes 388
  23.9 46.8 %all-to-all-start = ((bf16[32,32,768]{2,1,0:T(8,128)(2,1)}), bf16[32,32,768]{2,1,0:T(8,128)(2,1)S(1)}, u32[]{:S(2)}, u32[]{:S(2)}) async-start(bf16[32,32,768]{2,1,0:T(8,128)(2,1)} %broadcast_select_fusion), calls=%async_computation | async-start | bytes 3145728 | tf_op jit(solution)/shard_map/all_to_all | solution.py:187
  32.4 91.3 %collective-permute-start = (bf16[512,2048]{1,0:T(8,128)(2,1)}, bf16[512,2048]{1,0:T(8,128)(2,1)}, u32[]{:S(2)}, u32[]{:S(2)}) collective-permute-start(bf16[512,2048]{1,0:T(8,128)(2,1)} %param.22), channel_id=1, source_target_pairs={{0,1},{1,2},{2,3},{3,0},{4,5},{5,6},{6,7},{7,4},{8,9},{9,10},{10,1... | collective-permute-start | bytes 6291464 | tf_op jit(solution)/shard_map/ppermute | solution.py:173
  33.9 93.8 %collective-permute-start.1 = (bf16[512,2048]{1,0:T(8,128)(2,1)}, bf16[512,2048]{1,0:T(8,128)(2,1)}, u32[]{:S(2)}, u32[]{:S(2)}) collective-permute-start(bf16[512,2048]{1,0:T(8,128)(2,1)} %param.22), channel_id=1, source_target_pairs={{0,2},{1,3},{2,0},{3,1},{4,6},{5,7},{6,4},{7,5},{8,10},{9,11},{10,... | collective-permute-start | bytes 6291464 | tf_op jit(solution)/shard_map/ppermute | solution.py:173
  36.7 91.0 %collective-permute-start.2 = (bf16[512,2048]{1,0:T(8,128)(2,1)}, bf16[512,2048]{1,0:T(8,128)(2,1)}, u32[]{:S(2)}, u32[]{:S(2)}) collective-permute-start(bf16[512,2048]{1,0:T(8,128)(2,1)} %param.22), channel_id=1, source_target_pairs={{0,3},{1,0},{2,1},{3,2},{4,7},{5,4},{6,5},{7,6},{8,11},{9,8},{10,9... | collective-permute-start | bytes 6291464 | tf_op jit(solution)/shard_map/ppermute | solution.py:173
  82.0 5.7 %copy-start.2 = (bf16[512,16,128]{2,1,0:T(8,128)(2,1)S(1)}, bf16[512,16,128]{2,1,0:T(8,128)(2,1)}, u32[]{:S(2)}) copy-start(bf16[512,16,128]{2,1,0:T(8,128)(2,1)} %ck_ref.1) | copy-start | bytes 6291460
  82.0 5.7 %copy-start.5 = (s32[1,512]{1,0:T(1,128)S(1)}, s32[1,512]{1,0:T(1,128)}, u32[]{:S(2)}) copy-start(s32[1,512]{1,0:T(1,128)} %param.31) | copy-start | bytes 6148
  82.0 5.7 %copy-start.7 = (s32[1,32]{1,0:T(1,128)S(1)}, s32[1,32]{1,0:T(1,128)}, u32[]{:S(2)}) copy-start(s32[1,32]{1,0:T(1,128)} %param.29) | copy-start | bytes 388
  87.8 1.0 copy-start.4
  117.4 1.0 copy-start.3
  118.4 22.1 %all-to-all-start.1 = ((bf16[32,32,512]{2,1,0:T(8,128)(2,1)}), bf16[32,32,512]{2,1,0:T(8,128)(2,1)S(1)}, u32[]{:S(2)}, u32[]{:S(2)}) async-start(bf16[32,32,512]{2,1,0:T(8,128)(2,1)} %copy-done.3), calls=%async_computation.1 | async-start | bytes 2097152 | tf_op jit(solution)/shard_map/all_to_all | solution.py:195
  143.4 14.3 %all-to-all-start.2 = ((bf16[4,128,512]{2,1,0:T(8,128)(2,1)}), bf16[4,128,512]{2,1,0:T(8,128)(2,1)S(1)}, u32[]{:S(2)}, u32[]{:S(2)}) async-start(bf16[4,128,512]{2,1,0:T(8,128)(2,1)} %broadcast_select_fusion.1), calls=%async_computation.2 | async-start | bytes 1048576 | tf_op jit(solution)/shard_map/all_to_all | solution.py:199
  147.7 44.4 %all-gather.5.cloned.1.call-start = ((), (), s32[]{:S(2)}) async-start(), calls=%async_computation.5 | async-start | bytes 4718592 | tf_op jit(solution)/shard_map/all_gather | solution.py:211
  157.7 4.9 %copy-start.10 = (f32[2048]{0:T(1024)S(1)}, f32[2048]{0:T(1024)}, u32[]{:S(2)}) copy-start(f32[2048]{0:T(1024)} %param.18) | copy-start | bytes 24580
  163.6 93.4 %reduce-scatter.2.cloned.1.call-start = ((), (), s32[]{:S(2)}) async-start(), calls=%async_computation.6 | async-start | bytes 4718592 | tf_op jit(solution)/shard_map/reduce_scatter | solution.py:236
  163.7 48.3 %collective-permute-start.3 = (bf16[256,2048]{1,0:T(8,128)(2,1)}, bf16[256,2048]{1,0:T(8,128)(2,1)S(1)}, u32[]{:S(2)}, u32[]{:S(2)}) collective-permute-start(bf16[256,2048]{1,0:T(8,128)(2,1)} %param.25), channel_id=1, source_target_pairs={{0,32},{32,64},{64,96},{96,0},{1,33},{33,65},{65,97},{97,1},{2,34}... | collective-permute-start | bytes 3145736 | tf_op jit(solution)/shard_map/ppermute | solution.py:169
  163.8 48.2 %collective-permute-start.4 = (bf16[256,2048]{1,0:T(8,128)(2,1)}, bf16[256,2048]{1,0:T(8,128)(2,1)S(1)}, u32[]{:S(2)}, u32[]{:S(2)}) collective-permute-start(bf16[256,2048]{1,0:T(8,128)(2,1)} %param.25), channel_id=1, source_target_pairs={{0,64},{32,96},{64,0},{96,32},{1,65},{33,97},{65,1},{97,33},{2,66}... | collective-permute-start | bytes 3145736 | tf_op jit(solution)/shard_map/ppermute | solution.py:169
  166.2 46.5 %collective-permute-start.5 = (bf16[256,2048]{1,0:T(8,128)(2,1)}, bf16[256,2048]{1,0:T(8,128)(2,1)}, u32[]{:S(2)}, u32[]{:S(2)}) collective-permute-start(bf16[256,2048]{1,0:T(8,128)(2,1)} %param.25), channel_id=1, source_target_pairs={{0,96},{32,0},{64,32},{96,64},{1,97},{33,1},{65,33},{97,65},{2,98}... | collective-permute-start | bytes 3145736 | tf_op jit(solution)/shard_map/ppermute | solution.py:169
  205.9 7.4 %copy-start.11 = (bf16[256,2048]{1,0:T(8,128)(2,1)S(1)}, bf16[256,2048]{1,0:T(8,128)(2,1)}, u32[]{:S(2)}) copy-start(bf16[256,2048]{1,0:T(8,128)(2,1)} %param.25) | copy-start | bytes 3145732
  211.9 1.0 copy-start.12
  211.9 1.3 copy-start.13
  213.3 45.8 %copy-start.1 = (bf16[2048,512]{1,0:T(8,128)(2,1)S(1)}, bf16[2048,512]{1,0:T(8,128)(2,1)}, u32[]{:S(2)}) copy-start(bf16[2048,512]{1,0:T(8,128)(2,1)} %param.19) | copy-start | bytes 6291460
Sparse Core Ops, SparseCore 0:
  10.6 102.4 all-gather.2
  163.7 28.2 all-gather.4
  221.9 35.1 reduce-scatter.1

commit v14 on v13

--- a/solution.py
+++ b/solution.py
@@ -211,25 +211,15 @@
     piece = lax.all_gather(mlp_in, "rzc", axis=0, tiled=True)
     both = jnp.dot(piece, gate_up_w, preferred_element_type=jnp.float32)
     width = w_gate.shape[1]
-    hidden = jnp.concatenate(
-        [
-            jax.nn.silu(both[:, 2 * k * width:(2 * k + 1) * width])
-            * both[:, (2 * k + 1) * width:(2 * k + 2) * width]
-            for k in range(ring)
-        ],
-        axis=1,
-    ).astype(jnp.bfloat16)
+    units = w_down.shape[0]
+    blocks = []
+    for shift in range(ring):
+        block = (lax.axis_index("ry") - shift) % ring
+        gate = lax.dynamic_slice_in_dim(both, 2 * block * width, width, axis=1)
+        upper = lax.dynamic_slice_in_dim(both, (2 * block + 1) * width, width, axis=1)
+        blocks.append(jax.nn.silu(gate) * upper)
+    hidden = jnp.concatenate(blocks, axis=1).astype(jnp.bfloat16)
     down_parts, hidden = lax.optimization_barrier((down_parts, hidden))
-    units = w_down.shape[0]
-    hidden = jnp.concatenate(
-        [
-            lax.dynamic_slice_in_dim(
-                hidden, ((lax.axis_index("ry") - shift) % ring) * units, units, axis=1
-            )
-            for shift in range(ring)
-        ],
-        axis=1,
-    )
     partial = jnp.dot(
         hidden, jnp.concatenate(down_parts, axis=0), preferred_element_type=jnp.float32
     )

time: 266 us -> 266 us (level)
  no operation moved by 1% of the time
where the time goes in v14:
time: 266 us; the launch traced here: 265 us
  waiting for transfers between devices  117 us (44%)
  matrix products  30.7 us (12%)
  Pallas kernels  28.6 us (11%)
  starting transfers between devices  28 us (11%)
  other arithmetic  27 us (10%)
  local copies, waits for them, and re-layouts  20.2 us (8%)
  between operations  14.1 us (5%)
    reduce_scatter x1, waiting for transfers between devices, body(): lax.psum_scatter(partial.astype(jnp.bfloat16), 'rzc', scatter_dimension=0...  35.6 us
    all_to_all x1, waiting for transfers between devices, body(): lax.all_to_all(send_qkv, REQ, split_axis=0, concat_axis=0, tiled=True)  30.7 us
    pallas_call x1, Pallas kernels, owner_attention(): pl.pallas_call(attention_kernel, out_shape=(jax.ShapeDtypeStruct((sources...  28.6 us
    all_gather x1, waiting for transfers between devices, body(): piece = lax.all_gather(mlp_in, 'rzc', axis=0, tiled=True)  24.1 us
    dot_general x1, matrix products, body(): both = jnp.dot(piece, gate_up_w, preferred_element_type=jnp.float32)  12.5 us
    all_to_all x1, waiting for transfers between devices, body(): lax.all_to_all(attn_rows.reshape(groups, quarter, -1), 'grp', split_axis=...  10 us
    dot_general x1, matrix products, body(): jnp.dot(hidden, jnp.concatenate(down_parts, axis=0), preferred_element_ty...  8.46 us
    all_to_all x1, starting transfers between devices, body(): lax.all_to_all(send_qkv, REQ, split_axis=0, concat_axis=0, tiled=True)  8.42 us
  transfers between devices with their start and end apart: 12, of which 8 were waited for; matrix products, arithmetic and copies ran while one was open for 20% of the time, Pallas kernels for 11%

profile of v14, /device:TPU:0, one launch (start us, length us, event | category | flops | bytes accessed | tf_op | source)
XLA Modules:
  0.0 265.2 jit_solution(14878162864698912469)
XLA Ops:
  7.2 3.2 %pad_maximum_fusion.1 = bf16[2048,512]{1,0:T(8,128)(2,1)} fusion(bf16[2048,256]{1,0:T(8,128)(2,1)} %param.24, bf16[2048,256]{1,0:T(8,128)(2,1)} %param.23), kind=kLoop, calls=%fused_computation.27 | loop fusion | flops 4194304 | bytes 4194304 | tf_op jit(solution)/shard_map/concatenate | solution.py:166
  10.5 2.2 fusion
  12.7 2.5 convolution_convert_fusion.1
  15.3 0.9 convolution_convert_fusion.2
  16.2 1.4 convolution_convert_fusion
  18.5 4.0 %gather_fusion = bf16[1024,768]{1,0:T(8,128)(2,1)S(1)} fusion(bf16[512,768]{1,0:T(8,128)(2,1)S(1)} %copy.21, s32[1024]{0:T(1024)S(1)} %broadcast_clamp_fusion), kind=kCustom, calls=%fused_computation | custom fusion | bytes 3149824 | tf_op jit(solution)/shard_map/jit(_take)/gather | solution.py:184
  22.6 1.4 broadcast_select_fusion
  23.9 8.4 %all-to-all-start = ((bf16[32,32,768]{2,1,0:T(8,128)(2,1)}), bf16[32,32,768]{2,1,0:T(8,128)(2,1)S(1)}, u32[]{:S(2)}, u32[]{:S(2)}) async-start(bf16[32,32,768]{2,1,0:T(8,128)(2,1)} %broadcast_select_fusion), calls=%async_computation | async-start | bytes 3145728 | tf_op jit(solution)/shard_map/all_to_all | solution.py:187
  32.4 1.6 collective-permute-start
  33.9 2.7 %collective-permute-start.1 = (bf16[512,2048]{1,0:T(8,128)(2,1)}, bf16[512,2048]{1,0:T(8,128)(2,1)}, u32[]{:S(2)}, u32[]{:S(2)}) collective-permute-start(bf16[512,2048]{1,0:T(8,128)(2,1)} %param.22), channel_id=1, source_target_pairs={{0,2},{1,3},{2,0},{3,1},{4,6},{5,7},{6,4},{7,5},{8,10},{9,11},{10,... | collective-permute-start | bytes 6291464 | tf_op jit(solution)/shard_map/ppermute | solution.py:173
  36.6 1.4 collective-permute-start.2
  38.2 1.9 multiply_cosine_fusion
  40.0 30.7 %all-to-all-done = bf16[32,32,768]{2,1,0:T(8,128)(2,1)S(1)} async-done(((bf16[32,32,768]{2,1,0:T(8,128)(2,1)}), bf16[32,32,768]{2,1,0:T(8,128)(2,1)S(1)}, u32[]{:S(2)}, u32[]{:S(2)}) %all-to-all-start) | async-done | bytes 1572896 | tf_op jit(solution)/shard_map/all_to_all | solution.py:187
  70.8 0.8 fusion.35
  71.8 1.0 fusion.36
  72.9 0.4 fusion.20
  73.3 0.3 pad_maximum_fusion.5
  73.6 1.3 copy.24
  74.9 1.3 convert_element_type.86.k_ref
  76.2 1.1 slice.32
  77.3 2.8 %reshape.161 = bf16[32,32,8,64]{3,2,1,0:T(8,128)(2,1)S(1)} reshape(bf16[32,32,512]{2,1,0:T(8,128)(2,1)} %slice.32) | data formatting | bytes 2097152 | tf_op jit(solution)/shard_map/reshape | solution.py:116
  80.1 1.9 fusion.4
  82.0 2.5 pad_maximum_fusion.2
  84.5 3.2 %convert_element_type.83.q_ref = bf16[32,32,512]{2,1,0:T(8,128)(2,1)S(1)} reshape(bf16[32,32,8,64]{3,2,1,0:T(8,128)(2,1)} %pad_maximum_fusion.2) | data formatting | bytes 2097152 | tf_op jit(solution)/shard_map/convert_element_type | solution.py:116
  87.8 0.9 copy-done.4
  88.7 28.6 %shard_map.175 = (bf16[32,32,512]{2,1,0:T(8,128)(2,1)S(1)}, bf16[512,16,128]{2,1,0:T(8,128)(2,1)}, bf16[512,16,128]{2,1,0:T(8,128)(2,1)}) custom-call(s32[512]{0:T(512)S(1)} %bitcast.26, s32[32]{0:T(128)S(1)} %bitcast.28, s32[32]{0:T(128)S(1)} %bitcast.29, bf16[32,32,512]{2,1,0:T(8,128)(2,1)S(1)} %convert_element_type.83.q_ref, ...), custom_call_target="tpu_custom_call" | custom-call | tf_op jit(solution)/shard_map/pallas_call | solution.py:125
  117.3 1.0 copy-done.3
  118.4 5.2 %all-to-all-start.1 = ((bf16[32,32,512]{2,1,0:T(8,128)(2,1)}), bf16[32,32,512]{2,1,0:T(8,128)(2,1)S(1)}, u32[]{:S(2)}, u32[]{:S(2)}) async-start(bf16[32,32,512]{2,1,0:T(8,128)(2,1)} %copy-done.3), calls=%async_computation.1 | async-start | bytes 2097152 | tf_op jit(solution)/shard_map/all_to_all | solution.py:195
  123.7 4.0 %collective-permute-done.1 = bf16[512,2048]{1,0:T(8,128)(2,1)} collective-permute-done((bf16[512,2048]{1,0:T(8,128)(2,1)}, bf16[512,2048]{1,0:T(8,128)(2,1)}, u32[]{:S(2)}, u32[]{:S(2)}) %collective-permute-start.1) | collective-permute-done | bytes 2097184 | tf_op jit(solution)/shard_map/ppermute | solution.py:173
  127.7 7.1 %pad_maximum_fusion = bf16[2048,2048]{1,0:T(8,128)(2,1)} fusion(bf16[512,2048]{1,0:T(8,128)(2,1)} %collective-permute-done.2, bf16[512,2048]{1,0:T(8,128)(2,1)} %collective-permute-done.1, bf16[512,2048]{1,0:T(8,128)(2,1)} %collective-permute-done, bf16[512,2048]{1,0:T(8,128)(2,1)} %param.22), kind=kLoop, calls=%fused_computation.2 | loop fusion | flops 33554432 | bytes 16777216 | tf_op jit(solution)/shard_map/concatenate | solution.py:196
  134.7 5.7 %all-to-all-done.1 = bf16[32,32,512]{2,1,0:T(8,128)(2,1)S(1)} async-done(((bf16[32,32,512]{2,1,0:T(8,128)(2,1)}), bf16[32,32,512]{2,1,0:T(8,128)(2,1)S(1)}, u32[]{:S(2)}, u32[]{:S(2)}) %all-to-all-start.1) | async-done | bytes 1048608 | tf_op jit(solution)/shard_map/all_to_all | solution.py:195
  140.5 2.0 gather_fusion.1
  142.4 0.9 broadcast_select_fusion.1
  143.4 4.3 %all-to-all-start.2 = ((bf16[4,128,512]{2,1,0:T(8,128)(2,1)}), bf16[4,128,512]{2,1,0:T(8,128)(2,1)S(1)}, u32[]{:S(2)}, u32[]{:S(2)}) async-start(bf16[4,128,512]{2,1,0:T(8,128)(2,1)} %broadcast_select_fusion.1), calls=%async_computation.2 | async-start | bytes 1048576 | tf_op jit(solution)/shard_map/all_to_all | solution.py:199
  147.7 10.0 %all-to-all-done.2 = bf16[4,128,512]{2,1,0:T(8,128)(2,1)S(1)} async-done(((bf16[4,128,512]{2,1,0:T(8,128)(2,1)}), bf16[4,128,512]{2,1,0:T(8,128)(2,1)S(1)}, u32[]{:S(2)}, u32[]{:S(2)}) %all-to-all-start.2) | async-done | bytes 524320 | tf_op jit(solution)/shard_map/all_to_all | solution.py:199
  157.7 4.9 %multiply_reduce_fusion = (f32[128]{0:T(128)S(1)}, f32[128,2048]{1,0:T(8,128)S(1)}) fusion(bf16[2048,2048]{1,0:T(8,128)(2,1)} %pad_maximum_fusion, bf16[128,512]{1,0:T(8,128)(2,1)S(1)} %get-tuple-element.40, bf16[128,512]{1,0:T(8,128)(2,1)S(1)} %get-tuple-element.41, bf16[128,512]{1,0:T(8,128)(2,1)S(1)} %get-tuple-element.42, ...), kind=kOutput, calls=%fused_computation.48 | convolution fusion | flops 1077149568 | bytes 10486276 | tf_op jit(solution)/shard_map/dot_general | solution.py:205
  162.6 0.9 multiply_convert_fusion.4
  163.8 2.5 collective-permute-start.4
  166.2 1.7 collective-permute-start.5
  167.9 24.1 %all-gather.5.cloned.1.call-done = bf16[1024,2048]{1,0:T(8,128)(2,1)} async-done(((bf16[128,2048]{1,0:T(8,128)(2,1)}), bf16[1024,2048]{1,0:T(8,128)(2,1)}) %all-gather.5.cloned.1.call-update) | async-done | bytes 4194320 | tf_op jit(solution)/shard_map/all_gather | solution.py:211
  192.1 12.5 %fusion.37 = f32[1024,2048]{1,0:T(8,128)S(1)} fusion(bf16[1024,2048]{1,0:T(8,128)(2,1)} %all-gather.5.cloned.1.call-done, bf16[2048,2048]{1,0:T(8,128)(2,1)} %all-gather.3.cloned.1.call-done), kind=kOutput, calls=%fused_computation.86 | convolution fusion | flops 8589934592 | bytes 20971520 | tf_op jit(solution)/shard_map/dot_general | solution.py:212
  204.5 1.5 multiply_convert_fusion.3
  206.0 0.3 pad_maximum_fusion.3
  206.3 5.7 %collective-permute-done.3 = bf16[256,2048]{1,0:T(8,128)(2,1)} collective-permute-done((bf16[256,2048]{1,0:T(8,128)(2,1)}, bf16[256,2048]{1,0:T(8,128)(2,1)}, u32[]{:S(2)}, u32[]{:S(2)}) %collective-permute-start.3) | collective-permute-done | bytes 1048608 | tf_op jit(solution)/shard_map/ppermute | solution.py:169
  212.0 0.6 collective-permute-done.5
  212.7 8.5 %fusion.15 = bf16[1024,2048]{1,0:T(8,128)(2,1)} fusion(bf16[1024,1024]{1,0:T(8,128)(2,1)S(1)} %pad_maximum_fusion.3, bf16[256,2048]{1,0:T(8,128)(2,1)} %collective-permute-done.5, bf16[256,2048]{1,0:T(8,128)(2,1)} %collective-permute-done.4, bf16[256,2048]{1,0:T(8,128)(2,1)} %collective-permute-done.3, bf16[256,2048]{1,0:T(8,128)(2,1)S(1)} %copy-done.11), kind=kOutput, calls=%fused_computation.24 | convolution fusion | flops 4313841664 | bytes 10485760 | tf_op jit(solution)/shard_map/dot_general | solution.py:223
  221.1 35.6 %reduce-scatter.2.cloned.1.call-done = bf16[128,2048]{1,0:T(8,128)(2,1)} async-done(((bf16[1024,2048]{1,0:T(8,128)(2,1)}), bf16[128,2048]{1,0:T(8,128)(2,1)}) %reduce-scatter.2.cloned.1.call-update) | async-done | bytes 524304 | tf_op jit(solution)/shard_map/reduce_scatter | solution.py:226
  256.7 2.0 add_convert_fusion
  (56 shorter events, 1.5 us)
Async XLA Ops:
  7.2 9.1 %copy-start = (bf16[2048,512]{1,0:T(8,128)(2,1)S(1)}, bf16[2048,512]{1,0:T(8,128)(2,1)}, u32[]{:S(2)}) copy-start(bf16[2048,512]{1,0:T(8,128)(2,1)} %param.19) | copy-start | bytes 6291460
  7.2 5.5 %copy-start.14 = (f32[2048]{0:T(1024)S(1)}, f32[2048]{0:T(1024)}, u32[]{:S(2)}) copy-start(f32[2048]{0:T(1024)} %param.17) | copy-start | bytes 24580
  7.2 5.5 %copy-start.12 = (bf16[2048,128]{1,0:T(8,128)(2,1)S(1)}, bf16[2048,128]{1,0:T(8,128)(2,1)}, u32[]{:S(2)}) copy-start(bf16[2048,128]{1,0:T(8,128)(2,1)} %param.21) | copy-start | bytes 1572868
  7.2 133.3 %all-gather.3.cloned.1.call-start = ((), (), s32[]{:S(2)}) async-start(), calls=%async_computation.4 | async-start | bytes 10485760 | tf_op jit(solution)/shard_map/all_gather | solution.py:166
  10.4 4.8 %copy-start.13 = (bf16[2048,128]{1,0:T(8,128)(2,1)S(1)}, bf16[2048,128]{1,0:T(8,128)(2,1)}, u32[]{:S(2)}) copy-start(bf16[2048,128]{1,0:T(8,128)(2,1)} %param.20) | copy-start | bytes 1572868
  10.5 4.8 %copy-start.8 = (bf16[512,2048]{1,0:T(8,128)(2,1)S(1)}, bf16[512,2048]{1,0:T(8,128)(2,1)}, u32[]{:S(2)}) copy-start(bf16[512,2048]{1,0:T(8,128)(2,1)} %param.16) | copy-start | bytes 6291460
  16.2 1.8 copy-start.9
  22.5 15.6 %copy-start.6 = (s32[1,32]{1,0:T(1,128)S(1)}, s32[1,32]{1,0:T(1,128)}, u32[]{:S(2)}) copy-start(s32[1,32]{1,0:T(1,128)} %param.30) | copy-start | bytes 388
  23.9 46.9 %all-to-all-start = ((bf16[32,32,768]{2,1,0:T(8,128)(2,1)}), bf16[32,32,768]{2,1,0:T(8,128)(2,1)S(1)}, u32[]{:S(2)}, u32[]{:S(2)}) async-start(bf16[32,32,768]{2,1,0:T(8,128)(2,1)} %broadcast_select_fusion), calls=%async_computation | async-start | bytes 3145728 | tf_op jit(solution)/shard_map/all_to_all | solution.py:187
  32.4 91.3 %collective-permute-start = (bf16[512,2048]{1,0:T(8,128)(2,1)}, bf16[512,2048]{1,0:T(8,128)(2,1)}, u32[]{:S(2)}, u32[]{:S(2)}) collective-permute-start(bf16[512,2048]{1,0:T(8,128)(2,1)} %param.22), channel_id=1, source_target_pairs={{0,1},{1,2},{2,3},{3,0},{4,5},{5,6},{6,7},{7,4},{8,9},{9,10},{10,1... | collective-permute-start | bytes 6291464 | tf_op jit(solution)/shard_map/ppermute | solution.py:173
  33.9 93.8 %collective-permute-start.1 = (bf16[512,2048]{1,0:T(8,128)(2,1)}, bf16[512,2048]{1,0:T(8,128)(2,1)}, u32[]{:S(2)}, u32[]{:S(2)}) collective-permute-start(bf16[512,2048]{1,0:T(8,128)(2,1)} %param.22), channel_id=1, source_target_pairs={{0,2},{1,3},{2,0},{3,1},{4,6},{5,7},{6,4},{7,5},{8,10},{9,11},{10,... | collective-permute-start | bytes 6291464 | tf_op jit(solution)/shard_map/ppermute | solution.py:173
  36.6 91.0 %collective-permute-start.2 = (bf16[512,2048]{1,0:T(8,128)(2,1)}, bf16[512,2048]{1,0:T(8,128)(2,1)}, u32[]{:S(2)}, u32[]{:S(2)}) collective-permute-start(bf16[512,2048]{1,0:T(8,128)(2,1)} %param.22), channel_id=1, source_target_pairs={{0,3},{1,0},{2,1},{3,2},{4,7},{5,4},{6,5},{7,6},{8,11},{9,8},{10,9... | collective-permute-start | bytes 6291464 | tf_op jit(solution)/shard_map/ppermute | solution.py:173
  82.0 5.7 %copy-start.2 = (bf16[512,16,128]{2,1,0:T(8,128)(2,1)S(1)}, bf16[512,16,128]{2,1,0:T(8,128)(2,1)}, u32[]{:S(2)}) copy-start(bf16[512,16,128]{2,1,0:T(8,128)(2,1)} %ck_ref.1) | copy-start | bytes 6291460
  82.0 5.7 %copy-start.5 = (s32[1,512]{1,0:T(1,128)S(1)}, s32[1,512]{1,0:T(1,128)}, u32[]{:S(2)}) copy-start(s32[1,512]{1,0:T(1,128)} %param.31) | copy-start | bytes 6148
  82.0 5.7 %copy-start.7 = (s32[1,32]{1,0:T(1,128)S(1)}, s32[1,32]{1,0:T(1,128)}, u32[]{:S(2)}) copy-start(s32[1,32]{1,0:T(1,128)} %param.29) | copy-start | bytes 388
  87.8 1.0 copy-start.4
  117.3 1.1 copy-start.3
  118.4 22.1 %all-to-all-start.1 = ((bf16[32,32,512]{2,1,0:T(8,128)(2,1)}), bf16[32,32,512]{2,1,0:T(8,128)(2,1)S(1)}, u32[]{:S(2)}, u32[]{:S(2)}) async-start(bf16[32,32,512]{2,1,0:T(8,128)(2,1)} %copy-done.3), calls=%async_computation.1 | async-start | bytes 2097152 | tf_op jit(solution)/shard_map/all_to_all | solution.py:195
  143.4 14.3 %all-to-all-start.2 = ((bf16[4,128,512]{2,1,0:T(8,128)(2,1)}), bf16[4,128,512]{2,1,0:T(8,128)(2,1)S(1)}, u32[]{:S(2)}, u32[]{:S(2)}) async-start(bf16[4,128,512]{2,1,0:T(8,128)(2,1)} %broadcast_select_fusion.1), calls=%async_computation.2 | async-start | bytes 1048576 | tf_op jit(solution)/shard_map/all_to_all | solution.py:199
  147.7 44.4 %all-gather.5.cloned.1.call-start = ((), (), s32[]{:S(2)}) async-start(), calls=%async_computation.5 | async-start | bytes 4718592 | tf_op jit(solution)/shard_map/all_gather | solution.py:211
  157.7 4.9 %copy-start.10 = (f32[2048]{0:T(1024)S(1)}, f32[2048]{0:T(1024)}, u32[]{:S(2)}) copy-start(f32[2048]{0:T(1024)} %param.18) | copy-start | bytes 24580
  163.6 93.1 %reduce-scatter.2.cloned.1.call-start = ((), (), s32[]{:S(2)}) async-start(), calls=%async_computation.6 | async-start | bytes 4718592 | tf_op jit(solution)/shard_map/reduce_scatter | solution.py:226
  163.7 48.4 %collective-permute-start.3 = (bf16[256,2048]{1,0:T(8,128)(2,1)}, bf16[256,2048]{1,0:T(8,128)(2,1)}, u32[]{:S(2)}, u32[]{:S(2)}) collective-permute-start(bf16[256,2048]{1,0:T(8,128)(2,1)} %param.25), channel_id=1, source_target_pairs={{0,32},{32,64},{64,96},{96,0},{1,33},{33,65},{65,97},{97,1},{2,34}... | collective-permute-start | bytes 3145736 | tf_op jit(solution)/shard_map/ppermute | solution.py:169
  163.8 48.3 %collective-permute-start.4 = (bf16[256,2048]{1,0:T(8,128)(2,1)}, bf16[256,2048]{1,0:T(8,128)(2,1)}, u32[]{:S(2)}, u32[]{:S(2)}) collective-permute-start(bf16[256,2048]{1,0:T(8,128)(2,1)} %param.25), channel_id=1, source_target_pairs={{0,64},{32,96},{64,0},{96,32},{1,65},{33,97},{65,1},{97,33},{2,66}... | collective-permute-start | bytes 3145736 | tf_op jit(solution)/shard_map/ppermute | solution.py:169
  166.2 46.5 %collective-permute-start.5 = (bf16[256,2048]{1,0:T(8,128)(2,1)}, bf16[256,2048]{1,0:T(8,128)(2,1)}, u32[]{:S(2)}, u32[]{:S(2)}) collective-permute-start(bf16[256,2048]{1,0:T(8,128)(2,1)} %param.25), channel_id=1, source_target_pairs={{0,96},{32,0},{64,32},{96,64},{1,97},{33,1},{65,33},{97,65},{2,98}... | collective-permute-start | bytes 3145736 | tf_op jit(solution)/shard_map/ppermute | solution.py:169
  206.0 6.6 %copy-start.11 = (bf16[256,2048]{1,0:T(8,128)(2,1)S(1)}, bf16[256,2048]{1,0:T(8,128)(2,1)}, u32[]{:S(2)}) copy-start(bf16[256,2048]{1,0:T(8,128)(2,1)} %param.25) | copy-start | bytes 3145732
  212.7 46.0 %copy-start.1 = (bf16[2048,512]{1,0:T(8,128)(2,1)S(1)}, bf16[2048,512]{1,0:T(8,128)(2,1)}, u32[]{:S(2)}) copy-start(bf16[2048,512]{1,0:T(8,128)(2,1)} %param.19) | copy-start | bytes 6291460
Sparse Core Ops, SparseCore 0:
  10.6 102.4 all-gather.2
  163.7 28.2 all-gather.4
  221.3 35.4 reduce-scatter.1

commit v15 on v13

--- a/solution.py
+++ b/solution.py
@@ -62,10 +62,9 @@
     def per_source(s, carry):
         prior = prior_ref[s]
         length = len_ref[s]
-        for i in range(MAXP):
-            page = table_ref[s * MAXP + i]
-            kbuf[i * PAGE:(i + 1) * PAGE, :] = ck_ref[page]
-            vbuf[i * PAGE:(i + 1) * PAGE, :] = cv_ref[page]
+        pages = [table_ref[s * MAXP + i] for i in range(MAXP)]
+        old_keys = jnp.concatenate([ck_ref[page] for page in pages], axis=0)
+        old_values = jnp.concatenate([cv_ref[page] for page in pages], axis=0)
         j_col = lax.broadcasted_iota(jnp.int32, (CONTEXT, pair_rows), 0)
         t_row = lax.broadcasted_iota(jnp.int32, (CONTEXT, pair_rows), 1)
         select = jnp.logical_and(j_col == prior + t_row, t_row < length).astype(jnp.bfloat16)
@@ -73,8 +72,8 @@
         fresh = jnp.logical_and(j_only >= prior, j_only < prior + length)
         k_new = jnp.dot(select, k_ref[s], preferred_element_type=jnp.float32).astype(jnp.bfloat16)
         v_new = jnp.dot(select, v_ref[s], preferred_element_type=jnp.float32).astype(jnp.bfloat16)
-        keys = jnp.where(fresh, k_new, kbuf[...])
-        values = jnp.where(fresh, v_new, vbuf[...])
+        keys = jnp.where(fresh, k_new, old_keys)
+        values = jnp.where(fresh, v_new, old_values)
         for i in range(MAXP):
             page = table_ref[s * MAXP + i]
             nk_ref[page] = keys[i * PAGE:(i + 1) * PAGE, :]

time: 266 us -> 266 us (level)
  no operation moved by 1% of the time
where the time goes in v15:
time: 266 us; the launch traced here: 265 us
  waiting for transfers between devices  116 us (44%)
  matrix products  30.8 us (12%)
  Pallas kernels  28.3 us (11%)
  starting transfers between devices  28 us (11%)
  other arithmetic  26.9 us (10%)
  local copies, waits for them, and re-layouts  20.8 us (8%)
  between operations  14.1 us (5%)
    reduce_scatter x1, waiting for transfers between devices, body(): lax.psum_scatter(partial.astype(jnp.bfloat16), 'rzc', scatter_dimension=0...  35.2 us
    all_to_all x1, waiting for transfers between devices, body(): lax.all_to_all(send_qkv, REQ, split_axis=0, concat_axis=0, tiled=True)  30.7 us
    pallas_call x1, Pallas kernels, owner_attention(): pl.pallas_call(attention_kernel, out_shape=(jax.ShapeDtypeStruct((sources...  28.3 us
    all_gather x1, waiting for transfers between devices, body(): piece = lax.all_gather(mlp_in, 'rzc', axis=0, tiled=True)  24.1 us
    dot_general x1, matrix products, body(): both = jnp.dot(piece, gate_up_w, preferred_element_type=jnp.float32)  12.5 us
    all_to_all x1, waiting for transfers between devices, body(): lax.all_to_all(attn_rows.reshape(groups, quarter, -1), 'grp', split_axis=...  10 us
    dot_general x1, matrix products, body(): jnp.dot(hidden, jnp.concatenate(down_parts, axis=0), preferred_element_ty...  8.49 us
    all_to_all x1, starting transfers between devices, body(): lax.all_to_all(send_qkv, REQ, split_axis=0, concat_axis=0, tiled=True)  8.41 us
  transfers between devices with their start and end apart: 12, of which 8 were waited for; matrix products, arithmetic and copies ran while one was open for 20% of the time, Pallas kernels for 11%

profile of v15, /device:TPU:0, one launch (start us, length us, event | category | flops | bytes accessed | tf_op | source)
XLA Modules:
  0.0 265.2 jit_solution(15258766080236441570)
XLA Ops:
  7.2 3.2 %pad_maximum_fusion.1 = bf16[2048,512]{1,0:T(8,128)(2,1)} fusion(bf16[2048,256]{1,0:T(8,128)(2,1)} %param.24, bf16[2048,256]{1,0:T(8,128)(2,1)} %param.23), kind=kLoop, calls=%fused_computation.27 | loop fusion | flops 4194304 | bytes 4194304 | tf_op jit(solution)/shard_map/concatenate | solution.py:165
  10.5 2.2 fusion
  12.7 2.5 convolution_convert_fusion.1
  15.3 0.9 convolution_convert_fusion.2
  16.3 1.4 convolution_convert_fusion
  18.5 4.0 %gather_fusion = bf16[1024,768]{1,0:T(8,128)(2,1)S(1)} fusion(bf16[512,768]{1,0:T(8,128)(2,1)S(1)} %copy.21, s32[1024]{0:T(1024)S(1)} %broadcast_clamp_fusion), kind=kCustom, calls=%fused_computation | custom fusion | bytes 3149824 | tf_op jit(solution)/shard_map/jit(_take)/gather | solution.py:183
  22.6 1.4 broadcast_select_fusion
  23.9 8.4 %all-to-all-start = ((bf16[32,32,768]{2,1,0:T(8,128)(2,1)}), bf16[32,32,768]{2,1,0:T(8,128)(2,1)S(1)}, u32[]{:S(2)}, u32[]{:S(2)}) async-start(bf16[32,32,768]{2,1,0:T(8,128)(2,1)} %broadcast_select_fusion), calls=%async_computation | async-start | bytes 3145728 | tf_op jit(solution)/shard_map/all_to_all | solution.py:186
  32.4 1.6 collective-permute-start
  33.9 2.7 %collective-permute-start.1 = (bf16[512,2048]{1,0:T(8,128)(2,1)}, bf16[512,2048]{1,0:T(8,128)(2,1)}, u32[]{:S(2)}, u32[]{:S(2)}) collective-permute-start(bf16[512,2048]{1,0:T(8,128)(2,1)} %param.22), channel_id=1, source_target_pairs={{0,2},{1,3},{2,0},{3,1},{4,6},{5,7},{6,4},{7,5},{8,10},{9,11},{10,... | collective-permute-start | bytes 6291464 | tf_op jit(solution)/shard_map/ppermute | solution.py:172
  36.7 1.4 collective-permute-start.2
  38.2 1.9 multiply_cosine_fusion
  40.1 30.7 %all-to-all-done = bf16[32,32,768]{2,1,0:T(8,128)(2,1)S(1)} async-done(((bf16[32,32,768]{2,1,0:T(8,128)(2,1)}), bf16[32,32,768]{2,1,0:T(8,128)(2,1)S(1)}, u32[]{:S(2)}, u32[]{:S(2)}) %all-to-all-start) | async-done | bytes 1572896 | tf_op jit(solution)/shard_map/all_to_all | solution.py:186
  70.8 0.8 fusion.46
  71.8 1.0 fusion.47
  72.9 0.4 fusion.27
  73.3 0.3 pad_maximum_fusion.5
  73.6 1.3 copy.24
  74.9 1.3 convert_element_type.86.k_ref
  76.3 1.1 slice.64
  77.3 2.8 %reshape.161 = bf16[32,32,8,64]{3,2,1,0:T(8,128)(2,1)S(1)} reshape(bf16[32,32,512]{2,1,0:T(8,128)(2,1)} %slice.64) | data formatting | bytes 2097152 | tf_op jit(solution)/shard_map/reshape | solution.py:115
  80.1 1.9 fusion.4
  82.1 2.5 pad_maximum_fusion.2
  84.5 3.2 %convert_element_type.83.q_ref = bf16[32,32,512]{2,1,0:T(8,128)(2,1)S(1)} reshape(bf16[32,32,8,64]{3,2,1,0:T(8,128)(2,1)} %pad_maximum_fusion.2) | data formatting | bytes 2097152 | tf_op jit(solution)/shard_map/convert_element_type | solution.py:115
  87.8 0.9 copy-done.4
  88.7 28.3 %shard_map.175 = (bf16[32,32,512]{2,1,0:T(8,128)(2,1)S(1)}, bf16[512,16,128]{2,1,0:T(8,128)(2,1)}, bf16[512,16,128]{2,1,0:T(8,128)(2,1)}) custom-call(s32[512]{0:T(512)S(1)} %bitcast.25, s32[32]{0:T(128)S(1)} %bitcast.27, s32[32]{0:T(128)S(1)} %bitcast.28, bf16[32,32,512]{2,1,0:T(8,128)(2,1)S(1)} %convert_element_type.83.q_ref, ...), custom_call_target="tpu_custom_call" | custom-call | tf_op jit(solution)/shard_map/pallas_call | solution.py:124
  117.0 1.0 copy-done.3
  118.1 5.2 %all-to-all-start.1 = ((bf16[32,32,512]{2,1,0:T(8,128)(2,1)}), bf16[32,32,512]{2,1,0:T(8,128)(2,1)S(1)}, u32[]{:S(2)}, u32[]{:S(2)}) async-start(bf16[32,32,512]{2,1,0:T(8,128)(2,1)} %copy-done.3), calls=%async_computation.1 | async-start | bytes 2097152 | tf_op jit(solution)/shard_map/all_to_all | solution.py:194
  123.3 4.4 %collective-permute-done.1 = bf16[512,2048]{1,0:T(8,128)(2,1)} collective-permute-done((bf16[512,2048]{1,0:T(8,128)(2,1)}, bf16[512,2048]{1,0:T(8,128)(2,1)}, u32[]{:S(2)}, u32[]{:S(2)}) %collective-permute-start.1) | collective-permute-done | bytes 2097184 | tf_op jit(solution)/shard_map/ppermute | solution.py:172
  127.7 7.0 %pad_maximum_fusion = bf16[2048,2048]{1,0:T(8,128)(2,1)} fusion(bf16[512,2048]{1,0:T(8,128)(2,1)} %collective-permute-done.2, bf16[512,2048]{1,0:T(8,128)(2,1)} %collective-permute-done.1, bf16[512,2048]{1,0:T(8,128)(2,1)} %collective-permute-done, bf16[512,2048]{1,0:T(8,128)(2,1)} %param.22), kind=kLoop, calls=%fused_computation.2 | loop fusion | flops 33554432 | bytes 16777216 | tf_op jit(solution)/shard_map/concatenate | solution.py:195
  134.7 5.3 %all-to-all-done.1 = bf16[32,32,512]{2,1,0:T(8,128)(2,1)S(1)} async-done(((bf16[32,32,512]{2,1,0:T(8,128)(2,1)}), bf16[32,32,512]{2,1,0:T(8,128)(2,1)S(1)}, u32[]{:S(2)}, u32[]{:S(2)}) %all-to-all-start.1) | async-done | bytes 1048608 | tf_op jit(solution)/shard_map/all_to_all | solution.py:194
  140.0 2.0 gather_fusion.1
  142.0 0.9 broadcast_select_fusion.1
  143.0 4.4 %all-to-all-start.2 = ((bf16[4,128,512]{2,1,0:T(8,128)(2,1)}), bf16[4,128,512]{2,1,0:T(8,128)(2,1)S(1)}, u32[]{:S(2)}, u32[]{:S(2)}) async-start(bf16[4,128,512]{2,1,0:T(8,128)(2,1)} %broadcast_select_fusion.1), calls=%async_computation.2 | async-start | bytes 1048576 | tf_op jit(solution)/shard_map/all_to_all | solution.py:198
  147.3 10.0 %all-to-all-done.2 = bf16[4,128,512]{2,1,0:T(8,128)(2,1)S(1)} async-done(((bf16[4,128,512]{2,1,0:T(8,128)(2,1)}), bf16[4,128,512]{2,1,0:T(8,128)(2,1)S(1)}, u32[]{:S(2)}, u32[]{:S(2)}) %all-to-all-start.2) | async-done | bytes 524320 | tf_op jit(solution)/shard_map/all_to_all | solution.py:198
  157.4 4.9 %multiply_reduce_fusion = (f32[128]{0:T(128)S(1)}, f32[128,2048]{1,0:T(8,128)S(1)}) fusion(bf16[2048,2048]{1,0:T(8,128)(2,1)} %pad_maximum_fusion, bf16[128,512]{1,0:T(8,128)(2,1)S(1)} %get-tuple-element.44, bf16[128,512]{1,0:T(8,128)(2,1)S(1)} %get-tuple-element.45, bf16[128,512]{1,0:T(8,128)(2,1)S(1)} %get-tuple-element.46, ...), kind=kOutput, calls=%fused_computation.59 | convolution fusion | flops 1077149568 | bytes 10486276 | tf_op jit(solution)/shard_map/dot_general | solution.py:204
  162.3 0.9 multiply_convert_fusion
  163.4 2.5 collective-permute-start.4
  165.9 1.7 collective-permute-start.5
  167.6 24.1 %all-gather.5.cloned.1.call-done = bf16[1024,2048]{1,0:T(8,128)(2,1)} async-done(((bf16[128,2048]{1,0:T(8,128)(2,1)}), bf16[1024,2048]{1,0:T(8,128)(2,1)}) %all-gather.5.cloned.1.call-update) | async-done | bytes 4194320 | tf_op jit(solution)/shard_map/all_gather | solution.py:210
  191.7 12.5 %fusion.48 = f32[1024,2048]{1,0:T(8,128)S(1)} fusion(bf16[1024,2048]{1,0:T(8,128)(2,1)} %all-gather.5.cloned.1.call-done, bf16[2048,2048]{1,0:T(8,128)(2,1)} %all-gather.3.cloned.1.call-done), kind=kOutput, calls=%fused_computation.101 | convolution fusion | flops 8589934592 | bytes 20971520 | tf_op jit(solution)/shard_map/dot_general | solution.py:211
  204.2 1.4 fusion.33
  205.9 5.7 %collective-permute-done.3 = bf16[256,2048]{1,0:T(8,128)(2,1)S(1)} collective-permute-done((bf16[256,2048]{1,0:T(8,128)(2,1)}, bf16[256,2048]{1,0:T(8,128)(2,1)S(1)}, u32[]{:S(2)}, u32[]{:S(2)}) %collective-permute-start.3) | collective-permute-done | bytes 1048608 | tf_op jit(solution)/shard_map/ppermute | solution.py:168
  211.6 0.7 collective-permute-done.5
  212.6 0.3 copy-done.13
  212.9 8.5 %fusion.15 = bf16[1024,2048]{1,0:T(8,128)(2,1)} fusion(bf16[256,2048]{1,0:T(8,128)(2,1)} %collective-permute-done.5, bf16[256,2048]{1,0:T(8,128)(2,1)} %copy-done.13, bf16[256,2048]{1,0:T(8,128)(2,1)} %copy-done.12, bf16[256,2048]{1,0:T(8,128)(2,1)S(1)} %copy-done.11, bf16[1024,256]{1,0:T(8,128)(2,1)S(1)} %get-tuple-element.36, ...), kind=kOutput, calls=%fused_computation.24 | convolution fusion | flops 4322230272 | bytes 10485760 | tf_op jit(solution)/shard_map/dot_general | solution.py:232
  221.5 35.2 %reduce-scatter.2.cloned.1.call-done = bf16[128,2048]{1,0:T(8,128)(2,1)} async-done(((bf16[1024,2048]{1,0:T(8,128)(2,1)}), bf16[128,2048]{1,0:T(8,128)(2,1)}) %reduce-scatter.2.cloned.1.call-update) | async-done | bytes 524304 | tf_op jit(solution)/shard_map/reduce_scatter | solution.py:235
  256.7 2.0 add_convert_fusion
  (61 shorter events, 2.1 us)
Async XLA Ops:
  7.2 9.1 %copy-start = (bf16[2048,512]{1,0:T(8,128)(2,1)S(1)}, bf16[2048,512]{1,0:T(8,128)(2,1)}, u32[]{:S(2)}) copy-start(bf16[2048,512]{1,0:T(8,128)(2,1)} %param.19) | copy-start | bytes 6291460
  7.2 5.5 %copy-start.16 = (f32[2048]{0:T(1024)S(1)}, f32[2048]{0:T(1024)}, u32[]{:S(2)}) copy-start(f32[2048]{0:T(1024)} %param.17) | copy-start | bytes 24580
  7.2 5.5 %copy-start.14 = (bf16[2048,128]{1,0:T(8,128)(2,1)S(1)}, bf16[2048,128]{1,0:T(8,128)(2,1)}, u32[]{:S(2)}) copy-start(bf16[2048,128]{1,0:T(8,128)(2,1)} %param.21) | copy-start | bytes 1572868
  7.2 132.8 %all-gather.3.cloned.1.call-start = ((), (), s32[]{:S(2)}) async-start(), calls=%async_computation.4 | async-start | bytes 10485760 | tf_op jit(solution)/shard_map/all_gather | solution.py:165
  10.4 4.8 %copy-start.15 = (bf16[2048,128]{1,0:T(8,128)(2,1)S(1)}, bf16[2048,128]{1,0:T(8,128)(2,1)}, u32[]{:S(2)}) copy-start(bf16[2048,128]{1,0:T(8,128)(2,1)} %param.20) | copy-start | bytes 1572868
  10.5 4.8 %copy-start.8 = (bf16[512,2048]{1,0:T(8,128)(2,1)S(1)}, bf16[512,2048]{1,0:T(8,128)(2,1)}, u32[]{:S(2)}) copy-start(bf16[512,2048]{1,0:T(8,128)(2,1)} %param.16) | copy-start | bytes 6291460
  16.2 1.8 copy-start.9
  22.5 15.6 %copy-start.6 = (s32[1,32]{1,0:T(1,128)S(1)}, s32[1,32]{1,0:T(1,128)}, u32[]{:S(2)}) copy-start(s32[1,32]{1,0:T(1,128)} %param.30) | copy-start | bytes 388
  23.9 46.8 %all-to-all-start = ((bf16[32,32,768]{2,1,0:T(8,128)(2,1)}), bf16[32,32,768]{2,1,0:T(8,128)(2,1)S(1)}, u32[]{:S(2)}, u32[]{:S(2)}) async-start(bf16[32,32,768]{2,1,0:T(8,128)(2,1)} %broadcast_select_fusion), calls=%async_computation | async-start | bytes 3145728 | tf_op jit(solution)/shard_map/all_to_all | solution.py:186
  32.4 90.9 %collective-permute-start = (bf16[512,2048]{1,0:T(8,128)(2,1)}, bf16[512,2048]{1,0:T(8,128)(2,1)}, u32[]{:S(2)}, u32[]{:S(2)}) collective-permute-start(bf16[512,2048]{1,0:T(8,128)(2,1)} %param.22), channel_id=1, source_target_pairs={{0,1},{1,2},{2,3},{3,0},{4,5},{5,6},{6,7},{7,4},{8,9},{9,10},{10,1... | collective-permute-start | bytes 6291464 | tf_op jit(solution)/shard_map/ppermute | solution.py:172
  33.9 93.8 %collective-permute-start.1 = (bf16[512,2048]{1,0:T(8,128)(2,1)}, bf16[512,2048]{1,0:T(8,128)(2,1)}, u32[]{:S(2)}, u32[]{:S(2)}) collective-permute-start(bf16[512,2048]{1,0:T(8,128)(2,1)} %param.22), channel_id=1, source_target_pairs={{0,2},{1,3},{2,0},{3,1},{4,6},{5,7},{6,4},{7,5},{8,10},{9,11},{10,... | collective-permute-start | bytes 6291464 | tf_op jit(solution)/shard_map/ppermute | solution.py:172
  36.7 91.0 %collective-permute-start.2 = (bf16[512,2048]{1,0:T(8,128)(2,1)}, bf16[512,2048]{1,0:T(8,128)(2,1)}, u32[]{:S(2)}, u32[]{:S(2)}) collective-permute-start(bf16[512,2048]{1,0:T(8,128)(2,1)} %param.22), channel_id=1, source_target_pairs={{0,3},{1,0},{2,1},{3,2},{4,7},{5,4},{6,5},{7,6},{8,11},{9,8},{10,9... | collective-permute-start | bytes 6291464 | tf_op jit(solution)/shard_map/ppermute | solution.py:172
  82.0 5.7 %copy-start.2 = (bf16[512,16,128]{2,1,0:T(8,128)(2,1)S(1)}, bf16[512,16,128]{2,1,0:T(8,128)(2,1)}, u32[]{:S(2)}) copy-start(bf16[512,16,128]{2,1,0:T(8,128)(2,1)} %ck_ref.1) | copy-start | bytes 6291460
  82.0 5.7 %copy-start.5 = (s32[1,512]{1,0:T(1,128)S(1)}, s32[1,512]{1,0:T(1,128)}, u32[]{:S(2)}) copy-start(s32[1,512]{1,0:T(1,128)} %param.31) | copy-start | bytes 6148
  82.0 5.7 %copy-start.7 = (s32[1,32]{1,0:T(1,128)S(1)}, s32[1,32]{1,0:T(1,128)}, u32[]{:S(2)}) copy-start(s32[1,32]{1,0:T(1,128)} %param.29) | copy-start | bytes 388
  87.8 1.0 copy-start.4
  117.0 1.0 copy-start.3
  118.1 22.0 %all-to-all-start.1 = ((bf16[32,32,512]{2,1,0:T(8,128)(2,1)}), bf16[32,32,512]{2,1,0:T(8,128)(2,1)S(1)}, u32[]{:S(2)}, u32[]{:S(2)}) async-start(bf16[32,32,512]{2,1,0:T(8,128)(2,1)} %copy-done.3), calls=%async_computation.1 | async-start | bytes 2097152 | tf_op jit(solution)/shard_map/all_to_all | solution.py:194
  143.0 14.4 %all-to-all-start.2 = ((bf16[4,128,512]{2,1,0:T(8,128)(2,1)}), bf16[4,128,512]{2,1,0:T(8,128)(2,1)S(1)}, u32[]{:S(2)}, u32[]{:S(2)}) async-start(bf16[4,128,512]{2,1,0:T(8,128)(2,1)} %broadcast_select_fusion.1), calls=%async_computation.2 | async-start | bytes 1048576 | tf_op jit(solution)/shard_map/all_to_all | solution.py:198
  147.3 44.4 %all-gather.5.cloned.1.call-start = ((), (), s32[]{:S(2)}) async-start(), calls=%async_computation.5 | async-start | bytes 4718592 | tf_op jit(solution)/shard_map/all_gather | solution.py:210
  157.4 4.9 %copy-start.10 = (f32[2048]{0:T(1024)S(1)}, f32[2048]{0:T(1024)}, u32[]{:S(2)}) copy-start(f32[2048]{0:T(1024)} %param.18) | copy-start | bytes 24580
  163.3 93.4 %reduce-scatter.2.cloned.1.call-start = ((), (), s32[]{:S(2)}) async-start(), calls=%async_computation.6 | async-start | bytes 4718592 | tf_op jit(solution)/shard_map/reduce_scatter | solution.py:235
  163.3 48.3 %collective-permute-start.3 = (bf16[256,2048]{1,0:T(8,128)(2,1)}, bf16[256,2048]{1,0:T(8,128)(2,1)S(1)}, u32[]{:S(2)}, u32[]{:S(2)}) collective-permute-start(bf16[256,2048]{1,0:T(8,128)(2,1)} %param.25), channel_id=1, source_target_pairs={{0,32},{32,64},{64,96},{96,0},{1,33},{33,65},{65,97},{97,1},{2,34}... | collective-permute-start | bytes 3145736 | tf_op jit(solution)/shard_map/ppermute | solution.py:168
  163.4 48.2 %collective-permute-start.4 = (bf16[256,2048]{1,0:T(8,128)(2,1)}, bf16[256,2048]{1,0:T(8,128)(2,1)S(1)}, u32[]{:S(2)}, u32[]{:S(2)}) collective-permute-start(bf16[256,2048]{1,0:T(8,128)(2,1)} %param.25), channel_id=1, source_target_pairs={{0,64},{32,96},{64,0},{96,32},{1,65},{33,97},{65,1},{97,33},{2,66}... | collective-permute-start | bytes 3145736 | tf_op jit(solution)/shard_map/ppermute | solution.py:168
  165.9 46.5 %collective-permute-start.5 = (bf16[256,2048]{1,0:T(8,128)(2,1)}, bf16[256,2048]{1,0:T(8,128)(2,1)}, u32[]{:S(2)}, u32[]{:S(2)}) collective-permute-start(bf16[256,2048]{1,0:T(8,128)(2,1)} %param.25), channel_id=1, source_target_pairs={{0,96},{32,0},{64,32},{96,64},{1,97},{33,1},{65,33},{97,65},{2,98}... | collective-permute-start | bytes 3145736 | tf_op jit(solution)/shard_map/ppermute | solution.py:168
  205.6 7.4 %copy-start.11 = (bf16[256,2048]{1,0:T(8,128)(2,1)S(1)}, bf16[256,2048]{1,0:T(8,128)(2,1)}, u32[]{:S(2)}) copy-start(bf16[256,2048]{1,0:T(8,128)(2,1)} %param.25) | copy-start | bytes 3145732
  211.6 1.0 copy-start.12
  211.6 1.3 copy-start.13
  212.9 45.7 %copy-start.1 = (bf16[2048,512]{1,0:T(8,128)(2,1)S(1)}, bf16[2048,512]{1,0:T(8,128)(2,1)}, u32[]{:S(2)}) copy-start(bf16[2048,512]{1,0:T(8,128)(2,1)} %param.19) | copy-start | bytes 6291460
Sparse Core Ops, SparseCore 0:
  10.6 102.4 all-gather.2
  163.4 28.2 all-gather.4
  221.6 35.0 reduce-scatter.1
